TPU v7x, 32 devices: a whole 2x2x4 slice. The times are simulated.
32 devices in a mesh: groups: 2 (over x), adapter: 8 (over z, y), tensor: 2 (over core).
Axes of the slice: x: 2, y: 2, z: 4, core: 2. Of those that a mesh axis runs over, the one named last changes fastest.
Arguments:
- acts: bfloat16 [8, 768, 8192], P('groups', 'adapter', 'tensor'), parts along dimension 0, may hold values from -6 to 6
- value_weight: bfloat16 [8192, 1024], P('tensor'), may hold values from -0.0625 to 0.0625
- adapter_down: bfloat16 [16, 64, 8192], P('adapter', None, 'tensor'), may hold values from -0.0625 to 0.0625
- adapter_up: bfloat16 [16, 64, 1024], P('adapter', None, 'tensor'), may hold values from -0.75 to 0.75
- block_slots: int32 [8, 48], P('groups', 'adapter'), parts along dimension 0, may hold values from 0 to 2, as said below
- transfer_offset: int32 [8], P('groups'), parts along dimension 0, may hold values from 1 to 7
- transfer_slot: int32 [8, 8], P('groups', 'adapter'), parts along dimension 0, may hold values from 0 to 1
Outputs:
- mixed: bfloat16 [8, 768, 1024], P('groups', 'adapter', 'tensor'), parts along dimension 0
There are 2 independent parts, one for each index of `groups`. A program takes and returns all parts, laid end to end along the dimension named above; an argument that names none is the same for every part. Nothing has to cross between parts.
Inputs may be any that keep to these rules, and one draw needn't show every extreme that they name: `block_slots`: slot 2 names the adapter handed over to the block's server in that step. In every step the blocks of every server use each slot below 2 at least once and slot 2 from 1 to 4 times; in every step some server uses slot 2 exactly 4 times.
All inputs are finite; a program needn't handle non-finite values.
Results may differ from a plain program's by a relative error of at most 0.0039.
Values may be sent and summed in bfloat16 or wider, within the bound.
No kernel may reach another device: no remote copies, remote signals or barrier semaphores. Data moves between devices by JAX's collectives and lax.ppermute only.
A program may use at most 64 MiB of HBM per device.

v0:
```python
import jax
import jax.numpy as jnp
from jax import lax
from jax.sharding import PartitionSpec as P


def from_behind(value, axis, steps):
    count = lax.axis_size(axis)
    pairs = [(source, (source + steps) % count) for source in range(count)]
    return lax.ppermute(value, axis, pairs)


def contract_last(left, right):
    return lax.dot_general(
        left, right, (((1,), (1,)), ((), ())), preferred_element_type=jnp.float32
    )


def slot_table(row_slot, slot_count):
    return (row_slot[:, None] == jnp.arange(slot_count, dtype=jnp.int32)[None, :]).astype(
        jnp.float32
    )


def select_rank(rank_wide, slot_mask, rank_width):
    row_total = rank_wide.shape[0]
    shaped = rank_wide.reshape(row_total, slot_mask.shape[1], rank_width)
    return jnp.sum(shaped * slot_mask[:, :, None], axis=1)


def spread_rank(reduced, slot_mask):
    row_total = reduced.shape[0]
    placed = reduced[:, None, :] * slot_mask[:, :, None].astype(reduced.dtype)
    return placed.reshape(row_total, slot_mask.shape[1] * reduced.shape[1])


def body(acts, value_weight, adapter_down, adapter_up, block_slots, transfer_offset, transfer_slot):
    devices = lax.axis_size("adapter")
    tree_levels = devices.bit_length() - 1
    rows_dev = acts.shape[1]
    halved_width = acts.shape[2]
    rank_width = adapter_down.shape[1]
    holding_count = adapter_down.shape[0]
    block_count = block_slots.shape[1]
    block_rows = rows_dev // block_count
    results = []
    for step_index in range(acts.shape[0]):
        tokens = acts[step_index]
        partial_base = jnp.dot(tokens, value_weight, preferred_element_type=jnp.float32)
        base_part = lax.psum_scatter(partial_base, "tensor", scatter_dimension=1, tiled=True)
        offset = transfer_offset[step_index]
        passed_slot = transfer_slot[step_index, 0]
        row_slot = jnp.repeat(block_slots[step_index], block_rows)
        passed_down = lax.dynamic_index_in_dim(adapter_down, passed_slot, 0, keepdims=False)
        passed_up = lax.dynamic_index_in_dim(adapter_up, passed_slot, 0, keepdims=False)
        carry_state = jnp.concatenate([passed_down, passed_up], axis=1)
        for level_index in range(tree_levels):
            shifted = from_behind(carry_state, "adapter", 1 << level_index)
            chosen_bit = jnp.right_shift(offset, level_index) % 2 == 1
            carry_state = jnp.where(chosen_bit, shifted, carry_state)
        gathered_down = jnp.concatenate([adapter_down, carry_state[None, :, :halved_width]], axis=0)
        gathered_up = jnp.concatenate([adapter_up, carry_state[None, :, halved_width:]], axis=0)
        gathered_down = gathered_down.reshape((holding_count + 1) * rank_width, halved_width)
        gathered_up = gathered_up.reshape((holding_count + 1) * rank_width, gathered_up.shape[2])
        slot_mask = slot_table(row_slot, holding_count + 1)
        rank_wide = contract_last(tokens, gathered_down)
        picked_rank = select_rank(rank_wide, slot_mask, rank_width)
        summed = lax.psum(picked_rank, "tensor")
        reduced = summed.astype(jnp.bfloat16)
        low_rank = jnp.dot(
            spread_rank(reduced, slot_mask), gathered_up, preferred_element_type=jnp.float32
        )
        results.append((base_part + low_rank).astype(jnp.bfloat16))
    return jnp.stack(results)


def solution(mesh):
    in_specs = (
        P("groups", "adapter", "tensor"),
        P("tensor", None),
        P("adapter", None, "tensor"),
        P("adapter", None, "tensor"),
        P("groups", "adapter"),
        P("groups"),
        P("groups", "adapter"),
    )
    out_specs = P("groups", "adapter", "tensor")
    return jax.shard_map(body, mesh=mesh, in_specs=in_specs, out_specs=out_specs, check_vma=False)
```

profile of v0, /device:TPU:7, one launch (start us, length us, event | category | flops | bytes accessed | tf_op | source)
XLA Modules:
  0.0 255.2 jit_solution(13627061330274381942)
XLA Ops:
  6.5 5.9 %fusion.26 = f32[96,1024]{1,0:T(8,128)} fusion(bf16[4096,1024]{1,0:T(8,128)(2,1)} %param.8, bf16[4,96,4096]{2,1,0:T(8,128)(2,1)} %param.7), kind=kOutput, calls=%fused_computation.34 | convolution fusion | flops 805306368 | bytes 9568256 | tf_op jit(solution)/shard_map/dot_general | solution.py:49
  12.5 0.6 fusion.65
  20.7 2.9 %dynamic-slice_bitcast_fusion.3 = (bf16[64,4096]{1,0:T(8,128)(2,1)}, bf16[64,4096]{1,0:T(8,128)(2,1)}, bf16[64,4096]{1,0:T(8,128)(2,1)S(1)}, bf16[64,4096]{1,0:T(8,128)(2,1)S(1)}) fusion(bf16[2,64,4096]{2,1,0:T(8,128)(2,1)} %param.9, s32[]{:T(128)S(6)} %select_n.149, s32[]{:T(128)S(6)} %select_n.159, s32[]{:T(128)S(6)} %select_n.169, s32[]{:T(128)S(6)} %select_n.179), kind=kLoop, calls=%fused_computation.67 | loop fusion | bytes 4194320 | tf_op jit(solution)/shard_map/jit(dynamic_index_in_dim)/squeeze | solution.py:54
  23.6 0.9 pad_maximum_fusion.7
  24.6 1.2 collective-permute-start.9
  25.8 0.9 pad_maximum_fusion.6
  26.7 1.6 collective-permute-start.6
  28.2 5.6 %fusion.22 = f32[96,1024]{1,0:T(8,128)} fusion(bf16[4096,1024]{1,0:T(8,128)(2,1)} %param.8, bf16[4,96,4096]{2,1,0:T(8,128)(2,1)S(1)} %copy-done), kind=kOutput, calls=%fused_computation.30 | convolution fusion | flops 805306368 | bytes 9568256 | tf_op jit(solution)/shard_map/dot_general | solution.py:49
  33.9 1.9 pad_maximum_fusion.5
  35.8 0.9 collective-permute-start.3
  36.7 5.6 %fusion.18 = f32[96,1024]{1,0:T(8,128)} fusion(bf16[4096,1024]{1,0:T(8,128)(2,1)} %param.8, bf16[4,96,4096]{2,1,0:T(8,128)(2,1)S(1)} %copy-done), kind=kOutput, calls=%fused_computation.26 | convolution fusion | flops 805306368 | bytes 9568256 | tf_op jit(solution)/shard_map/dot_general | solution.py:49
  42.4 1.9 pad_maximum_fusion.4
  44.3 1.2 collective-permute-start
  45.5 5.6 %fusion.14 = f32[96,1024]{1,0:T(8,128)} fusion(bf16[4096,1024]{1,0:T(8,128)(2,1)} %param.8, bf16[4,96,4096]{2,1,0:T(8,128)(2,1)S(1)} %copy-done), kind=kOutput, calls=%fused_computation.22 | convolution fusion | flops 805306368 | bytes 9568256 | tf_op jit(solution)/shard_map/dot_general | solution.py:49
  51.2 0.6 fusion.64
  59.3 0.6 slice_bitcast_fusion.11
  60.1 0.7 broadcast_in_dim.56
  60.8 0.7 broadcast_in_dim.62
  62.1 0.7 broadcast_in_dim.59
  62.8 0.6 eq.154
  63.9 0.6 fusion.55
  64.5 1.2 fusion.57
  65.7 1.4 broadcast_select_fusion
  67.2 1.7 collective-permute-start.10
  68.8 1.2 broadcast_select_fusion.3
  70.2 1.2 broadcast_select_fusion.6
  71.4 1.2 collective-permute-start.4
  72.6 4.4 %collective-permute-done = bf16[64,4608]{1,0:T(8,128)(2,1)} collective-permute-done((bf16[64,4608]{1,0:T(8,128)(2,1)}, bf16[64,4608]{1,0:T(8,128)(2,1)}, u32[]{:S(2)}, u32[]{:S(2)}) %collective-permute-start) | collective-permute-done | bytes 589856 | tf_op jit(solution)/shard_map/ppermute | solution.py:10
  77.0 1.2 broadcast_select_fusion.9
  78.2 1.7 collective-permute-start.1
  79.9 12.2 %collective-permute-done.10 = bf16[64,4608]{1,0:T(8,128)(2,1)S(1)} collective-permute-done((bf16[64,4608]{1,0:T(8,128)(2,1)S(1)}, bf16[64,4608]{1,0:T(8,128)(2,1)S(1)}, u32[]{:S(2)}, u32[]{:S(2)}) %collective-permute-start.10) | collective-permute-done | bytes 589856 | tf_op jit(solution)/shard_map/ppermute | solution.py:10
  92.2 12.5 %collective-permute-done.7 = bf16[64,4608]{1,0:T(8,128)(2,1)S(1)} collective-permute-done((bf16[64,4608]{1,0:T(8,128)(2,1)S(1)}, bf16[64,4608]{1,0:T(8,128)(2,1)S(1)}, u32[]{:S(2)}, u32[]{:S(2)}) %collective-permute-start.7) | collective-permute-done | bytes 589856 | tf_op jit(solution)/shard_map/ppermute | solution.py:10
  104.9 12.5 %collective-permute-done.4 = bf16[64,4608]{1,0:T(8,128)(2,1)S(1)} collective-permute-done((bf16[64,4608]{1,0:T(8,128)(2,1)S(1)}, bf16[64,4608]{1,0:T(8,128)(2,1)S(1)}, u32[]{:S(2)}, u32[]{:S(2)}) %collective-permute-start.4) | collective-permute-done | bytes 589856 | tf_op jit(solution)/shard_map/ppermute | solution.py:10
  117.5 12.5 %collective-permute-done.1 = bf16[64,4608]{1,0:T(8,128)(2,1)S(1)} collective-permute-done((bf16[64,4608]{1,0:T(8,128)(2,1)S(1)}, bf16[64,4608]{1,0:T(8,128)(2,1)S(1)}, u32[]{:S(2)}, u32[]{:S(2)}) %collective-permute-start.1) | collective-permute-done | bytes 589856 | tf_op jit(solution)/shard_map/ppermute | solution.py:10
  130.1 89.0 %collective-permute-done.5 = bf16[64,4608]{1,0:T(8,128)(2,1)S(1)} collective-permute-done((bf16[64,4608]{1,0:T(8,128)(2,1)S(1)}, bf16[64,4608]{1,0:T(8,128)(2,1)S(1)}, u32[]{:S(2)}, u32[]{:S(2)}) %collective-permute-start.5) | collective-permute-done | bytes 589856 | tf_op jit(solution)/shard_map/ppermute | solution.py:10
  219.3 12.5 %collective-permute-done.2 = bf16[64,4608]{1,0:T(8,128)(2,1)S(1)} collective-permute-done((bf16[64,4608]{1,0:T(8,128)(2,1)S(1)}, bf16[64,4608]{1,0:T(8,128)(2,1)S(1)}, u32[]{:S(2)}, u32[]{:S(2)}) %collective-permute-start.2) | collective-permute-done | bytes 589856 | tf_op jit(solution)/shard_map/ppermute | solution.py:10
  232.0 0.8 copy-done.8
  233.0 0.8 copy-done.9
  234.8 0.6 fusion.24
  236.6 0.6 fusion.12
  237.3 4.3 %all-reduce = (bf16[96,64]{0,1:T(8,128)(2,1)S(1)}, bf16[96,64]{0,1:T(8,128)(2,1)S(1)}, bf16[96,64]{0,1:T(8,128)(2,1)S(1)}, bf16[96,64]{0,1:T(8,128)(2,1)S(1)}) all-reduce(f32[96,64]{0,1:T(8,128)S(1)} %get-tuple-element.41, f32[96,64]{0,1:T(8,128)S(1)} %get-tuple-element.42, ...), channel_id=1, replica_groups=mesh['groups'=2,'adapter'=8,'tensor'=2] {'tensor'}, use_global_device_ids=true, to_apply=%region_11.12 | all-reduce | flops 24576 | bytes 147456 | tf_op jit(solution)/shard_map/psum | solution.py:68
  241.6 1.1 fusion.11
  242.8 1.1 fusion.10
  243.9 0.8 slice_bitcast_fusion.5
  244.7 1.1 fusion.9
  245.9 0.9 slice_bitcast_fusion.4
  246.7 1.1 fusion.8
  247.8 0.8 pad_maximum_fusion.8
  (76 shorter events, 4.9 us)
Async XLA Ops:
  6.5 6.0 %copy-start.10 = (s32[4,1]{0,1:T(1,128)S(1)}, s32[4,1]{0,1:T(1,128)}, u32[]{:S(2)}) copy-start(s32[4,1]{0,1:T(1,128)} %param.13) | copy-start | bytes 52
  6.5 14.2 %copy-start.2 = (bf16[2,64,512]{2,1,0:T(8,128)(2,1)S(1)}, bf16[2,64,512]{2,1,0:T(8,128)(2,1)}, u32[]{:S(2)}) copy-start(bf16[2,64,512]{2,1,0:T(8,128)(2,1)} %param.10) | copy-start | bytes 393220
  6.5 235.0 %reduce-scatter.5.cloned.1.call-start = ((), (), s32[]{:S(2)}) async-start(), calls=%async_computation.4 | async-start | bytes 589824 | tf_op jit(solution)/shard_map/reduce_scatter | solution.py:50
  12.4 230.3 %reduce-scatter.7.cloned.1.call-start = ((), (), s32[]{:S(2)}) async-start(), calls=%async_computation.5 | async-start | bytes 589824 | tf_op jit(solution)/shard_map/reduce_scatter | solution.py:50
  20.7 7.5 %copy-start = (bf16[4,96,4096]{2,1,0:T(8,128)(2,1)S(1)}, bf16[4,96,4096]{2,1,0:T(8,128)(2,1)}, u32[]{:S(2)}) copy-start(bf16[4,96,4096]{2,1,0:T(8,128)(2,1)} %param.7) | copy-start | bytes 9437188
  23.6 2.2 copy-start.5
  23.6 3.0 %copy-start.7 = (bf16[64,4096]{1,0:T(8,128)(2,1)}, bf16[64,4096]{1,0:T(8,128)(2,1)S(1)}, u32[]{:S(2)}) copy-start(bf16[64,4096]{1,0:T(8,128)(2,1)S(1)} %get-tuple-element.16) | copy-start | bytes 1572868
  24.6 41.1 %collective-permute-start.9 = (bf16[64,4608]{1,0:T(8,128)(2,1)}, bf16[64,4608]{1,0:T(8,128)(2,1)}, u32[]{:S(2)}, u32[]{:S(2)}) collective-permute-start(bf16[64,4608]{1,0:T(8,128)(2,1)} %pad_maximum_fusion.7), channel_id=1, source_target_pairs={{0,2},{2,4},{4,6},{6,8},{8,10},{10,12},{12,14},{14,0},{1,3},{3,5},... | collective-permute-start | bytes 1769480 | tf_op jit(solution)/shard_map/ppermute | solution.py:10
  26.7 42.1 %collective-permute-start.6 = (bf16[64,4608]{1,0:T(8,128)(2,1)}, bf16[64,4608]{1,0:T(8,128)(2,1)}, u32[]{:S(2)}, u32[]{:S(2)}) collective-permute-start(bf16[64,4608]{1,0:T(8,128)(2,1)} %pad_maximum_fusion.6), channel_id=1, source_target_pairs={{0,2},{2,4},{4,6},{6,8},{8,10},{10,12},{12,14},{14,0},{1,3},{3,5},... | collective-permute-start | bytes 1769480 | tf_op jit(solution)/shard_map/ppermute | solution.py:10
  33.9 210.9 %reduce-scatter.9.cloned.1.call-start = ((), (), s32[]{:S(2)}) async-start(), calls=%async_computation.6 | async-start | bytes 589824 | tf_op jit(solution)/shard_map/reduce_scatter | solution.py:50
  35.8 34.4 %collective-permute-start.3 = (bf16[64,4608]{1,0:T(8,128)(2,1)}, bf16[64,4608]{1,0:T(8,128)(2,1)}, u32[]{:S(2)}, u32[]{:S(2)}) collective-permute-start(bf16[64,4608]{1,0:T(8,128)(2,1)} %pad_maximum_fusion.5), channel_id=1, source_target_pairs={{0,2},{2,4},{4,6},{6,8},{8,10},{10,12},{12,14},{14,0},{1,3},{3,5},... | collective-permute-start | bytes 1769480 | tf_op jit(solution)/shard_map/ppermute | solution.py:10
  42.3 204.4 %reduce-scatter.11.cloned.1.call-start = ((), (), s32[]{:S(2)}) async-start(), calls=%async_computation.7 | async-start | bytes 589824 | tf_op jit(solution)/shard_map/reduce_scatter | solution.py:50
  44.3 6.9 %copy-start.11 = (s32[4]{0:T(128)S(1)}, s32[4]{0:T(128)}, u32[]{:S(2)}) copy-start(s32[4]{0:T(128)} %param.12) | copy-start | bytes 52
  44.3 15.0 %copy-start.14 = (s32[4,6]{1,0:T(4,128)S(1)}, s32[4,6]{1,0:T(4,128)}, u32[]{:S(2)}) copy-start(s32[4,6]{1,0:T(4,128)} %param.11) | copy-start | bytes 292
  44.3 32.7 %collective-permute-start = (bf16[64,4608]{1,0:T(8,128)(2,1)}, bf16[64,4608]{1,0:T(8,128)(2,1)}, u32[]{:S(2)}, u32[]{:S(2)}) collective-permute-start(bf16[64,4608]{1,0:T(8,128)(2,1)} %pad_maximum_fusion.4), channel_id=1, source_target_pairs={{0,2},{2,4},{4,6},{6,8},{8,10},{10,12},{12,14},{14,0},{1,3},{3,5},... | collective-permute-start | bytes 1769480 | tf_op jit(solution)/shard_map/ppermute | solution.py:10
  63.4 5.4 %copy-start.6 = (bf16[64,4096]{1,0:T(8,128)(2,1)S(1)}, bf16[64,4096]{1,0:T(8,128)(2,1)}, u32[]{:S(2)}) copy-start(bf16[64,4096]{1,0:T(8,128)(2,1)} %copy-done.5) | copy-start | bytes 1572868
  65.7 4.4 %copy-start.4 = (bf16[64,4096]{1,0:T(8,128)(2,1)S(1)}, bf16[64,4096]{1,0:T(8,128)(2,1)}, u32[]{:S(2)}) copy-start(bf16[64,4096]{1,0:T(8,128)(2,1)} %get-tuple-element.14) | copy-start | bytes 1572868
  67.1 9.9 %copy-start.3 = (bf16[64,4096]{1,0:T(8,128)(2,1)S(1)}, bf16[64,4096]{1,0:T(8,128)(2,1)}, u32[]{:S(2)}) copy-start(bf16[64,4096]{1,0:T(8,128)(2,1)} %get-tuple-element.13) | copy-start | bytes 1572868
  67.2 24.9 %collective-permute-start.10 = (bf16[64,4608]{1,0:T(8,128)(2,1)S(1)}, bf16[64,4608]{1,0:T(8,128)(2,1)S(1)}, u32[]{:S(2)}, u32[]{:S(2)}) collective-permute-start(bf16[64,4608]{1,0:T(8,128)(2,1)S(1)} %broadcast_select_fusion), channel_id=1, source_target_pairs={{0,4},{2,6},{4,8},{6,10},{8,12},{10,14},{12,0},{14,2},{1,5},{3,7},... | collective-permute-start | bytes 1769480 | tf_op jit(solution)/shard_map/ppermute | solution.py:10
  70.0 34.7 %collective-permute-start.7 = (bf16[64,4608]{1,0:T(8,128)(2,1)S(1)}, bf16[64,4608]{1,0:T(8,128)(2,1)S(1)}, u32[]{:S(2)}, u32[]{:S(2)}) collective-permute-start(bf16[64,4608]{1,0:T(8,128)(2,1)S(1)} %broadcast_select_fusion.3), channel_id=1, source_target_pairs={{0,4},{2,6},{4,8},{6,10},{8,12},{10,14},{12,0},{14,2},{1,5},{3,7},... | collective-permute-start | bytes 1769480 | tf_op jit(solution)/shard_map/ppermute | solution.py:10
  71.4 46.0 %collective-permute-start.4 = (bf16[64,4608]{1,0:T(8,128)(2,1)S(1)}, bf16[64,4608]{1,0:T(8,128)(2,1)S(1)}, u32[]{:S(2)}, u32[]{:S(2)}) collective-permute-start(bf16[64,4608]{1,0:T(8,128)(2,1)S(1)} %broadcast_select_fusion.6), channel_id=1, source_target_pairs={{0,4},{2,6},{4,8},{6,10},{8,12},{10,14},{12,0},{14,2},{1,5},{3,7},... | collective-permute-start | bytes 1769480 | tf_op jit(solution)/shard_map/ppermute | solution.py:10
  78.2 51.8 %collective-permute-start.1 = (bf16[64,4608]{1,0:T(8,128)(2,1)S(1)}, bf16[64,4608]{1,0:T(8,128)(2,1)S(1)}, u32[]{:S(2)}, u32[]{:S(2)}) collective-permute-start(bf16[64,4608]{1,0:T(8,128)(2,1)S(1)} %broadcast_select_fusion.9), channel_id=1, source_target_pairs={{0,4},{2,6},{4,8},{6,10},{8,12},{10,14},{12,0},{14,2},{1,5},{3,7},... | collective-permute-start | bytes 1769480 | tf_op jit(solution)/shard_map/ppermute | solution.py:10
  92.1 139.8 %collective-permute-start.11 = (bf16[64,4608]{1,0:T(8,128)(2,1)S(1)}, bf16[64,4608]{1,0:T(8,128)(2,1)S(1)}, u32[]{:S(2)}, u32[]{:S(2)}) collective-permute-start(bf16[64,4608]{1,0:T(8,128)(2,1)S(1)} %broadcast_select_fusion.1), channel_id=1, source_target_pairs={{0,8},{2,10},{4,12},{6,14},{8,0},{10,2},{12,4},{14,6},{1,9},{3,11}... | collective-permute-start | bytes 1769480 | tf_op jit(solution)/shard_map/ppermute | solution.py:10
  104.8 128.1 %collective-permute-start.8 = (bf16[64,4608]{1,0:T(8,128)(2,1)S(1)}, bf16[64,4608]{1,0:T(8,128)(2,1)S(1)}, u32[]{:S(2)}, u32[]{:S(2)}) collective-permute-start(bf16[64,4608]{1,0:T(8,128)(2,1)S(1)} %broadcast_select_fusion.4), channel_id=1, source_target_pairs={{0,8},{2,10},{4,12},{6,14},{8,0},{10,2},{12,4},{14,6},{1,9},{3,11}... | collective-permute-start | bytes 1769480 | tf_op jit(solution)/shard_map/ppermute | solution.py:10
  117.4 101.7 %collective-permute-start.5 = (bf16[64,4608]{1,0:T(8,128)(2,1)S(1)}, bf16[64,4608]{1,0:T(8,128)(2,1)S(1)}, u32[]{:S(2)}, u32[]{:S(2)}) collective-permute-start(bf16[64,4608]{1,0:T(8,128)(2,1)S(1)} %broadcast_select_fusion.7), channel_id=1, source_target_pairs={{0,8},{2,10},{4,12},{6,14},{8,0},{10,2},{12,4},{14,6},{1,9},{3,11}... | collective-permute-start | bytes 1769480 | tf_op jit(solution)/shard_map/ppermute | solution.py:10
  130.1 101.7 %collective-permute-start.2 = (bf16[64,4608]{1,0:T(8,128)(2,1)S(1)}, bf16[64,4608]{1,0:T(8,128)(2,1)S(1)}, u32[]{:S(2)}, u32[]{:S(2)}) collective-permute-start(bf16[64,4608]{1,0:T(8,128)(2,1)S(1)} %broadcast_select_fusion.10), channel_id=1, source_target_pairs={{0,8},{2,10},{4,12},{6,14},{8,0},{10,2},{12,4},{14,6},{1,9},{3,11}... | collective-permute-start | bytes 1769480 | tf_op jit(solution)/shard_map/ppermute | solution.py:10
  232.0 0.8 copy-start.8
  232.9 1.4 copy-start.1
  233.0 0.8 copy-start.9
  236.6 6.1 %copy-start.13 = (bf16[96,3]{0,1:T(4,128)(2,1)S(1)}, bf16[96,3]{0,1:T(4,128)(2,1)}, u32[]{:S(2)}) copy-start(bf16[96,3]{0,1:T(4,128)(2,1)} %get-tuple-element.27) | copy-start | bytes 1732
  236.6 8.1 %copy-start.12 = (bf16[96,3]{0,1:T(4,128)(2,1)S(1)}, bf16[96,3]{0,1:T(4,128)(2,1)}, u32[]{:S(2)}) copy-start(bf16[96,3]{0,1:T(4,128)(2,1)} %get-tuple-element.29) | copy-start | bytes 1732
Sparse Core Ops, SparseCore 0:
  12.6 9.6 reduce-scatter.4
  34.0 9.2 reduce-scatter.6
  45.5 8.9 reduce-scatter.8
  56.7 9.0 reduce-scatter.10
where the time goes:
time: 256 us; the launch traced here: 255 us
  waiting for transfers between devices  156 us (61%)
  matrix products  29.5 us (12%)
  between operations  28.6 us (11%)
  other arithmetic  14.7 us (6%)
  local copies, waits for them, and re-layouts  12.3 us (5%)
  starting transfers between devices  10.1 us (4%)
  blocking collectives  4.27 us (2%)
    ppermute x12, waiting for transfers between devices, from_behind(): return lax.ppermute(value, axis, pairs)  156 us
    dot_general x4, matrix products, body(): jnp.dot(tokens, value_weight, preferred_element_type=jnp.float32)  22.6 us
    ppermute x12, starting transfers between devices, from_behind(): return lax.ppermute(value, axis, pairs)  9.93 us
    concatenate x4, other arithmetic, body(): carry_state = jnp.concatenate([passed_down, passed_up], axis=1)  5.59 us
    select_n x12, other arithmetic, body(): carry_state = jnp.where(chosen_bit, shifted, carry_state)  5.52 us
  transfers between devices with their start and end apart: 16, of which 7 were waited for; matrix products, arithmetic and copies ran while one was open for 18% of the time, Pallas kernels for 0%

commit v1 on v0

v1 whole, which is shorter than its diff:
```python
import functools

import jax
import jax.numpy as jnp
from jax import lax
from jax.experimental import pallas as pl
from jax.experimental.pallas import tpu as pltpu
from jax.sharding import PartitionSpec as P

STRIPES = 8


def contract_last(left, right):
    return lax.dot_general(
        left, right, (((left.ndim - 1,), (right.ndim - 1,)), ((), ())), preferred_element_type=jnp.float32
    )


def cut_kernel(wide, narrow, rows, piece_ref, down_ref, up_ref, *rest):
    outs, sem = rest[:-1], rest[-1]
    copies = []
    for index, out_ref in enumerate(outs):
        start = pl.multiple_of(piece_ref[index] * rows, rows)
        copies.append(pltpu.make_async_copy(
            down_ref.at[:, pl.ds(start, rows), :], out_ref.at[:, :, pl.ds(0, wide)], sem.at[2 * index]))
        copies.append(pltpu.make_async_copy(
            up_ref.at[:, pl.ds(start, rows), :], out_ref.at[:, :, pl.ds(wide, narrow)], sem.at[2 * index + 1]))
    for copy in copies:
        copy.start()
    for copy in copies:
        copy.wait()


def cut_stripes(pieces, adapter_down, adapter_up, stripe_count):
    held, rank, wide = adapter_down.shape
    narrow = adapter_up.shape[2]
    rows = rank // STRIPES
    out = jax.ShapeDtypeStruct((held, rows, wide + narrow), adapter_down.dtype)
    return pl.pallas_call(
        functools.partial(cut_kernel, wide, narrow, rows),
        out_shape=[out] * stripe_count,
        in_specs=[pl.BlockSpec(memory_space=pltpu.SMEM)] + [pl.BlockSpec(memory_space=pl.ANY)] * 2,
        out_specs=[pl.BlockSpec(memory_space=pl.ANY)] * stripe_count,
        scratch_shapes=[pltpu.SemaphoreType.DMA((2 * stripe_count,))],
    )(pieces, adapter_down, adapter_up)


def pick_kernel(server_count, steps, held, choice_ref, *rest):
    servers, rest = rest[:server_count], rest[server_count:]
    outs, (bank, in_sem, out_sem) = rest[:STRIPES], rest[STRIPES:]
    loads = [
        pltpu.make_async_copy(ref, bank.at[pl.ds(index * held, held)], in_sem.at[index])
        for index, ref in enumerate(servers)
    ]
    for load in loads:
        load.start()
    for load in loads:
        load.wait()
    stores = [
        pltpu.make_async_copy(
            bank.at[choice_ref[asker * steps + step]], out_ref.at[step], out_sem.at[asker * steps + step])
        for asker, out_ref in enumerate(outs)
        for step in range(steps)
    ]
    for store in stores:
        store.start()
    for store in stores:
        store.wait()


def pick_stripes(choice, servers, steps):
    held, rows, width = servers[0].shape
    out = jax.ShapeDtypeStruct((steps, rows, width), servers[0].dtype)
    bank_bytes = len(servers) * held * rows * width * 2
    return pl.pallas_call(
        functools.partial(pick_kernel, len(servers), steps, held),
        out_shape=[out] * STRIPES,
        in_specs=[pl.BlockSpec(memory_space=pltpu.SMEM)] + [pl.BlockSpec(memory_space=pl.ANY)] * len(servers),
        out_specs=[pl.BlockSpec(memory_space=pl.ANY)] * STRIPES,
        scratch_shapes=[
            pltpu.VMEM((len(servers) * held, rows, width), servers[0].dtype),
            pltpu.SemaphoreType.DMA((len(servers),)),
            pltpu.SemaphoreType.DMA((STRIPES * steps,)),
        ],
        compiler_params=pltpu.CompilerParams(vmem_limit_bytes=bank_bytes + (4 << 20)),
    )(choice, *servers)


def body(acts, value_weight, adapter_down, adapter_up, block_slots, transfer_offset, transfer_slot):
    groups, servers = lax.axis_size("groups"), lax.axis_size("adapter")
    parts = STRIPES // groups
    halves = servers // parts
    steps, rows_dev, wide = acts.shape
    held, rank, _ = adapter_down.shape
    narrow = adapter_up.shape[2]
    block_rows = rows_dev // block_slots.shape[1]
    group, server = lax.axis_index("groups"), lax.axis_index("adapter")
    side = lax.axis_index("tensor")
    part = server % parts
    half = server // parts

    pieces = (group * parts + jnp.bitwise_xor(part, jnp.arange(parts, dtype=jnp.int32))).astype(jnp.int32)
    stripes = cut_stripes(pieces, adapter_down, adapter_up, parts)
    banked = [stripes[0]]
    for k in range(1, servers):
        banked.append(lax.ppermute(
            stripes[k % parts], "adapter", [(i, i ^ k) for i in range(servers)]))

    asked = transfer_offset * held + transfer_slot[:, 0]
    asked = lax.all_gather(asked, ("groups", "adapter")).reshape(groups, servers, steps)
    offsets, slots = asked // held, asked % held
    asker = jnp.bitwise_xor(group * parts + part, jnp.arange(STRIPES, dtype=jnp.int32))
    ask_group, ask_server = asker // parts, half * parts + asker % parts
    source = (ask_server[:, None] - offsets[ask_group, ask_server]) % servers
    slot = slots[ask_group[:, None], source, jnp.arange(steps)[None, :]]
    choice = (jnp.bitwise_xor(source, server) * held + slot).astype(jnp.int32).reshape(-1)

    tokens = acts.reshape(steps * rows_dev, wide)
    partial_base = jnp.dot(tokens, value_weight, preferred_element_type=jnp.float32)
    swap = [(0, 1), (1, 0)]
    half_width = partial_base.shape[1] // 2
    mine = lax.dynamic_slice_in_dim(partial_base, side * half_width, half_width, 1)
    others = lax.dynamic_slice_in_dim(partial_base, (1 - side) * half_width, half_width, 1)
    base = mine + lax.ppermute(others, "tensor", swap)
    partial_own = contract_last(tokens, adapter_down.reshape(held * rank, wide))
    own = (partial_own + lax.ppermute(partial_own, "tensor", swap)).astype(jnp.bfloat16)
    row_slot = jnp.repeat(block_slots.reshape(-1), block_rows)
    own_slot = jnp.arange(held * rank, dtype=jnp.int32) // rank
    own = jnp.where(row_slot[:, None] == own_slot[None, :], own, jnp.zeros_like(own))
    base = base + jnp.dot(own, adapter_up.reshape(held * rank, narrow), preferred_element_type=jnp.float32)

    picked = pick_stripes(choice, banked, steps)
    given = [picked[0]]
    for k in range(1, STRIPES):
        pairs = []
        for g in range(groups):
            for i in range(servers):
                other = (g * parts + i % parts) ^ k
                pairs.append((g * servers + i, (other // parts) * servers + (i // parts) * parts + other % parts))
        given.append(lax.ppermute(picked[k], ("groups", "adapter"), pairs))
    passed = jnp.concatenate(given, axis=1)
    partial_passed = lax.dot_general(
        acts, passed[:, :, :wide], (((2,), (2,)), ((0,), (0,))), preferred_element_type=jnp.float32)
    reduced = (partial_passed + lax.ppermute(partial_passed, "tensor", swap)).astype(jnp.bfloat16)
    is_passed = row_slot.reshape(steps, rows_dev, 1) == held
    reduced = jnp.where(is_passed, reduced, jnp.zeros_like(reduced))
    low_rank = lax.dot_general(
        reduced, passed[:, :, wide:], (((2,), (1,)), ((0,), (0,))), preferred_element_type=jnp.float32)
    return (base.reshape(steps, rows_dev, narrow) + low_rank).astype(jnp.bfloat16)


def solution(mesh):
    in_specs = (
        P("groups", "adapter", "tensor"),
        P("tensor", None),
        P("adapter", None, "tensor"),
        P("adapter", None, "tensor"),
        P("groups", "adapter"),
        P("groups"),
        P("groups", "adapter"),
    )
    out_specs = P("groups", "adapter", "tensor")
    return jax.shard_map(body, mesh=mesh, in_specs=in_specs, out_specs=out_specs, check_vma=False)
```

time: 256 us -> 120 us (0.47)
  the two profiles are of different devices: /device:TPU:7 before, /device:TPU:0 now
where the time goes in v1:
time: 120 us; the launch traced here: 119 us
  waiting for transfers between devices  40.3 us (34%)
  Pallas kernels  25.9 us (22%)
  starting transfers between devices  21.1 us (18%)
  blocking collectives  13.6 us (11%)
  matrix products  10.6 us (9%)
  local copies, waits for them, and re-layouts  4.73 us (4%)
  other arithmetic  2.32 us (2%)
    ppermute x7, waiting for transfers between devices, body(): given.append(lax.ppermute(picked[k], ('groups', 'adapter'), pairs))  29.5 us
    pallas_call x1, Pallas kernels, cut_stripes(): pl.pallas_call(functools.partial(cut_kernel, wide, narrow, rows), out_sha...  19.8 us
    unnamed x1, blocking collectives  13.6 us
    ppermute x7, starting transfers between devices, body(): lax.ppermute(stripes[k % parts], 'adapter', [(i, i ^ k) for i in range(se...  13.2 us
    ppermute x7, waiting for transfers between devices, body(): lax.ppermute(stripes[k % parts], 'adapter', [(i, i ^ k) for i in range(se...  9.45 us
    ppermute x7, starting transfers between devices, body(): given.append(lax.ppermute(picked[k], ('groups', 'adapter'), pairs))  7.76 us
    dot_general x1, matrix products, body(): jnp.dot(tokens, value_weight, preferred_element_type=jnp.float32)  7.04 us
    pallas_call x1, Pallas kernels, pick_stripes(): pl.pallas_call(functools.partial(pick_kernel, len(servers), steps, held),...  6.03 us
  transfers between devices with their start and end apart: 17, of which 7 were waited for; matrix products, arithmetic and copies ran while one was open for 13% of the time, Pallas kernels for 5%

profile of v1, /device:TPU:0, one launch (start us, length us, event | category | flops | bytes accessed | tf_op | source)
XLA Modules:
  0.0 119.3 jit_solution(15271001120562965429)
XLA Ops:
  0.0 0.5 xor_add_fusion.piece_ref
  0.5 19.8 %shard_map.73 = (bf16[2,8,4608]{2,1,0:T(8,128)(2,1)}, bf16[2,8,4608]{2,1,0:T(8,128)(2,1)}, bf16[2,8,4608]{2,1,0:T(8,128)(2,1)}, bf16[2,8,4608]{2,1,0:T(8,128)(2,1)}) custom-call(s32[4]{0:T(128)} %xor_add_fusion.piece_ref, bf16[2,64,4096]{2,1,0:T(8,128)(2,1)} %down_ref.1, bf16[2,64,512]{2,1,0:T(8,128)(2,1)} %up_ref.1), custom_call_target="tpu_custom_call" | custom-call | tf_op jit(solution)/shard_map/pallas_call | solution.py:39
  20.4 3.0 %collective-permute-start.2 = (bf16[2,8,4608]{2,1,0:T(8,128)(2,1)}, bf16[2,8,4608]{2,1,0:T(8,128)(2,1)S(1)}, u32[]{:S(2)}, u32[]{:S(2)}) collective-permute-start(bf16[2,8,4608]{2,1,0:T(8,128)(2,1)} %get-tuple-element.18), channel_id=1, source_target_pairs={{0,2},{2,0},{4,6},{6,4},{8,10},{10,8},{12,14},{14,12},{1,3},{3,1},... | collective-permute-start | bytes 442376 | tf_op jit(solution)/shard_map/ppermute | solution.py:106
  23.4 2.5 %collective-permute-start.6 = (bf16[2,8,4608]{2,1,0:T(8,128)(2,1)}, bf16[2,8,4608]{2,1,0:T(8,128)(2,1)}, u32[]{:S(2)}, u32[]{:S(2)}) collective-permute-start(bf16[2,8,4608]{2,1,0:T(8,128)(2,1)} %get-tuple-element.18), channel_id=1, source_target_pairs={{0,10},{2,8},{4,14},{6,12},{8,2},{10,0},{12,6},{14,4},{1,11},{3,9}... | collective-permute-start | bytes 442376 | tf_op jit(solution)/shard_map/ppermute | solution.py:106
  25.9 1.6 %collective-permute-start.3 = (bf16[2,8,4608]{2,1,0:T(8,128)(2,1)}, bf16[2,8,4608]{2,1,0:T(8,128)(2,1)}, u32[]{:S(2)}, u32[]{:S(2)}) collective-permute-start(bf16[2,8,4608]{2,1,0:T(8,128)(2,1)} %get-tuple-element.19), channel_id=1, source_target_pairs={{0,4},{2,6},{4,0},{6,2},{8,12},{10,14},{12,8},{14,10},{1,5},{3,7},... | collective-permute-start | bytes 442376 | tf_op jit(solution)/shard_map/ppermute | solution.py:106
  27.5 1.9 %collective-permute-start.4 = (bf16[2,8,4608]{2,1,0:T(8,128)(2,1)}, bf16[2,8,4608]{2,1,0:T(8,128)(2,1)}, u32[]{:S(2)}, u32[]{:S(2)}) collective-permute-start(bf16[2,8,4608]{2,1,0:T(8,128)(2,1)} %get-tuple-element.20), channel_id=1, source_target_pairs={{0,6},{2,4},{4,2},{6,0},{8,14},{10,12},{12,10},{14,8},{1,7},{3,5},... | collective-permute-start | bytes 442376 | tf_op jit(solution)/shard_map/ppermute | solution.py:106
  29.4 1.2 %dynamic-slice = u32[1]{0:T(128)} dynamic-slice(u32[32]{0:T(128)} %constant.168, u32[]{:T(128)S(6)} %add.182), dynamic_slice_sizes={1} | dynamic-slice | bytes 12
  31.3 0.8 fusion.35
  32.1 13.6 %all-reduce = s32[64]{0:T(128)S(1)} all-reduce(s32[64]{0:T(128)S(1)} %fusion.35), channel_id=2, replica_groups=mesh['groups'=2,'adapter'=8,'tensor'=2] {'groups','adapter'}, use_global_device_ids=true, to_apply=%add | all-reduce | flops 64 | bytes 512
  45.7 0.1 reshape.232
  45.8 0.6 gather_fusion
  46.4 0.1 copy.10
  46.4 0.1 broadcast_subtract_fusion
  46.5 0.1 copy.11
  46.6 0.1 reshape.239
  46.7 0.1 sub.55
  46.8 7.0 %fusion.39 = f32[384,1024]{1,0:T(8,128)} fusion(bf16[384,4096]{1,0:T(8,128)(2,1)S(1)} %bitcast.27, bf16[4096,1024]{1,0:T(8,128)(2,1)} %param.8), kind=kOutput, calls=%fused_computation.88 | convolution fusion | flops 3221225472 | bytes 13107200 | tf_op jit(solution)/shard_map/dot_general | solution.py:119
  53.8 1.7 %fusion.40 = f32[384,128]{1,0:T(8,128)} fusion(bf16[384,4096]{1,0:T(8,128)(2,1)S(1)} %bitcast.28, bf16[128,4096]{1,0:T(8,128)(2,1)S(1)} %bitcast.29), kind=kOutput, calls=%fused_computation.89 | convolution fusion | flops 402653184 | bytes 4390912 | tf_op jit(solution)/shard_map/dot_general | solution.py:14
  55.5 0.7 gather_fusion.1
  56.2 3.5 %collective-permute-start.8 = (bf16[2,8,4608]{2,1,0:T(8,128)(2,1)}, bf16[2,8,4608]{2,1,0:T(8,128)(2,1)}, u32[]{:S(2)}, u32[]{:S(2)}) collective-permute-start(bf16[2,8,4608]{2,1,0:T(8,128)(2,1)} %get-tuple-element.20), channel_id=1, source_target_pairs={{0,14},{2,12},{4,10},{6,8},{8,6},{10,4},{12,2},{14,0},{1,15},{3,13... | collective-permute-start | bytes 442376 | tf_op jit(solution)/shard_map/ppermute | solution.py:106
  59.7 0.7 collective-permute-start.5
  60.4 0.1 reshape.228
  60.5 0.1 broadcast_in_dim.38
  60.6 0.1 eq.44
  60.7 0.1 broadcast_in_dim.17
  60.7 0.1 eq.38
  60.8 1.2 %constant_dynamic-slice_fusion = f32[384,512]{1,0:T(8,128)S(1)} fusion(f32[384,1024]{1,0:T(8,128)} %fusion.39, s32[]{:T(128)S(6)} %select_n.133), kind=kLoop, calls=%fused_computation.85 | loop fusion | bytes 1572868 | tf_op jit(solution)/shard_map/dynamic_slice | solution.py:123
  62.0 0.1 collective-permute-start
  62.1 9.4 %collective-permute-done.5.rest_4_ = bf16[2,8,4608]{2,1,0:T(8,128)(2,1)} collective-permute-done((bf16[2,8,4608]{2,1,0:T(8,128)(2,1)S(1)}, bf16[2,8,4608]{2,1,0:T(8,128)(2,1)}, u32[]{:S(2)}, u32[]{:S(2)}) %collective-permute-start.5) | collective-permute-done | bytes 147488 | tf_op jit(solution)/shard_map/ppermute | solution.py:106
  71.6 6.0 %shard_map.74 = (bf16[4,8,4608]{2,1,0:T(8,128)(2,1)S(1)}, bf16[4,8,4608]{2,1,0:T(8,128)(2,1)S(1)}, bf16[4,8,4608]{2,1,0:T(8,128)(2,1)S(1)}, bf16[4,8,4608]{2,1,0...) custom-call(s32[32]{0:T(128)S(1)} %fusion.26.choice_ref, ...), custom_call_target="tpu_custom_call" | custom-call | tf_op jit(solution)/shard_map/pallas_call | solution.py:75
  77.6 0.9 collective-permute-start.9
  78.5 2.6 %collective-permute-start.11 = (bf16[4,8,4608]{2,1,0:T(8,128)(2,1)S(1)}, bf16[4,8,4608]{2,1,0:T(8,128)(2,1)S(1)}, u32[]{:S(2)}, u32[]{:S(2)}) collective-permute-start(bf16[4,8,4608]{2,1,0:T(8,128)(2,1)S(1)} %get-tuple-element.24), channel_id=1, source_target_pairs={{0,6},{2,4},{4,2},{6,0},{8,14},{10,12},{12,10},{14,8},{16,22},{18,... | collective-permute-start | bytes 884744 | tf_op jit(solution)/shard_map/ppermute | solution.py:140
  81.2 5.9 %collective-permute-done.9 = bf16[4,8,4608]{2,1,0:T(8,128)(2,1)S(1)} collective-permute-done((bf16[4,8,4608]{2,1,0:T(8,128)(2,1)S(1)}, bf16[4,8,4608]{2,1,0:T(8,128)(2,1)S(1)}, u32[]{:S(2)}, u32[]{:S(2)}) %collective-permute-start.9) | collective-permute-done | bytes 294944 | tf_op jit(solution)/shard_map/ppermute | solution.py:140
  87.1 0.6 collective-permute-start.12
  87.7 0.7 collective-permute-done.10
  88.4 1.2 %collective-permute-start.13 = (bf16[4,8,4608]{2,1,0:T(8,128)(2,1)S(1)}, bf16[4,8,4608]{2,1,0:T(8,128)(2,1)S(1)}, u32[]{:S(2)}, u32[]{:S(2)}) collective-permute-start(bf16[4,8,4608]{2,1,0:T(8,128)(2,1)S(1)} %get-tuple-element.26), channel_id=1, source_target_pairs={{0,18},{2,16},{4,22},{6,20},{8,26},{10,24},{12,30},{14,28},{16,2},... | collective-permute-start | bytes 884744 | tf_op jit(solution)/shard_map/ppermute | solution.py:140
  89.6 5.0 %collective-permute-done.11 = bf16[4,8,4608]{2,1,0:T(8,128)(2,1)S(1)} collective-permute-done((bf16[4,8,4608]{2,1,0:T(8,128)(2,1)S(1)}, bf16[4,8,4608]{2,1,0:T(8,128)(2,1)S(1)}, u32[]{:S(2)}, u32[]{:S(2)}) %collective-permute-start.11) | collective-permute-done | bytes 294944 | tf_op jit(solution)/shard_map/ppermute | solution.py:140
  94.6 1.5 %collective-permute-start.14 = (bf16[4,8,4608]{2,1,0:T(8,128)(2,1)S(1)}, bf16[4,8,4608]{2,1,0:T(8,128)(2,1)S(1)}, u32[]{:S(2)}, u32[]{:S(2)}) collective-permute-start(bf16[4,8,4608]{2,1,0:T(8,128)(2,1)S(1)} %get-tuple-element.27), channel_id=1, source_target_pairs={{0,20},{2,22},{4,16},{6,18},{8,28},{10,30},{12,24},{14,26},{16,4},... | collective-permute-start | bytes 884744 | tf_op jit(solution)/shard_map/ppermute | solution.py:140
  96.1 0.9 collective-permute-done.12
  97.0 0.9 collective-permute-start.15
  97.9 17.0 %collective-permute-done.13 = bf16[4,8,4608]{2,1,0:T(8,128)(2,1)S(1)} collective-permute-done((bf16[4,8,4608]{2,1,0:T(8,128)(2,1)S(1)}, bf16[4,8,4608]{2,1,0:T(8,128)(2,1)S(1)}, u32[]{:S(2)}, u32[]{:S(2)}) %collective-permute-start.13) | collective-permute-done | bytes 294944 | tf_op jit(solution)/shard_map/ppermute | solution.py:140
  115.1 0.0 copy-start.5
  115.1 1.2 %fusion.2 = f32[4,96,64]{1,2,0:T(8,128)S(1)} fusion(bf16[4,96,4096]{2,1,0:T(8,128)(2,1)S(1)} %copy-done, bf16[4,64,4608]{2,1,0:T(8,128)(2,1)S(1)} %constant_dynamic-update-slice_fusion), kind=kOutput, calls=%fused_computation.4 | convolution fusion | flops 201326592 | bytes 5341184 | tf_op jit(solution)/shard_map/dot_general | solution.py:142
  116.4 0.1 collective-permute-start.16
  116.5 1.3 %collective-permute-done.16 = f32[4,96,64]{1,2,0:T(8,128)S(1)} collective-permute-done((f32[4,96,64]{1,2,0:T(8,128)S(1)}, f32[4,96,64]{1,2,0:T(8,128)S(1)}, u32[]{:S(2)}, u32[]{:S(2)}) %collective-permute-start.16) | collective-permute-done | bytes 98336 | tf_op jit(solution)/shard_map/ppermute | solution.py:144
  117.8 0.3 fusion.5
  118.1 0.3 add_add_fusion
  118.4 0.9 add_convert_fusion
  (42 shorter events, 0.3 us)
Async XLA Ops:
  0.0 46.8 %copy-start = (bf16[4,96,4096]{2,1,0:T(8,128)(2,1)S(1)}, bf16[4,96,4096]{2,1,0:T(8,128)(2,1)}, u32[]{:S(2)}) copy-start(bf16[4,96,4096]{2,1,0:T(8,128)(2,1)} %param.7) | copy-start | bytes 9437188
  20.4 35.9 %collective-permute-start.2 = (bf16[2,8,4608]{2,1,0:T(8,128)(2,1)}, bf16[2,8,4608]{2,1,0:T(8,128)(2,1)S(1)}, u32[]{:S(2)}, u32[]{:S(2)}) collective-permute-start(bf16[2,8,4608]{2,1,0:T(8,128)(2,1)} %get-tuple-element.18), channel_id=1, source_target_pairs={{0,2},{2,0},{4,6},{6,4},{8,10},{10,8},{12,14},{14,12},{1,3},{3,1},... | collective-permute-start | bytes 442376 | tf_op jit(solution)/shard_map/ppermute | solution.py:106
  23.4 48.2 %collective-permute-start.6 = (bf16[2,8,4608]{2,1,0:T(8,128)(2,1)}, bf16[2,8,4608]{2,1,0:T(8,128)(2,1)}, u32[]{:S(2)}, u32[]{:S(2)}) collective-permute-start(bf16[2,8,4608]{2,1,0:T(8,128)(2,1)} %get-tuple-element.18), channel_id=1, source_target_pairs={{0,10},{2,8},{4,14},{6,12},{8,2},{10,0},{12,6},{14,4},{1,11},{3,9}... | collective-permute-start | bytes 442376 | tf_op jit(solution)/shard_map/ppermute | solution.py:106
  25.9 33.8 %collective-permute-start.3 = (bf16[2,8,4608]{2,1,0:T(8,128)(2,1)}, bf16[2,8,4608]{2,1,0:T(8,128)(2,1)}, u32[]{:S(2)}, u32[]{:S(2)}) collective-permute-start(bf16[2,8,4608]{2,1,0:T(8,128)(2,1)} %get-tuple-element.19), channel_id=1, source_target_pairs={{0,4},{2,6},{4,0},{6,2},{8,12},{10,14},{12,8},{14,10},{1,5},{3,7},... | collective-permute-start | bytes 442376 | tf_op jit(solution)/shard_map/ppermute | solution.py:106
  27.5 44.0 %collective-permute-start.7 = (bf16[2,8,4608]{2,1,0:T(8,128)(2,1)}, bf16[2,8,4608]{2,1,0:T(8,128)(2,1)}, u32[]{:S(2)}, u32[]{:S(2)}) collective-permute-start(bf16[2,8,4608]{2,1,0:T(8,128)(2,1)} %get-tuple-element.19), channel_id=1, source_target_pairs={{0,12},{2,14},{4,8},{6,10},{8,4},{10,6},{12,0},{14,2},{1,13},{3,15... | collective-permute-start | bytes 442376 | tf_op jit(solution)/shard_map/ppermute | solution.py:106
  27.5 34.5 %collective-permute-start.4 = (bf16[2,8,4608]{2,1,0:T(8,128)(2,1)}, bf16[2,8,4608]{2,1,0:T(8,128)(2,1)}, u32[]{:S(2)}, u32[]{:S(2)}) collective-permute-start(bf16[2,8,4608]{2,1,0:T(8,128)(2,1)} %get-tuple-element.20), channel_id=1, source_target_pairs={{0,6},{2,4},{4,2},{6,0},{8,14},{10,12},{12,10},{14,8},{1,7},{3,5},... | collective-permute-start | bytes 442376 | tf_op jit(solution)/shard_map/ppermute | solution.py:106
  46.8 7.1 %copy-start.2 = (bf16[2,64,4096]{2,1,0:T(8,128)(2,1)S(1)}, bf16[2,64,4096]{2,1,0:T(8,128)(2,1)}, u32[]{:S(2)}) copy-start(bf16[2,64,4096]{2,1,0:T(8,128)(2,1)} %down_ref.1) | copy-start | bytes 3145732
  55.5 0.7 copy-start.6
  55.5 4.2 %copy-start.1 = (bf16[2,8,4608]{2,1,0:T(8,128)(2,1)S(1)}, bf16[2,8,4608]{2,1,0:T(8,128)(2,1)}, u32[]{:S(2)}) copy-start(bf16[2,8,4608]{2,1,0:T(8,128)(2,1)} %get-tuple-element.17.rest_0_) | copy-start | bytes 442372
  56.2 15.3 %collective-permute-start.8 = (bf16[2,8,4608]{2,1,0:T(8,128)(2,1)}, bf16[2,8,4608]{2,1,0:T(8,128)(2,1)}, u32[]{:S(2)}, u32[]{:S(2)}) collective-permute-start(bf16[2,8,4608]{2,1,0:T(8,128)(2,1)} %get-tuple-element.20), channel_id=1, source_target_pairs={{0,14},{2,12},{4,10},{6,8},{8,6},{10,4},{12,2},{14,0},{1,15},{3,13... | collective-permute-start | bytes 442376 | tf_op jit(solution)/shard_map/ppermute | solution.py:106
  59.7 11.8 %collective-permute-start.5 = (bf16[2,8,4608]{2,1,0:T(8,128)(2,1)S(1)}, bf16[2,8,4608]{2,1,0:T(8,128)(2,1)}, u32[]{:S(2)}, u32[]{:S(2)}) collective-permute-start(bf16[2,8,4608]{2,1,0:T(8,128)(2,1)S(1)} %copy-done.1), channel_id=1, source_target_pairs={{0,8},{2,10},{4,12},{6,14},{8,0},{10,2},{12,4},{14,6},{1,9},{3,11}... | collective-permute-start | bytes 442376 | tf_op jit(solution)/shard_map/ppermute | solution.py:106
  62.0 56.1 %collective-permute-start = (f32[384,512]{1,0:T(8,128)S(1)}, f32[384,512]{1,0:T(8,128)S(1)}, u32[]{:S(2)}, u32[]{:S(2)}) collective-permute-start(f32[384,512]{1,0:T(8,128)S(1)} %constant_dynamic-slice_fusion), channel_id=1, source_target_pairs={{0,1},{1,0},{2,3},{3,2},{4,5},{5,4},{6,7},{7,6},{8,9},{9,8},{10,11... | collective-permute-start | bytes 2359304 | tf_op jit(solution)/shard_map/ppermute | solution.py:124
  71.5 46.5 %collective-permute-start.1 = (f32[384,128]{1,0:T(8,128)}, f32[384,128]{1,0:T(8,128)S(1)}, u32[]{:S(2)}, u32[]{:S(2)}) collective-permute-start(f32[384,128]{1,0:T(8,128)} %fusion.40), channel_id=1, source_target_pairs={{0,1},{1,0},{2,3},{3,2},{4,5},{5,4},{6,7},{7,6},{8,9},{9,8},{10,11... | collective-permute-start | bytes 589832 | tf_op jit(solution)/shard_map/ppermute | solution.py:126
  77.6 9.5 %collective-permute-start.9 = (bf16[4,8,4608]{2,1,0:T(8,128)(2,1)S(1)}, bf16[4,8,4608]{2,1,0:T(8,128)(2,1)S(1)}, u32[]{:S(2)}, u32[]{:S(2)}) collective-permute-start(bf16[4,8,4608]{2,1,0:T(8,128)(2,1)S(1)} %get-tuple-element.22), channel_id=1, source_target_pairs={{0,2},{2,0},{4,6},{6,4},{8,10},{10,8},{12,14},{14,12},{16,18},{18,... | collective-permute-start | bytes 884744 | tf_op jit(solution)/shard_map/ppermute | solution.py:140
  78.5 9.8 %collective-permute-start.10 = (bf16[4,8,4608]{2,1,0:T(8,128)(2,1)S(1)}, bf16[4,8,4608]{2,1,0:T(8,128)(2,1)S(1)}, u32[]{:S(2)}, u32[]{:S(2)}) collective-permute-start(bf16[4,8,4608]{2,1,0:T(8,128)(2,1)S(1)} %get-tuple-element.23), channel_id=1, source_target_pairs={{0,4},{2,6},{4,0},{6,2},{8,12},{10,14},{12,8},{14,10},{16,20},{18,... | collective-permute-start | bytes 884744 | tf_op jit(solution)/shard_map/ppermute | solution.py:140
  78.5 16.1 %collective-permute-start.11 = (bf16[4,8,4608]{2,1,0:T(8,128)(2,1)S(1)}, bf16[4,8,4608]{2,1,0:T(8,128)(2,1)S(1)}, u32[]{:S(2)}, u32[]{:S(2)}) collective-permute-start(bf16[4,8,4608]{2,1,0:T(8,128)(2,1)S(1)} %get-tuple-element.24), channel_id=1, source_target_pairs={{0,6},{2,4},{4,2},{6,0},{8,14},{10,12},{12,10},{14,8},{16,22},{18,... | collective-permute-start | bytes 884744 | tf_op jit(solution)/shard_map/ppermute | solution.py:140
  87.1 9.9 %collective-permute-start.12 = (bf16[4,8,4608]{2,1,0:T(8,128)(2,1)S(1)}, bf16[4,8,4608]{2,1,0:T(8,128)(2,1)S(1)}, u32[]{:S(2)}, u32[]{:S(2)}) collective-permute-start(bf16[4,8,4608]{2,1,0:T(8,128)(2,1)S(1)} %get-tuple-element.25), channel_id=1, source_target_pairs={{0,16},{2,18},{4,20},{6,22},{8,24},{10,26},{12,28},{14,30},{16,0},... | collective-permute-start | bytes 884744 | tf_op jit(solution)/shard_map/ppermute | solution.py:140
  88.4 26.6 %collective-permute-start.13 = (bf16[4,8,4608]{2,1,0:T(8,128)(2,1)S(1)}, bf16[4,8,4608]{2,1,0:T(8,128)(2,1)S(1)}, u32[]{:S(2)}, u32[]{:S(2)}) collective-permute-start(bf16[4,8,4608]{2,1,0:T(8,128)(2,1)S(1)} %get-tuple-element.26), channel_id=1, source_target_pairs={{0,18},{2,16},{4,22},{6,20},{8,26},{10,24},{12,30},{14,28},{16,2},... | collective-permute-start | bytes 884744 | tf_op jit(solution)/shard_map/ppermute | solution.py:140
  94.6 20.4 %collective-permute-start.14 = (bf16[4,8,4608]{2,1,0:T(8,128)(2,1)S(1)}, bf16[4,8,4608]{2,1,0:T(8,128)(2,1)S(1)}, u32[]{:S(2)}, u32[]{:S(2)}) collective-permute-start(bf16[4,8,4608]{2,1,0:T(8,128)(2,1)S(1)} %get-tuple-element.27), channel_id=1, source_target_pairs={{0,20},{2,22},{4,16},{6,18},{8,28},{10,30},{12,24},{14,26},{16,4},... | collective-permute-start | bytes 884744 | tf_op jit(solution)/shard_map/ppermute | solution.py:140
  97.0 18.0 %collective-permute-start.15 = (bf16[4,8,4608]{2,1,0:T(8,128)(2,1)S(1)}, bf16[4,8,4608]{2,1,0:T(8,128)(2,1)S(1)}, u32[]{:S(2)}, u32[]{:S(2)}) collective-permute-start(bf16[4,8,4608]{2,1,0:T(8,128)(2,1)S(1)} %get-tuple-element.28), channel_id=1, source_target_pairs={{0,22},{2,20},{4,18},{6,16},{8,30},{10,28},{12,26},{14,24},{16,6},... | collective-permute-start | bytes 884744 | tf_op jit(solution)/shard_map/ppermute | solution.py:140
  115.1 3.0 %copy-start.3 = (f32[384,1024]{1,0:T(8,128)S(1)}, f32[384,1024]{1,0:T(8,128)}, u32[]{:S(2)}) copy-start(f32[384,1024]{1,0:T(8,128)} %fusion.39) | copy-start | bytes 4718596
  115.1 3.0 %copy-start.4 = (f32[384,128]{1,0:T(8,128)S(1)}, f32[384,128]{1,0:T(8,128)}, u32[]{:S(2)}) copy-start(f32[384,128]{1,0:T(8,128)} %fusion.40) | copy-start | bytes 589828
  115.1 3.0 %copy-start.5 = (bf16[2,64,512]{2,1,0:T(8,128)(2,1)S(1)}, bf16[2,64,512]{2,1,0:T(8,128)(2,1)}, u32[]{:S(2)}) copy-start(bf16[2,64,512]{2,1,0:T(8,128)(2,1)} %up_ref.1) | copy-start | bytes 393220
  116.4 1.4 %collective-permute-start.16 = (f32[4,96,64]{1,2,0:T(8,128)S(1)}, f32[4,96,64]{1,2,0:T(8,128)S(1)}, u32[]{:S(2)}, u32[]{:S(2)}) collective-permute-start(f32[4,96,64]{1,2,0:T(8,128)S(1)} %fusion.2), channel_id=1, source_target_pairs={{0,1},{1,0},{2,3},{3,2},{4,5},{5,4},{6,7},{7,6},{8,9},{9,8},{10,11... | collective-permute-start | bytes 294920 | tf_op jit(solution)/shard_map/ppermute | solution.py:144

commit v2 on v1

--- a/solution.py
+++ b/solution.py
@@ -16,19 +16,10 @@
     )
 
 
-def cut_kernel(wide, narrow, rows, piece_ref, down_ref, up_ref, *rest):
-    outs, sem = rest[:-1], rest[-1]
-    copies = []
+def cut_kernel(wide, piece_ref, down_ref, up_ref, *outs):
     for index, out_ref in enumerate(outs):
-        start = pl.multiple_of(piece_ref[index] * rows, rows)
-        copies.append(pltpu.make_async_copy(
-            down_ref.at[:, pl.ds(start, rows), :], out_ref.at[:, :, pl.ds(0, wide)], sem.at[2 * index]))
-        copies.append(pltpu.make_async_copy(
-            up_ref.at[:, pl.ds(start, rows), :], out_ref.at[:, :, pl.ds(wide, narrow)], sem.at[2 * index + 1]))
-    for copy in copies:
-        copy.start()
-    for copy in copies:
-        copy.wait()
+        out_ref[:, :, :wide] = down_ref[:, piece_ref[index]]
+        out_ref[:, :, wide:] = up_ref[:, piece_ref[index]]
 
 
 def cut_stripes(pieces, adapter_down, adapter_up, stripe_count):
@@ -36,53 +27,41 @@
     narrow = adapter_up.shape[2]
     rows = rank // STRIPES
     out = jax.ShapeDtypeStruct((held, rows, wide + narrow), adapter_down.dtype)
+    vmem = pl.BlockSpec(memory_space=pltpu.VMEM)
     return pl.pallas_call(
-        functools.partial(cut_kernel, wide, narrow, rows),
+        functools.partial(cut_kernel, wide),
         out_shape=[out] * stripe_count,
-        in_specs=[pl.BlockSpec(memory_space=pltpu.SMEM)] + [pl.BlockSpec(memory_space=pl.ANY)] * 2,
-        out_specs=[pl.BlockSpec(memory_space=pl.ANY)] * stripe_count,
-        scratch_shapes=[pltpu.SemaphoreType.DMA((2 * stripe_count,))],
-    )(pieces, adapter_down, adapter_up)
+        in_specs=[pl.BlockSpec(memory_space=pltpu.SMEM), vmem, vmem],
+        out_specs=[vmem] * stripe_count,
+    )(
+        pieces,
+        adapter_down.reshape(held, STRIPES, rows, wide),
+        adapter_up.reshape(held, STRIPES, rows, narrow),
+    )
 
 
 def pick_kernel(server_count, steps, held, choice_ref, *rest):
-    servers, rest = rest[:server_count], rest[server_count:]
-    outs, (bank, in_sem, out_sem) = rest[:STRIPES], rest[STRIPES:]
-    loads = [
-        pltpu.make_async_copy(ref, bank.at[pl.ds(index * held, held)], in_sem.at[index])
-        for index, ref in enumerate(servers)
-    ]
-    for load in loads:
-        load.start()
-    for load in loads:
-        load.wait()
-    stores = [
-        pltpu.make_async_copy(
-            bank.at[choice_ref[asker * steps + step]], out_ref.at[step], out_sem.at[asker * steps + step])
-        for asker, out_ref in enumerate(outs)
-        for step in range(steps)
-    ]
-    for store in stores:
-        store.start()
-    for store in stores:
-        store.wait()
+    servers, outs, bank = rest[:server_count], rest[server_count:-1], rest[-1]
+    for index, ref in enumerate(servers):
+        bank[index * held:(index + 1) * held] = ref[...]
+    for asker, out_ref in enumerate(outs):
+        for step in range(steps):
+            out_ref[step] = bank[choice_ref[asker * steps + step]]
 
 
 def pick_stripes(choice, servers, steps):
     held, rows, width = servers[0].shape
     out = jax.ShapeDtypeStruct((steps, rows, width), servers[0].dtype)
     bank_bytes = len(servers) * held * rows * width * 2
+    out_bytes = STRIPES * steps * rows * width * 2
+    vmem = pl.BlockSpec(memory_space=pltpu.VMEM)
     return pl.pallas_call(
         functools.partial(pick_kernel, len(servers), steps, held),
         out_shape=[out] * STRIPES,
-        in_specs=[pl.BlockSpec(memory_space=pltpu.SMEM)] + [pl.BlockSpec(memory_space=pl.ANY)] * len(servers),
-        out_specs=[pl.BlockSpec(memory_space=pl.ANY)] * STRIPES,
-        scratch_shapes=[
-            pltpu.VMEM((len(servers) * held, rows, width), servers[0].dtype),
-            pltpu.SemaphoreType.DMA((len(servers),)),
-            pltpu.SemaphoreType.DMA((STRIPES * steps,)),
-        ],
-        compiler_params=pltpu.CompilerParams(vmem_limit_bytes=bank_bytes + (4 << 20)),
+        in_specs=[pl.BlockSpec(memory_space=pltpu.SMEM)] + [vmem] * len(servers),
+        out_specs=[vmem] * STRIPES,
+        scratch_shapes=[pltpu.VMEM((len(servers) * held, rows, width), servers[0].dtype)],
+        compiler_params=pltpu.CompilerParams(vmem_limit_bytes=2 * bank_bytes + out_bytes + (4 << 20)),
     )(choice, *servers)
 
 
@@ -115,6 +94,8 @@
     slot = slots[ask_group[:, None], source, jnp.arange(steps)[None, :]]
     choice = (jnp.bitwise_xor(source, server) * held + slot).astype(jnp.int32).reshape(-1)
 
+    acts, *banked[1:6] = lax.optimization_barrier((acts, *banked[1:6]))
+
     tokens = acts.reshape(steps * rows_dev, wide)
     partial_base = jnp.dot(tokens, value_weight, preferred_element_type=jnp.float32)
     swap = [(0, 1), (1, 0)]
@@ -128,6 +109,8 @@
     own_slot = jnp.arange(held * rank, dtype=jnp.int32) // rank
     own = jnp.where(row_slot[:, None] == own_slot[None, :], own, jnp.zeros_like(own))
     base = base + jnp.dot(own, adapter_up.reshape(held * rank, narrow), preferred_element_type=jnp.float32)
+
+    base, *banked = lax.optimization_barrier((base, *banked))
 
     picked = pick_stripes(choice, banked, steps)
     given = [picked[0]]

time: 120 us -> 92.1 us (0.77)
  Pallas kernels: 25.9 us -> 3.81 us
  waiting for transfers between devices: 40.3 us -> 27.7 us
  matrix products: 10.6 us -> 13 us
  local copies, waits for them, and re-layouts: 4.73 us -> 6.54 us
  other arithmetic: 2.32 us -> 3.53 us
    pallas_call x1, Pallas kernels: 19.8 us -> 2.36 us  [cut_stripes(): pl.pallas_call(functools.partial(cut_kernel, wide), out_shape=[out] * str...]
    ppermute x7, waiting for transfers between devices: 9.45 us -> 0.02 us  [body(): lax.ppermute(stripes[k % parts], 'adapter', [(i, i ^ k) for i in range(se...]
    pallas_call x1, Pallas kernels: 6.03 us -> 1.45 us  [pick_stripes(): pl.pallas_call(functools.partial(pick_kernel, len(servers), steps, held),...]
    ppermute x7, waiting for transfers between devices: 29.5 us -> 25.5 us  [body(): given.append(lax.ppermute(picked[k], ('groups', 'adapter'), pairs))]
    dot_general x1, matrix products: 0.31 us -> 2.37 us  [body(): jnp.dot(own, adapter_up.reshape(held * rank, narrow), preferred_element_t...]
    unnamed x23, local copies, waits for them, and re-layouts: 1.42 us -> 2.76 us
    dot_general x1, matrix products: 7.04 us -> 5.79 us  [body(): jnp.dot(tokens, value_weight, preferred_element_type=jnp.float32)]
  transfers between devices with their start and end apart: 17 -> 17, of which waited for: 7 -> 6; matrix products, arithmetic and copies ran while one was open for 13% -> 18% of each run, Pallas kernels for 5% -> 0%
where the time goes in v2:
time: 92.1 us; the launch traced here: 91.8 us
  waiting for transfers between devices  27.7 us (30%)
  starting transfers between devices  21.7 us (24%)
  blocking collectives  14.7 us (16%)
  matrix products  13 us (14%)
  local copies, waits for them, and re-layouts  6.54 us (7%)
  Pallas kernels  3.81 us (4%)
  other arithmetic  3.53 us (4%)
    ppermute x7, waiting for transfers between devices, body(): given.append(lax.ppermute(picked[k], ('groups', 'adapter'), pairs))  25.5 us
    unnamed x1, blocking collectives  14.7 us
    ppermute x7, starting transfers between devices, body(): lax.ppermute(stripes[k % parts], 'adapter', [(i, i ^ k) for i in range(se...  12.7 us
    ppermute x7, starting transfers between devices, body(): given.append(lax.ppermute(picked[k], ('groups', 'adapter'), pairs))  8.38 us
    dot_general x1, matrix products, body(): jnp.dot(tokens, value_weight, preferred_element_type=jnp.float32)  5.79 us
    unnamed x23, local copies, waits for them, and re-layouts  2.76 us
    dot_general x1, matrix products, body(): jnp.dot(own, adapter_up.reshape(held * rank, narrow), preferred_element_t...  2.37 us
    pallas_call x1, Pallas kernels, cut_stripes(): pl.pallas_call(functools.partial(cut_kernel, wide), out_shape=[out] * str...  2.36 us
  transfers between devices with their start and end apart: 17, of which 6 were waited for; matrix products, arithmetic and copies ran while one was open for 18% of the time, Pallas kernels for 0%

profile of v2, /device:TPU:0, one launch (start us, length us, event | category | flops | bytes accessed | tf_op | source)
XLA Modules:
  0.0 91.8 jit_solution(18038097437382437916)
XLA Ops:
  0.0 0.5 xor_add_fusion.piece_ref
  0.5 2.4 %shard_map.73 = (bf16[2,8,4608]{2,1,0:T(8,128)(2,1)}, bf16[2,8,4608]{2,1,0:T(8,128)(2,1)}, bf16[2,8,4608]{2,1,0:T(8,128)(2,1)}, bf16[2,8,4608]{2,1,0:T(8,128)(2,1)}) custom-call(s32[4]{0:T(128)} %xor_add_fusion.piece_ref, bf16[2,8,8,4096]{3,2,1,0:T(8,128)(2,1)} %bitcast.29, bf16[2,8,8,512]{3,2,1,0:T(8,128)(2,1)} %bitcast.32), custom_call_target="tpu_custom_call" | custom-call | tf_op jit(solution)/shard_map/pallas_call | solution.py:31
  2.9 3.0 %collective-permute-start = (bf16[2,8,4608]{2,1,0:T(8,128)(2,1)}, bf16[2,8,4608]{2,1,0:T(8,128)(2,1)S(1)}, u32[]{:S(2)}, u32[]{:S(2)}) collective-permute-start(bf16[2,8,4608]{2,1,0:T(8,128)(2,1)} %get-tuple-element.32), channel_id=1, source_target_pairs={{0,2},{2,0},{4,6},{6,4},{8,10},{10,8},{12,14},{14,12},{1,3},{3,1},... | collective-permute-start | bytes 442376 | tf_op jit(solution)/shard_map/ppermute | solution.py:85
  5.9 2.5 %collective-permute-start.4 = (bf16[2,8,4608]{2,1,0:T(8,128)(2,1)}, bf16[2,8,4608]{2,1,0:T(8,128)(2,1)S(1)}, u32[]{:S(2)}, u32[]{:S(2)}) collective-permute-start(bf16[2,8,4608]{2,1,0:T(8,128)(2,1)} %get-tuple-element.32), channel_id=1, source_target_pairs={{0,10},{2,8},{4,14},{6,12},{8,2},{10,0},{12,6},{14,4},{1,11},{3,9}... | collective-permute-start | bytes 442376 | tf_op jit(solution)/shard_map/ppermute | solution.py:85
  8.4 1.6 %collective-permute-start.1 = (bf16[2,8,4608]{2,1,0:T(8,128)(2,1)}, bf16[2,8,4608]{2,1,0:T(8,128)(2,1)}, u32[]{:S(2)}, u32[]{:S(2)}) collective-permute-start(bf16[2,8,4608]{2,1,0:T(8,128)(2,1)} %get-tuple-element.33), channel_id=1, source_target_pairs={{0,4},{2,6},{4,0},{6,2},{8,12},{10,14},{12,8},{14,10},{1,5},{3,7},... | collective-permute-start | bytes 442376 | tf_op jit(solution)/shard_map/ppermute | solution.py:85
  10.0 1.4 %collective-permute-start.2 = (bf16[2,8,4608]{2,1,0:T(8,128)(2,1)}, bf16[2,8,4608]{2,1,0:T(8,128)(2,1)}, u32[]{:S(2)}, u32[]{:S(2)}) collective-permute-start(bf16[2,8,4608]{2,1,0:T(8,128)(2,1)} %get-tuple-element.34), channel_id=1, source_target_pairs={{0,6},{2,4},{4,2},{6,0},{8,14},{10,12},{12,10},{14,8},{1,7},{3,5},... | collective-permute-start | bytes 442376 | tf_op jit(solution)/shard_map/ppermute | solution.py:85
  11.4 0.3 collective-permute-start.3
  11.8 0.8 reshape.236
  12.5 0.1 broadcast_in_dim.17
  12.6 0.1 eq.38
  12.7 1.3 %dynamic-slice = u32[1]{0:T(128)} dynamic-slice(u32[32]{0:T(128)} %constant.168, u32[]{:T(128)S(6)} %add.182), dynamic_slice_sizes={1} | dynamic-slice | bytes 12
  14.6 0.8 fusion.32
  15.4 14.7 %all-reduce = s32[64]{0:T(128)S(1)} all-reduce(s32[64]{0:T(128)S(1)} %fusion.32), channel_id=2, replica_groups=mesh['groups'=2,'adapter'=8,'tensor'=2] {'groups','adapter'}, use_global_device_ids=true, to_apply=%add | all-reduce | flops 64 | bytes 512
  30.1 0.1 reshape.240
  30.2 0.6 gather_fusion
  30.7 0.1 copy.10
  30.8 0.1 copy.11
  30.9 0.1 reshape.247
  31.0 0.6 collective-permute-start.7
  31.6 3.3 %collective-permute-start.8 = (bf16[2,8,4608]{2,1,0:T(8,128)(2,1)}, bf16[2,8,4608]{2,1,0:T(8,128)(2,1)}, u32[]{:S(2)}, u32[]{:S(2)}) collective-permute-start(bf16[2,8,4608]{2,1,0:T(8,128)(2,1)} %get-tuple-element.34), channel_id=1, source_target_pairs={{0,14},{2,12},{4,10},{6,8},{8,6},{10,4},{12,2},{14,0},{1,15},{3,13... | collective-permute-start | bytes 442376 | tf_op jit(solution)/shard_map/ppermute | solution.py:85
  34.9 5.8 %fusion.36 = f32[384,1024]{1,0:T(8,128)S(1)} fusion(bf16[384,4096]{1,0:T(8,128)(2,1)S(1)} %bitcast.27, bf16[4096,1024]{1,0:T(8,128)(2,1)} %param.8), kind=kOutput, calls=%fused_computation.87 | convolution fusion | flops 3221225472 | bytes 13107200 | tf_op jit(solution)/shard_map/dot_general | solution.py:100
  40.7 1.2 %copy-done.2 = f32[384,1024]{1,0:T(8,128)} copy-done((f32[384,1024]{1,0:T(8,128)}, f32[384,1024]{1,0:T(8,128)S(1)}, u32[]{:S(2)}) %copy-start.2) | copy-done | bytes 1572888
  41.9 1.0 %constant_dynamic-slice_fusion = f32[384,512]{1,0:T(8,128)} fusion(f32[384,1024]{1,0:T(8,128)S(1)} %fusion.36, s32[]{:T(128)S(6)} %select_n.134), kind=kLoop, calls=%fused_computation.84 | loop fusion | bytes 1572868 | tf_op jit(solution)/shard_map/dynamic_slice | solution.py:104
  42.9 0.1 broadcast_subtract_fusion
  42.9 0.1 sub.55
  43.0 0.7 gather_fusion.1
  43.7 2.3 %fusion.37 = f32[384,128]{1,0:T(8,128)S(1)} fusion(bf16[384,4096]{1,0:T(8,128)(2,1)S(1)} %bitcast.28, bf16[128,4096]{1,0:T(8,128)(2,1)} %bitcast.30), kind=kOutput, calls=%fused_computation.88 | convolution fusion | flops 402653184 | bytes 4390912 | tf_op jit(solution)/shard_map/dot_general | solution.py:14
  46.1 0.0 copy-start.1
  46.1 0.6 collective-permute-start.6
  46.7 1.1 %collective-permute-done.6 = f32[384,128]{1,0:T(8,128)S(1)} collective-permute-done((f32[384,128]{1,0:T(8,128)S(1)}, f32[384,128]{1,0:T(8,128)S(1)}, u32[]{:S(2)}, u32[]{:S(2)}) %collective-permute-start.6) | collective-permute-done | bytes 196640 | tf_op jit(solution)/shard_map/ppermute | solution.py:107
  47.8 2.4 %add_add_fusion = f32[384,512]{1,0:T(8,128)} fusion(f32[384,512]{1,0:T(8,128)} %collective-permute-done.5, f32[384,1024]{1,0:T(8,128)S(1)} %copy-done.3, s32[]{:T(128)S(6)} %select_n.133, bf16[128,512]{1,0:T(8,128)(2,1)S(1)} %bitcast.33, f32[384,128]{1,0:T(8,128)S(1)} %fusion.37, f32[384,128]{1,0:T(8,128)S(1)} %collective-permute-done.6, ...), kind=kOutput, calls=%fused_computation.5 | convolution fusion | flops 50921472 | bytes 2885636 | tf_op jit(solution)/shard_map/dot_general | solution.py:111
  50.1 1.4 %shard_map.74 = (bf16[4,8,4608]{2,1,0:T(8,128)(2,1)S(1)}, bf16[4,8,4608]{2,1,0:T(8,128)(2,1)S(1)}, bf16[4,8,4608]{2,1,0:T(8,128)(2,1)S(1)}, bf16[4,8,4608]{2,1,0...) custom-call(s32[32]{0:T(128)S(1)} %fusion.23.choice_ref, ...), custom_call_target="tpu_custom_call" | custom-call | tf_op jit(solution)/shard_map/pallas_call | solution.py:58
  51.6 1.6 %collective-permute-start.9 = (bf16[4,8,4608]{2,1,0:T(8,128)(2,1)S(1)}, bf16[4,8,4608]{2,1,0:T(8,128)(2,1)S(1)}, u32[]{:S(2)}, u32[]{:S(2)}) collective-permute-start(bf16[4,8,4608]{2,1,0:T(8,128)(2,1)S(1)} %get-tuple-element.52), channel_id=1, source_target_pairs={{0,2},{2,0},{4,6},{6,4},{8,10},{10,8},{12,14},{14,12},{16,18},{18,... | collective-permute-start | bytes 884744 | tf_op jit(solution)/shard_map/ppermute | solution.py:123
  53.1 2.0 %collective-permute-start.11 = (bf16[4,8,4608]{2,1,0:T(8,128)(2,1)S(1)}, bf16[4,8,4608]{2,1,0:T(8,128)(2,1)S(1)}, u32[]{:S(2)}, u32[]{:S(2)}) collective-permute-start(bf16[4,8,4608]{2,1,0:T(8,128)(2,1)S(1)} %get-tuple-element.54), channel_id=1, source_target_pairs={{0,6},{2,4},{4,2},{6,0},{8,14},{10,12},{12,10},{14,8},{16,22},{18,... | collective-permute-start | bytes 884744 | tf_op jit(solution)/shard_map/ppermute | solution.py:123
  55.2 0.5 collective-permute-start.12
  55.7 2.4 %collective-permute-start.13 = (bf16[4,8,4608]{2,1,0:T(8,128)(2,1)S(1)}, bf16[4,8,4608]{2,1,0:T(8,128)(2,1)S(1)}, u32[]{:S(2)}, u32[]{:S(2)}) collective-permute-start(bf16[4,8,4608]{2,1,0:T(8,128)(2,1)S(1)} %get-tuple-element.56), channel_id=1, source_target_pairs={{0,18},{2,16},{4,22},{6,20},{8,26},{10,24},{12,30},{14,28},{16,2},... | collective-permute-start | bytes 884744 | tf_op jit(solution)/shard_map/ppermute | solution.py:123
  58.1 2.8 %collective-permute-done.9 = bf16[4,8,4608]{2,1,0:T(8,128)(2,1)S(1)} collective-permute-done((bf16[4,8,4608]{2,1,0:T(8,128)(2,1)S(1)}, bf16[4,8,4608]{2,1,0:T(8,128)(2,1)S(1)}, u32[]{:S(2)}, u32[]{:S(2)}) %collective-permute-start.9) | collective-permute-done | bytes 294944 | tf_op jit(solution)/shard_map/ppermute | solution.py:123
  61.0 2.0 %collective-permute-done.10 = bf16[4,8,4608]{2,1,0:T(8,128)(2,1)S(1)} collective-permute-done((bf16[4,8,4608]{2,1,0:T(8,128)(2,1)S(1)}, bf16[4,8,4608]{2,1,0:T(8,128)(2,1)S(1)}, u32[]{:S(2)}, u32[]{:S(2)}) %collective-permute-start.10) | collective-permute-done | bytes 294944 | tf_op jit(solution)/shard_map/ppermute | solution.py:123
  63.0 1.9 %collective-permute-start.15 = (bf16[4,8,4608]{2,1,0:T(8,128)(2,1)S(1)}, bf16[4,8,4608]{2,1,0:T(8,128)(2,1)S(1)}, u32[]{:S(2)}, u32[]{:S(2)}) collective-permute-start(bf16[4,8,4608]{2,1,0:T(8,128)(2,1)S(1)} %get-tuple-element.58), channel_id=1, source_target_pairs={{0,22},{2,20},{4,18},{6,16},{8,30},{10,28},{12,26},{14,24},{16,6},... | collective-permute-start | bytes 884744 | tf_op jit(solution)/shard_map/ppermute | solution.py:123
  64.9 8.3 %collective-permute-done.11 = bf16[4,8,4608]{2,1,0:T(8,128)(2,1)S(1)} collective-permute-done((bf16[4,8,4608]{2,1,0:T(8,128)(2,1)S(1)}, bf16[4,8,4608]{2,1,0:T(8,128)(2,1)S(1)}, u32[]{:S(2)}, u32[]{:S(2)}) %collective-permute-start.11) | collective-permute-done | bytes 294944 | tf_op jit(solution)/shard_map/ppermute | solution.py:123
  73.2 12.3 %collective-permute-done.13 = bf16[4,8,4608]{2,1,0:T(8,128)(2,1)S(1)} collective-permute-done((bf16[4,8,4608]{2,1,0:T(8,128)(2,1)S(1)}, bf16[4,8,4608]{2,1,0:T(8,128)(2,1)S(1)}, u32[]{:S(2)}, u32[]{:S(2)}) %collective-permute-start.13) | collective-permute-done | bytes 294944 | tf_op jit(solution)/shard_map/ppermute | solution.py:123
  85.7 1.2 %fusion = f32[4,96,64]{1,2,0:T(8,128)S(1)} fusion(bf16[4,96,4096]{2,1,0:T(8,128)(2,1)S(1)} %copy-done, bf16[4,64,4608]{2,1,0:T(8,128)(2,1)S(1)} %constant_dynamic-update-slice_fusion), kind=kOutput, calls=%fused_computation.2 | convolution fusion | flops 201326592 | bytes 5341184 | tf_op jit(solution)/shard_map/dot_general | solution.py:125
  87.0 0.2 copy-done.5
  87.1 0.1 broadcast_in_dim.38
  87.2 0.1 eq.44
  87.3 1.2 %collective-permute-done.16 = f32[4,96,64]{1,2,0:T(8,128)S(1)} collective-permute-done((f32[4,96,64]{1,2,0:T(8,128)S(1)}, f32[4,96,64]{1,2,0:T(8,128)S(1)}, u32[]{:S(2)}, u32[]{:S(2)}) %collective-permute-start.16) | collective-permute-done | bytes 98336 | tf_op jit(solution)/shard_map/ppermute | solution.py:127
  88.5 1.3 %fusion.2 = f32[4,96,512]{2,1,0:T(8,128)S(1)} fusion(bf16[4,64,4608]{2,1,0:T(8,128)(2,1)} %copy-done.5, f32[4,96,64]{1,2,0:T(8,128)S(1)} %fusion, f32[4,96,64]{1,2,0:T(8,128)S(1)} %collective-permute-done.16, pred[4,96]{1,0:T(4,128)(4,1)S(1)} %eq.44), kind=kOutput, calls=%fused_computation.6 | convolution fusion | flops 25239552 | bytes 1245568 | tf_op jit(solution)/shard_map/dot_general | solution.py:130
  89.7 2.0 %add_convert_fusion = bf16[4,96,512]{2,1,0:T(8,128)(2,1)} fusion(f32[4,96,512]{2,1,0:T(8,128)} %bitcast.31, f32[4,96,512]{2,1,0:T(8,128)S(1)} %fusion.2), kind=kLoop, calls=%fused_computation.4 | loop fusion | flops 393216 | bytes 1966080 | tf_op jit(solution)/shard_map/convert_element_type | solution.py:132
  (42 shorter events, 0.3 us)
Async XLA Ops:
  0.0 34.9 %copy-start = (bf16[4,96,4096]{2,1,0:T(8,128)(2,1)S(1)}, bf16[4,96,4096]{2,1,0:T(8,128)(2,1)}, u32[]{:S(2)}) copy-start(bf16[4,96,4096]{2,1,0:T(8,128)(2,1)} %param.7) | copy-start | bytes 9437188
  2.9 28.1 %collective-permute-start = (bf16[2,8,4608]{2,1,0:T(8,128)(2,1)}, bf16[2,8,4608]{2,1,0:T(8,128)(2,1)S(1)}, u32[]{:S(2)}, u32[]{:S(2)}) collective-permute-start(bf16[2,8,4608]{2,1,0:T(8,128)(2,1)} %get-tuple-element.32), channel_id=1, source_target_pairs={{0,2},{2,0},{4,6},{6,4},{8,10},{10,8},{12,14},{14,12},{1,3},{3,1},... | collective-permute-start | bytes 442376 | tf_op jit(solution)/shard_map/ppermute | solution.py:85
  5.9 29.0 %collective-permute-start.4 = (bf16[2,8,4608]{2,1,0:T(8,128)(2,1)}, bf16[2,8,4608]{2,1,0:T(8,128)(2,1)S(1)}, u32[]{:S(2)}, u32[]{:S(2)}) collective-permute-start(bf16[2,8,4608]{2,1,0:T(8,128)(2,1)} %get-tuple-element.32), channel_id=1, source_target_pairs={{0,10},{2,8},{4,14},{6,12},{8,2},{10,0},{12,6},{14,4},{1,11},{3,9}... | collective-permute-start | bytes 442376 | tf_op jit(solution)/shard_map/ppermute | solution.py:85
  8.4 23.2 %collective-permute-start.1 = (bf16[2,8,4608]{2,1,0:T(8,128)(2,1)}, bf16[2,8,4608]{2,1,0:T(8,128)(2,1)}, u32[]{:S(2)}, u32[]{:S(2)}) collective-permute-start(bf16[2,8,4608]{2,1,0:T(8,128)(2,1)} %get-tuple-element.33), channel_id=1, source_target_pairs={{0,4},{2,6},{4,0},{6,2},{8,12},{10,14},{12,8},{14,10},{1,5},{3,7},... | collective-permute-start | bytes 442376 | tf_op jit(solution)/shard_map/ppermute | solution.py:85
  10.0 24.9 %collective-permute-start.2 = (bf16[2,8,4608]{2,1,0:T(8,128)(2,1)}, bf16[2,8,4608]{2,1,0:T(8,128)(2,1)}, u32[]{:S(2)}, u32[]{:S(2)}) collective-permute-start(bf16[2,8,4608]{2,1,0:T(8,128)(2,1)} %get-tuple-element.34), channel_id=1, source_target_pairs={{0,6},{2,4},{4,2},{6,0},{8,14},{10,12},{12,10},{14,8},{1,7},{3,5},... | collective-permute-start | bytes 442376 | tf_op jit(solution)/shard_map/ppermute | solution.py:85
  11.4 23.5 %collective-permute-start.3 = (bf16[2,8,4608]{2,1,0:T(8,128)(2,1)}, bf16[2,8,4608]{2,1,0:T(8,128)(2,1)}, u32[]{:S(2)}, u32[]{:S(2)}) collective-permute-start(bf16[2,8,4608]{2,1,0:T(8,128)(2,1)} %get-tuple-element.43.rest_0_), channel_id=1, source_target_pairs={{0,8},{2,10},{4,12},{6,14},{8,0},{10,2},{12,4},{14,6},{1,9},{3,11}... | collective-permute-start | bytes 442376 | tf_op jit(solution)/shard_map/ppermute | solution.py:85
  31.0 19.1 %collective-permute-start.7 = (bf16[2,8,4608]{2,1,0:T(8,128)(2,1)}, bf16[2,8,4608]{2,1,0:T(8,128)(2,1)}, u32[]{:S(2)}, u32[]{:S(2)}) collective-permute-start(bf16[2,8,4608]{2,1,0:T(8,128)(2,1)} %get-tuple-element.33), channel_id=1, source_target_pairs={{0,12},{2,14},{4,8},{6,10},{8,4},{10,6},{12,0},{14,2},{1,13},{3,15... | collective-permute-start | bytes 442376 | tf_op jit(solution)/shard_map/ppermute | solution.py:85
  31.6 18.5 %collective-permute-start.8 = (bf16[2,8,4608]{2,1,0:T(8,128)(2,1)}, bf16[2,8,4608]{2,1,0:T(8,128)(2,1)}, u32[]{:S(2)}, u32[]{:S(2)}) collective-permute-start(bf16[2,8,4608]{2,1,0:T(8,128)(2,1)} %get-tuple-element.34), channel_id=1, source_target_pairs={{0,14},{2,12},{4,10},{6,8},{8,6},{10,4},{12,2},{14,0},{1,15},{3,13... | collective-permute-start | bytes 442376 | tf_op jit(solution)/shard_map/ppermute | solution.py:85
  40.7 1.2 %copy-start.2 = (f32[384,1024]{1,0:T(8,128)}, f32[384,1024]{1,0:T(8,128)S(1)}, u32[]{:S(2)}) copy-start(f32[384,1024]{1,0:T(8,128)S(1)} %fusion.36) | copy-start | bytes 4718596
  42.9 4.9 %collective-permute-start.5 = (f32[384,512]{1,0:T(8,128)}, f32[384,512]{1,0:T(8,128)}, u32[]{:S(2)}, u32[]{:S(2)}) collective-permute-start(f32[384,512]{1,0:T(8,128)} %constant_dynamic-slice_fusion), channel_id=1, source_target_pairs={{0,1},{1,0},{2,3},{3,2},{4,5},{5,4},{6,7},{7,6},{8,9},{9,8},{10,11... | collective-permute-start | bytes 2359304 | tf_op jit(solution)/shard_map/ppermute | solution.py:105
  43.7 4.0 %copy-start.3 = (f32[384,1024]{1,0:T(8,128)S(1)}, f32[384,1024]{1,0:T(8,128)}, u32[]{:S(2)}) copy-start(f32[384,1024]{1,0:T(8,128)} %copy-done.2) | copy-start | bytes 4718596
  43.7 4.0 %copy-start.4 = (bf16[2,64,512]{2,1,0:T(8,128)(2,1)S(1)}, bf16[2,64,512]{2,1,0:T(8,128)(2,1)}, u32[]{:S(2)}) copy-start(bf16[2,64,512]{2,1,0:T(8,128)(2,1)} %param.10) | copy-start | bytes 393220
  46.1 4.0 %copy-start.1 = (bf16[2,8,4608]{2,1,0:T(8,128)(2,1)S(1)}, bf16[2,8,4608]{2,1,0:T(8,128)(2,1)}, u32[]{:S(2)}) copy-start(bf16[2,8,4608]{2,1,0:T(8,128)(2,1)} %get-tuple-element.43.rest_0_) | copy-start | bytes 442372
  46.1 1.6 %collective-permute-start.6 = (f32[384,128]{1,0:T(8,128)S(1)}, f32[384,128]{1,0:T(8,128)S(1)}, u32[]{:S(2)}, u32[]{:S(2)}) collective-permute-start(f32[384,128]{1,0:T(8,128)S(1)} %fusion.37), channel_id=1, source_target_pairs={{0,1},{1,0},{2,3},{3,2},{4,5},{5,4},{6,7},{7,6},{8,9},{9,8},{10,11... | collective-permute-start | bytes 589832 | tf_op jit(solution)/shard_map/ppermute | solution.py:107
  51.6 9.4 %collective-permute-start.9 = (bf16[4,8,4608]{2,1,0:T(8,128)(2,1)S(1)}, bf16[4,8,4608]{2,1,0:T(8,128)(2,1)S(1)}, u32[]{:S(2)}, u32[]{:S(2)}) collective-permute-start(bf16[4,8,4608]{2,1,0:T(8,128)(2,1)S(1)} %get-tuple-element.52), channel_id=1, source_target_pairs={{0,2},{2,0},{4,6},{6,4},{8,10},{10,8},{12,14},{14,12},{16,18},{18,... | collective-permute-start | bytes 884744 | tf_op jit(solution)/shard_map/ppermute | solution.py:123
  53.1 9.9 %collective-permute-start.10 = (bf16[4,8,4608]{2,1,0:T(8,128)(2,1)S(1)}, bf16[4,8,4608]{2,1,0:T(8,128)(2,1)S(1)}, u32[]{:S(2)}, u32[]{:S(2)}) collective-permute-start(bf16[4,8,4608]{2,1,0:T(8,128)(2,1)S(1)} %get-tuple-element.53), channel_id=1, source_target_pairs={{0,4},{2,6},{4,0},{6,2},{8,12},{10,14},{12,8},{14,10},{16,20},{18,... | collective-permute-start | bytes 884744 | tf_op jit(solution)/shard_map/ppermute | solution.py:123
  53.1 20.0 %collective-permute-start.11 = (bf16[4,8,4608]{2,1,0:T(8,128)(2,1)S(1)}, bf16[4,8,4608]{2,1,0:T(8,128)(2,1)S(1)}, u32[]{:S(2)}, u32[]{:S(2)}) collective-permute-start(bf16[4,8,4608]{2,1,0:T(8,128)(2,1)S(1)} %get-tuple-element.54), channel_id=1, source_target_pairs={{0,6},{2,4},{4,2},{6,0},{8,14},{10,12},{12,10},{14,8},{16,22},{18,... | collective-permute-start | bytes 884744 | tf_op jit(solution)/shard_map/ppermute | solution.py:123
  55.2 18.0 %collective-permute-start.12 = (bf16[4,8,4608]{2,1,0:T(8,128)(2,1)S(1)}, bf16[4,8,4608]{2,1,0:T(8,128)(2,1)S(1)}, u32[]{:S(2)}, u32[]{:S(2)}) collective-permute-start(bf16[4,8,4608]{2,1,0:T(8,128)(2,1)S(1)} %get-tuple-element.55), channel_id=1, source_target_pairs={{0,16},{2,18},{4,20},{6,22},{8,24},{10,26},{12,28},{14,30},{16,0},... | collective-permute-start | bytes 884744 | tf_op jit(solution)/shard_map/ppermute | solution.py:123
  55.7 29.9 %collective-permute-start.13 = (bf16[4,8,4608]{2,1,0:T(8,128)(2,1)S(1)}, bf16[4,8,4608]{2,1,0:T(8,128)(2,1)S(1)}, u32[]{:S(2)}, u32[]{:S(2)}) collective-permute-start(bf16[4,8,4608]{2,1,0:T(8,128)(2,1)S(1)} %get-tuple-element.56), channel_id=1, source_target_pairs={{0,18},{2,16},{4,22},{6,20},{8,26},{10,24},{12,30},{14,28},{16,2},... | collective-permute-start | bytes 884744 | tf_op jit(solution)/shard_map/ppermute | solution.py:123
  60.9 24.6 %collective-permute-start.14 = (bf16[4,8,4608]{2,1,0:T(8,128)(2,1)S(1)}, bf16[4,8,4608]{2,1,0:T(8,128)(2,1)S(1)}, u32[]{:S(2)}, u32[]{:S(2)}) collective-permute-start(bf16[4,8,4608]{2,1,0:T(8,128)(2,1)S(1)} %get-tuple-element.57), channel_id=1, source_target_pairs={{0,20},{2,22},{4,16},{6,18},{8,28},{10,30},{12,24},{14,26},{16,4},... | collective-permute-start | bytes 884744 | tf_op jit(solution)/shard_map/ppermute | solution.py:123
  63.0 22.6 %collective-permute-start.15 = (bf16[4,8,4608]{2,1,0:T(8,128)(2,1)S(1)}, bf16[4,8,4608]{2,1,0:T(8,128)(2,1)S(1)}, u32[]{:S(2)}, u32[]{:S(2)}) collective-permute-start(bf16[4,8,4608]{2,1,0:T(8,128)(2,1)S(1)} %get-tuple-element.58), channel_id=1, source_target_pairs={{0,22},{2,20},{4,18},{6,16},{8,30},{10,28},{12,26},{14,24},{16,6},... | collective-permute-start | bytes 884744 | tf_op jit(solution)/shard_map/ppermute | solution.py:123
  85.7 1.4 %copy-start.5 = (bf16[4,64,4608]{2,1,0:T(8,128)(2,1)}, bf16[4,64,4608]{2,1,0:T(8,128)(2,1)S(1)}, u32[]{:S(2)}) copy-start(bf16[4,64,4608]{2,1,0:T(8,128)(2,1)S(1)} %constant_dynamic-update-slice_fusion) | copy-start | bytes 7077892
  85.7 1.4 %copy-start.6 = (s32[4,6]{1,0:T(4,128)S(1)}, s32[4,6]{1,0:T(4,128)}, u32[]{:S(2)}) copy-start(s32[4,6]{1,0:T(4,128)} %param.11) | copy-start | bytes 292
  87.1 1.3 %collective-permute-start.16 = (f32[4,96,64]{1,2,0:T(8,128)S(1)}, f32[4,96,64]{1,2,0:T(8,128)S(1)}, u32[]{:S(2)}, u32[]{:S(2)}) collective-permute-start(f32[4,96,64]{1,2,0:T(8,128)S(1)} %fusion), channel_id=1, source_target_pairs={{0,1},{1,0},{2,3},{3,2},{4,5},{5,4},{6,7},{7,6},{8,9},{9,8},{10,11... | collective-permute-start | bytes 294920 | tf_op jit(solution)/shard_map/ppermute | solution.py:127

commit v3 on v2

--- a/solution.py
+++ b/solution.py
@@ -85,6 +85,8 @@
         banked.append(lax.ppermute(
             stripes[k % parts], "adapter", [(i, i ^ k) for i in range(servers)]))
 
+    transfer_slot, *banked[1:3] = lax.optimization_barrier((transfer_slot, *banked[1:3]))
+
     asked = transfer_offset * held + transfer_slot[:, 0]
     asked = lax.all_gather(asked, ("groups", "adapter")).reshape(groups, servers, steps)
     offsets, slots = asked // held, asked % held
@@ -94,7 +96,17 @@
     slot = slots[ask_group[:, None], source, jnp.arange(steps)[None, :]]
     choice = (jnp.bitwise_xor(source, server) * held + slot).astype(jnp.int32).reshape(-1)
 
-    acts, *banked[1:6] = lax.optimization_barrier((acts, *banked[1:6]))
+    picked = pick_stripes(choice, banked, steps)
+    given = [picked[0]]
+    for k in range(1, STRIPES):
+        pairs = []
+        for g in range(groups):
+            for i in range(servers):
+                other = (g * parts + i % parts) ^ k
+                pairs.append((g * servers + i, (other // parts) * servers + (i // parts) * parts + other % parts))
+        given.append(lax.ppermute(picked[k], ("groups", "adapter"), pairs))
+
+    acts, *given[1:4] = lax.optimization_barrier((acts, *given[1:4]))
 
     tokens = acts.reshape(steps * rows_dev, wide)
     partial_base = jnp.dot(tokens, value_weight, preferred_element_type=jnp.float32)
@@ -110,17 +122,8 @@
     own = jnp.where(row_slot[:, None] == own_slot[None, :], own, jnp.zeros_like(own))
     base = base + jnp.dot(own, adapter_up.reshape(held * rank, narrow), preferred_element_type=jnp.float32)
 
-    base, *banked = lax.optimization_barrier((base, *banked))
+    base, *given[4:] = lax.optimization_barrier((base, *given[4:]))
 
-    picked = pick_stripes(choice, banked, steps)
-    given = [picked[0]]
-    for k in range(1, STRIPES):
-        pairs = []
-        for g in range(groups):
-            for i in range(servers):
-                other = (g * parts + i % parts) ^ k
-                pairs.append((g * servers + i, (other // parts) * servers + (i // parts) * parts + other % parts))
-        given.append(lax.ppermute(picked[k], ("groups", "adapter"), pairs))
     passed = jnp.concatenate(given, axis=1)
     partial_passed = lax.dot_general(
         acts, passed[:, :, :wide], (((2,), (2,)), ((0,), (0,))), preferred_element_type=jnp.float32)

time: 92.1 us -> 88.5 us (0.961); the launches traced: 91.8 us -> 87.1 us
  waiting for transfers between devices: 27.7 us -> 22.4 us
  blocking collectives: 14.7 us -> 17.5 us
  matrix products: 13 us -> 10.6 us
  starting transfers between devices: 21.7 us -> 23.9 us
  local copies, waits for them, and re-layouts: 6.54 us -> 4.52 us
    ppermute x7, waiting for transfers between devices: 25.5 us -> 18.5 us  [body(): given.append(lax.ppermute(picked[k], ('groups', 'adapter'), pairs))]
    ppermute x7, starting transfers between devices: 8.38 us -> 11.3 us  [body(): given.append(lax.ppermute(picked[k], ('groups', 'adapter'), pairs))]
    unnamed x1, blocking collectives: 14.7 us -> 17.5 us
    ppermute x7, waiting for transfers between devices: 0.02 us -> 1.68 us  [body(): lax.ppermute(stripes[k % parts], 'adapter', [(i, i ^ k) for i in range(se...]
    dot_general x1, matrix products: 2.33 us -> 0.98 us  [contract_last(): lax.dot_general(left, right, (((left.ndim - 1,), (right.ndim - 1,)), ((),...]
    dot_general x1, matrix products: 2.37 us -> 1.22 us  [body(): jnp.dot(own, adapter_up.reshape(held * rank, narrow), preferred_element_t...]
    unnamed x23 -> x21, local copies, waits for them, and re-layouts: 2.76 us -> 1.64 us
  transfers between devices with their start and end apart: 17 -> 17, of which waited for: 6 -> 5; matrix products, arithmetic and copies ran while one was open for 18% -> 15% of each run, Pallas kernels for 0% -> 0%
where the time goes in v3:
time: 88.5 us; the launch traced here: 87.1 us
  starting transfers between devices  23.9 us (27%)
  waiting for transfers between devices  22.4 us (25%)
  blocking collectives  17.5 us (20%)
  matrix products  10.6 us (12%)
  local copies, waits for them, and re-layouts  4.52 us (5%)
  Pallas kernels  3.83 us (4%)
  other arithmetic  3.5 us (4%)
  between operations  0.94 us (1%)
    ppermute x7, waiting for transfers between devices, body(): given.append(lax.ppermute(picked[k], ('groups', 'adapter'), pairs))  18.5 us
    unnamed x1, blocking collectives  17.5 us
    ppermute x7, starting transfers between devices, body(): lax.ppermute(stripes[k % parts], 'adapter', [(i, i ^ k) for i in range(se...  11.9 us
    ppermute x7, starting transfers between devices, body(): given.append(lax.ppermute(picked[k], ('groups', 'adapter'), pairs))  11.3 us
    dot_general x1, matrix products, body(): jnp.dot(tokens, value_weight, preferred_element_type=jnp.float32)  5.87 us
    pallas_call x1, Pallas kernels, cut_stripes(): pl.pallas_call(functools.partial(cut_kernel, wide), out_shape=[out] * str...  2.34 us
    convert_element_type x1, other arithmetic, body(): (base.reshape(steps, rows_dev, narrow) + low_rank).astype(jnp.bfloat16)  2.04 us
  transfers between devices with their start and end apart: 17, of which 5 were waited for; matrix products, arithmetic and copies ran while one was open for 15% of the time, Pallas kernels for 0%

profile of v3, /device:TPU:0, one launch (start us, length us, event | category | flops | bytes accessed | tf_op | source)
XLA Modules:
  0.0 87.1 jit_solution(3814330649533287690)
XLA Ops:
  0.0 0.5 xor_add_fusion.piece_ref
  0.5 2.3 %shard_map.73 = (bf16[2,8,4608]{2,1,0:T(8,128)(2,1)}, bf16[2,8,4608]{2,1,0:T(8,128)(2,1)}, bf16[2,8,4608]{2,1,0:T(8,128)(2,1)}, bf16[2,8,4608]{2,1,0:T(8,128)(2,1)}) custom-call(s32[4]{0:T(128)} %xor_add_fusion.piece_ref, bf16[2,8,8,4096]{3,2,1,0:T(8,128)(2,1)} %bitcast.29, bf16[2,8,8,512]{3,2,1,0:T(8,128)(2,1)} %bitcast.32), custom_call_target="tpu_custom_call" | custom-call | tf_op jit(solution)/shard_map/pallas_call | solution.py:31
  2.9 3.0 %collective-permute-start = (bf16[2,8,4608]{2,1,0:T(8,128)(2,1)}, bf16[2,8,4608]{2,1,0:T(8,128)(2,1)S(1)}, u32[]{:S(2)}, u32[]{:S(2)}) collective-permute-start(bf16[2,8,4608]{2,1,0:T(8,128)(2,1)} %get-tuple-element.29), channel_id=1, source_target_pairs={{0,2},{2,0},{4,6},{6,4},{8,10},{10,8},{12,14},{14,12},{1,3},{3,1},... | collective-permute-start | bytes 442376 | tf_op jit(solution)/shard_map/ppermute | solution.py:85
  5.8 2.5 %collective-permute-start.4 = (bf16[2,8,4608]{2,1,0:T(8,128)(2,1)}, bf16[2,8,4608]{2,1,0:T(8,128)(2,1)}, u32[]{:S(2)}, u32[]{:S(2)}) collective-permute-start(bf16[2,8,4608]{2,1,0:T(8,128)(2,1)} %get-tuple-element.29), channel_id=1, source_target_pairs={{0,10},{2,8},{4,14},{6,12},{8,2},{10,0},{12,6},{14,4},{1,11},{3,9}... | collective-permute-start | bytes 442376 | tf_op jit(solution)/shard_map/ppermute | solution.py:85
  8.4 1.6 %collective-permute-start.1 = (bf16[2,8,4608]{2,1,0:T(8,128)(2,1)}, bf16[2,8,4608]{2,1,0:T(8,128)(2,1)}, u32[]{:S(2)}, u32[]{:S(2)}) collective-permute-start(bf16[2,8,4608]{2,1,0:T(8,128)(2,1)} %get-tuple-element.30), channel_id=1, source_target_pairs={{0,4},{2,6},{4,0},{6,2},{8,12},{10,14},{12,8},{14,10},{1,5},{3,7},... | collective-permute-start | bytes 442376 | tf_op jit(solution)/shard_map/ppermute | solution.py:85
  10.0 1.9 %collective-permute-start.2 = (bf16[2,8,4608]{2,1,0:T(8,128)(2,1)}, bf16[2,8,4608]{2,1,0:T(8,128)(2,1)}, u32[]{:S(2)}, u32[]{:S(2)}) collective-permute-start(bf16[2,8,4608]{2,1,0:T(8,128)(2,1)} %get-tuple-element.35), channel_id=1, source_target_pairs={{0,6},{2,4},{4,2},{6,0},{8,14},{10,12},{12,10},{14,8},{1,7},{3,5},... | collective-permute-start | bytes 442376 | tf_op jit(solution)/shard_map/ppermute | solution.py:85
  11.8 0.8 reshape.237
  12.6 0.1 broadcast_in_dim.38
  12.7 0.1 eq.38
  12.8 1.3 %dynamic-slice = u32[1]{0:T(128)} dynamic-slice(u32[32]{0:T(128)} %constant.168, u32[]{:T(128)S(6)} %add.182), dynamic_slice_sizes={1} | dynamic-slice | bytes 12
  14.8 3.0 %collective-permute-start.6 = (bf16[2,8,4608]{2,1,0:T(8,128)(2,1)}, bf16[2,8,4608]{2,1,0:T(8,128)(2,1)}, u32[]{:S(2)}, u32[]{:S(2)}) collective-permute-start(bf16[2,8,4608]{2,1,0:T(8,128)(2,1)} %get-tuple-element.35), channel_id=1, source_target_pairs={{0,14},{2,12},{4,10},{6,8},{8,6},{10,4},{12,2},{14,0},{1,15},{3,13... | collective-permute-start | bytes 442376 | tf_op jit(solution)/shard_map/ppermute | solution.py:85
  17.8 1.7 %collective-permute-done.1.rest_2_ = bf16[2,8,4608]{2,1,0:T(8,128)(2,1)} collective-permute-done((bf16[2,8,4608]{2,1,0:T(8,128)(2,1)}, bf16[2,8,4608]{2,1,0:T(8,128)(2,1)}, u32[]{:S(2)}, u32[]{:S(2)}) %collective-permute-start.1) | collective-permute-done | bytes 147488 | tf_op jit(solution)/shard_map/ppermute | solution.py:85
  19.5 0.8 fusion.32
  20.2 17.5 %all-reduce = s32[64]{0:T(128)S(1)} all-reduce(s32[64]{0:T(128)S(1)} %fusion.32), channel_id=2, replica_groups=mesh['groups'=2,'adapter'=8,'tensor'=2] {'groups','adapter'}, use_global_device_ids=true, to_apply=%add | all-reduce | flops 64 | bytes 512
  37.7 0.1 reshape.235
  37.8 0.6 gather_fusion
  38.4 0.1 copy.10
  38.5 0.1 broadcast_subtract_fusion
  38.5 0.1 sub.53
  38.6 0.1 copy.11
  38.7 0.1 reshape.247
  38.8 0.7 gather_fusion.1
  39.6 1.5 %shard_map.74 = (bf16[4,8,4608]{2,1,0:T(8,128)(2,1)S(1)}, bf16[4,8,4608]{2,1,0:T(8,128)(2,1)S(1)}, bf16[4,8,4608]{2,1,0:T(8,128)(2,1)S(1)}, bf16[4,8,4608]{2,1,0...) custom-call(s32[32]{0:T(128)S(1)} %fusion.23.choice_ref, ...), custom_call_target="tpu_custom_call" | custom-call | tf_op jit(solution)/shard_map/pallas_call | solution.py:58
  41.1 1.6 %collective-permute-start.7 = (bf16[4,8,4608]{2,1,0:T(8,128)(2,1)S(1)}, bf16[4,8,4608]{2,1,0:T(8,128)(2,1)S(1)}, u32[]{:S(2)}, u32[]{:S(2)}) collective-permute-start(bf16[4,8,4608]{2,1,0:T(8,128)(2,1)S(1)} %get-tuple-element.36), channel_id=1, source_target_pairs={{0,2},{2,0},{4,6},{6,4},{8,10},{10,8},{12,14},{14,12},{16,18},{18,... | collective-permute-start | bytes 884744 | tf_op jit(solution)/shard_map/ppermute | solution.py:107
  42.6 2.0 %collective-permute-start.9 = (bf16[4,8,4608]{2,1,0:T(8,128)(2,1)S(1)}, bf16[4,8,4608]{2,1,0:T(8,128)(2,1)S(1)}, u32[]{:S(2)}, u32[]{:S(2)}) collective-permute-start(bf16[4,8,4608]{2,1,0:T(8,128)(2,1)S(1)} %get-tuple-element.38), channel_id=1, source_target_pairs={{0,6},{2,4},{4,2},{6,0},{8,14},{10,12},{12,10},{14,8},{16,22},{18,... | collective-permute-start | bytes 884744 | tf_op jit(solution)/shard_map/ppermute | solution.py:107
  44.6 0.5 collective-permute-start.12
  45.2 2.4 %collective-permute-start.13 = (bf16[4,8,4608]{2,1,0:T(8,128)(2,1)S(1)}, bf16[4,8,4608]{2,1,0:T(8,128)(2,1)S(1)}, u32[]{:S(2)}, u32[]{:S(2)}) collective-permute-start(bf16[4,8,4608]{2,1,0:T(8,128)(2,1)S(1)} %get-tuple-element.41), channel_id=1, source_target_pairs={{0,18},{2,16},{4,22},{6,20},{8,26},{10,24},{12,30},{14,28},{16,2},... | collective-permute-start | bytes 884744 | tf_op jit(solution)/shard_map/ppermute | solution.py:107
  47.6 12.2 %collective-permute-done.7 = bf16[4,8,4608]{2,1,0:T(8,128)(2,1)S(1)} collective-permute-done((bf16[4,8,4608]{2,1,0:T(8,128)(2,1)S(1)}, bf16[4,8,4608]{2,1,0:T(8,128)(2,1)S(1)}, u32[]{:S(2)}, u32[]{:S(2)}) %collective-permute-start.7) | collective-permute-done | bytes 294944 | tf_op jit(solution)/shard_map/ppermute | solution.py:107
  59.9 0.4 collective-permute-start.14
  60.3 0.0 copy-start.2
  60.3 5.9 %fusion.36 = f32[384,1024]{1,0:T(8,128)S(1)} fusion(bf16[384,4096]{1,0:T(8,128)(2,1)S(1)} %bitcast.27, bf16[4096,1024]{1,0:T(8,128)(2,1)} %param.8), kind=kOutput, calls=%fused_computation.87 | convolution fusion | flops 3221225472 | bytes 13107200 | tf_op jit(solution)/shard_map/dot_general | solution.py:112
  66.2 0.1 constant_dynamic-slice_fusion
  66.3 0.1 collective-permute-start.10
  66.4 0.0 copy-start.3
  66.4 1.0 %fusion.37 = f32[384,128]{1,0:T(8,128)S(1)} fusion(bf16[384,4096]{1,0:T(8,128)(2,1)S(1)} %bitcast.28, bf16[128,4096]{1,0:T(8,128)(2,1)S(1)} %bitcast.30), kind=kOutput, calls=%fused_computation.88 | convolution fusion | flops 402653184 | bytes 4390912 | tf_op jit(solution)/shard_map/dot_general | solution.py:14
  67.4 0.5 collective-permute-start.11
  67.9 1.0 %collective-permute-done.11 = f32[384,128]{1,0:T(8,128)S(1)} collective-permute-done((f32[384,128]{1,0:T(8,128)S(1)}, f32[384,128]{1,0:T(8,128)S(1)}, u32[]{:S(2)}, u32[]{:S(2)}) %collective-permute-start.11) | collective-permute-done | bytes 196640 | tf_op jit(solution)/shard_map/ppermute | solution.py:119
  69.0 4.4 %collective-permute-start.15 = (bf16[4,8,4608]{2,1,0:T(8,128)(2,1)S(1)}, bf16[4,8,4608]{2,1,0:T(8,128)(2,1)S(1)}, u32[]{:S(2)}, u32[]{:S(2)}) collective-permute-start(bf16[4,8,4608]{2,1,0:T(8,128)(2,1)S(1)} %get-tuple-element.43), channel_id=1, source_target_pairs={{0,22},{2,20},{4,18},{6,16},{8,30},{10,28},{12,26},{14,24},{16,6},... | collective-permute-start | bytes 884744 | tf_op jit(solution)/shard_map/ppermute | solution.py:107
  73.4 1.2 %add_add_fusion = f32[384,512]{1,0:T(8,128)} fusion(f32[384,512]{1,0:T(8,128)S(1)} %collective-permute-done.10, f32[384,1024]{1,0:T(8,128)S(1)} %fusion.36, s32[]{:T(128)S(6)} %select_n.146, bf16[128,512]{1,0:T(8,128)(2,1)S(1)} %bitcast.33, f32[384,128]{1,0:T(8,128)S(1)} %fusion.37, f32[384,128]{1,0:T(8,128)S(1)} %collective-permute-done.11, ...), kind=kOutput, calls=%fused_computation.5 | convolution fusion | flops 50921472 | bytes 2885636 | tf_op jit(solution)/shard_map/dot_general | solution.py:123
  74.7 6.3 %collective-permute-done.15 = bf16[4,8,4608]{2,1,0:T(8,128)(2,1)S(1)} collective-permute-done((bf16[4,8,4608]{2,1,0:T(8,128)(2,1)S(1)}, bf16[4,8,4608]{2,1,0:T(8,128)(2,1)S(1)}, u32[]{:S(2)}, u32[]{:S(2)}) %collective-permute-start.15) | collective-permute-done | bytes 294944 | tf_op jit(solution)/shard_map/ppermute | solution.py:107
  81.0 0.0 copy-start.5
  81.0 1.2 %fusion = f32[4,96,64]{1,2,0:T(8,128)S(1)} fusion(bf16[4,96,4096]{2,1,0:T(8,128)(2,1)S(1)} %copy-done, bf16[4,64,4608]{2,1,0:T(8,128)(2,1)S(1)} %constant_dynamic-update-slice_fusion), kind=kOutput, calls=%fused_computation.2 | convolution fusion | flops 201326592 | bytes 5341184 | tf_op jit(solution)/shard_map/dot_general | solution.py:128
  82.3 0.2 copy-done.4
  82.5 0.1 broadcast_in_dim.40
  82.5 0.1 eq.44
  82.6 1.2 %collective-permute-done.16 = f32[4,96,64]{1,2,0:T(8,128)S(1)} collective-permute-done((f32[4,96,64]{1,2,0:T(8,128)S(1)}, f32[4,96,64]{1,2,0:T(8,128)S(1)}, u32[]{:S(2)}, u32[]{:S(2)}) %collective-permute-start.16) | collective-permute-done | bytes 98336 | tf_op jit(solution)/shard_map/ppermute | solution.py:130
  83.8 1.3 %fusion.2 = f32[4,96,512]{2,1,0:T(8,128)S(1)} fusion(bf16[4,64,4608]{2,1,0:T(8,128)(2,1)} %copy-done.4, f32[4,96,64]{1,2,0:T(8,128)S(1)} %fusion, f32[4,96,64]{1,2,0:T(8,128)S(1)} %collective-permute-done.16, pred[4,96]{1,0:T(4,128)(4,1)S(1)} %eq.44), kind=kOutput, calls=%fused_computation.6 | convolution fusion | flops 25239552 | bytes 1245568 | tf_op jit(solution)/shard_map/dot_general | solution.py:133
  85.1 2.0 %add_convert_fusion = bf16[4,96,512]{2,1,0:T(8,128)(2,1)} fusion(f32[4,96,512]{2,1,0:T(8,128)} %bitcast.31, f32[4,96,512]{2,1,0:T(8,128)S(1)} %fusion.2), kind=kLoop, calls=%fused_computation.4 | loop fusion | flops 393216 | bytes 1966080 | tf_op jit(solution)/shard_map/convert_element_type | solution.py:135
  (40 shorter events, 0.3 us)
Async XLA Ops:
  0.0 60.3 %copy-start = (bf16[4,96,4096]{2,1,0:T(8,128)(2,1)S(1)}, bf16[4,96,4096]{2,1,0:T(8,128)(2,1)}, u32[]{:S(2)}) copy-start(bf16[4,96,4096]{2,1,0:T(8,128)(2,1)} %param.7) | copy-start | bytes 9437188
  2.9 36.7 %copy-start.1 = (bf16[2,8,4608]{2,1,0:T(8,128)(2,1)S(1)}, bf16[2,8,4608]{2,1,0:T(8,128)(2,1)}, u32[]{:S(2)}) copy-start(bf16[2,8,4608]{2,1,0:T(8,128)(2,1)} %get-tuple-element.32.rest_0_) | copy-start | bytes 442372
  2.9 11.9 %collective-permute-start = (bf16[2,8,4608]{2,1,0:T(8,128)(2,1)}, bf16[2,8,4608]{2,1,0:T(8,128)(2,1)S(1)}, u32[]{:S(2)}, u32[]{:S(2)}) collective-permute-start(bf16[2,8,4608]{2,1,0:T(8,128)(2,1)} %get-tuple-element.29), channel_id=1, source_target_pairs={{0,2},{2,0},{4,6},{6,4},{8,10},{10,8},{12,14},{14,12},{1,3},{3,1},... | collective-permute-start | bytes 442376 | tf_op jit(solution)/shard_map/ppermute | solution.py:85
  5.8 33.7 %collective-permute-start.4 = (bf16[2,8,4608]{2,1,0:T(8,128)(2,1)}, bf16[2,8,4608]{2,1,0:T(8,128)(2,1)}, u32[]{:S(2)}, u32[]{:S(2)}) collective-permute-start(bf16[2,8,4608]{2,1,0:T(8,128)(2,1)} %get-tuple-element.29), channel_id=1, source_target_pairs={{0,10},{2,8},{4,14},{6,12},{8,2},{10,0},{12,6},{14,4},{1,11},{3,9}... | collective-permute-start | bytes 442376 | tf_op jit(solution)/shard_map/ppermute | solution.py:85
  8.4 11.1 %collective-permute-start.1 = (bf16[2,8,4608]{2,1,0:T(8,128)(2,1)}, bf16[2,8,4608]{2,1,0:T(8,128)(2,1)}, u32[]{:S(2)}, u32[]{:S(2)}) collective-permute-start(bf16[2,8,4608]{2,1,0:T(8,128)(2,1)} %get-tuple-element.30), channel_id=1, source_target_pairs={{0,4},{2,6},{4,0},{6,2},{8,12},{10,14},{12,8},{14,10},{1,5},{3,7},... | collective-permute-start | bytes 442376 | tf_op jit(solution)/shard_map/ppermute | solution.py:85
  10.0 29.6 %collective-permute-start.5 = (bf16[2,8,4608]{2,1,0:T(8,128)(2,1)}, bf16[2,8,4608]{2,1,0:T(8,128)(2,1)}, u32[]{:S(2)}, u32[]{:S(2)}) collective-permute-start(bf16[2,8,4608]{2,1,0:T(8,128)(2,1)} %get-tuple-element.30), channel_id=1, source_target_pairs={{0,12},{2,14},{4,8},{6,10},{8,4},{10,6},{12,0},{14,2},{1,13},{3,15... | collective-permute-start | bytes 442376 | tf_op jit(solution)/shard_map/ppermute | solution.py:85
  10.0 29.6 %collective-permute-start.2 = (bf16[2,8,4608]{2,1,0:T(8,128)(2,1)}, bf16[2,8,4608]{2,1,0:T(8,128)(2,1)}, u32[]{:S(2)}, u32[]{:S(2)}) collective-permute-start(bf16[2,8,4608]{2,1,0:T(8,128)(2,1)} %get-tuple-element.35), channel_id=1, source_target_pairs={{0,6},{2,4},{4,2},{6,0},{8,14},{10,12},{12,10},{14,8},{1,7},{3,5},... | collective-permute-start | bytes 442376 | tf_op jit(solution)/shard_map/ppermute | solution.py:85
  14.8 24.8 %collective-permute-start.6 = (bf16[2,8,4608]{2,1,0:T(8,128)(2,1)}, bf16[2,8,4608]{2,1,0:T(8,128)(2,1)}, u32[]{:S(2)}, u32[]{:S(2)}) collective-permute-start(bf16[2,8,4608]{2,1,0:T(8,128)(2,1)} %get-tuple-element.35), channel_id=1, source_target_pairs={{0,14},{2,12},{4,10},{6,8},{8,6},{10,4},{12,2},{14,0},{1,15},{3,13... | collective-permute-start | bytes 442376 | tf_op jit(solution)/shard_map/ppermute | solution.py:85
  19.4 20.1 %collective-permute-start.3 = (bf16[2,8,4608]{2,1,0:T(8,128)(2,1)}, bf16[2,8,4608]{2,1,0:T(8,128)(2,1)}, u32[]{:S(2)}, u32[]{:S(2)}) collective-permute-start(bf16[2,8,4608]{2,1,0:T(8,128)(2,1)} %get-tuple-element.32.rest_0_), channel_id=1, source_target_pairs={{0,8},{2,10},{4,12},{6,14},{8,0},{10,2},{12,4},{14,6},{1,9},{3,11}... | collective-permute-start | bytes 442376 | tf_op jit(solution)/shard_map/ppermute | solution.py:85
  41.1 18.8 %collective-permute-start.7 = (bf16[4,8,4608]{2,1,0:T(8,128)(2,1)S(1)}, bf16[4,8,4608]{2,1,0:T(8,128)(2,1)S(1)}, u32[]{:S(2)}, u32[]{:S(2)}) collective-permute-start(bf16[4,8,4608]{2,1,0:T(8,128)(2,1)S(1)} %get-tuple-element.36), channel_id=1, source_target_pairs={{0,2},{2,0},{4,6},{6,4},{8,10},{10,8},{12,14},{14,12},{16,18},{18,... | collective-permute-start | bytes 884744 | tf_op jit(solution)/shard_map/ppermute | solution.py:107
  42.6 17.6 %collective-permute-start.8 = (bf16[4,8,4608]{2,1,0:T(8,128)(2,1)S(1)}, bf16[4,8,4608]{2,1,0:T(8,128)(2,1)S(1)}, u32[]{:S(2)}, u32[]{:S(2)}) collective-permute-start(bf16[4,8,4608]{2,1,0:T(8,128)(2,1)S(1)} %get-tuple-element.37), channel_id=1, source_target_pairs={{0,4},{2,6},{4,0},{6,2},{8,12},{10,14},{12,8},{14,10},{16,20},{18,... | collective-permute-start | bytes 884744 | tf_op jit(solution)/shard_map/ppermute | solution.py:107
  42.6 17.6 %collective-permute-start.9 = (bf16[4,8,4608]{2,1,0:T(8,128)(2,1)S(1)}, bf16[4,8,4608]{2,1,0:T(8,128)(2,1)S(1)}, u32[]{:S(2)}, u32[]{:S(2)}) collective-permute-start(bf16[4,8,4608]{2,1,0:T(8,128)(2,1)S(1)} %get-tuple-element.38), channel_id=1, source_target_pairs={{0,6},{2,4},{4,2},{6,0},{8,14},{10,12},{12,10},{14,8},{16,22},{18,... | collective-permute-start | bytes 884744 | tf_op jit(solution)/shard_map/ppermute | solution.py:107
  44.6 30.0 %collective-permute-start.12 = (bf16[4,8,4608]{2,1,0:T(8,128)(2,1)S(1)}, bf16[4,8,4608]{2,1,0:T(8,128)(2,1)S(1)}, u32[]{:S(2)}, u32[]{:S(2)}) collective-permute-start(bf16[4,8,4608]{2,1,0:T(8,128)(2,1)S(1)} %get-tuple-element.40), channel_id=1, source_target_pairs={{0,16},{2,18},{4,20},{6,22},{8,24},{10,26},{12,28},{14,30},{16,0},... | collective-permute-start | bytes 884744 | tf_op jit(solution)/shard_map/ppermute | solution.py:107
  45.2 29.5 %collective-permute-start.13 = (bf16[4,8,4608]{2,1,0:T(8,128)(2,1)S(1)}, bf16[4,8,4608]{2,1,0:T(8,128)(2,1)S(1)}, u32[]{:S(2)}, u32[]{:S(2)}) collective-permute-start(bf16[4,8,4608]{2,1,0:T(8,128)(2,1)S(1)} %get-tuple-element.41), channel_id=1, source_target_pairs={{0,18},{2,16},{4,22},{6,20},{8,26},{10,24},{12,30},{14,28},{16,2},... | collective-permute-start | bytes 884744 | tf_op jit(solution)/shard_map/ppermute | solution.py:107
  59.9 14.8 %collective-permute-start.14 = (bf16[4,8,4608]{2,1,0:T(8,128)(2,1)S(1)}, bf16[4,8,4608]{2,1,0:T(8,128)(2,1)S(1)}, u32[]{:S(2)}, u32[]{:S(2)}) collective-permute-start(bf16[4,8,4608]{2,1,0:T(8,128)(2,1)S(1)} %get-tuple-element.42), channel_id=1, source_target_pairs={{0,20},{2,22},{4,16},{6,18},{8,28},{10,30},{12,24},{14,26},{16,4},... | collective-permute-start | bytes 884744 | tf_op jit(solution)/shard_map/ppermute | solution.py:107
  60.3 6.1 %copy-start.2 = (bf16[2,64,4096]{2,1,0:T(8,128)(2,1)S(1)}, bf16[2,64,4096]{2,1,0:T(8,128)(2,1)}, u32[]{:S(2)}) copy-start(bf16[2,64,4096]{2,1,0:T(8,128)(2,1)} %param.9) | copy-start | bytes 3145732
  66.3 7.1 %collective-permute-start.10 = (f32[384,512]{1,0:T(8,128)S(1)}, f32[384,512]{1,0:T(8,128)S(1)}, u32[]{:S(2)}, u32[]{:S(2)}) collective-permute-start(f32[384,512]{1,0:T(8,128)S(1)} %constant_dynamic-slice_fusion), channel_id=1, source_target_pairs={{0,1},{1,0},{2,3},{3,2},{4,5},{5,4},{6,7},{7,6},{8,9},{9,8},{10,11... | collective-permute-start | bytes 2359304 | tf_op jit(solution)/shard_map/ppermute | solution.py:117
  66.4 7.1 %copy-start.3 = (bf16[2,64,512]{2,1,0:T(8,128)(2,1)S(1)}, bf16[2,64,512]{2,1,0:T(8,128)(2,1)}, u32[]{:S(2)}) copy-start(bf16[2,64,512]{2,1,0:T(8,128)(2,1)} %param.10) | copy-start | bytes 393220
  67.4 1.6 %collective-permute-start.11 = (f32[384,128]{1,0:T(8,128)S(1)}, f32[384,128]{1,0:T(8,128)S(1)}, u32[]{:S(2)}, u32[]{:S(2)}) collective-permute-start(f32[384,128]{1,0:T(8,128)S(1)} %fusion.37), channel_id=1, source_target_pairs={{0,1},{1,0},{2,3},{3,2},{4,5},{5,4},{6,7},{7,6},{8,9},{9,8},{10,11... | collective-permute-start | bytes 589832 | tf_op jit(solution)/shard_map/ppermute | solution.py:119
  69.0 11.9 %collective-permute-start.15 = (bf16[4,8,4608]{2,1,0:T(8,128)(2,1)S(1)}, bf16[4,8,4608]{2,1,0:T(8,128)(2,1)S(1)}, u32[]{:S(2)}, u32[]{:S(2)}) collective-permute-start(bf16[4,8,4608]{2,1,0:T(8,128)(2,1)S(1)} %get-tuple-element.43), channel_id=1, source_target_pairs={{0,22},{2,20},{4,18},{6,16},{8,30},{10,28},{12,26},{14,24},{16,6},... | collective-permute-start | bytes 884744 | tf_op jit(solution)/shard_map/ppermute | solution.py:107
  81.0 1.4 %copy-start.4 = (bf16[4,64,4608]{2,1,0:T(8,128)(2,1)}, bf16[4,64,4608]{2,1,0:T(8,128)(2,1)S(1)}, u32[]{:S(2)}) copy-start(bf16[4,64,4608]{2,1,0:T(8,128)(2,1)S(1)} %constant_dynamic-update-slice_fusion) | copy-start | bytes 7077892
  81.0 1.4 %copy-start.5 = (s32[4,6]{1,0:T(4,128)S(1)}, s32[4,6]{1,0:T(4,128)}, u32[]{:S(2)}) copy-start(s32[4,6]{1,0:T(4,128)} %param.11) | copy-start | bytes 292
  82.5 1.3 %collective-permute-start.16 = (f32[4,96,64]{1,2,0:T(8,128)S(1)}, f32[4,96,64]{1,2,0:T(8,128)S(1)}, u32[]{:S(2)}, u32[]{:S(2)}) collective-permute-start(f32[4,96,64]{1,2,0:T(8,128)S(1)} %fusion), channel_id=1, source_target_pairs={{0,1},{1,0},{2,3},{3,2},{4,5},{5,4},{6,7},{7,6},{8,9},{9,8},{10,11... | collective-permute-start | bytes 294920 | tf_op jit(solution)/shard_map/ppermute | solution.py:130

commit v4 on v2

--- a/solution.py
+++ b/solution.py
@@ -65,6 +65,118 @@
     )(choice, *servers)
 
 
+def products_kernel(side_ref, acts_ref, weight_ref, down_ref, send_ref, keep_ref):
+    step = pl.program_id(0)
+    blocks, width = pl.num_programs(0) // 2, weight_ref.shape[1]
+    narrow = send_ref.shape[1] - down_ref.shape[0]
+    product = jnp.dot(acts_ref[...], weight_ref[...], preferred_element_type=jnp.float32)
+    for block in range(narrow // width):
+        @pl.when(step == block)
+        def _():
+            send_ref[:, block * width:(block + 1) * width] = product
+
+        @pl.when(step == blocks + block)
+        def _():
+            keep_ref[:, block * width:(block + 1) * width] = product
+
+    @pl.when(step == 0)
+    def _():
+        own = contract_last(acts_ref[...], down_ref[...])
+        send_ref[:, narrow:] = own
+        keep_ref[:, narrow:] = own
+
+
+def products(side, tokens, weight, down):
+    rows, depth = tokens.shape
+    columns = weight.shape[1]
+    width = 256
+    blocks = columns // 2 // width
+    out = jax.ShapeDtypeStruct((rows, columns // 2 + down.shape[0]), jnp.float32)
+
+    def weight_block(step, side_ref):
+        half = jnp.where(step < blocks, 1 - side_ref[0], side_ref[0])
+        return 0, half * blocks + step % blocks
+
+    def whole(step, side_ref):
+        return 0, 0
+
+    return pl.pallas_call(
+        products_kernel,
+        out_shape=[out, out],
+        grid_spec=pltpu.PrefetchScalarGridSpec(
+            num_scalar_prefetch=1,
+            grid=(2 * blocks,),
+            in_specs=[
+                pl.BlockSpec(tokens.shape, whole),
+                pl.BlockSpec((depth, width), weight_block),
+                pl.BlockSpec(down.shape, whole),
+            ],
+            out_specs=[pl.BlockSpec(out.shape, whole)] * 2,
+        ),
+        compiler_params=pltpu.CompilerParams(vmem_limit_bytes=48 << 20),
+        cost_estimate=pl.CostEstimate(flops=0, bytes_accessed=0, transcendentals=0),
+    )(side, tokens, weight, down)
+
+
+def final_kernel(slots_ref, keep_ref, arrived_ref, partial_ref, other_ref, own_up_ref, up_ref, out_ref, own, passed):
+    steps, rows, narrow = out_ref.shape
+    rank, held = up_ref.shape[1], own_up_ref.shape[0] // up_ref.shape[1]
+    block_rows = rows // slots_ref.shape[1]
+    for step in range(steps):
+        for block in range(slots_ref.shape[1]):
+            slot = slots_ref[step, block]
+            here = slice(step * rows + block * block_rows, step * rows + (block + 1) * block_rows)
+            mine = (keep_ref[here, narrow:] + arrived_ref[here, narrow:]).astype(own.dtype)
+            column = lax.broadcasted_iota(jnp.int32, mine.shape, 1) // rank
+            own[here] = jnp.where(column == slot, mine, jnp.zeros_like(mine))
+            given = (partial_ref[here] + other_ref[here]).astype(passed.dtype)
+            passed[here] = jnp.where(slot == held, given, jnp.zeros_like(given))
+    for step in range(steps):
+        here = slice(step * rows, (step + 1) * rows)
+        base = keep_ref[here, :narrow] + arrived_ref[here, :narrow]
+        base += jnp.dot(own[here], own_up_ref[...], preferred_element_type=jnp.float32)
+        base += jnp.dot(passed[here], up_ref[step], preferred_element_type=jnp.float32)
+        out_ref[step] = base.astype(out_ref.dtype)
+
+
+def finish(slots, keep, arrived, partial, other, own_up, handed):
+    steps, rank, both = handed.shape
+    held_rank, narrow = own_up.shape
+    rows = keep.shape[0]
+    vmem = pl.BlockSpec(memory_space=pltpu.VMEM)
+    last = both // narrow - 1
+    return pl.pallas_call(
+        final_kernel,
+        out_shape=jax.ShapeDtypeStruct((steps, rows // steps, narrow), jnp.bfloat16),
+        grid=(1,),
+        in_specs=[pl.BlockSpec(memory_space=pltpu.SMEM)] + [vmem] * 5
+        + [pl.BlockSpec((steps, rank, narrow), lambda step: (0, 0, last))],
+        out_specs=vmem,
+        scratch_shapes=[
+            pltpu.VMEM((rows, held_rank), jnp.bfloat16),
+            pltpu.VMEM((rows, rank), jnp.bfloat16),
+        ],
+    )(slots, keep, arrived, partial, other, own_up, handed)
+
+
+def rank_kernel(acts_ref, handed_ref, out_ref):
+    steps, rows, wide = acts_ref.shape
+    for step in range(steps):
+        out_ref[step * rows:(step + 1) * rows] = contract_last(acts_ref[step], handed_ref[step, :, :wide])
+
+
+def rank_part(acts, handed):
+    steps, rows, _ = acts.shape
+    vmem = pl.BlockSpec(memory_space=pltpu.VMEM)
+    return pl.pallas_call(
+        rank_kernel,
+        out_shape=jax.ShapeDtypeStruct((steps * rows, handed.shape[1]), jnp.float32),
+        in_specs=[vmem, vmem],
+        out_specs=vmem,
+        compiler_params=pltpu.CompilerParams(vmem_limit_bytes=16 << 20),
+    )(acts, handed)
+
+
 def body(acts, value_weight, adapter_down, adapter_up, block_slots, transfer_offset, transfer_slot):
     groups, servers = lax.axis_size("groups"), lax.axis_size("adapter")
     parts = STRIPES // groups
@@ -72,7 +184,6 @@
     steps, rows_dev, wide = acts.shape
     held, rank, _ = adapter_down.shape
     narrow = adapter_up.shape[2]
-    block_rows = rows_dev // block_slots.shape[1]
     group, server = lax.axis_index("groups"), lax.axis_index("adapter")
     side = lax.axis_index("tensor")
     part = server % parts
@@ -80,10 +191,13 @@
 
     pieces = (group * parts + jnp.bitwise_xor(part, jnp.arange(parts, dtype=jnp.int32))).astype(jnp.int32)
     stripes = cut_stripes(pieces, adapter_down, adapter_up, parts)
-    banked = [stripes[0]]
-    for k in range(1, servers):
-        banked.append(lax.ppermute(
-            stripes[k % parts], "adapter", [(i, i ^ k) for i in range(servers)]))
+    banked = {0: stripes[0]}
+    for k in [1, 2, 3, 4, 5, 6, 7, *range(STRIPES, servers)]:
+        banked[k] = lax.ppermute(stripes[k % parts], "adapter", [(i, i ^ k) for i in range(servers)])
+    early = [1, 2]
+    transfer_slot, *arrived = lax.optimization_barrier((transfer_slot, *[banked[k] for k in early]))
+    banked.update(zip(early, arrived))
+    banked = [banked[k] for k in range(servers)]
 
     asked = transfer_offset * held + transfer_slot[:, 0]
     asked = lax.all_gather(asked, ("groups", "adapter")).reshape(groups, servers, steps)
@@ -94,42 +208,33 @@
     slot = slots[ask_group[:, None], source, jnp.arange(steps)[None, :]]
     choice = (jnp.bitwise_xor(source, server) * held + slot).astype(jnp.int32).reshape(-1)
 
-    acts, *banked[1:6] = lax.optimization_barrier((acts, *banked[1:6]))
-
-    tokens = acts.reshape(steps * rows_dev, wide)
-    partial_base = jnp.dot(tokens, value_weight, preferred_element_type=jnp.float32)
-    swap = [(0, 1), (1, 0)]
-    half_width = partial_base.shape[1] // 2
-    mine = lax.dynamic_slice_in_dim(partial_base, side * half_width, half_width, 1)
-    others = lax.dynamic_slice_in_dim(partial_base, (1 - side) * half_width, half_width, 1)
-    base = mine + lax.ppermute(others, "tensor", swap)
-    partial_own = contract_last(tokens, adapter_down.reshape(held * rank, wide))
-    own = (partial_own + lax.ppermute(partial_own, "tensor", swap)).astype(jnp.bfloat16)
-    row_slot = jnp.repeat(block_slots.reshape(-1), block_rows)
-    own_slot = jnp.arange(held * rank, dtype=jnp.int32) // rank
-    own = jnp.where(row_slot[:, None] == own_slot[None, :], own, jnp.zeros_like(own))
-    base = base + jnp.dot(own, adapter_up.reshape(held * rank, narrow), preferred_element_type=jnp.float32)
-
-    base, *banked = lax.optimization_barrier((base, *banked))
-
     picked = pick_stripes(choice, banked, steps)
-    given = [picked[0]]
-    for k in range(1, STRIPES):
+    given = {0: picked[0]}
+    for k in (4, 1, 2, 7, 3, 5, 6):
         pairs = []
         for g in range(groups):
             for i in range(servers):
                 other = (g * parts + i % parts) ^ k
                 pairs.append((g * servers + i, (other // parts) * servers + (i // parts) * parts + other % parts))
-        given.append(lax.ppermute(picked[k], ("groups", "adapter"), pairs))
-    passed = jnp.concatenate(given, axis=1)
-    partial_passed = lax.dot_general(
-        acts, passed[:, :, :wide], (((2,), (2,)), ((0,), (0,))), preferred_element_type=jnp.float32)
-    reduced = (partial_passed + lax.ppermute(partial_passed, "tensor", swap)).astype(jnp.bfloat16)
-    is_passed = row_slot.reshape(steps, rows_dev, 1) == held
-    reduced = jnp.where(is_passed, reduced, jnp.zeros_like(reduced))
-    low_rank = lax.dot_general(
-        reduced, passed[:, :, wide:], (((2,), (1,)), ((0,), (0,))), preferred_element_type=jnp.float32)
-    return (base.reshape(steps, rows_dev, narrow) + low_rank).astype(jnp.bfloat16)
+        given[k] = lax.ppermute(picked[k], ("groups", "adapter"), pairs)
+    early = [4, 1, 2]
+    acts, *arrived = lax.optimization_barrier((acts, *[given[k] for k in early]))
+    given.update(zip(early, arrived))
+    late = [k for k in range(1, STRIPES) if k not in early]
+
+    swap = [(0, 1), (1, 0)]
+    send, keep = products(
+        side.astype(jnp.int32)[None], acts.reshape(steps * rows_dev, wide), value_weight,
+        adapter_down.reshape(held * rank, wide))
+    arrived = lax.ppermute(send, "tensor", swap)
+    arrived, *others = lax.optimization_barrier((arrived, *[given[k] for k in late]))
+    given.update(zip(late, others))
+
+    handed = jnp.concatenate([given[k] for k in range(STRIPES)], axis=1)
+    partial = rank_part(acts, handed)
+    other = lax.ppermute(partial, "tensor", swap)
+    return finish(
+        block_slots, keep, arrived, partial, other, adapter_up.reshape(held * rank, narrow), handed)
 
 
 def solution(mesh):

time: 92.1 us -> 82.3 us (0.89); the launches traced: 91.8 us -> 80.8 us
  matrix products: 13 us -> 0 us
  Pallas kernels: 3.81 us -> 14.7 us
  waiting for transfers between devices: 27.7 us -> 21.3 us
  starting transfers between devices: 21.7 us -> 19.3 us
  blocking collectives: 14.7 us -> 16.9 us
  other arithmetic: 3.53 us -> 1.46 us
    dot_general x5 -> x0, matrix products: 13 us -> none  [the longest x1 5.79 us: body(): jnp.dot(tokens, value_weight, preferred_element_type=jnp.float32)]
    pallas_call x0 -> x3, Pallas kernels: none -> 11.2 us  [the longest x1 7.4 us: products(): pl.pallas_call(products_kernel, out_shape=[out, out], grid_spec=pltpu.Pre...]
    ppermute x10 -> x9, waiting for transfers between devices: 27.7 us -> 18.7 us  [the longest x7 15.1 us: body(): given[k] = lax.ppermute(picked[k], ('groups', 'adapter'), pairs)]
    ppermute x7, waiting for transfers between devices: 0.02 us -> 2.67 us  [body(): lax.ppermute(stripes[k % parts], 'adapter', [(i, i ^ k) for i in range(se...]
    unnamed x1, blocking collectives: 14.7 us -> 16.9 us
    convert_element_type x1 -> x0, other arithmetic: 2.04 us -> none  [body(): (base.reshape(steps, rows_dev, narrow) + low_rank).astype(jnp.bfloat16)]
    unnamed x23 -> x29, local copies, waits for them, and re-layouts: 2.76 us -> 4.51 us
    ppermute x10 -> x9, starting transfers between devices: 8.96 us -> 7.42 us  [the longest x7 7.21 us: body(): given[k] = lax.ppermute(picked[k], ('groups', 'adapter'), pairs)]
  transfers between devices with their start and end apart: 17 -> 16, of which waited for: 6 -> 6; matrix products, arithmetic and copies ran while one was open for 18% -> 5% of each run, Pallas kernels for 0% -> 9%
where the time goes in v4:
time: 82.3 us; the launch traced here: 80.8 us
  waiting for transfers between devices  21.3 us (26%)
  starting transfers between devices  19.3 us (23%)
  blocking collectives  16.9 us (21%)
  Pallas kernels  14.7 us (18%)
  local copies, waits for them, and re-layouts  6.23 us (8%)
  other arithmetic  1.46 us (2%)
  between operations  0.83 us (1%)
    unnamed x1, blocking collectives  16.9 us
    ppermute x7, waiting for transfers between devices, body(): given[k] = lax.ppermute(picked[k], ('groups', 'adapter'), pairs)  15.1 us
    ppermute x7, starting transfers between devices, body(): lax.ppermute(stripes[k % parts], 'adapter', [(i, i ^ k) for i in range(se...  11.9 us
    pallas_call x1, Pallas kernels, products(): pl.pallas_call(products_kernel, out_shape=[out, out], grid_spec=pltpu.Pre...  7.4 us
    ppermute x7, starting transfers between devices, body(): given[k] = lax.ppermute(picked[k], ('groups', 'adapter'), pairs)  7.21 us
    unnamed x29, local copies, waits for them, and re-layouts  4.51 us
    pallas_call x1, Pallas kernels, finish(): pl.pallas_call(final_kernel, out_shape=jax.ShapeDtypeStruct((steps, rows...  2.82 us
    ppermute x7, waiting for transfers between devices, body(): lax.ppermute(stripes[k % parts], 'adapter', [(i, i ^ k) for i in range(se...  2.67 us
  transfers between devices with their start and end apart: 16, of which 6 were waited for; matrix products, arithmetic and copies ran while one was open for 5% of the time, Pallas kernels for 9%

profile of v4, /device:TPU:0, one launch (start us, length us, event | category | flops | bytes accessed | tf_op | source)
XLA Modules:
  0.0 80.8 jit_solution(4149359737114105047)
XLA Ops:
  0.0 0.5 xor_add_fusion.piece_ref
  0.5 2.1 %shard_map.73 = (bf16[2,8,4608]{2,1,0:T(8,128)(2,1)}, bf16[2,8,4608]{2,1,0:T(8,128)(2,1)}, bf16[2,8,4608]{2,1,0:T(8,128)(2,1)}, bf16[2,8,4608]{2,1,0:T(8,128)(2,1)}) custom-call(s32[4]{0:T(128)} %xor_add_fusion.piece_ref, bf16[2,8,8,4096]{3,2,1,0:T(8,128)(2,1)} %bitcast.22, bf16[2,8,8,512]{3,2,1,0:T(8,128)(2,1)} %bitcast.24), custom_call_target="tpu_custom_call" | custom-call | tf_op jit(solution)/shard_map/pallas_call | solution.py:31
  2.6 3.0 %collective-permute-start = (bf16[2,8,4608]{2,1,0:T(8,128)(2,1)}, bf16[2,8,4608]{2,1,0:T(8,128)(2,1)S(1)}, u32[]{:S(2)}, u32[]{:S(2)}) collective-permute-start(bf16[2,8,4608]{2,1,0:T(8,128)(2,1)} %get-tuple-element.31), channel_id=1, source_target_pairs={{0,2},{2,0},{4,6},{6,4},{8,10},{10,8},{12,14},{14,12},{1,3},{3,1},... | collective-permute-start | bytes 442376 | tf_op jit(solution)/shard_map/ppermute | solution.py:196
  5.6 2.5 %collective-permute-start.4 = (bf16[2,8,4608]{2,1,0:T(8,128)(2,1)}, bf16[2,8,4608]{2,1,0:T(8,128)(2,1)}, u32[]{:S(2)}, u32[]{:S(2)}) collective-permute-start(bf16[2,8,4608]{2,1,0:T(8,128)(2,1)} %get-tuple-element.31), channel_id=1, source_target_pairs={{0,10},{2,8},{4,14},{6,12},{8,2},{10,0},{12,6},{14,4},{1,11},{3,9}... | collective-permute-start | bytes 442376 | tf_op jit(solution)/shard_map/ppermute | solution.py:196
  8.1 1.6 %collective-permute-start.1 = (bf16[2,8,4608]{2,1,0:T(8,128)(2,1)}, bf16[2,8,4608]{2,1,0:T(8,128)(2,1)S(1)}, u32[]{:S(2)}, u32[]{:S(2)}) collective-permute-start(bf16[2,8,4608]{2,1,0:T(8,128)(2,1)} %get-tuple-element.32), channel_id=1, source_target_pairs={{0,4},{2,6},{4,0},{6,2},{8,12},{10,14},{12,8},{14,10},{1,5},{3,7},... | collective-permute-start | bytes 442376 | tf_op jit(solution)/shard_map/ppermute | solution.py:196
  9.7 0.0 collective-permute-start.5
  9.7 1.9 %collective-permute-start.2 = (bf16[2,8,4608]{2,1,0:T(8,128)(2,1)}, bf16[2,8,4608]{2,1,0:T(8,128)(2,1)}, u32[]{:S(2)}, u32[]{:S(2)}) collective-permute-start(bf16[2,8,4608]{2,1,0:T(8,128)(2,1)} %get-tuple-element.37), channel_id=1, source_target_pairs={{0,6},{2,4},{4,2},{6,0},{8,14},{10,12},{12,10},{14,8},{1,7},{3,5},... | collective-permute-start | bytes 442376 | tf_op jit(solution)/shard_map/ppermute | solution.py:196
  11.6 1.2 %dynamic-slice = u32[1]{0:T(128)} dynamic-slice(u32[32]{0:T(128)} %constant.143, u32[]{:T(128)S(6)} %add.149), dynamic_slice_sizes={1} | dynamic-slice | bytes 12
  13.4 0.0 collective-permute-done.rest_1_
  13.4 3.0 %collective-permute-start.6 = (bf16[2,8,4608]{2,1,0:T(8,128)(2,1)}, bf16[2,8,4608]{2,1,0:T(8,128)(2,1)}, u32[]{:S(2)}, u32[]{:S(2)}) collective-permute-start(bf16[2,8,4608]{2,1,0:T(8,128)(2,1)} %get-tuple-element.37), channel_id=1, source_target_pairs={{0,14},{2,12},{4,10},{6,8},{8,6},{10,4},{12,2},{14,0},{1,15},{3,13... | collective-permute-start | bytes 442376 | tf_op jit(solution)/shard_map/ppermute | solution.py:196
  16.4 2.7 %collective-permute-done.1.rest_2_ = bf16[2,8,4608]{2,1,0:T(8,128)(2,1)S(1)} collective-permute-done((bf16[2,8,4608]{2,1,0:T(8,128)(2,1)}, bf16[2,8,4608]{2,1,0:T(8,128)(2,1)S(1)}, u32[]{:S(2)}, u32[]{:S(2)}) %collective-permute-start.1) | collective-permute-done | bytes 147488 | tf_op jit(solution)/shard_map/ppermute | solution.py:196
  19.1 0.7 copy-done.6
  19.7 0.0 collective-permute-start.3
  19.7 0.8 fusion.20
  20.5 16.9 %all-reduce = s32[64]{0:T(128)S(1)} all-reduce(s32[64]{0:T(128)S(1)} %fusion.20), channel_id=2, replica_groups=mesh['groups'=2,'adapter'=8,'tensor'=2] {'groups','adapter'}, use_global_device_ids=true, to_apply=%add | all-reduce | flops 64 | bytes 512
  37.4 0.1 reshape.201
  37.5 0.6 gather_fusion
  38.1 0.1 copy.10
  38.2 0.1 broadcast_subtract_fusion
  38.3 0.1 sub.44
  38.4 0.1 copy.11
  38.5 0.1 reshape.211
  38.5 0.7 gather_fusion.1
  39.3 0.0 collective-permute-done.3.rest_4_
  39.3 0.0 collective-permute-done.4.rest_5_
  39.3 0.0 collective-permute-done.6.rest_7_
  39.3 1.2 %copy-done.7 = bf16[2,8,4608]{2,1,0:T(8,128)(2,1)S(1)} copy-done((bf16[2,8,4608]{2,1,0:T(8,128)(2,1)S(1)}, bf16[2,8,4608]{2,1,0:T(8,128)(2,1)}, u32[]{:S(2)}) %copy-start.7) | copy-done | bytes 147480
  40.5 1.4 %shard_map.74 = (bf16[4,8,4608]{2,1,0:T(8,128)(2,1)S(1)}, bf16[4,8,4608]{2,1,0:T(8,128)(2,1)S(1)}, bf16[4,8,4608]{2,1,0:T(8,128)(2,1)S(1)}, bf16[4,8,4608]{2,1,0...) custom-call(s32[32]{0:T(128)S(1)} %fusion.11.choice_ref, ...), custom_call_target="tpu_custom_call" | custom-call | tf_op jit(solution)/shard_map/pallas_call | solution.py:58
  42.0 0.6 collective-permute-start.7
  42.6 1.5 %collective-permute-start.8 = (bf16[4,8,4608]{2,1,0:T(8,128)(2,1)S(1)}, bf16[4,8,4608]{2,1,0:T(8,128)(2,1)S(1)}, u32[]{:S(2)}, u32[]{:S(2)}) collective-permute-start(bf16[4,8,4608]{2,1,0:T(8,128)(2,1)S(1)} %get-tuple-element.39), channel_id=1, source_target_pairs={{0,2},{2,0},{4,6},{6,4},{8,10},{10,8},{12,14},{14,12},{16,18},{18,... | collective-permute-start | bytes 884744 | tf_op jit(solution)/shard_map/ppermute | solution.py:219
  44.0 0.0 collective-permute-start.9
  44.1 2.0 %collective-permute-start.11 = (bf16[4,8,4608]{2,1,0:T(8,128)(2,1)S(1)}, bf16[4,8,4608]{2,1,0:T(8,128)(2,1)S(1)}, u32[]{:S(2)}, u32[]{:S(2)}) collective-permute-start(bf16[4,8,4608]{2,1,0:T(8,128)(2,1)S(1)} %get-tuple-element.44), channel_id=1, source_target_pairs={{0,6},{2,4},{4,2},{6,0},{8,14},{10,12},{12,10},{14,8},{16,22},{18,... | collective-permute-start | bytes 884744 | tf_op jit(solution)/shard_map/ppermute | solution.py:219
  46.1 2.4 %collective-permute-start.12 = (bf16[4,8,4608]{2,1,0:T(8,128)(2,1)S(1)}, bf16[4,8,4608]{2,1,0:T(8,128)(2,1)S(1)}, u32[]{:S(2)}, u32[]{:S(2)}) collective-permute-start(bf16[4,8,4608]{2,1,0:T(8,128)(2,1)S(1)} %get-tuple-element.45), channel_id=1, source_target_pairs={{0,18},{2,16},{4,22},{6,20},{8,26},{10,24},{12,30},{14,28},{16,2},... | collective-permute-start | bytes 884744 | tf_op jit(solution)/shard_map/ppermute | solution.py:219
  48.5 3.1 %collective-permute-done.7 = bf16[4,8,4608]{2,1,0:T(8,128)(2,1)S(1)} collective-permute-done((bf16[4,8,4608]{2,1,0:T(8,128)(2,1)S(1)}, bf16[4,8,4608]{2,1,0:T(8,128)(2,1)S(1)}, u32[]{:S(2)}, u32[]{:S(2)}) %collective-permute-start.7) | collective-permute-done | bytes 294944 | tf_op jit(solution)/shard_map/ppermute | solution.py:219
  51.6 11.8 %collective-permute-done.8 = bf16[4,8,4608]{2,1,0:T(8,128)(2,1)S(1)} collective-permute-done((bf16[4,8,4608]{2,1,0:T(8,128)(2,1)S(1)}, bf16[4,8,4608]{2,1,0:T(8,128)(2,1)S(1)}, u32[]{:S(2)}, u32[]{:S(2)}) %collective-permute-start.8) | collective-permute-done | bytes 294944 | tf_op jit(solution)/shard_map/ppermute | solution.py:219
  63.4 0.7 collective-permute-start.14
  64.1 0.0 collective-permute-done.9
  64.1 7.4 %shard_map.75 = (f32[384,640]{1,0:T(8,128)S(1)}, f32[384,640]{1,0:T(8,128)S(1)}) custom-call(s32[1]{0:T(128)} %bitcast.side_ref, bf16[384,4096]{1,0:T(8,128)(2,1)S(1)} %bitcast.21, bf16[4096,1024]{1,0:T(8,128)(2,1)} %weight_ref.1, bf16[128,4096]{1,0:T(8,128)(2,1)S(1)} %bitcast.23), custom_call_target="tpu_custom_call" | custom-call | tf_op jit(solution)/shard_map/pallas_call | solution.py:103
  71.5 0.1 collective-permute-start.10
  71.7 0.0 collective-permute-done.12
  71.7 0.2 collective-permute-done.14
  71.9 2.2 %collective-permute-done.10.arrived_ref = f32[384,640]{1,0:T(8,128)S(1)} collective-permute-done((f32[384,640]{1,0:T(8,128)S(1)}, f32[384,640]{1,0:T(8,128)S(1)}, u32[]{:S(2)}, u32[]{:S(2)}) %collective-permute-start.10) | collective-permute-done | bytes 983072 | tf_op jit(solution)/shard_map/ppermute | solution.py:229
  74.3 1.0 %shard_map.76.partial_ref = f32[384,64]{1,0:T(8,128)S(1)} custom-call(bf16[4,96,4096]{2,1,0:T(8,128)(2,1)S(1)} %copy-done, bf16[4,64,4608]{2,1,0:T(8,128)(2,1)S(1)} %constant_dynamic-update-slice_fusion.handed_ref.up_ref), custom_call_target="tpu_custom_call" | custom-call | tf_op jit(solution)/shard_map/pallas_call | solution.py:171
  75.3 0.6 copy-done.1
  75.9 0.1 collective-permute-start.15
  76.0 1.3 %collective-permute-done.15.other_ref = f32[384,64]{1,0:T(8,128)S(1)} collective-permute-done((f32[384,64]{1,0:T(8,128)S(1)}, f32[384,64]{1,0:T(8,128)S(1)}, u32[]{:S(2)}, u32[]{:S(2)}) %collective-permute-start.15) | collective-permute-done | bytes 98336 | tf_op jit(solution)/shard_map/ppermute | solution.py:235
  77.3 0.7 copy-done.9
  78.0 2.8 %shard_map.77 = bf16[4,96,512]{2,1,0:T(8,128)(2,1)} custom-call(s32[4,6]{1,0:T(4,128)} %slots_ref.1, f32[384,640]{1,0:T(8,128)} %copy-done.3, f32[384,640]{1,0:T(8,128)} %copy-done.8, f32[384,64]{1,0:T(8,128)} %copy-done.4, f32[384,64]{1,0:T(8,128)} %copy-done.9, bf16[128,512]{1,0:T(8,128)(2,1)} %bitcast.25, bf16[4,64,4608]{2,1,0:T(8,128)(2,1)} %copy-done.1), custom_call_target="tpu_custom_call" | custom-call | tf_op jit(solution)/shard_map/pallas_call | solution.py:148
  (35 shorter events, 0.3 us)
Async XLA Ops:
  2.6 36.7 %copy-start.5 = (bf16[2,8,4608]{2,1,0:T(8,128)(2,1)S(1)}, bf16[2,8,4608]{2,1,0:T(8,128)(2,1)}, u32[]{:S(2)}) copy-start(bf16[2,8,4608]{2,1,0:T(8,128)(2,1)} %get-tuple-element.34.rest_0_) | copy-start | bytes 442372
  2.6 10.8 %collective-permute-start = (bf16[2,8,4608]{2,1,0:T(8,128)(2,1)}, bf16[2,8,4608]{2,1,0:T(8,128)(2,1)S(1)}, u32[]{:S(2)}, u32[]{:S(2)}) collective-permute-start(bf16[2,8,4608]{2,1,0:T(8,128)(2,1)} %get-tuple-element.31), channel_id=1, source_target_pairs={{0,2},{2,0},{4,6},{6,4},{8,10},{10,8},{12,14},{14,12},{1,3},{3,1},... | collective-permute-start | bytes 442376 | tf_op jit(solution)/shard_map/ppermute | solution.py:196
  5.6 33.7 %collective-permute-start.4 = (bf16[2,8,4608]{2,1,0:T(8,128)(2,1)}, bf16[2,8,4608]{2,1,0:T(8,128)(2,1)}, u32[]{:S(2)}, u32[]{:S(2)}) collective-permute-start(bf16[2,8,4608]{2,1,0:T(8,128)(2,1)} %get-tuple-element.31), channel_id=1, source_target_pairs={{0,10},{2,8},{4,14},{6,12},{8,2},{10,0},{12,6},{14,4},{1,11},{3,9}... | collective-permute-start | bytes 442376 | tf_op jit(solution)/shard_map/ppermute | solution.py:196
  8.1 11.0 %collective-permute-start.1 = (bf16[2,8,4608]{2,1,0:T(8,128)(2,1)}, bf16[2,8,4608]{2,1,0:T(8,128)(2,1)S(1)}, u32[]{:S(2)}, u32[]{:S(2)}) collective-permute-start(bf16[2,8,4608]{2,1,0:T(8,128)(2,1)} %get-tuple-element.32), channel_id=1, source_target_pairs={{0,4},{2,6},{4,0},{6,2},{8,12},{10,14},{12,8},{14,10},{1,5},{3,7},... | collective-permute-start | bytes 442376 | tf_op jit(solution)/shard_map/ppermute | solution.py:196
  9.7 29.6 %collective-permute-start.5 = (bf16[2,8,4608]{2,1,0:T(8,128)(2,1)}, bf16[2,8,4608]{2,1,0:T(8,128)(2,1)}, u32[]{:S(2)}, u32[]{:S(2)}) collective-permute-start(bf16[2,8,4608]{2,1,0:T(8,128)(2,1)} %get-tuple-element.32), channel_id=1, source_target_pairs={{0,12},{2,14},{4,8},{6,10},{8,4},{10,6},{12,0},{14,2},{1,13},{3,15... | collective-permute-start | bytes 442376 | tf_op jit(solution)/shard_map/ppermute | solution.py:196
  9.7 29.6 %collective-permute-start.2 = (bf16[2,8,4608]{2,1,0:T(8,128)(2,1)}, bf16[2,8,4608]{2,1,0:T(8,128)(2,1)}, u32[]{:S(2)}, u32[]{:S(2)}) collective-permute-start(bf16[2,8,4608]{2,1,0:T(8,128)(2,1)} %get-tuple-element.37), channel_id=1, source_target_pairs={{0,6},{2,4},{4,2},{6,0},{8,14},{10,12},{12,10},{14,8},{1,7},{3,5},... | collective-permute-start | bytes 442376 | tf_op jit(solution)/shard_map/ppermute | solution.py:196
  13.4 25.9 %collective-permute-start.6 = (bf16[2,8,4608]{2,1,0:T(8,128)(2,1)}, bf16[2,8,4608]{2,1,0:T(8,128)(2,1)}, u32[]{:S(2)}, u32[]{:S(2)}) collective-permute-start(bf16[2,8,4608]{2,1,0:T(8,128)(2,1)} %get-tuple-element.37), channel_id=1, source_target_pairs={{0,14},{2,12},{4,10},{6,8},{8,6},{10,4},{12,2},{14,0},{1,15},{3,13... | collective-permute-start | bytes 442376 | tf_op jit(solution)/shard_map/ppermute | solution.py:196
  19.1 0.7 copy-start.6
  19.7 19.6 %collective-permute-start.3 = (bf16[2,8,4608]{2,1,0:T(8,128)(2,1)}, bf16[2,8,4608]{2,1,0:T(8,128)(2,1)}, u32[]{:S(2)}, u32[]{:S(2)}) collective-permute-start(bf16[2,8,4608]{2,1,0:T(8,128)(2,1)} %get-tuple-element.34.rest_0_), channel_id=1, source_target_pairs={{0,8},{2,10},{4,12},{6,14},{8,0},{10,2},{12,4},{14,6},{1,9},{3,11}... | collective-permute-start | bytes 442376 | tf_op jit(solution)/shard_map/ppermute | solution.py:196
  38.5 25.6 %copy-start = (bf16[4,96,4096]{2,1,0:T(8,128)(2,1)S(1)}, bf16[4,96,4096]{2,1,0:T(8,128)(2,1)}, u32[]{:S(2)}) copy-start(bf16[4,96,4096]{2,1,0:T(8,128)(2,1)} %acts_ref) | copy-start | bytes 9437188
  39.3 24.8 %copy-start.2 = (bf16[2,64,4096]{2,1,0:T(8,128)(2,1)S(1)}, bf16[2,64,4096]{2,1,0:T(8,128)(2,1)}, u32[]{:S(2)}) copy-start(bf16[2,64,4096]{2,1,0:T(8,128)(2,1)} %param.9) | copy-start | bytes 3145732
  39.3 1.2 %copy-start.7 = (bf16[2,8,4608]{2,1,0:T(8,128)(2,1)S(1)}, bf16[2,8,4608]{2,1,0:T(8,128)(2,1)}, u32[]{:S(2)}) copy-start(bf16[2,8,4608]{2,1,0:T(8,128)(2,1)} %copy-done.6) | copy-start | bytes 442372
  42.0 9.6 %collective-permute-start.7 = (bf16[4,8,4608]{2,1,0:T(8,128)(2,1)S(1)}, bf16[4,8,4608]{2,1,0:T(8,128)(2,1)S(1)}, u32[]{:S(2)}, u32[]{:S(2)}) collective-permute-start(bf16[4,8,4608]{2,1,0:T(8,128)(2,1)S(1)} %get-tuple-element.38), channel_id=1, source_target_pairs={{0,16},{2,18},{4,20},{6,22},{8,24},{10,26},{12,28},{14,30},{16,0},... | collective-permute-start | bytes 884744 | tf_op jit(solution)/shard_map/ppermute | solution.py:219
  42.6 20.8 %collective-permute-start.8 = (bf16[4,8,4608]{2,1,0:T(8,128)(2,1)S(1)}, bf16[4,8,4608]{2,1,0:T(8,128)(2,1)S(1)}, u32[]{:S(2)}, u32[]{:S(2)}) collective-permute-start(bf16[4,8,4608]{2,1,0:T(8,128)(2,1)S(1)} %get-tuple-element.39), channel_id=1, source_target_pairs={{0,2},{2,0},{4,6},{6,4},{8,10},{10,8},{12,14},{14,12},{16,18},{18,... | collective-permute-start | bytes 884744 | tf_op jit(solution)/shard_map/ppermute | solution.py:219
  44.0 20.0 %collective-permute-start.9 = (bf16[4,8,4608]{2,1,0:T(8,128)(2,1)S(1)}, bf16[4,8,4608]{2,1,0:T(8,128)(2,1)S(1)}, u32[]{:S(2)}, u32[]{:S(2)}) collective-permute-start(bf16[4,8,4608]{2,1,0:T(8,128)(2,1)S(1)} %get-tuple-element.40), channel_id=1, source_target_pairs={{0,4},{2,6},{4,0},{6,2},{8,12},{10,14},{12,8},{14,10},{16,20},{18,... | collective-permute-start | bytes 884744 | tf_op jit(solution)/shard_map/ppermute | solution.py:219
  44.1 27.6 %collective-permute-start.11 = (bf16[4,8,4608]{2,1,0:T(8,128)(2,1)S(1)}, bf16[4,8,4608]{2,1,0:T(8,128)(2,1)S(1)}, u32[]{:S(2)}, u32[]{:S(2)}) collective-permute-start(bf16[4,8,4608]{2,1,0:T(8,128)(2,1)S(1)} %get-tuple-element.44), channel_id=1, source_target_pairs={{0,6},{2,4},{4,2},{6,0},{8,14},{10,12},{12,10},{14,8},{16,22},{18,... | collective-permute-start | bytes 884744 | tf_op jit(solution)/shard_map/ppermute | solution.py:219
  46.1 25.6 %collective-permute-start.12 = (bf16[4,8,4608]{2,1,0:T(8,128)(2,1)S(1)}, bf16[4,8,4608]{2,1,0:T(8,128)(2,1)S(1)}, u32[]{:S(2)}, u32[]{:S(2)}) collective-permute-start(bf16[4,8,4608]{2,1,0:T(8,128)(2,1)S(1)} %get-tuple-element.45), channel_id=1, source_target_pairs={{0,18},{2,16},{4,22},{6,20},{8,26},{10,24},{12,30},{14,28},{16,2},... | collective-permute-start | bytes 884744 | tf_op jit(solution)/shard_map/ppermute | solution.py:219
  51.6 20.1 %collective-permute-start.13 = (bf16[4,8,4608]{2,1,0:T(8,128)(2,1)S(1)}, bf16[4,8,4608]{2,1,0:T(8,128)(2,1)S(1)}, u32[]{:S(2)}, u32[]{:S(2)}) collective-permute-start(bf16[4,8,4608]{2,1,0:T(8,128)(2,1)S(1)} %get-tuple-element.46), channel_id=1, source_target_pairs={{0,20},{2,22},{4,16},{6,18},{8,28},{10,30},{12,24},{14,26},{16,4},... | collective-permute-start | bytes 884744 | tf_op jit(solution)/shard_map/ppermute | solution.py:219
  63.4 8.5 %collective-permute-start.14 = (bf16[4,8,4608]{2,1,0:T(8,128)(2,1)S(1)}, bf16[4,8,4608]{2,1,0:T(8,128)(2,1)S(1)}, u32[]{:S(2)}, u32[]{:S(2)}) collective-permute-start(bf16[4,8,4608]{2,1,0:T(8,128)(2,1)S(1)} %get-tuple-element.47), channel_id=1, source_target_pairs={{0,22},{2,20},{4,18},{6,16},{8,30},{10,28},{12,26},{14,24},{16,6},... | collective-permute-start | bytes 884744 | tf_op jit(solution)/shard_map/ppermute | solution.py:219
  71.5 3.8 %copy-start.3 = (f32[384,640]{1,0:T(8,128)}, f32[384,640]{1,0:T(8,128)S(1)}, u32[]{:S(2)}) copy-start(f32[384,640]{1,0:T(8,128)S(1)} %get-tuple-element.42.keep_ref) | copy-start | bytes 2949124
  71.5 2.6 %collective-permute-start.10 = (f32[384,640]{1,0:T(8,128)S(1)}, f32[384,640]{1,0:T(8,128)S(1)}, u32[]{:S(2)}, u32[]{:S(2)}) collective-permute-start(f32[384,640]{1,0:T(8,128)S(1)} %get-tuple-element.43), channel_id=1, source_target_pairs={{0,1},{1,0},{2,3},{3,2},{4,5},{5,4},{6,7},{7,6},{8,9},{9,8},{10,11... | collective-permute-start | bytes 2949128 | tf_op jit(solution)/shard_map/ppermute | solution.py:229
  74.2 1.1 %copy-start.8 = (f32[384,640]{1,0:T(8,128)}, f32[384,640]{1,0:T(8,128)S(1)}, u32[]{:S(2)}) copy-start(f32[384,640]{1,0:T(8,128)S(1)} %collective-permute-done.10.arrived_ref) | copy-start | bytes 2949124
  74.3 1.6 %copy-start.1 = (bf16[4,64,4608]{2,1,0:T(8,128)(2,1)}, bf16[4,64,4608]{2,1,0:T(8,128)(2,1)S(1)}, u32[]{:S(2)}) copy-start(bf16[4,64,4608]{2,1,0:T(8,128)(2,1)S(1)} %constant_dynamic-update-slice_fusion.handed_ref.up_ref) | copy-start | bytes 7077892
  75.9 1.4 %copy-start.4 = (f32[384,64]{1,0:T(8,128)}, f32[384,64]{1,0:T(8,128)S(1)}, u32[]{:S(2)}) copy-start(f32[384,64]{1,0:T(8,128)S(1)} %shard_map.76.partial_ref) | copy-start | bytes 294916
  75.9 1.4 %collective-permute-start.15 = (f32[384,64]{1,0:T(8,128)S(1)}, f32[384,64]{1,0:T(8,128)S(1)}, u32[]{:S(2)}, u32[]{:S(2)}) collective-permute-start(f32[384,64]{1,0:T(8,128)S(1)} %shard_map.76.partial_ref), channel_id=1, source_target_pairs={{0,1},{1,0},{2,3},{3,2},{4,5},{5,4},{6,7},{7,6},{8,9},{9,8},{10,11... | collective-permute-start | bytes 294920 | tf_op jit(solution)/shard_map/ppermute | solution.py:235
  77.3 0.7 copy-start.9

commit v5 on v4

--- a/solution.py
+++ b/solution.py
@@ -16,40 +16,57 @@
     )
 
 
-def cut_kernel(wide, piece_ref, down_ref, up_ref, *outs):
+def place():
+    parts = STRIPES // lax.axis_size("groups")
+    group, server = lax.axis_index("groups"), lax.axis_index("adapter")
+    return group, server, lax.rem(server, parts), lax.div(server, parts)
+
+
+def cut_kernel(down_ref, up_ref, *outs):
+    wide = down_ref.shape[-1]
+    group, _, part, _ = place()
     for index, out_ref in enumerate(outs):
-        out_ref[:, :, :wide] = down_ref[:, piece_ref[index]]
-        out_ref[:, :, wide:] = up_ref[:, piece_ref[index]]
-
-
-def cut_stripes(pieces, adapter_down, adapter_up, stripe_count):
+        stripe = group * len(outs) + jnp.bitwise_xor(part, index)
+        out_ref[:, :, :wide] = down_ref[:, stripe]
+        out_ref[:, :, wide:] = up_ref[:, stripe]
+
+
+def cut_stripes(adapter_down, adapter_up, stripe_count):
     held, rank, wide = adapter_down.shape
     narrow = adapter_up.shape[2]
     rows = rank // STRIPES
     out = jax.ShapeDtypeStruct((held, rows, wide + narrow), adapter_down.dtype)
     vmem = pl.BlockSpec(memory_space=pltpu.VMEM)
     return pl.pallas_call(
-        functools.partial(cut_kernel, wide),
+        cut_kernel,
         out_shape=[out] * stripe_count,
-        in_specs=[pl.BlockSpec(memory_space=pltpu.SMEM), vmem, vmem],
+        in_specs=[vmem, vmem],
         out_specs=[vmem] * stripe_count,
+        compiler_params=pltpu.CompilerParams(vmem_limit_bytes=8 << 20),
     )(
-        pieces,
         adapter_down.reshape(held, STRIPES, rows, wide),
         adapter_up.reshape(held, STRIPES, rows, narrow),
     )
 
 
-def pick_kernel(server_count, steps, held, choice_ref, *rest):
+def pick_kernel(server_count, steps, held, asked_ref, *rest):
     servers, outs, bank = rest[:server_count], rest[server_count:-1], rest[-1]
     for index, ref in enumerate(servers):
         bank[index * held:(index + 1) * held] = ref[...]
-    for asker, out_ref in enumerate(outs):
+    parts = STRIPES // lax.axis_size("groups")
+    group, server, part, half = place()
+    for index, out_ref in enumerate(outs):
+        asker_group = jnp.bitwise_xor(group, index // parts)
+        asker = half * parts + jnp.bitwise_xor(part, index % parts)
         for step in range(steps):
-            out_ref[step] = bank[choice_ref[asker * steps + step]]
-
-
-def pick_stripes(choice, servers, steps):
+            table = asker_group * server_count
+            offset = lax.div(asked_ref[(table + asker) * steps + step], held)
+            source = lax.rem(asker - offset + server_count, server_count)
+            slot = lax.rem(asked_ref[(table + source) * steps + step], held)
+            out_ref[step] = bank[jnp.bitwise_xor(source, server) * held + slot]
+
+
+def pick_stripes(asked, servers, steps):
     held, rows, width = servers[0].shape
     out = jax.ShapeDtypeStruct((steps, rows, width), servers[0].dtype)
     bank_bytes = len(servers) * held * rows * width * 2
@@ -62,7 +79,7 @@
         out_specs=[vmem] * STRIPES,
         scratch_shapes=[pltpu.VMEM((len(servers) * held, rows, width), servers[0].dtype)],
         compiler_params=pltpu.CompilerParams(vmem_limit_bytes=2 * bank_bytes + out_bytes + (4 << 20)),
-    )(choice, *servers)
+    )(asked, *servers)
 
 
 def products_kernel(side_ref, acts_ref, weight_ref, down_ref, send_ref, keep_ref):
@@ -120,7 +137,8 @@
 
 def final_kernel(slots_ref, keep_ref, arrived_ref, partial_ref, other_ref, own_up_ref, up_ref, out_ref, own, passed):
     steps, rows, narrow = out_ref.shape
-    rank, held = up_ref.shape[1], own_up_ref.shape[0] // up_ref.shape[1]
+    _, rank, both = up_ref.shape
+    held = own_up_ref.shape[0] // rank
     block_rows = rows // slots_ref.shape[1]
     for step in range(steps):
         for block in range(slots_ref.shape[1]):
@@ -135,27 +153,25 @@
         here = slice(step * rows, (step + 1) * rows)
         base = keep_ref[here, :narrow] + arrived_ref[here, :narrow]
         base += jnp.dot(own[here], own_up_ref[...], preferred_element_type=jnp.float32)
-        base += jnp.dot(passed[here], up_ref[step], preferred_element_type=jnp.float32)
+        base += jnp.dot(passed[here], up_ref[step, :, both - narrow:], preferred_element_type=jnp.float32)
         out_ref[step] = base.astype(out_ref.dtype)
 
 
 def finish(slots, keep, arrived, partial, other, own_up, handed):
-    steps, rank, both = handed.shape
+    steps, rank, _ = handed.shape
     held_rank, narrow = own_up.shape
     rows = keep.shape[0]
     vmem = pl.BlockSpec(memory_space=pltpu.VMEM)
-    last = both // narrow - 1
     return pl.pallas_call(
         final_kernel,
         out_shape=jax.ShapeDtypeStruct((steps, rows // steps, narrow), jnp.bfloat16),
-        grid=(1,),
-        in_specs=[pl.BlockSpec(memory_space=pltpu.SMEM)] + [vmem] * 5
-        + [pl.BlockSpec((steps, rank, narrow), lambda step: (0, 0, last))],
+        in_specs=[pl.BlockSpec(memory_space=pltpu.SMEM)] + [vmem] * 6,
         out_specs=vmem,
         scratch_shapes=[
             pltpu.VMEM((rows, held_rank), jnp.bfloat16),
             pltpu.VMEM((rows, rank), jnp.bfloat16),
         ],
+        compiler_params=pltpu.CompilerParams(vmem_limit_bytes=12 << 20),
     )(slots, keep, arrived, partial, other, own_up, handed)
 
 
@@ -180,17 +196,12 @@
 def body(acts, value_weight, adapter_down, adapter_up, block_slots, transfer_offset, transfer_slot):
     groups, servers = lax.axis_size("groups"), lax.axis_size("adapter")
     parts = STRIPES // groups
-    halves = servers // parts
     steps, rows_dev, wide = acts.shape
     held, rank, _ = adapter_down.shape
     narrow = adapter_up.shape[2]
-    group, server = lax.axis_index("groups"), lax.axis_index("adapter")
     side = lax.axis_index("tensor")
-    part = server % parts
-    half = server // parts
-
-    pieces = (group * parts + jnp.bitwise_xor(part, jnp.arange(parts, dtype=jnp.int32))).astype(jnp.int32)
-    stripes = cut_stripes(pieces, adapter_down, adapter_up, parts)
+
+    stripes = cut_stripes(adapter_down, adapter_up, parts)
     banked = {0: stripes[0]}
     for k in [1, 2, 3, 4, 5, 6, 7, *range(STRIPES, servers)]:
         banked[k] = lax.ppermute(stripes[k % parts], "adapter", [(i, i ^ k) for i in range(servers)])
@@ -200,15 +211,9 @@
     banked = [banked[k] for k in range(servers)]
 
     asked = transfer_offset * held + transfer_slot[:, 0]
-    asked = lax.all_gather(asked, ("groups", "adapter")).reshape(groups, servers, steps)
-    offsets, slots = asked // held, asked % held
-    asker = jnp.bitwise_xor(group * parts + part, jnp.arange(STRIPES, dtype=jnp.int32))
-    ask_group, ask_server = asker // parts, half * parts + asker % parts
-    source = (ask_server[:, None] - offsets[ask_group, ask_server]) % servers
-    slot = slots[ask_group[:, None], source, jnp.arange(steps)[None, :]]
-    choice = (jnp.bitwise_xor(source, server) * held + slot).astype(jnp.int32).reshape(-1)
-
-    picked = pick_stripes(choice, banked, steps)
+    asked = lax.all_gather(asked, ("groups", "adapter")).reshape(-1)
+
+    picked = pick_stripes(asked, banked, steps)
     given = {0: picked[0]}
     for k in (4, 1, 2, 7, 3, 5, 6):
         pairs = []

time: 82.3 us -> 79.1 us (0.961)
  the two profiles are of different devices: /device:TPU:0 before, /device:TPU:9 now
where the time goes in v5:
time: 79.1 us; the launch traced here: 78.8 us
  starting transfers between devices  40.3 us (51%)
  blocking collectives  17.3 us (22%)
  Pallas kernels  11 us (14%)
  local copies, waits for them, and re-layouts  5.47 us (7%)
  waiting for transfers between devices  3.21 us (4%)
  between operations  0.81 us (1%)
    ppermute x1, starting transfers between devices, body(): arrived = lax.ppermute(send, 'tensor', swap)  19 us
    unnamed x1, blocking collectives  17.3 us
    ppermute x7, starting transfers between devices, body(): given[k] = lax.ppermute(picked[k], ('groups', 'adapter'), pairs)  12.4 us
    ppermute x7, starting transfers between devices, body(): lax.ppermute(stripes[k % parts], 'adapter', [(i, i ^ k) for i in range(se...  8.41 us
    pallas_call x1, Pallas kernels, products(): pl.pallas_call(products_kernel, out_shape=[out, out], grid_spec=pltpu.Pre...  7.41 us
    unnamed x21, local copies, waits for them, and re-layouts  5.45 us
    ppermute x1, waiting for transfers between devices, body(): arrived = lax.ppermute(send, 'tensor', swap)  2.1 us
    pallas_call x1, Pallas kernels, finish(): pl.pallas_call(final_kernel, out_shape=jax.ShapeDtypeStruct((steps, rows...  1.69 us
  transfers between devices with their start and end apart: 16, of which 2 were waited for; matrix products, arithmetic and copies ran while one was open for 3% of the time, Pallas kernels for 9%

profile of v5, /device:TPU:9, one launch (start us, length us, event | category | flops | bytes accessed | tf_op | source)
XLA Modules:
  0.0 78.8 jit_solution(6267290974120098053)
XLA Ops:
  0.0 0.0 copy-start.1
  0.0 1.2 %copy-done.1 = bf16[2,64,4096]{2,1,0:T(8,128)(2,1)S(1)} copy-done((bf16[2,64,4096]{2,1,0:T(8,128)(2,1)S(1)}, bf16[2,64,4096]{2,1,0:T(8,128)(2,1)}, u32[]{:S(2)}) %copy-start.1) | copy-done | bytes 1048600
  1.2 0.9 %copy-done.3 = bf16[2,64,512]{2,1,0:T(8,128)(2,1)S(1)} copy-done((bf16[2,64,512]{2,1,0:T(8,128)(2,1)S(1)}, bf16[2,64,512]{2,1,0:T(8,128)(2,1)}, u32[]{:S(2)}) %copy-start.3) | copy-done | bytes 131096
  2.2 1.3 %collective-permute-start = (bf16[2,8,4608]{2,1,0:T(8,128)(2,1)S(1)}, bf16[2,8,4608]{2,1,0:T(8,128)(2,1)S(1)}, u32[]{:S(2)}, u32[]{:S(2)}) collective-permute-start(bf16[2,8,4608]{2,1,0:T(8,128)(2,1)S(1)} %get-tuple-element.31), channel_id=1, source_target_pairs={{0,2},{2,0},{4,6},{6,4},{8,10},{10,8},{12,14},{14,12},{1,3},{3,1},... | collective-permute-start | bytes 442376 | tf_op jit(solution)/shard_map/ppermute | solution.py:207
  3.5 0.2 collective-permute-start.1
  3.6 2.3 %collective-permute-start.4 = (bf16[2,8,4608]{2,1,0:T(8,128)(2,1)S(1)}, bf16[2,8,4608]{2,1,0:T(8,128)(2,1)S(1)}, u32[]{:S(2)}, u32[]{:S(2)}) collective-permute-start(bf16[2,8,4608]{2,1,0:T(8,128)(2,1)S(1)} %get-tuple-element.31), channel_id=1, source_target_pairs={{0,10},{2,8},{4,14},{6,12},{8,2},{10,0},{12,6},{14,4},{1,11},{3,9}... | collective-permute-start | bytes 442376 | tf_op jit(solution)/shard_map/ppermute | solution.py:207
  5.9 0.2 collective-permute-start.5
  6.1 2.1 %collective-permute-start.2 = (bf16[2,8,4608]{2,1,0:T(8,128)(2,1)S(1)}, bf16[2,8,4608]{2,1,0:T(8,128)(2,1)S(1)}, u32[]{:S(2)}, u32[]{:S(2)}) collective-permute-start(bf16[2,8,4608]{2,1,0:T(8,128)(2,1)S(1)} %get-tuple-element.37), channel_id=1, source_target_pairs={{0,6},{2,4},{4,2},{6,0},{8,14},{10,12},{12,10},{14,8},{1,7},{3,5},... | collective-permute-start | bytes 442376 | tf_op jit(solution)/shard_map/ppermute | solution.py:207
  8.2 1.3 %dynamic-slice = u32[1]{0:T(128)} dynamic-slice(u32[32]{0:T(128)} %constant.12, u32[]{:T(128)S(6)} %add.4), dynamic_slice_sizes={1} | dynamic-slice | bytes 12
  10.1 0.0 collective-permute-done.rest_1_
  10.1 2.4 %collective-permute-start.6 = (bf16[2,8,4608]{2,1,0:T(8,128)(2,1)S(1)}, bf16[2,8,4608]{2,1,0:T(8,128)(2,1)S(1)}, u32[]{:S(2)}, u32[]{:S(2)}) collective-permute-start(bf16[2,8,4608]{2,1,0:T(8,128)(2,1)S(1)} %get-tuple-element.37), channel_id=1, source_target_pairs={{0,14},{2,12},{4,10},{6,8},{8,6},{10,4},{12,2},{14,0},{1,15},{3,13... | collective-permute-start | bytes 442376 | tf_op jit(solution)/shard_map/ppermute | solution.py:207
  12.4 0.0 collective-permute-done.1.rest_2_
  12.4 0.1 collective-permute-start.3
  12.5 0.8 fusion
  13.3 17.3 %all-reduce.asked_ref = s32[64]{0:T(128)S(1)} all-reduce(s32[64]{0:T(128)S(1)} %fusion), channel_id=2, replica_groups=mesh['groups'=2,'adapter'=8,'tensor'=2] {'groups','adapter'}, use_global_device_ids=true, to_apply=%add | all-reduce | flops 64 | bytes 512
  30.6 0.0 collective-permute-done.2.rest_3_
  30.6 0.0 collective-permute-done.3.rest_4_
  30.6 0.0 collective-permute-done.4.rest_5_
  30.6 0.0 collective-permute-done.5.rest_6_
  30.6 0.0 collective-permute-done.6.rest_7_
  30.6 0.9 %shard_map.74 = (bf16[4,8,4608]{2,1,0:T(8,128)(2,1)S(1)}, bf16[4,8,4608]{2,1,0:T(8,128)(2,1)S(1)}, bf16[4,8,4608]{2,1,0:T(8,128)(2,1)S(1)}, bf16[4,8,4608]{2,1,0...) custom-call(s32[64]{0:T(128)S(1)} %all-reduce.asked_ref, ...), custom_call_target="tpu_custom_call" | custom-call | tf_op jit(solution)/shard_map/pallas_call | solution.py:75
  31.5 1.3 %collective-permute-start.7 = (bf16[4,8,4608]{2,1,0:T(8,128)(2,1)S(1)}, bf16[4,8,4608]{2,1,0:T(8,128)(2,1)S(1)}, u32[]{:S(2)}, u32[]{:S(2)}) collective-permute-start(bf16[4,8,4608]{2,1,0:T(8,128)(2,1)S(1)} %get-tuple-element.38), channel_id=1, source_target_pairs={{0,16},{2,18},{4,20},{6,22},{8,24},{10,26},{12,28},{14,30},{16,0},... | collective-permute-start | bytes 884744 | tf_op jit(solution)/shard_map/ppermute | solution.py:224
  32.8 1.4 %collective-permute-start.8 = (bf16[4,8,4608]{2,1,0:T(8,128)(2,1)S(1)}, bf16[4,8,4608]{2,1,0:T(8,128)(2,1)S(1)}, u32[]{:S(2)}, u32[]{:S(2)}) collective-permute-start(bf16[4,8,4608]{2,1,0:T(8,128)(2,1)S(1)} %get-tuple-element.39), channel_id=1, source_target_pairs={{0,2},{2,0},{4,6},{6,4},{8,10},{10,8},{12,14},{14,12},{16,18},{18,... | collective-permute-start | bytes 884744 | tf_op jit(solution)/shard_map/ppermute | solution.py:224
  34.2 3.2 %collective-permute-start.9 = (bf16[4,8,4608]{2,1,0:T(8,128)(2,1)S(1)}, bf16[4,8,4608]{2,1,0:T(8,128)(2,1)S(1)}, u32[]{:S(2)}, u32[]{:S(2)}) collective-permute-start(bf16[4,8,4608]{2,1,0:T(8,128)(2,1)S(1)} %get-tuple-element.40), channel_id=1, source_target_pairs={{0,4},{2,6},{4,0},{6,2},{8,12},{10,14},{12,8},{14,10},{16,20},{18,... | collective-permute-start | bytes 884744 | tf_op jit(solution)/shard_map/ppermute | solution.py:224
  37.5 0.0 collective-permute-start.11
  37.5 2.1 %collective-permute-start.12 = (bf16[4,8,4608]{2,1,0:T(8,128)(2,1)S(1)}, bf16[4,8,4608]{2,1,0:T(8,128)(2,1)S(1)}, u32[]{:S(2)}, u32[]{:S(2)}) collective-permute-start(bf16[4,8,4608]{2,1,0:T(8,128)(2,1)S(1)} %get-tuple-element.45), channel_id=1, source_target_pairs={{0,18},{2,16},{4,22},{6,20},{8,26},{10,24},{12,30},{14,28},{16,2},... | collective-permute-start | bytes 884744 | tf_op jit(solution)/shard_map/ppermute | solution.py:224
  39.6 0.0 collective-permute-done.7
  39.6 1.5 %collective-permute-start.13 = (bf16[4,8,4608]{2,1,0:T(8,128)(2,1)S(1)}, bf16[4,8,4608]{2,1,0:T(8,128)(2,1)S(1)}, u32[]{:S(2)}, u32[]{:S(2)}) collective-permute-start(bf16[4,8,4608]{2,1,0:T(8,128)(2,1)S(1)} %get-tuple-element.46), channel_id=1, source_target_pairs={{0,20},{2,22},{4,16},{6,18},{8,28},{10,30},{12,24},{14,26},{16,4},... | collective-permute-start | bytes 884744 | tf_op jit(solution)/shard_map/ppermute | solution.py:224
  41.1 0.0 collective-permute-done.8
  41.1 2.9 %collective-permute-start.14 = (bf16[4,8,4608]{2,1,0:T(8,128)(2,1)S(1)}, bf16[4,8,4608]{2,1,0:T(8,128)(2,1)S(1)}, u32[]{:S(2)}, u32[]{:S(2)}) collective-permute-start(bf16[4,8,4608]{2,1,0:T(8,128)(2,1)S(1)} %get-tuple-element.47), channel_id=1, source_target_pairs={{0,22},{2,20},{4,18},{6,16},{8,30},{10,28},{12,26},{14,24},{16,6},... | collective-permute-start | bytes 884744 | tf_op jit(solution)/shard_map/ppermute | solution.py:224
  44.0 0.0 collective-permute-done.9
  44.0 0.0 copy-done.2
  44.0 1.9 %copy-done = bf16[4,96,4096]{2,1,0:T(8,128)(2,1)S(1)} copy-done((bf16[4,96,4096]{2,1,0:T(8,128)(2,1)S(1)}, bf16[4,96,4096]{2,1,0:T(8,128)(2,1)}, u32[]{:S(2)}) %copy-start) | copy-done | bytes 3145752
  45.9 7.4 %shard_map.75 = (f32[384,640]{1,0:T(8,128)S(1)}, f32[384,640]{1,0:T(8,128)S(1)}) custom-call(s32[1]{0:T(128)} %bitcast.side_ref, bf16[384,4096]{1,0:T(8,128)(2,1)S(1)} %bitcast.11, bf16[4096,1024]{1,0:T(8,128)(2,1)} %weight_ref.1, bf16[128,4096]{1,0:T(8,128)(2,1)S(1)} %bitcast.13), custom_call_target="tpu_custom_call" | custom-call | tf_op jit(solution)/shard_map/pallas_call | solution.py:120
  53.3 19.0 %collective-permute-start.10 = (f32[384,640]{1,0:T(8,128)S(1)}, f32[384,640]{1,0:T(8,128)S(1)}, u32[]{:S(2)}, u32[]{:S(2)}) collective-permute-start(f32[384,640]{1,0:T(8,128)S(1)} %get-tuple-element.43), channel_id=1, source_target_pairs={{0,1},{1,0},{2,3},{3,2},{4,5},{5,4},{6,7},{7,6},{8,9},{9,8},{10,11... | collective-permute-start | bytes 2949128 | tf_op jit(solution)/shard_map/ppermute | solution.py:234
  72.4 0.0 collective-permute-done.11
  72.4 0.0 collective-permute-done.12
  72.4 0.0 collective-permute-done.13
  72.4 0.0 collective-permute-done.14
  72.4 2.1 %collective-permute-done.10.arrived_ref = f32[384,640]{1,0:T(8,128)S(1)} collective-permute-done((f32[384,640]{1,0:T(8,128)S(1)}, f32[384,640]{1,0:T(8,128)S(1)}, u32[]{:S(2)}, u32[]{:S(2)}) %collective-permute-start.10) | collective-permute-done | bytes 983072 | tf_op jit(solution)/shard_map/ppermute | solution.py:234
  74.6 0.0 copy-start.4
  74.7 0.0 copy-start.5
  74.7 1.0 %shard_map.76.partial_ref = f32[384,64]{1,0:T(8,128)S(1)} custom-call(bf16[4,96,4096]{2,1,0:T(8,128)(2,1)S(1)} %copy-done, bf16[4,64,4608]{2,1,0:T(8,128)(2,1)S(1)} %constant_dynamic-update-slice_fusion.handed_ref.up_ref), custom_call_target="tpu_custom_call" | custom-call | tf_op jit(solution)/shard_map/pallas_call | solution.py:187
  75.6 0.4 collective-permute-start.15
  76.1 1.1 %collective-permute-done.15.other_ref = f32[384,64]{1,0:T(8,128)S(1)} collective-permute-done((f32[384,64]{1,0:T(8,128)S(1)}, f32[384,64]{1,0:T(8,128)S(1)}, u32[]{:S(2)}, u32[]{:S(2)}) %collective-permute-start.15) | collective-permute-done | bytes 98336 | tf_op jit(solution)/shard_map/ppermute | solution.py:240
  77.1 0.0 copy-done.4
  77.2 0.0 copy-done.5
  77.2 1.7 %shard_map.77 = bf16[4,96,512]{2,1,0:T(8,128)(2,1)} custom-call(s32[4,6]{1,0:T(4,128)S(1)} %copy-done.5, f32[384,640]{1,0:T(8,128)S(1)} %get-tuple-element.42.keep_ref, f32[384,640]{1,0:T(8,128)S(1)} %collective-permute-done.10.arrived_ref, f32[384,64]{1,0:T(8,128)S(1)} %shard_map.76.partial_ref, f32[384,64]{1,0:T(8,128)S(1)} %collective-permute-done.15.other_ref, ...), custom_call_target="tpu_custom_call" | custom-call | tf_op jit(solution)/shard_map/pallas_call | solution.py:165
  (13 shorter events, 0.2 us)
Async XLA Ops:
  0.0 1.2 %copy-start.1 = (bf16[2,64,4096]{2,1,0:T(8,128)(2,1)S(1)}, bf16[2,64,4096]{2,1,0:T(8,128)(2,1)}, u32[]{:S(2)}) copy-start(bf16[2,64,4096]{2,1,0:T(8,128)(2,1)} %param.9) | copy-start | bytes 3145732
  1.2 0.9 %copy-start.3 = (bf16[2,64,512]{2,1,0:T(8,128)(2,1)S(1)}, bf16[2,64,512]{2,1,0:T(8,128)(2,1)}, u32[]{:S(2)}) copy-start(bf16[2,64,512]{2,1,0:T(8,128)(2,1)} %param.10) | copy-start | bytes 393220
  2.1 41.8 %copy-start.2 = (bf16[2,64,4096]{2,1,0:T(8,128)(2,1)S(1)}, bf16[2,64,4096]{2,1,0:T(8,128)(2,1)}, u32[]{:S(2)}) copy-start(bf16[2,64,4096]{2,1,0:T(8,128)(2,1)} %param.9) | copy-start | bytes 3145732
  2.2 7.9 %collective-permute-start = (bf16[2,8,4608]{2,1,0:T(8,128)(2,1)S(1)}, bf16[2,8,4608]{2,1,0:T(8,128)(2,1)S(1)}, u32[]{:S(2)}, u32[]{:S(2)}) collective-permute-start(bf16[2,8,4608]{2,1,0:T(8,128)(2,1)S(1)} %get-tuple-element.31), channel_id=1, source_target_pairs={{0,2},{2,0},{4,6},{6,4},{8,10},{10,8},{12,14},{14,12},{1,3},{3,1},... | collective-permute-start | bytes 442376 | tf_op jit(solution)/shard_map/ppermute | solution.py:207
  3.5 9.0 %collective-permute-start.1 = (bf16[2,8,4608]{2,1,0:T(8,128)(2,1)S(1)}, bf16[2,8,4608]{2,1,0:T(8,128)(2,1)S(1)}, u32[]{:S(2)}, u32[]{:S(2)}) collective-permute-start(bf16[2,8,4608]{2,1,0:T(8,128)(2,1)S(1)} %get-tuple-element.32), channel_id=1, source_target_pairs={{0,4},{2,6},{4,0},{6,2},{8,12},{10,14},{12,8},{14,10},{1,5},{3,7},... | collective-permute-start | bytes 442376 | tf_op jit(solution)/shard_map/ppermute | solution.py:207
  3.6 27.0 %collective-permute-start.4 = (bf16[2,8,4608]{2,1,0:T(8,128)(2,1)S(1)}, bf16[2,8,4608]{2,1,0:T(8,128)(2,1)S(1)}, u32[]{:S(2)}, u32[]{:S(2)}) collective-permute-start(bf16[2,8,4608]{2,1,0:T(8,128)(2,1)S(1)} %get-tuple-element.31), channel_id=1, source_target_pairs={{0,10},{2,8},{4,14},{6,12},{8,2},{10,0},{12,6},{14,4},{1,11},{3,9}... | collective-permute-start | bytes 442376 | tf_op jit(solution)/shard_map/ppermute | solution.py:207
  5.9 24.7 %collective-permute-start.5 = (bf16[2,8,4608]{2,1,0:T(8,128)(2,1)S(1)}, bf16[2,8,4608]{2,1,0:T(8,128)(2,1)S(1)}, u32[]{:S(2)}, u32[]{:S(2)}) collective-permute-start(bf16[2,8,4608]{2,1,0:T(8,128)(2,1)S(1)} %get-tuple-element.32), channel_id=1, source_target_pairs={{0,12},{2,14},{4,8},{6,10},{8,4},{10,6},{12,0},{14,2},{1,13},{3,15... | collective-permute-start | bytes 442376 | tf_op jit(solution)/shard_map/ppermute | solution.py:207
  6.1 24.5 %collective-permute-start.2 = (bf16[2,8,4608]{2,1,0:T(8,128)(2,1)S(1)}, bf16[2,8,4608]{2,1,0:T(8,128)(2,1)S(1)}, u32[]{:S(2)}, u32[]{:S(2)}) collective-permute-start(bf16[2,8,4608]{2,1,0:T(8,128)(2,1)S(1)} %get-tuple-element.37), channel_id=1, source_target_pairs={{0,6},{2,4},{4,2},{6,0},{8,14},{10,12},{12,10},{14,8},{1,7},{3,5},... | collective-permute-start | bytes 442376 | tf_op jit(solution)/shard_map/ppermute | solution.py:207
  10.1 20.6 %collective-permute-start.6 = (bf16[2,8,4608]{2,1,0:T(8,128)(2,1)S(1)}, bf16[2,8,4608]{2,1,0:T(8,128)(2,1)S(1)}, u32[]{:S(2)}, u32[]{:S(2)}) collective-permute-start(bf16[2,8,4608]{2,1,0:T(8,128)(2,1)S(1)} %get-tuple-element.37), channel_id=1, source_target_pairs={{0,14},{2,12},{4,10},{6,8},{8,6},{10,4},{12,2},{14,0},{1,15},{3,13... | collective-permute-start | bytes 442376 | tf_op jit(solution)/shard_map/ppermute | solution.py:207
  12.4 18.2 %collective-permute-start.3 = (bf16[2,8,4608]{2,1,0:T(8,128)(2,1)S(1)}, bf16[2,8,4608]{2,1,0:T(8,128)(2,1)S(1)}, u32[]{:S(2)}, u32[]{:S(2)}) collective-permute-start(bf16[2,8,4608]{2,1,0:T(8,128)(2,1)S(1)} %get-tuple-element.34.rest_0_), channel_id=1, source_target_pairs={{0,8},{2,10},{4,12},{6,14},{8,0},{10,2},{12,4},{14,6},{1,9},{3,11}... | collective-permute-start | bytes 442376 | tf_op jit(solution)/shard_map/ppermute | solution.py:207
  31.5 8.1 %collective-permute-start.7 = (bf16[4,8,4608]{2,1,0:T(8,128)(2,1)S(1)}, bf16[4,8,4608]{2,1,0:T(8,128)(2,1)S(1)}, u32[]{:S(2)}, u32[]{:S(2)}) collective-permute-start(bf16[4,8,4608]{2,1,0:T(8,128)(2,1)S(1)} %get-tuple-element.38), channel_id=1, source_target_pairs={{0,16},{2,18},{4,20},{6,22},{8,24},{10,26},{12,28},{14,30},{16,0},... | collective-permute-start | bytes 884744 | tf_op jit(solution)/shard_map/ppermute | solution.py:224
  32.8 8.3 %collective-permute-start.8 = (bf16[4,8,4608]{2,1,0:T(8,128)(2,1)S(1)}, bf16[4,8,4608]{2,1,0:T(8,128)(2,1)S(1)}, u32[]{:S(2)}, u32[]{:S(2)}) collective-permute-start(bf16[4,8,4608]{2,1,0:T(8,128)(2,1)S(1)} %get-tuple-element.39), channel_id=1, source_target_pairs={{0,2},{2,0},{4,6},{6,4},{8,10},{10,8},{12,14},{14,12},{16,18},{18,... | collective-permute-start | bytes 884744 | tf_op jit(solution)/shard_map/ppermute | solution.py:224
  34.2 9.7 %collective-permute-start.9 = (bf16[4,8,4608]{2,1,0:T(8,128)(2,1)S(1)}, bf16[4,8,4608]{2,1,0:T(8,128)(2,1)S(1)}, u32[]{:S(2)}, u32[]{:S(2)}) collective-permute-start(bf16[4,8,4608]{2,1,0:T(8,128)(2,1)S(1)} %get-tuple-element.40), channel_id=1, source_target_pairs={{0,4},{2,6},{4,0},{6,2},{8,12},{10,14},{12,8},{14,10},{16,20},{18,... | collective-permute-start | bytes 884744 | tf_op jit(solution)/shard_map/ppermute | solution.py:224
  37.5 34.9 %collective-permute-start.11 = (bf16[4,8,4608]{2,1,0:T(8,128)(2,1)S(1)}, bf16[4,8,4608]{2,1,0:T(8,128)(2,1)S(1)}, u32[]{:S(2)}, u32[]{:S(2)}) collective-permute-start(bf16[4,8,4608]{2,1,0:T(8,128)(2,1)S(1)} %get-tuple-element.44), channel_id=1, source_target_pairs={{0,6},{2,4},{4,2},{6,0},{8,14},{10,12},{12,10},{14,8},{16,22},{18,... | collective-permute-start | bytes 884744 | tf_op jit(solution)/shard_map/ppermute | solution.py:224
  37.5 34.9 %collective-permute-start.12 = (bf16[4,8,4608]{2,1,0:T(8,128)(2,1)S(1)}, bf16[4,8,4608]{2,1,0:T(8,128)(2,1)S(1)}, u32[]{:S(2)}, u32[]{:S(2)}) collective-permute-start(bf16[4,8,4608]{2,1,0:T(8,128)(2,1)S(1)} %get-tuple-element.45), channel_id=1, source_target_pairs={{0,18},{2,16},{4,22},{6,20},{8,26},{10,24},{12,30},{14,28},{16,2},... | collective-permute-start | bytes 884744 | tf_op jit(solution)/shard_map/ppermute | solution.py:224
  39.6 32.8 %collective-permute-start.13 = (bf16[4,8,4608]{2,1,0:T(8,128)(2,1)S(1)}, bf16[4,8,4608]{2,1,0:T(8,128)(2,1)S(1)}, u32[]{:S(2)}, u32[]{:S(2)}) collective-permute-start(bf16[4,8,4608]{2,1,0:T(8,128)(2,1)S(1)} %get-tuple-element.46), channel_id=1, source_target_pairs={{0,20},{2,22},{4,16},{6,18},{8,28},{10,30},{12,24},{14,26},{16,4},... | collective-permute-start | bytes 884744 | tf_op jit(solution)/shard_map/ppermute | solution.py:224
  41.1 31.3 %collective-permute-start.14 = (bf16[4,8,4608]{2,1,0:T(8,128)(2,1)S(1)}, bf16[4,8,4608]{2,1,0:T(8,128)(2,1)S(1)}, u32[]{:S(2)}, u32[]{:S(2)}) collective-permute-start(bf16[4,8,4608]{2,1,0:T(8,128)(2,1)S(1)} %get-tuple-element.47), channel_id=1, source_target_pairs={{0,22},{2,20},{4,18},{6,16},{8,30},{10,28},{12,26},{14,24},{16,6},... | collective-permute-start | bytes 884744 | tf_op jit(solution)/shard_map/ppermute | solution.py:224
  44.0 1.9 %copy-start = (bf16[4,96,4096]{2,1,0:T(8,128)(2,1)S(1)}, bf16[4,96,4096]{2,1,0:T(8,128)(2,1)}, u32[]{:S(2)}) copy-start(bf16[4,96,4096]{2,1,0:T(8,128)(2,1)} %acts_ref) | copy-start | bytes 9437188
  53.3 21.2 %collective-permute-start.10 = (f32[384,640]{1,0:T(8,128)S(1)}, f32[384,640]{1,0:T(8,128)S(1)}, u32[]{:S(2)}, u32[]{:S(2)}) collective-permute-start(f32[384,640]{1,0:T(8,128)S(1)} %get-tuple-element.43), channel_id=1, source_target_pairs={{0,1},{1,0},{2,3},{3,2},{4,5},{5,4},{6,7},{7,6},{8,9},{9,8},{10,11... | collective-permute-start | bytes 2949128 | tf_op jit(solution)/shard_map/ppermute | solution.py:234
  74.6 2.5 %copy-start.4 = (bf16[2,64,512]{2,1,0:T(8,128)(2,1)S(1)}, bf16[2,64,512]{2,1,0:T(8,128)(2,1)}, u32[]{:S(2)}) copy-start(bf16[2,64,512]{2,1,0:T(8,128)(2,1)} %param.10) | copy-start | bytes 393220
  74.7 2.5 %copy-start.5 = (s32[4,6]{1,0:T(4,128)S(1)}, s32[4,6]{1,0:T(4,128)}, u32[]{:S(2)}) copy-start(s32[4,6]{1,0:T(4,128)} %slots_ref.1) | copy-start | bytes 292
  75.6 1.5 %collective-permute-start.15 = (f32[384,64]{1,0:T(8,128)S(1)}, f32[384,64]{1,0:T(8,128)S(1)}, u32[]{:S(2)}, u32[]{:S(2)}) collective-permute-start(f32[384,64]{1,0:T(8,128)S(1)} %shard_map.76.partial_ref), channel_id=1, source_target_pairs={{0,1},{1,0},{2,3},{3,2},{4,5},{5,4},{6,7},{7,6},{8,9},{9,8},{10,11... | collective-permute-start | bytes 294920 | tf_op jit(solution)/shard_map/ppermute | solution.py:240

commit v6 on v5

--- a/solution.py
+++ b/solution.py
@@ -82,60 +82,51 @@
     )(asked, *servers)
 
 
-def products_kernel(side_ref, acts_ref, weight_ref, down_ref, send_ref, keep_ref):
+def product_kernel(half_ref, acts_ref, weight_ref, *rest):
+    out_ref = rest[-1]
     step = pl.program_id(0)
-    blocks, width = pl.num_programs(0) // 2, weight_ref.shape[1]
-    narrow = send_ref.shape[1] - down_ref.shape[0]
+    width = weight_ref.shape[1]
     product = jnp.dot(acts_ref[...], weight_ref[...], preferred_element_type=jnp.float32)
-    for block in range(narrow // width):
+    for block in range(out_ref.shape[1] // width):
         @pl.when(step == block)
         def _():
-            send_ref[:, block * width:(block + 1) * width] = product
-
-        @pl.when(step == blocks + block)
+            out_ref[:, block * width:(block + 1) * width] = product
+
+    if len(rest) == 2:
+        @pl.when(step == 0)
         def _():
-            keep_ref[:, block * width:(block + 1) * width] = product
-
-    @pl.when(step == 0)
-    def _():
-        own = contract_last(acts_ref[...], down_ref[...])
-        send_ref[:, narrow:] = own
-        keep_ref[:, narrow:] = own
-
-
-def products(side, tokens, weight, down):
+            out_ref[:, out_ref.shape[1] - rest[0].shape[0]:] = contract_last(acts_ref[...], rest[0][...])
+
+
+def product(half, tokens, weight, *down):
     rows, depth = tokens.shape
-    columns = weight.shape[1]
+    narrow = weight.shape[1] // 2
     width = 256
-    blocks = columns // 2 // width
-    out = jax.ShapeDtypeStruct((rows, columns // 2 + down.shape[0]), jnp.float32)
-
-    def weight_block(step, side_ref):
-        half = jnp.where(step < blocks, 1 - side_ref[0], side_ref[0])
-        return 0, half * blocks + step % blocks
-
-    def whole(step, side_ref):
+    blocks = narrow // width
+    out = jax.ShapeDtypeStruct((rows, narrow + sum(each.shape[0] for each in down)), jnp.float32)
+
+    def whole(step, half_ref):
         return 0, 0
 
     return pl.pallas_call(
-        products_kernel,
-        out_shape=[out, out],
+        product_kernel,
+        out_shape=out,
         grid_spec=pltpu.PrefetchScalarGridSpec(
             num_scalar_prefetch=1,
-            grid=(2 * blocks,),
+            grid=(blocks,),
             in_specs=[
                 pl.BlockSpec(tokens.shape, whole),
-                pl.BlockSpec((depth, width), weight_block),
-                pl.BlockSpec(down.shape, whole),
+                pl.BlockSpec((depth, width), lambda step, half_ref: (0, half_ref[0] * blocks + step)),
+                *[pl.BlockSpec(each.shape, whole) for each in down],
             ],
-            out_specs=[pl.BlockSpec(out.shape, whole)] * 2,
+            out_specs=pl.BlockSpec(out.shape, whole),
         ),
-        compiler_params=pltpu.CompilerParams(vmem_limit_bytes=48 << 20),
+        compiler_params=pltpu.CompilerParams(vmem_limit_bytes=44 << 20),
         cost_estimate=pl.CostEstimate(flops=0, bytes_accessed=0, transcendentals=0),
-    )(side, tokens, weight, down)
-
-
-def final_kernel(slots_ref, keep_ref, arrived_ref, partial_ref, other_ref, own_up_ref, up_ref, out_ref, own, passed):
+    )(half, tokens, weight, *down)
+
+
+def final_kernel(slots_ref, keep_ref, send_ref, arrived_ref, partial_ref, other_ref, own_up_ref, up_ref, out_ref, own, passed):
     steps, rows, narrow = out_ref.shape
     _, rank, both = up_ref.shape
     held = own_up_ref.shape[0] // rank
@@ -144,20 +135,20 @@
         for block in range(slots_ref.shape[1]):
             slot = slots_ref[step, block]
             here = slice(step * rows + block * block_rows, step * rows + (block + 1) * block_rows)
-            mine = (keep_ref[here, narrow:] + arrived_ref[here, narrow:]).astype(own.dtype)
+            mine = (send_ref[here, narrow:] + arrived_ref[here, narrow:]).astype(own.dtype)
             column = lax.broadcasted_iota(jnp.int32, mine.shape, 1) // rank
             own[here] = jnp.where(column == slot, mine, jnp.zeros_like(mine))
             given = (partial_ref[here] + other_ref[here]).astype(passed.dtype)
             passed[here] = jnp.where(slot == held, given, jnp.zeros_like(given))
     for step in range(steps):
         here = slice(step * rows, (step + 1) * rows)
-        base = keep_ref[here, :narrow] + arrived_ref[here, :narrow]
+        base = keep_ref[here] + arrived_ref[here, :narrow]
         base += jnp.dot(own[here], own_up_ref[...], preferred_element_type=jnp.float32)
         base += jnp.dot(passed[here], up_ref[step, :, both - narrow:], preferred_element_type=jnp.float32)
         out_ref[step] = base.astype(out_ref.dtype)
 
 
-def finish(slots, keep, arrived, partial, other, own_up, handed):
+def finish(slots, keep, send, arrived, partial, other, own_up, handed):
     steps, rank, _ = handed.shape
     held_rank, narrow = own_up.shape
     rows = keep.shape[0]
@@ -165,14 +156,14 @@
     return pl.pallas_call(
         final_kernel,
         out_shape=jax.ShapeDtypeStruct((steps, rows // steps, narrow), jnp.bfloat16),
-        in_specs=[pl.BlockSpec(memory_space=pltpu.SMEM)] + [vmem] * 6,
+        in_specs=[pl.BlockSpec(memory_space=pltpu.SMEM)] + [vmem] * 7,
         out_specs=vmem,
         scratch_shapes=[
             pltpu.VMEM((rows, held_rank), jnp.bfloat16),
             pltpu.VMEM((rows, rank), jnp.bfloat16),
         ],
         compiler_params=pltpu.CompilerParams(vmem_limit_bytes=12 << 20),
-    )(slots, keep, arrived, partial, other, own_up, handed)
+    )(slots, keep, send, arrived, partial, other, own_up, handed)
 
 
 def rank_kernel(acts_ref, handed_ref, out_ref):
@@ -199,7 +190,7 @@
     steps, rows_dev, wide = acts.shape
     held, rank, _ = adapter_down.shape
     narrow = adapter_up.shape[2]
-    side = lax.axis_index("tensor")
+    side = lax.axis_index("tensor").astype(jnp.int32)
 
     stripes = cut_stripes(adapter_down, adapter_up, parts)
     banked = {0: stripes[0]}
@@ -222,24 +213,26 @@
                 other = (g * parts + i % parts) ^ k
                 pairs.append((g * servers + i, (other // parts) * servers + (i // parts) * parts + other % parts))
         given[k] = lax.ppermute(picked[k], ("groups", "adapter"), pairs)
-    early = [4, 1, 2]
-    acts, *arrived = lax.optimization_barrier((acts, *[given[k] for k in early]))
-    given.update(zip(early, arrived))
-    late = [k for k in range(1, STRIPES) if k not in early]
-
     swap = [(0, 1), (1, 0)]
-    send, keep = products(
-        side.astype(jnp.int32)[None], acts.reshape(steps * rows_dev, wide), value_weight,
-        adapter_down.reshape(held * rank, wide))
+    tokens = acts.reshape(steps * rows_dev, wide)
+    early = [4]
+    other_side, *waited = lax.optimization_barrier((1 - side, *[given[k] for k in early]))
+    given.update(zip(early, waited))
+    send = product(other_side[None], tokens, value_weight, adapter_down.reshape(held * rank, wide))
     arrived = lax.ppermute(send, "tensor", swap)
-    arrived, *others = lax.optimization_barrier((arrived, *[given[k] for k in late]))
-    given.update(zip(late, others))
+    later = [1, 2]
+    side, send, *waited = lax.optimization_barrier((side, send, *[given[k] for k in later]))
+    given.update(zip(later, waited))
+    keep = product(side[None], tokens, value_weight)
+    late = [k for k in range(1, STRIPES) if k not in early + later]
+    keep, arrived, *waited = lax.optimization_barrier((keep, arrived, *[given[k] for k in late]))
+    given.update(zip(late, waited))
 
     handed = jnp.concatenate([given[k] for k in range(STRIPES)], axis=1)
     partial = rank_part(acts, handed)
     other = lax.ppermute(partial, "tensor", swap)
     return finish(
-        block_slots, keep, arrived, partial, other, adapter_up.reshape(held * rank, narrow), handed)
+        block_slots, keep, send, arrived, partial, other, adapter_up.reshape(held * rank, narrow), handed)
 
 
 def solution(mesh):

time: 79.1 us -> 74.1 us (0.937)
  the two profiles are of different devices: /device:TPU:9 before, /device:TPU:0 now
where the time goes in v6:
time: 74.1 us; the launch traced here: 73.9 us
  blocking collectives  20.6 us (28%)
  starting transfers between devices  19.2 us (26%)
  waiting for transfers between devices  15 us (20%)
  Pallas kernels  12 us (16%)
  local copies, waits for them, and re-layouts  5.51 us (7%)
  between operations  0.83 us (1%)
  other arithmetic  0.76 us (1%)
    unnamed x1, blocking collectives  20.6 us
    ppermute x7, waiting for transfers between devices, body(): given[k] = lax.ppermute(picked[k], ('groups', 'adapter'), pairs)  13.6 us
    ppermute x7, starting transfers between devices, body(): lax.ppermute(stripes[k % parts], 'adapter', [(i, i ^ k) for i in range(se...  12.6 us
    pallas_call x2, Pallas kernels, product(): pl.pallas_call(product_kernel, out_shape=out, grid_spec=pltpu.PrefetchSca...  8.39 us
    ppermute x7, starting transfers between devices, body(): given[k] = lax.ppermute(picked[k], ('groups', 'adapter'), pairs)  6.49 us
    unnamed x23, local copies, waits for them, and re-layouts  5.49 us
    pallas_call x1, Pallas kernels, finish(): pl.pallas_call(final_kernel, out_shape=jax.ShapeDtypeStruct((steps, rows...  1.7 us
  transfers between devices with their start and end apart: 16, of which 4 were waited for; matrix products, arithmetic and copies ran while one was open for 3% of the time, Pallas kernels for 11%

profile of v6, /device:TPU:0, one launch (start us, length us, event | category | flops | bytes accessed | tf_op | source)
XLA Modules:
  0.0 73.9 jit_solution(16912739344470093432)
XLA Ops:
  0.0 1.2 %copy-done.2 = bf16[2,64,4096]{2,1,0:T(8,128)(2,1)S(1)} copy-done((bf16[2,64,4096]{2,1,0:T(8,128)(2,1)S(1)}, bf16[2,64,4096]{2,1,0:T(8,128)(2,1)}, u32[]{:S(2)}) %copy-start.2) | copy-done | bytes 1048600
  1.2 0.9 %copy-done.4 = bf16[2,64,512]{2,1,0:T(8,128)(2,1)S(1)} copy-done((bf16[2,64,512]{2,1,0:T(8,128)(2,1)S(1)}, bf16[2,64,512]{2,1,0:T(8,128)(2,1)}, u32[]{:S(2)}) %copy-start.4) | copy-done | bytes 131096
  2.2 3.0 %collective-permute-start = (bf16[2,8,4608]{2,1,0:T(8,128)(2,1)S(1)}, bf16[2,8,4608]{2,1,0:T(8,128)(2,1)S(1)}, u32[]{:S(2)}, u32[]{:S(2)}) collective-permute-start(bf16[2,8,4608]{2,1,0:T(8,128)(2,1)S(1)} %get-tuple-element.32), channel_id=1, source_target_pairs={{0,2},{2,0},{4,6},{6,4},{8,10},{10,8},{12,14},{14,12},{1,3},{3,1},... | collective-permute-start | bytes 442376 | tf_op jit(solution)/shard_map/ppermute | solution.py:198
  5.2 1.6 %collective-permute-start.1 = (bf16[2,8,4608]{2,1,0:T(8,128)(2,1)S(1)}, bf16[2,8,4608]{2,1,0:T(8,128)(2,1)S(1)}, u32[]{:S(2)}, u32[]{:S(2)}) collective-permute-start(bf16[2,8,4608]{2,1,0:T(8,128)(2,1)S(1)} %get-tuple-element.33), channel_id=1, source_target_pairs={{0,4},{2,6},{4,0},{6,2},{8,12},{10,14},{12,8},{14,10},{1,5},{3,7},... | collective-permute-start | bytes 442376 | tf_op jit(solution)/shard_map/ppermute | solution.py:198
  6.8 2.5 %collective-permute-start.4 = (bf16[2,8,4608]{2,1,0:T(8,128)(2,1)S(1)}, bf16[2,8,4608]{2,1,0:T(8,128)(2,1)S(1)}, u32[]{:S(2)}, u32[]{:S(2)}) collective-permute-start(bf16[2,8,4608]{2,1,0:T(8,128)(2,1)S(1)} %get-tuple-element.32), channel_id=1, source_target_pairs={{0,10},{2,8},{4,14},{6,12},{8,2},{10,0},{12,6},{14,4},{1,11},{3,9}... | collective-permute-start | bytes 442376 | tf_op jit(solution)/shard_map/ppermute | solution.py:198
  9.3 0.0 collective-permute-start.5
  9.3 1.9 %collective-permute-start.2 = (bf16[2,8,4608]{2,1,0:T(8,128)(2,1)S(1)}, bf16[2,8,4608]{2,1,0:T(8,128)(2,1)S(1)}, u32[]{:S(2)}, u32[]{:S(2)}) collective-permute-start(bf16[2,8,4608]{2,1,0:T(8,128)(2,1)S(1)} %get-tuple-element.38), channel_id=1, source_target_pairs={{0,6},{2,4},{4,2},{6,0},{8,14},{10,12},{12,10},{14,8},{1,7},{3,5},... | collective-permute-start | bytes 442376 | tf_op jit(solution)/shard_map/ppermute | solution.py:198
  11.2 1.3 %dynamic-slice = u32[1]{0:T(128)} dynamic-slice(u32[32]{0:T(128)} %constant.14, u32[]{:T(128)S(6)} %add.4), dynamic_slice_sizes={1} | dynamic-slice | bytes 12
  13.1 0.0 collective-permute-done.rest_1_
  13.1 3.0 %collective-permute-start.6 = (bf16[2,8,4608]{2,1,0:T(8,128)(2,1)S(1)}, bf16[2,8,4608]{2,1,0:T(8,128)(2,1)S(1)}, u32[]{:S(2)}, u32[]{:S(2)}) collective-permute-start(bf16[2,8,4608]{2,1,0:T(8,128)(2,1)S(1)} %get-tuple-element.38), channel_id=1, source_target_pairs={{0,14},{2,12},{4,10},{6,8},{8,6},{10,4},{12,2},{14,0},{1,15},{3,13... | collective-permute-start | bytes 442376 | tf_op jit(solution)/shard_map/ppermute | solution.py:198
  16.1 0.0 collective-permute-done.1.rest_2_
  16.1 0.6 collective-permute-start.3
  16.8 0.8 %fusion = s32[64]{0:T(128)S(1)} fusion(s32[64]{0:T(128)S(1)} %broadcast.4, u32[]{:T(128)} %bitcast.3, s32[4,1]{0,1:T(1,128)} %param.13, s32[4]{0:T(128)} %param.12), kind=kLoop, calls=%fused_computation.9 | loop fusion | flops 8 | bytes 292
  17.5 20.6 %all-reduce.asked_ref = s32[64]{0:T(128)S(1)} all-reduce(s32[64]{0:T(128)S(1)} %fusion), channel_id=2, replica_groups=mesh['groups'=2,'adapter'=8,'tensor'=2] {'groups','adapter'}, use_global_device_ids=true, to_apply=%add | all-reduce | flops 64 | bytes 512
  38.1 0.0 collective-permute-done.2.rest_3_
  38.1 0.0 collective-permute-done.3.rest_4_
  38.1 0.0 collective-permute-done.4.rest_5_
  38.1 0.0 collective-permute-done.5.rest_6_
  38.1 0.0 collective-permute-done.6.rest_7_
  38.1 0.9 %shard_map.74 = (bf16[4,8,4608]{2,1,0:T(8,128)(2,1)S(1)}, bf16[4,8,4608]{2,1,0:T(8,128)(2,1)S(1)}, bf16[4,8,4608]{2,1,0:T(8,128)(2,1)S(1)}, bf16[4,8,4608]{2,1,0...) custom-call(s32[64]{0:T(128)S(1)} %all-reduce.asked_ref, ...), custom_call_target="tpu_custom_call" | custom-call | tf_op jit(solution)/shard_map/pallas_call | solution.py:75
  39.0 0.6 collective-permute-start.7
  39.6 1.5 %collective-permute-start.8 = (bf16[4,8,4608]{2,1,0:T(8,128)(2,1)S(1)}, bf16[4,8,4608]{2,1,0:T(8,128)(2,1)S(1)}, u32[]{:S(2)}, u32[]{:S(2)}) collective-permute-start(bf16[4,8,4608]{2,1,0:T(8,128)(2,1)S(1)} %get-tuple-element.41), channel_id=1, source_target_pairs={{0,2},{2,0},{4,6},{6,4},{8,10},{10,8},{12,14},{14,12},{16,18},{18,... | collective-permute-start | bytes 884744 | tf_op jit(solution)/shard_map/ppermute | solution.py:215
  41.1 0.0 collective-permute-start.9
  41.1 2.0 %collective-permute-start.11 = (bf16[4,8,4608]{2,1,0:T(8,128)(2,1)S(1)}, bf16[4,8,4608]{2,1,0:T(8,128)(2,1)S(1)}, u32[]{:S(2)}, u32[]{:S(2)}) collective-permute-start(bf16[4,8,4608]{2,1,0:T(8,128)(2,1)S(1)} %get-tuple-element.44), channel_id=1, source_target_pairs={{0,6},{2,4},{4,2},{6,0},{8,14},{10,12},{12,10},{14,8},{16,22},{18,... | collective-permute-start | bytes 884744 | tf_op jit(solution)/shard_map/ppermute | solution.py:215
  43.1 2.4 %collective-permute-start.12 = (bf16[4,8,4608]{2,1,0:T(8,128)(2,1)S(1)}, bf16[4,8,4608]{2,1,0:T(8,128)(2,1)S(1)}, u32[]{:S(2)}, u32[]{:S(2)}) collective-permute-start(bf16[4,8,4608]{2,1,0:T(8,128)(2,1)S(1)} %get-tuple-element.45), channel_id=1, source_target_pairs={{0,18},{2,16},{4,22},{6,20},{8,26},{10,24},{12,30},{14,28},{16,2},... | collective-permute-start | bytes 884744 | tf_op jit(solution)/shard_map/ppermute | solution.py:215
  45.5 2.6 %collective-permute-done.7 = bf16[4,8,4608]{2,1,0:T(8,128)(2,1)S(1)} collective-permute-done((bf16[4,8,4608]{2,1,0:T(8,128)(2,1)S(1)}, bf16[4,8,4608]{2,1,0:T(8,128)(2,1)S(1)}, u32[]{:S(2)}, u32[]{:S(2)}) %collective-permute-start.7) | collective-permute-done | bytes 294944 | tf_op jit(solution)/shard_map/ppermute | solution.py:215
  48.1 0.0 collective-permute-start.13
  48.1 0.0 copy-done.3
  48.1 1.9 %copy-done = bf16[4,96,4096]{2,1,0:T(8,128)(2,1)S(1)} copy-done((bf16[4,96,4096]{2,1,0:T(8,128)(2,1)S(1)}, bf16[4,96,4096]{2,1,0:T(8,128)(2,1)}, u32[]{:S(2)}) %copy-start) | copy-done | bytes 3145752
  50.0 4.7 %shard_map.75.send_ref = f32[384,640]{1,0:T(8,128)S(1)} custom-call(s32[1]{0:T(128)} %bitcast.4.half_ref, bf16[384,4096]{1,0:T(8,128)(2,1)S(1)} %bitcast.12, bf16[4096,1024]{1,0:T(8,128)(2,1)} %weight_ref.3, bf16[128,4096]{1,0:T(8,128)(2,1)S(1)} %bitcast.15), custom_call_target="tpu_custom_call" | custom-call | tf_op jit(solution)/shard_map/pallas_call | solution.py:111
  54.7 6.3 %collective-permute-done.8 = bf16[4,8,4608]{2,1,0:T(8,128)(2,1)S(1)} collective-permute-done((bf16[4,8,4608]{2,1,0:T(8,128)(2,1)S(1)}, bf16[4,8,4608]{2,1,0:T(8,128)(2,1)S(1)}, u32[]{:S(2)}, u32[]{:S(2)}) %collective-permute-start.8) | collective-permute-done | bytes 294944 | tf_op jit(solution)/shard_map/ppermute | solution.py:215
  61.0 0.0 collective-permute-start.14
  61.0 0.0 collective-permute-done.9
  61.0 0.0 collective-permute-start.10
  61.0 0.0 copy-done.1
  61.0 3.6 %shard_map.76.keep_ref = f32[384,512]{1,0:T(8,128)S(1)} custom-call(s32[1]{0:T(128)} %bitcast.7.half_ref, bf16[384,4096]{1,0:T(8,128)(2,1)S(1)} %bitcast.13, bf16[4096,1024]{1,0:T(8,128)(2,1)} %weight_ref.3), custom_call_target="tpu_custom_call" | custom-call | tf_op jit(solution)/shard_map/pallas_call | solution.py:111
  64.7 0.0 collective-permute-done.11
  64.8 0.0 collective-permute-done.12
  64.8 0.0 collective-permute-done.13
  64.8 4.7 %collective-permute-done.14 = bf16[4,8,4608]{2,1,0:T(8,128)(2,1)S(1)} collective-permute-done((bf16[4,8,4608]{2,1,0:T(8,128)(2,1)S(1)}, bf16[4,8,4608]{2,1,0:T(8,128)(2,1)S(1)}, u32[]{:S(2)}, u32[]{:S(2)}) %collective-permute-start.14) | collective-permute-done | bytes 294944 | tf_op jit(solution)/shard_map/ppermute | solution.py:215
  69.5 0.0 collective-permute-done.10.arrived_ref
  69.7 0.0 copy-start.5
  69.7 0.0 copy-start.6
  69.7 1.0 %shard_map.77.partial_ref = f32[384,64]{1,0:T(8,128)S(1)} custom-call(bf16[4,96,4096]{2,1,0:T(8,128)(2,1)S(1)} %copy-done.1, bf16[4,64,4608]{2,1,0:T(8,128)(2,1)S(1)} %constant_dynamic-update-slice_fusion.handed_ref.up_ref), custom_call_target="tpu_custom_call" | custom-call | tf_op jit(solution)/shard_map/pallas_call | solution.py:178
  70.7 0.1 collective-permute-start.15
  70.7 1.4 %collective-permute-done.15.other_ref = f32[384,64]{1,0:T(8,128)S(1)} collective-permute-done((f32[384,64]{1,0:T(8,128)S(1)}, f32[384,64]{1,0:T(8,128)S(1)}, u32[]{:S(2)}, u32[]{:S(2)}) %collective-permute-start.15) | collective-permute-done | bytes 98336 | tf_op jit(solution)/shard_map/ppermute | solution.py:233
  72.2 0.0 copy-done.5
  72.2 1.7 %shard_map.78 = bf16[4,96,512]{2,1,0:T(8,128)(2,1)} custom-call(s32[4,6]{1,0:T(4,128)S(1)} %copy-done.6, f32[384,512]{1,0:T(8,128)S(1)} %shard_map.76.keep_ref, f32[384,640]{1,0:T(8,128)S(1)} %shard_map.75.send_ref, f32[384,640]{1,0:T(8,128)S(1)} %collective-permute-done.10.arrived_ref, f32[384,64]{1,0:T(8,128)S(1)} %shard_map.77.partial_ref, ...), custom_call_target="tpu_custom_call" | custom-call | tf_op jit(solution)/shard_map/pallas_call | solution.py:156
  (16 shorter events, 0.2 us)
Async XLA Ops:
  0.0 1.2 %copy-start.2 = (bf16[2,64,4096]{2,1,0:T(8,128)(2,1)S(1)}, bf16[2,64,4096]{2,1,0:T(8,128)(2,1)}, u32[]{:S(2)}) copy-start(bf16[2,64,4096]{2,1,0:T(8,128)(2,1)} %param.9) | copy-start | bytes 3145732
  1.2 0.9 %copy-start.4 = (bf16[2,64,512]{2,1,0:T(8,128)(2,1)S(1)}, bf16[2,64,512]{2,1,0:T(8,128)(2,1)}, u32[]{:S(2)}) copy-start(bf16[2,64,512]{2,1,0:T(8,128)(2,1)} %param.10) | copy-start | bytes 393220
  2.1 46.0 %copy-start.3 = (bf16[2,64,4096]{2,1,0:T(8,128)(2,1)S(1)}, bf16[2,64,4096]{2,1,0:T(8,128)(2,1)}, u32[]{:S(2)}) copy-start(bf16[2,64,4096]{2,1,0:T(8,128)(2,1)} %param.9) | copy-start | bytes 3145732
  2.2 10.9 %collective-permute-start = (bf16[2,8,4608]{2,1,0:T(8,128)(2,1)S(1)}, bf16[2,8,4608]{2,1,0:T(8,128)(2,1)S(1)}, u32[]{:S(2)}, u32[]{:S(2)}) collective-permute-start(bf16[2,8,4608]{2,1,0:T(8,128)(2,1)S(1)} %get-tuple-element.32), channel_id=1, source_target_pairs={{0,2},{2,0},{4,6},{6,4},{8,10},{10,8},{12,14},{14,12},{1,3},{3,1},... | collective-permute-start | bytes 442376 | tf_op jit(solution)/shard_map/ppermute | solution.py:198
  5.2 10.9 %collective-permute-start.1 = (bf16[2,8,4608]{2,1,0:T(8,128)(2,1)S(1)}, bf16[2,8,4608]{2,1,0:T(8,128)(2,1)S(1)}, u32[]{:S(2)}, u32[]{:S(2)}) collective-permute-start(bf16[2,8,4608]{2,1,0:T(8,128)(2,1)S(1)} %get-tuple-element.33), channel_id=1, source_target_pairs={{0,4},{2,6},{4,0},{6,2},{8,12},{10,14},{12,8},{14,10},{1,5},{3,7},... | collective-permute-start | bytes 442376 | tf_op jit(solution)/shard_map/ppermute | solution.py:198
  6.8 31.3 %collective-permute-start.4 = (bf16[2,8,4608]{2,1,0:T(8,128)(2,1)S(1)}, bf16[2,8,4608]{2,1,0:T(8,128)(2,1)S(1)}, u32[]{:S(2)}, u32[]{:S(2)}) collective-permute-start(bf16[2,8,4608]{2,1,0:T(8,128)(2,1)S(1)} %get-tuple-element.32), channel_id=1, source_target_pairs={{0,10},{2,8},{4,14},{6,12},{8,2},{10,0},{12,6},{14,4},{1,11},{3,9}... | collective-permute-start | bytes 442376 | tf_op jit(solution)/shard_map/ppermute | solution.py:198
  9.3 28.8 %collective-permute-start.5 = (bf16[2,8,4608]{2,1,0:T(8,128)(2,1)S(1)}, bf16[2,8,4608]{2,1,0:T(8,128)(2,1)S(1)}, u32[]{:S(2)}, u32[]{:S(2)}) collective-permute-start(bf16[2,8,4608]{2,1,0:T(8,128)(2,1)S(1)} %get-tuple-element.33), channel_id=1, source_target_pairs={{0,12},{2,14},{4,8},{6,10},{8,4},{10,6},{12,0},{14,2},{1,13},{3,15... | collective-permute-start | bytes 442376 | tf_op jit(solution)/shard_map/ppermute | solution.py:198
  9.3 28.8 %collective-permute-start.2 = (bf16[2,8,4608]{2,1,0:T(8,128)(2,1)S(1)}, bf16[2,8,4608]{2,1,0:T(8,128)(2,1)S(1)}, u32[]{:S(2)}, u32[]{:S(2)}) collective-permute-start(bf16[2,8,4608]{2,1,0:T(8,128)(2,1)S(1)} %get-tuple-element.38), channel_id=1, source_target_pairs={{0,6},{2,4},{4,2},{6,0},{8,14},{10,12},{12,10},{14,8},{1,7},{3,5},... | collective-permute-start | bytes 442376 | tf_op jit(solution)/shard_map/ppermute | solution.py:198
  13.1 25.0 %collective-permute-start.6 = (bf16[2,8,4608]{2,1,0:T(8,128)(2,1)S(1)}, bf16[2,8,4608]{2,1,0:T(8,128)(2,1)S(1)}, u32[]{:S(2)}, u32[]{:S(2)}) collective-permute-start(bf16[2,8,4608]{2,1,0:T(8,128)(2,1)S(1)} %get-tuple-element.38), channel_id=1, source_target_pairs={{0,14},{2,12},{4,10},{6,8},{8,6},{10,4},{12,2},{14,0},{1,15},{3,13... | collective-permute-start | bytes 442376 | tf_op jit(solution)/shard_map/ppermute | solution.py:198
  16.1 22.0 %collective-permute-start.3 = (bf16[2,8,4608]{2,1,0:T(8,128)(2,1)S(1)}, bf16[2,8,4608]{2,1,0:T(8,128)(2,1)S(1)}, u32[]{:S(2)}, u32[]{:S(2)}) collective-permute-start(bf16[2,8,4608]{2,1,0:T(8,128)(2,1)S(1)} %get-tuple-element.35.rest_0_), channel_id=1, source_target_pairs={{0,8},{2,10},{4,12},{6,14},{8,0},{10,2},{12,4},{14,6},{1,9},{3,11}... | collective-permute-start | bytes 442376 | tf_op jit(solution)/shard_map/ppermute | solution.py:198
  39.0 9.1 %collective-permute-start.7 = (bf16[4,8,4608]{2,1,0:T(8,128)(2,1)S(1)}, bf16[4,8,4608]{2,1,0:T(8,128)(2,1)S(1)}, u32[]{:S(2)}, u32[]{:S(2)}) collective-permute-start(bf16[4,8,4608]{2,1,0:T(8,128)(2,1)S(1)} %get-tuple-element.39), channel_id=1, source_target_pairs={{0,16},{2,18},{4,20},{6,22},{8,24},{10,26},{12,28},{14,30},{16,0},... | collective-permute-start | bytes 884744 | tf_op jit(solution)/shard_map/ppermute | solution.py:215
  39.6 21.4 %collective-permute-start.8 = (bf16[4,8,4608]{2,1,0:T(8,128)(2,1)S(1)}, bf16[4,8,4608]{2,1,0:T(8,128)(2,1)S(1)}, u32[]{:S(2)}, u32[]{:S(2)}) collective-permute-start(bf16[4,8,4608]{2,1,0:T(8,128)(2,1)S(1)} %get-tuple-element.41), channel_id=1, source_target_pairs={{0,2},{2,0},{4,6},{6,4},{8,10},{10,8},{12,14},{14,12},{16,18},{18,... | collective-permute-start | bytes 884744 | tf_op jit(solution)/shard_map/ppermute | solution.py:215
  41.1 19.9 %collective-permute-start.9 = (bf16[4,8,4608]{2,1,0:T(8,128)(2,1)S(1)}, bf16[4,8,4608]{2,1,0:T(8,128)(2,1)S(1)}, u32[]{:S(2)}, u32[]{:S(2)}) collective-permute-start(bf16[4,8,4608]{2,1,0:T(8,128)(2,1)S(1)} %get-tuple-element.42), channel_id=1, source_target_pairs={{0,4},{2,6},{4,0},{6,2},{8,12},{10,14},{12,8},{14,10},{16,20},{18,... | collective-permute-start | bytes 884744 | tf_op jit(solution)/shard_map/ppermute | solution.py:215
  41.1 23.7 %collective-permute-start.11 = (bf16[4,8,4608]{2,1,0:T(8,128)(2,1)S(1)}, bf16[4,8,4608]{2,1,0:T(8,128)(2,1)S(1)}, u32[]{:S(2)}, u32[]{:S(2)}) collective-permute-start(bf16[4,8,4608]{2,1,0:T(8,128)(2,1)S(1)} %get-tuple-element.44), channel_id=1, source_target_pairs={{0,6},{2,4},{4,2},{6,0},{8,14},{10,12},{12,10},{14,8},{16,22},{18,... | collective-permute-start | bytes 884744 | tf_op jit(solution)/shard_map/ppermute | solution.py:215
  43.1 21.7 %collective-permute-start.12 = (bf16[4,8,4608]{2,1,0:T(8,128)(2,1)S(1)}, bf16[4,8,4608]{2,1,0:T(8,128)(2,1)S(1)}, u32[]{:S(2)}, u32[]{:S(2)}) collective-permute-start(bf16[4,8,4608]{2,1,0:T(8,128)(2,1)S(1)} %get-tuple-element.45), channel_id=1, source_target_pairs={{0,18},{2,16},{4,22},{6,20},{8,26},{10,24},{12,30},{14,28},{16,2},... | collective-permute-start | bytes 884744 | tf_op jit(solution)/shard_map/ppermute | solution.py:215
  48.1 16.7 %collective-permute-start.13 = (bf16[4,8,4608]{2,1,0:T(8,128)(2,1)S(1)}, bf16[4,8,4608]{2,1,0:T(8,128)(2,1)S(1)}, u32[]{:S(2)}, u32[]{:S(2)}) collective-permute-start(bf16[4,8,4608]{2,1,0:T(8,128)(2,1)S(1)} %get-tuple-element.46), channel_id=1, source_target_pairs={{0,20},{2,22},{4,16},{6,18},{8,28},{10,30},{12,24},{14,26},{16,4},... | collective-permute-start | bytes 884744 | tf_op jit(solution)/shard_map/ppermute | solution.py:215
  48.1 1.9 %copy-start = (bf16[4,96,4096]{2,1,0:T(8,128)(2,1)S(1)}, bf16[4,96,4096]{2,1,0:T(8,128)(2,1)}, u32[]{:S(2)}) copy-start(bf16[4,96,4096]{2,1,0:T(8,128)(2,1)} %acts_ref.1) | copy-start | bytes 9437188
  50.0 11.0 %copy-start.1 = (bf16[4,96,4096]{2,1,0:T(8,128)(2,1)S(1)}, bf16[4,96,4096]{2,1,0:T(8,128)(2,1)}, u32[]{:S(2)}) copy-start(bf16[4,96,4096]{2,1,0:T(8,128)(2,1)} %acts_ref.1) | copy-start | bytes 9437188
  61.0 8.5 %collective-permute-start.14 = (bf16[4,8,4608]{2,1,0:T(8,128)(2,1)S(1)}, bf16[4,8,4608]{2,1,0:T(8,128)(2,1)S(1)}, u32[]{:S(2)}, u32[]{:S(2)}) collective-permute-start(bf16[4,8,4608]{2,1,0:T(8,128)(2,1)S(1)} %get-tuple-element.47), channel_id=1, source_target_pairs={{0,22},{2,20},{4,18},{6,16},{8,30},{10,28},{12,26},{14,24},{16,6},... | collective-permute-start | bytes 884744 | tf_op jit(solution)/shard_map/ppermute | solution.py:215
  61.0 8.5 %collective-permute-start.10 = (f32[384,640]{1,0:T(8,128)S(1)}, f32[384,640]{1,0:T(8,128)S(1)}, u32[]{:S(2)}, u32[]{:S(2)}) collective-permute-start(f32[384,640]{1,0:T(8,128)S(1)} %shard_map.75.send_ref), channel_id=1, source_target_pairs={{0,1},{1,0},{2,3},{3,2},{4,5},{5,4},{6,7},{7,6},{8,9},{9,8},{10,11... | collective-permute-start | bytes 2949128 | tf_op jit(solution)/shard_map/ppermute | solution.py:222
  69.7 2.5 %copy-start.5 = (bf16[2,64,512]{2,1,0:T(8,128)(2,1)S(1)}, bf16[2,64,512]{2,1,0:T(8,128)(2,1)}, u32[]{:S(2)}) copy-start(bf16[2,64,512]{2,1,0:T(8,128)(2,1)} %param.10) | copy-start | bytes 393220
  69.7 2.5 %copy-start.6 = (s32[4,6]{1,0:T(4,128)S(1)}, s32[4,6]{1,0:T(4,128)}, u32[]{:S(2)}) copy-start(s32[4,6]{1,0:T(4,128)} %slots_ref.1) | copy-start | bytes 292
  70.7 1.5 %collective-permute-start.15 = (f32[384,64]{1,0:T(8,128)S(1)}, f32[384,64]{1,0:T(8,128)S(1)}, u32[]{:S(2)}, u32[]{:S(2)}) collective-permute-start(f32[384,64]{1,0:T(8,128)S(1)} %shard_map.77.partial_ref), channel_id=1, source_target_pairs={{0,1},{1,0},{2,3},{3,2},{4,5},{5,4},{6,7},{7,6},{8,9},{9,8},{10,11... | collective-permute-start | bytes 294920 | tf_op jit(solution)/shard_map/ppermute | solution.py:233

commit v7 on v6

--- a/solution.py
+++ b/solution.py
@@ -196,7 +196,7 @@
     banked = {0: stripes[0]}
     for k in [1, 2, 3, 4, 5, 6, 7, *range(STRIPES, servers)]:
         banked[k] = lax.ppermute(stripes[k % parts], "adapter", [(i, i ^ k) for i in range(servers)])
-    early = [1, 2]
+    early = [5]
     transfer_slot, *arrived = lax.optimization_barrier((transfer_slot, *[banked[k] for k in early]))
     banked.update(zip(early, arrived))
     banked = [banked[k] for k in range(servers)]

time: 74.1 us -> 71.9 us (0.970)
  blocking collectives: 20.6 us -> 14.8 us
  starting transfers between devices: 19.2 us -> 21.7 us
  waiting for transfers between devices: 15 us -> 16.1 us
    unnamed x1, blocking collectives: 20.6 us -> 14.8 us
    ppermute x7, waiting for transfers between devices: 0.02 us -> 2.85 us  [body(): lax.ppermute(stripes[k % parts], 'adapter', [(i, i ^ k) for i in range(se...]
    ppermute x7, waiting for transfers between devices: 13.6 us -> 11.9 us  [body(): given[k] = lax.ppermute(picked[k], ('groups', 'adapter'), pairs)]
    ppermute x7, starting transfers between devices: 12.6 us -> 14 us  [body(): lax.ppermute(stripes[k % parts], 'adapter', [(i, i ^ k) for i in range(se...]
    ppermute x7, starting transfers between devices: 6.49 us -> 7.6 us  [body(): given[k] = lax.ppermute(picked[k], ('groups', 'adapter'), pairs)]
  transfers between devices with their start and end apart: 16 -> 16, of which waited for: 4 -> 5; matrix products, arithmetic and copies ran while one was open for 3% -> 3% of each run, Pallas kernels for 11% -> 12%
where the time goes in v7:
time: 71.9 us; the launch traced here: 71.6 us
  starting transfers between devices  21.7 us (30%)
  waiting for transfers between devices  16.1 us (22%)
  blocking collectives  14.8 us (21%)
  Pallas kernels  12 us (17%)
  local copies, waits for them, and re-layouts  5.51 us (8%)
  between operations  0.81 us (1%)
  other arithmetic  0.77 us (1%)
    unnamed x1, blocking collectives  14.8 us
    ppermute x7, starting transfers between devices, body(): lax.ppermute(stripes[k % parts], 'adapter', [(i, i ^ k) for i in range(se...  14 us
    ppermute x7, waiting for transfers between devices, body(): given[k] = lax.ppermute(picked[k], ('groups', 'adapter'), pairs)  11.9 us
    pallas_call x2, Pallas kernels, product(): pl.pallas_call(product_kernel, out_shape=out, grid_spec=pltpu.PrefetchSca...  8.39 us
    ppermute x7, starting transfers between devices, body(): given[k] = lax.ppermute(picked[k], ('groups', 'adapter'), pairs)  7.6 us
    unnamed x23, local copies, waits for them, and re-layouts  5.49 us
    ppermute x7, waiting for transfers between devices, body(): lax.ppermute(stripes[k % parts], 'adapter', [(i, i ^ k) for i in range(se...  2.85 us
    pallas_call x1, Pallas kernels, finish(): pl.pallas_call(final_kernel, out_shape=jax.ShapeDtypeStruct((steps, rows...  1.69 us
  transfers between devices with their start and end apart: 16, of which 5 were waited for; matrix products, arithmetic and copies ran while one was open for 3% of the time, Pallas kernels for 12%

profile of v7, /device:TPU:0, one launch (start us, length us, event | category | flops | bytes accessed | tf_op | source)
XLA Modules:
  0.0 71.6 jit_solution(1388622554849880752)
XLA Ops:
  0.0 1.2 %copy-done.2 = bf16[2,64,4096]{2,1,0:T(8,128)(2,1)S(1)} copy-done((bf16[2,64,4096]{2,1,0:T(8,128)(2,1)S(1)}, bf16[2,64,4096]{2,1,0:T(8,128)(2,1)}, u32[]{:S(2)}) %copy-start.2) | copy-done | bytes 1048600
  1.2 0.9 %copy-done.4 = bf16[2,64,512]{2,1,0:T(8,128)(2,1)S(1)} copy-done((bf16[2,64,512]{2,1,0:T(8,128)(2,1)S(1)}, bf16[2,64,512]{2,1,0:T(8,128)(2,1)}, u32[]{:S(2)}) %copy-start.4) | copy-done | bytes 131096
  2.2 5.1 %collective-permute-start = (bf16[2,8,4608]{2,1,0:T(8,128)(2,1)S(1)}, bf16[2,8,4608]{2,1,0:T(8,128)(2,1)S(1)}, u32[]{:S(2)}, u32[]{:S(2)}) collective-permute-start(bf16[2,8,4608]{2,1,0:T(8,128)(2,1)S(1)} %get-tuple-element.31), channel_id=1, source_target_pairs={{0,10},{2,8},{4,14},{6,12},{8,2},{10,0},{12,6},{14,4},{1,11},{3,9}... | collective-permute-start | bytes 442376 | tf_op jit(solution)/shard_map/ppermute | solution.py:198
  7.2 0.5 collective-permute-start.1
  7.7 1.6 %collective-permute-start.2 = (bf16[2,8,4608]{2,1,0:T(8,128)(2,1)S(1)}, bf16[2,8,4608]{2,1,0:T(8,128)(2,1)S(1)}, u32[]{:S(2)}, u32[]{:S(2)}) collective-permute-start(bf16[2,8,4608]{2,1,0:T(8,128)(2,1)S(1)} %get-tuple-element.34), channel_id=1, source_target_pairs={{0,4},{2,6},{4,0},{6,2},{8,12},{10,14},{12,8},{14,10},{1,5},{3,7},... | collective-permute-start | bytes 442376 | tf_op jit(solution)/shard_map/ppermute | solution.py:198
  9.3 0.0 collective-permute-start.5
  9.3 1.8 %collective-permute-start.3 = (bf16[2,8,4608]{2,1,0:T(8,128)(2,1)S(1)}, bf16[2,8,4608]{2,1,0:T(8,128)(2,1)S(1)}, u32[]{:S(2)}, u32[]{:S(2)}) collective-permute-start(bf16[2,8,4608]{2,1,0:T(8,128)(2,1)S(1)} %get-tuple-element.35), channel_id=1, source_target_pairs={{0,6},{2,4},{4,2},{6,0},{8,14},{10,12},{12,10},{14,8},{1,7},{3,5},... | collective-permute-start | bytes 442376 | tf_op jit(solution)/shard_map/ppermute | solution.py:198
  11.2 1.3 %dynamic-slice = u32[1]{0:T(128)} dynamic-slice(u32[32]{0:T(128)} %constant.14, u32[]{:T(128)S(6)} %add.4), dynamic_slice_sizes={1} | dynamic-slice | bytes 12
  13.1 2.8 %collective-permute-done.rest_5_ = bf16[2,8,4608]{2,1,0:T(8,128)(2,1)S(1)} collective-permute-done((bf16[2,8,4608]{2,1,0:T(8,128)(2,1)S(1)}, bf16[2,8,4608]{2,1,0:T(8,128)(2,1)S(1)}, u32[]{:S(2)}, u32[]{:S(2)}) %collective-permute-start) | collective-permute-done | bytes 147488 | tf_op jit(solution)/shard_map/ppermute | solution.py:198
  15.9 5.0 %collective-permute-start.6 = (bf16[2,8,4608]{2,1,0:T(8,128)(2,1)S(1)}, bf16[2,8,4608]{2,1,0:T(8,128)(2,1)S(1)}, u32[]{:S(2)}, u32[]{:S(2)}) collective-permute-start(bf16[2,8,4608]{2,1,0:T(8,128)(2,1)S(1)} %get-tuple-element.35), channel_id=1, source_target_pairs={{0,14},{2,12},{4,10},{6,8},{8,6},{10,4},{12,2},{14,0},{1,15},{3,13... | collective-permute-start | bytes 442376 | tf_op jit(solution)/shard_map/ppermute | solution.py:198
  20.9 0.0 collective-permute-done.1.rest_1_
  20.9 0.0 collective-permute-start.4
  20.9 0.8 %fusion = s32[64]{0:T(128)S(1)} fusion(s32[64]{0:T(128)S(1)} %broadcast.4, u32[]{:T(128)} %bitcast.3, s32[4,1]{0,1:T(1,128)} %param.13, s32[4]{0:T(128)} %param.12), kind=kLoop, calls=%fused_computation.9 | loop fusion | flops 8 | bytes 292
  21.7 14.8 %all-reduce.asked_ref = s32[64]{0:T(128)S(1)} all-reduce(s32[64]{0:T(128)S(1)} %fusion), channel_id=2, replica_groups=mesh['groups'=2,'adapter'=8,'tensor'=2] {'groups','adapter'}, use_global_device_ids=true, to_apply=%add | all-reduce | flops 64 | bytes 512
  36.5 0.0 collective-permute-done.2.rest_2_
  36.5 0.0 collective-permute-done.3.rest_3_
  36.5 0.0 collective-permute-done.4.rest_4_
  36.5 0.0 collective-permute-done.5.rest_6_
  36.5 0.0 collective-permute-done.6.rest_7_
  36.5 0.9 %shard_map.74 = (bf16[4,8,4608]{2,1,0:T(8,128)(2,1)S(1)}, bf16[4,8,4608]{2,1,0:T(8,128)(2,1)S(1)}, bf16[4,8,4608]{2,1,0:T(8,128)(2,1)S(1)}, bf16[4,8,4608]{2,1,0...) custom-call(s32[64]{0:T(128)S(1)} %all-reduce.asked_ref, ...), custom_call_target="tpu_custom_call" | custom-call | tf_op jit(solution)/shard_map/pallas_call | solution.py:75
  37.4 0.6 collective-permute-start.7
  38.0 0.6 collective-permute-start.8
  38.6 0.3 collective-permute-start.9
  38.8 2.7 %collective-permute-start.11 = (bf16[4,8,4608]{2,1,0:T(8,128)(2,1)S(1)}, bf16[4,8,4608]{2,1,0:T(8,128)(2,1)S(1)}, u32[]{:S(2)}, u32[]{:S(2)}) collective-permute-start(bf16[4,8,4608]{2,1,0:T(8,128)(2,1)S(1)} %get-tuple-element.42), channel_id=1, source_target_pairs={{0,6},{2,4},{4,2},{6,0},{8,14},{10,12},{12,10},{14,8},{16,22},{18,... | collective-permute-start | bytes 884744 | tf_op jit(solution)/shard_map/ppermute | solution.py:215
  41.5 1.5 %collective-permute-start.12 = (bf16[4,8,4608]{2,1,0:T(8,128)(2,1)S(1)}, bf16[4,8,4608]{2,1,0:T(8,128)(2,1)S(1)}, u32[]{:S(2)}, u32[]{:S(2)}) collective-permute-start(bf16[4,8,4608]{2,1,0:T(8,128)(2,1)S(1)} %get-tuple-element.43), channel_id=1, source_target_pairs={{0,18},{2,16},{4,22},{6,20},{8,26},{10,24},{12,30},{14,28},{16,2},... | collective-permute-start | bytes 884744 | tf_op jit(solution)/shard_map/ppermute | solution.py:215
  43.0 4.4 %collective-permute-done.7 = bf16[4,8,4608]{2,1,0:T(8,128)(2,1)S(1)} collective-permute-done((bf16[4,8,4608]{2,1,0:T(8,128)(2,1)S(1)}, bf16[4,8,4608]{2,1,0:T(8,128)(2,1)S(1)}, u32[]{:S(2)}, u32[]{:S(2)}) %collective-permute-start.7) | collective-permute-done | bytes 294944 | tf_op jit(solution)/shard_map/ppermute | solution.py:215
  47.4 0.4 collective-permute-start.13
  47.8 0.0 copy-done.3
  47.8 1.9 %copy-done = bf16[4,96,4096]{2,1,0:T(8,128)(2,1)S(1)} copy-done((bf16[4,96,4096]{2,1,0:T(8,128)(2,1)S(1)}, bf16[4,96,4096]{2,1,0:T(8,128)(2,1)}, u32[]{:S(2)}) %copy-start) | copy-done | bytes 3145752
  49.7 4.7 %shard_map.75.send_ref = f32[384,640]{1,0:T(8,128)S(1)} custom-call(s32[1]{0:T(128)} %bitcast.4.half_ref, bf16[384,4096]{1,0:T(8,128)(2,1)S(1)} %bitcast.12, bf16[4096,1024]{1,0:T(8,128)(2,1)} %weight_ref.3, bf16[128,4096]{1,0:T(8,128)(2,1)S(1)} %bitcast.15), custom_call_target="tpu_custom_call" | custom-call | tf_op jit(solution)/shard_map/pallas_call | solution.py:111
  54.4 4.3 %collective-permute-done.8 = bf16[4,8,4608]{2,1,0:T(8,128)(2,1)S(1)} collective-permute-done((bf16[4,8,4608]{2,1,0:T(8,128)(2,1)S(1)}, bf16[4,8,4608]{2,1,0:T(8,128)(2,1)S(1)}, u32[]{:S(2)}, u32[]{:S(2)}) %collective-permute-start.8) | collective-permute-done | bytes 294944 | tf_op jit(solution)/shard_map/ppermute | solution.py:215
  58.8 1.7 %collective-permute-start.14 = (bf16[4,8,4608]{2,1,0:T(8,128)(2,1)S(1)}, bf16[4,8,4608]{2,1,0:T(8,128)(2,1)S(1)}, u32[]{:S(2)}, u32[]{:S(2)}) collective-permute-start(bf16[4,8,4608]{2,1,0:T(8,128)(2,1)S(1)} %get-tuple-element.45), channel_id=1, source_target_pairs={{0,22},{2,20},{4,18},{6,16},{8,30},{10,28},{12,26},{14,24},{16,6},... | collective-permute-start | bytes 884744 | tf_op jit(solution)/shard_map/ppermute | solution.py:215
  60.4 0.0 collective-permute-done.9
  60.4 0.0 collective-permute-start.10
  60.4 0.0 copy-done.1
  60.4 3.6 %shard_map.76.keep_ref = f32[384,512]{1,0:T(8,128)S(1)} custom-call(s32[1]{0:T(128)} %bitcast.7.half_ref, bf16[384,4096]{1,0:T(8,128)(2,1)S(1)} %bitcast.13, bf16[4096,1024]{1,0:T(8,128)(2,1)} %weight_ref.3), custom_call_target="tpu_custom_call" | custom-call | tf_op jit(solution)/shard_map/pallas_call | solution.py:111
  64.2 0.0 collective-permute-done.11
  64.2 0.0 collective-permute-done.12
  64.2 0.0 collective-permute-done.13
  64.2 3.1 %collective-permute-done.14 = bf16[4,8,4608]{2,1,0:T(8,128)(2,1)S(1)} collective-permute-done((bf16[4,8,4608]{2,1,0:T(8,128)(2,1)S(1)}, bf16[4,8,4608]{2,1,0:T(8,128)(2,1)S(1)}, u32[]{:S(2)}, u32[]{:S(2)}) %collective-permute-start.14) | collective-permute-done | bytes 294944 | tf_op jit(solution)/shard_map/ppermute | solution.py:215
  67.3 0.0 collective-permute-done.10.arrived_ref
  67.4 0.0 copy-start.5
  67.4 0.0 copy-start.6
  67.4 1.0 %shard_map.77.partial_ref = f32[384,64]{1,0:T(8,128)S(1)} custom-call(bf16[4,96,4096]{2,1,0:T(8,128)(2,1)S(1)} %copy-done.1, bf16[4,64,4608]{2,1,0:T(8,128)(2,1)S(1)} %constant_dynamic-update-slice_fusion.handed_ref.up_ref), custom_call_target="tpu_custom_call" | custom-call | tf_op jit(solution)/shard_map/pallas_call | solution.py:178
  68.4 0.1 collective-permute-start.15
  68.5 1.4 %collective-permute-done.15.other_ref = f32[384,64]{1,0:T(8,128)S(1)} collective-permute-done((f32[384,64]{1,0:T(8,128)S(1)}, f32[384,64]{1,0:T(8,128)S(1)}, u32[]{:S(2)}, u32[]{:S(2)}) %collective-permute-start.15) | collective-permute-done | bytes 98336 | tf_op jit(solution)/shard_map/ppermute | solution.py:233
  69.9 0.0 copy-done.5
  69.9 1.7 %shard_map.78 = bf16[4,96,512]{2,1,0:T(8,128)(2,1)} custom-call(s32[4,6]{1,0:T(4,128)S(1)} %copy-done.6, f32[384,512]{1,0:T(8,128)S(1)} %shard_map.76.keep_ref, f32[384,640]{1,0:T(8,128)S(1)} %shard_map.75.send_ref, f32[384,640]{1,0:T(8,128)S(1)} %collective-permute-done.10.arrived_ref, f32[384,64]{1,0:T(8,128)S(1)} %shard_map.77.partial_ref, ...), custom_call_target="tpu_custom_call" | custom-call | tf_op jit(solution)/shard_map/pallas_call | solution.py:156
  (16 shorter events, 0.2 us)
Async XLA Ops:
  0.0 1.2 %copy-start.2 = (bf16[2,64,4096]{2,1,0:T(8,128)(2,1)S(1)}, bf16[2,64,4096]{2,1,0:T(8,128)(2,1)}, u32[]{:S(2)}) copy-start(bf16[2,64,4096]{2,1,0:T(8,128)(2,1)} %param.9) | copy-start | bytes 3145732
  1.2 0.9 %copy-start.4 = (bf16[2,64,512]{2,1,0:T(8,128)(2,1)S(1)}, bf16[2,64,512]{2,1,0:T(8,128)(2,1)}, u32[]{:S(2)}) copy-start(bf16[2,64,512]{2,1,0:T(8,128)(2,1)} %param.10) | copy-start | bytes 393220
  2.1 45.6 %copy-start.3 = (bf16[2,64,4096]{2,1,0:T(8,128)(2,1)S(1)}, bf16[2,64,4096]{2,1,0:T(8,128)(2,1)}, u32[]{:S(2)}) copy-start(bf16[2,64,4096]{2,1,0:T(8,128)(2,1)} %param.9) | copy-start | bytes 3145732
  2.2 13.8 %collective-permute-start = (bf16[2,8,4608]{2,1,0:T(8,128)(2,1)S(1)}, bf16[2,8,4608]{2,1,0:T(8,128)(2,1)S(1)}, u32[]{:S(2)}, u32[]{:S(2)}) collective-permute-start(bf16[2,8,4608]{2,1,0:T(8,128)(2,1)S(1)} %get-tuple-element.31), channel_id=1, source_target_pairs={{0,10},{2,8},{4,14},{6,12},{8,2},{10,0},{12,6},{14,4},{1,11},{3,9}... | collective-permute-start | bytes 442376 | tf_op jit(solution)/shard_map/ppermute | solution.py:198
  7.2 13.7 %collective-permute-start.1 = (bf16[2,8,4608]{2,1,0:T(8,128)(2,1)S(1)}, bf16[2,8,4608]{2,1,0:T(8,128)(2,1)S(1)}, u32[]{:S(2)}, u32[]{:S(2)}) collective-permute-start(bf16[2,8,4608]{2,1,0:T(8,128)(2,1)S(1)} %get-tuple-element.31), channel_id=1, source_target_pairs={{0,2},{2,0},{4,6},{6,4},{8,10},{10,8},{12,14},{14,12},{1,3},{3,1},... | collective-permute-start | bytes 442376 | tf_op jit(solution)/shard_map/ppermute | solution.py:198
  7.7 28.7 %collective-permute-start.2 = (bf16[2,8,4608]{2,1,0:T(8,128)(2,1)S(1)}, bf16[2,8,4608]{2,1,0:T(8,128)(2,1)S(1)}, u32[]{:S(2)}, u32[]{:S(2)}) collective-permute-start(bf16[2,8,4608]{2,1,0:T(8,128)(2,1)S(1)} %get-tuple-element.34), channel_id=1, source_target_pairs={{0,4},{2,6},{4,0},{6,2},{8,12},{10,14},{12,8},{14,10},{1,5},{3,7},... | collective-permute-start | bytes 442376 | tf_op jit(solution)/shard_map/ppermute | solution.py:198
  9.3 27.2 %collective-permute-start.5 = (bf16[2,8,4608]{2,1,0:T(8,128)(2,1)S(1)}, bf16[2,8,4608]{2,1,0:T(8,128)(2,1)S(1)}, u32[]{:S(2)}, u32[]{:S(2)}) collective-permute-start(bf16[2,8,4608]{2,1,0:T(8,128)(2,1)S(1)} %get-tuple-element.34), channel_id=1, source_target_pairs={{0,12},{2,14},{4,8},{6,10},{8,4},{10,6},{12,0},{14,2},{1,13},{3,15... | collective-permute-start | bytes 442376 | tf_op jit(solution)/shard_map/ppermute | solution.py:198
  9.3 27.1 %collective-permute-start.3 = (bf16[2,8,4608]{2,1,0:T(8,128)(2,1)S(1)}, bf16[2,8,4608]{2,1,0:T(8,128)(2,1)S(1)}, u32[]{:S(2)}, u32[]{:S(2)}) collective-permute-start(bf16[2,8,4608]{2,1,0:T(8,128)(2,1)S(1)} %get-tuple-element.35), channel_id=1, source_target_pairs={{0,6},{2,4},{4,2},{6,0},{8,14},{10,12},{12,10},{14,8},{1,7},{3,5},... | collective-permute-start | bytes 442376 | tf_op jit(solution)/shard_map/ppermute | solution.py:198
  15.9 20.6 %collective-permute-start.6 = (bf16[2,8,4608]{2,1,0:T(8,128)(2,1)S(1)}, bf16[2,8,4608]{2,1,0:T(8,128)(2,1)S(1)}, u32[]{:S(2)}, u32[]{:S(2)}) collective-permute-start(bf16[2,8,4608]{2,1,0:T(8,128)(2,1)S(1)} %get-tuple-element.35), channel_id=1, source_target_pairs={{0,14},{2,12},{4,10},{6,8},{8,6},{10,4},{12,2},{14,0},{1,15},{3,13... | collective-permute-start | bytes 442376 | tf_op jit(solution)/shard_map/ppermute | solution.py:198
  20.9 15.6 %collective-permute-start.4 = (bf16[2,8,4608]{2,1,0:T(8,128)(2,1)S(1)}, bf16[2,8,4608]{2,1,0:T(8,128)(2,1)S(1)}, u32[]{:S(2)}, u32[]{:S(2)}) collective-permute-start(bf16[2,8,4608]{2,1,0:T(8,128)(2,1)S(1)} %get-tuple-element.33.rest_0_), channel_id=1, source_target_pairs={{0,8},{2,10},{4,12},{6,14},{8,0},{10,2},{12,4},{14,6},{1,9},{3,11}... | collective-permute-start | bytes 442376 | tf_op jit(solution)/shard_map/ppermute | solution.py:198
  37.4 10.0 %collective-permute-start.7 = (bf16[4,8,4608]{2,1,0:T(8,128)(2,1)S(1)}, bf16[4,8,4608]{2,1,0:T(8,128)(2,1)S(1)}, u32[]{:S(2)}, u32[]{:S(2)}) collective-permute-start(bf16[4,8,4608]{2,1,0:T(8,128)(2,1)S(1)} %get-tuple-element.37), channel_id=1, source_target_pairs={{0,16},{2,18},{4,20},{6,22},{8,24},{10,26},{12,28},{14,30},{16,0},... | collective-permute-start | bytes 884744 | tf_op jit(solution)/shard_map/ppermute | solution.py:215
  38.0 20.8 %collective-permute-start.8 = (bf16[4,8,4608]{2,1,0:T(8,128)(2,1)S(1)}, bf16[4,8,4608]{2,1,0:T(8,128)(2,1)S(1)}, u32[]{:S(2)}, u32[]{:S(2)}) collective-permute-start(bf16[4,8,4608]{2,1,0:T(8,128)(2,1)S(1)} %get-tuple-element.39), channel_id=1, source_target_pairs={{0,2},{2,0},{4,6},{6,4},{8,10},{10,8},{12,14},{14,12},{16,18},{18,... | collective-permute-start | bytes 884744 | tf_op jit(solution)/shard_map/ppermute | solution.py:215
  38.6 21.9 %collective-permute-start.9 = (bf16[4,8,4608]{2,1,0:T(8,128)(2,1)S(1)}, bf16[4,8,4608]{2,1,0:T(8,128)(2,1)S(1)}, u32[]{:S(2)}, u32[]{:S(2)}) collective-permute-start(bf16[4,8,4608]{2,1,0:T(8,128)(2,1)S(1)} %get-tuple-element.40), channel_id=1, source_target_pairs={{0,4},{2,6},{4,0},{6,2},{8,12},{10,14},{12,8},{14,10},{16,20},{18,... | collective-permute-start | bytes 884744 | tf_op jit(solution)/shard_map/ppermute | solution.py:215
  38.8 25.3 %collective-permute-start.11 = (bf16[4,8,4608]{2,1,0:T(8,128)(2,1)S(1)}, bf16[4,8,4608]{2,1,0:T(8,128)(2,1)S(1)}, u32[]{:S(2)}, u32[]{:S(2)}) collective-permute-start(bf16[4,8,4608]{2,1,0:T(8,128)(2,1)S(1)} %get-tuple-element.42), channel_id=1, source_target_pairs={{0,6},{2,4},{4,2},{6,0},{8,14},{10,12},{12,10},{14,8},{16,22},{18,... | collective-permute-start | bytes 884744 | tf_op jit(solution)/shard_map/ppermute | solution.py:215
  41.5 22.7 %collective-permute-start.12 = (bf16[4,8,4608]{2,1,0:T(8,128)(2,1)S(1)}, bf16[4,8,4608]{2,1,0:T(8,128)(2,1)S(1)}, u32[]{:S(2)}, u32[]{:S(2)}) collective-permute-start(bf16[4,8,4608]{2,1,0:T(8,128)(2,1)S(1)} %get-tuple-element.43), channel_id=1, source_target_pairs={{0,18},{2,16},{4,22},{6,20},{8,26},{10,24},{12,30},{14,28},{16,2},... | collective-permute-start | bytes 884744 | tf_op jit(solution)/shard_map/ppermute | solution.py:215
  47.4 16.8 %collective-permute-start.13 = (bf16[4,8,4608]{2,1,0:T(8,128)(2,1)S(1)}, bf16[4,8,4608]{2,1,0:T(8,128)(2,1)S(1)}, u32[]{:S(2)}, u32[]{:S(2)}) collective-permute-start(bf16[4,8,4608]{2,1,0:T(8,128)(2,1)S(1)} %get-tuple-element.44), channel_id=1, source_target_pairs={{0,20},{2,22},{4,16},{6,18},{8,28},{10,30},{12,24},{14,26},{16,4},... | collective-permute-start | bytes 884744 | tf_op jit(solution)/shard_map/ppermute | solution.py:215
  47.8 1.9 %copy-start = (bf16[4,96,4096]{2,1,0:T(8,128)(2,1)S(1)}, bf16[4,96,4096]{2,1,0:T(8,128)(2,1)}, u32[]{:S(2)}) copy-start(bf16[4,96,4096]{2,1,0:T(8,128)(2,1)} %acts_ref.1) | copy-start | bytes 9437188
  49.7 10.8 %copy-start.1 = (bf16[4,96,4096]{2,1,0:T(8,128)(2,1)S(1)}, bf16[4,96,4096]{2,1,0:T(8,128)(2,1)}, u32[]{:S(2)}) copy-start(bf16[4,96,4096]{2,1,0:T(8,128)(2,1)} %acts_ref.1) | copy-start | bytes 9437188
  58.8 8.5 %collective-permute-start.14 = (bf16[4,8,4608]{2,1,0:T(8,128)(2,1)S(1)}, bf16[4,8,4608]{2,1,0:T(8,128)(2,1)S(1)}, u32[]{:S(2)}, u32[]{:S(2)}) collective-permute-start(bf16[4,8,4608]{2,1,0:T(8,128)(2,1)S(1)} %get-tuple-element.45), channel_id=1, source_target_pairs={{0,22},{2,20},{4,18},{6,16},{8,30},{10,28},{12,26},{14,24},{16,6},... | collective-permute-start | bytes 884744 | tf_op jit(solution)/shard_map/ppermute | solution.py:215
  60.4 6.9 %collective-permute-start.10 = (f32[384,640]{1,0:T(8,128)S(1)}, f32[384,640]{1,0:T(8,128)S(1)}, u32[]{:S(2)}, u32[]{:S(2)}) collective-permute-start(f32[384,640]{1,0:T(8,128)S(1)} %shard_map.75.send_ref), channel_id=1, source_target_pairs={{0,1},{1,0},{2,3},{3,2},{4,5},{5,4},{6,7},{7,6},{8,9},{9,8},{10,11... | collective-permute-start | bytes 2949128 | tf_op jit(solution)/shard_map/ppermute | solution.py:222
  67.4 2.5 %copy-start.5 = (bf16[2,64,512]{2,1,0:T(8,128)(2,1)S(1)}, bf16[2,64,512]{2,1,0:T(8,128)(2,1)}, u32[]{:S(2)}) copy-start(bf16[2,64,512]{2,1,0:T(8,128)(2,1)} %param.10) | copy-start | bytes 393220
  67.4 2.5 %copy-start.6 = (s32[4,6]{1,0:T(4,128)S(1)}, s32[4,6]{1,0:T(4,128)}, u32[]{:S(2)}) copy-start(s32[4,6]{1,0:T(4,128)} %slots_ref.1) | copy-start | bytes 292
  68.4 1.5 %collective-permute-start.15 = (f32[384,64]{1,0:T(8,128)S(1)}, f32[384,64]{1,0:T(8,128)S(1)}, u32[]{:S(2)}, u32[]{:S(2)}) collective-permute-start(f32[384,64]{1,0:T(8,128)S(1)} %shard_map.77.partial_ref), channel_id=1, source_target_pairs={{0,1},{1,0},{2,3},{3,2},{4,5},{5,4},{6,7},{7,6},{8,9},{9,8},{10,11... | collective-permute-start | bytes 294920 | tf_op jit(solution)/shard_map/ppermute | solution.py:233

commit v8 on v7

--- a/solution.py
+++ b/solution.py
@@ -126,44 +126,62 @@
     )(half, tokens, weight, *down)
 
 
-def final_kernel(slots_ref, keep_ref, send_ref, arrived_ref, partial_ref, other_ref, own_up_ref, up_ref, out_ref, own, passed):
-    steps, rows, narrow = out_ref.shape
-    _, rank, both = up_ref.shape
-    held = own_up_ref.shape[0] // rank
-    block_rows = rows // slots_ref.shape[1]
+def base_kernel(rank, slots_ref, keep_ref, send_ref, arrived_ref, up_ref, out_ref, mask_ref, own):
+    rows, narrow = out_ref.shape
+    held = up_ref.shape[0] // rank
+    steps, blocks = slots_ref.shape
+    block_rows = rows // steps // blocks
     for step in range(steps):
-        for block in range(slots_ref.shape[1]):
+        for block in range(blocks):
             slot = slots_ref[step, block]
-            here = slice(step * rows + block * block_rows, step * rows + (block + 1) * block_rows)
+            start = (step * blocks + block) * block_rows
+            here = slice(start, start + block_rows)
             mine = (send_ref[here, narrow:] + arrived_ref[here, narrow:]).astype(own.dtype)
             column = lax.broadcasted_iota(jnp.int32, mine.shape, 1) // rank
             own[here] = jnp.where(column == slot, mine, jnp.zeros_like(mine))
-            given = (partial_ref[here] + other_ref[here]).astype(passed.dtype)
-            passed[here] = jnp.where(slot == held, given, jnp.zeros_like(given))
+            mask_ref[here] = jnp.full((block_rows, rank), (slot == held).astype(jnp.float32))
+    low_rank = jnp.dot(own[...], up_ref[...], preferred_element_type=jnp.float32)
+    out_ref[...] = keep_ref[...] + arrived_ref[:, :narrow] + low_rank
+
+
+def add_base(slots, keep, send, arrived, own_up, rank):
+    rows, narrow = keep.shape
+    vmem = pl.BlockSpec(memory_space=pltpu.VMEM)
+    return pl.pallas_call(
+        functools.partial(base_kernel, rank),
+        out_shape=[
+            jax.ShapeDtypeStruct((rows, narrow), jnp.float32),
+            jax.ShapeDtypeStruct((rows, rank), jnp.float32),
+        ],
+        in_specs=[pl.BlockSpec(memory_space=pltpu.SMEM)] + [vmem] * 4,
+        out_specs=[vmem] * 2,
+        scratch_shapes=[pltpu.VMEM((rows, own_up.shape[0]), jnp.bfloat16)],
+        compiler_params=pltpu.CompilerParams(vmem_limit_bytes=12 << 20),
+        cost_estimate=pl.CostEstimate(flops=0, bytes_accessed=0, transcendentals=0),
+    )(slots, keep, send, arrived, own_up)
+
+
+def final_kernel(base_ref, mask_ref, partial_ref, other_ref, up_ref, out_ref):
+    steps, rows, narrow = out_ref.shape
     for step in range(steps):
         here = slice(step * rows, (step + 1) * rows)
-        base = keep_ref[here] + arrived_ref[here, :narrow]
-        base += jnp.dot(own[here], own_up_ref[...], preferred_element_type=jnp.float32)
-        base += jnp.dot(passed[here], up_ref[step, :, both - narrow:], preferred_element_type=jnp.float32)
-        out_ref[step] = base.astype(out_ref.dtype)
-
-
-def finish(slots, keep, send, arrived, partial, other, own_up, handed):
-    steps, rank, _ = handed.shape
-    held_rank, narrow = own_up.shape
-    rows = keep.shape[0]
+        reduced = ((partial_ref[here] + other_ref[here]) * mask_ref[here]).astype(jnp.bfloat16)
+        up = up_ref[step, :, up_ref.shape[2] - narrow:]
+        low_rank = jnp.dot(reduced, up, preferred_element_type=jnp.float32)
+        out_ref[step] = (base_ref[here] + low_rank).astype(out_ref.dtype)
+
+
+def finish(base, mask, partial, other, handed):
+    steps = handed.shape[0]
+    rows, narrow = base.shape
     vmem = pl.BlockSpec(memory_space=pltpu.VMEM)
     return pl.pallas_call(
         final_kernel,
         out_shape=jax.ShapeDtypeStruct((steps, rows // steps, narrow), jnp.bfloat16),
-        in_specs=[pl.BlockSpec(memory_space=pltpu.SMEM)] + [vmem] * 7,
+        in_specs=[vmem] * 5,
         out_specs=vmem,
-        scratch_shapes=[
-            pltpu.VMEM((rows, held_rank), jnp.bfloat16),
-            pltpu.VMEM((rows, rank), jnp.bfloat16),
-        ],
         compiler_params=pltpu.CompilerParams(vmem_limit_bytes=12 << 20),
-    )(slots, keep, send, arrived, partial, other, own_up, handed)
+    )(base, mask, partial, other, handed)
 
 
 def rank_kernel(acts_ref, handed_ref, out_ref):
@@ -215,24 +233,24 @@
         given[k] = lax.ppermute(picked[k], ("groups", "adapter"), pairs)
     swap = [(0, 1), (1, 0)]
     tokens = acts.reshape(steps * rows_dev, wide)
-    early = [4]
+    early = [2]
     other_side, *waited = lax.optimization_barrier((1 - side, *[given[k] for k in early]))
     given.update(zip(early, waited))
     send = product(other_side[None], tokens, value_weight, adapter_down.reshape(held * rank, wide))
     arrived = lax.ppermute(send, "tensor", swap)
-    later = [1, 2]
+    later = [1, 4]
     side, send, *waited = lax.optimization_barrier((side, send, *[given[k] for k in later]))
     given.update(zip(later, waited))
     keep = product(side[None], tokens, value_weight)
     late = [k for k in range(1, STRIPES) if k not in early + later]
-    keep, arrived, *waited = lax.optimization_barrier((keep, arrived, *[given[k] for k in late]))
+    base, mask = add_base(block_slots, keep, send, arrived, adapter_up.reshape(held * rank, narrow), rank)
+    base, *waited = lax.optimization_barrier((base, *[given[k] for k in late]))
     given.update(zip(late, waited))
 
     handed = jnp.concatenate([given[k] for k in range(STRIPES)], axis=1)
     partial = rank_part(acts, handed)
     other = lax.ppermute(partial, "tensor", swap)
-    return finish(
-        block_slots, keep, send, arrived, partial, other, adapter_up.reshape(held * rank, narrow), handed)
+    return finish(base, mask, partial, other, handed)
 
 
 def solution(mesh):

time: 71.9 us -> 71.2 us (level)
  blocking collectives: 14.8 us -> 12.2 us
  waiting for transfers between devices: 16.1 us -> 17.7 us
    unnamed x1, blocking collectives: 14.8 us -> 12.2 us
    ppermute x7, waiting for transfers between devices: 2.85 us -> 4.57 us  [body(): lax.ppermute(stripes[k % parts], 'adapter', [(i, i ^ k) for i in range(se...]
    ppermute x7, starting transfers between devices: 14 us -> 15.1 us  [body(): lax.ppermute(stripes[k % parts], 'adapter', [(i, i ^ k) for i in range(se...]
    ppermute x7, starting transfers between devices: 7.6 us -> 6.65 us  [body(): given[k] = lax.ppermute(picked[k], ('groups', 'adapter'), pairs)]
    pallas_call x0 -> x1, Pallas kernels: none -> 0.82 us  [add_base(): pl.pallas_call(functools.partial(base_kernel, rank), out_shape=[jax.Shape...]
  transfers between devices with their start and end apart: 16 -> 16, of which waited for: 5 -> 5; matrix products, arithmetic and copies ran while one was open for 3% -> 3% of each run, Pallas kernels for 12% -> 13%
where the time goes in v8:
time: 71.2 us; the launch traced here: 71 us
  starting transfers between devices  21.8 us (31%)
  waiting for transfers between devices  17.7 us (25%)
  blocking collectives  12.2 us (17%)
  Pallas kernels  12.1 us (17%)
  local copies, waits for them, and re-layouts  5.46 us (8%)
  between operations  0.84 us (1%)
  other arithmetic  0.76 us (1%)
    ppermute x7, starting transfers between devices, body(): lax.ppermute(stripes[k % parts], 'adapter', [(i, i ^ k) for i in range(se...  15.1 us
    unnamed x1, blocking collectives  12.2 us
    ppermute x7, waiting for transfers between devices, body(): given[k] = lax.ppermute(picked[k], ('groups', 'adapter'), pairs)  11.7 us
    pallas_call x2, Pallas kernels, product(): pl.pallas_call(product_kernel, out_shape=out, grid_spec=pltpu.PrefetchSca...  8.43 us
    ppermute x7, starting transfers between devices, body(): given[k] = lax.ppermute(picked[k], ('groups', 'adapter'), pairs)  6.65 us
    unnamed x23, local copies, waits for them, and re-layouts  5.43 us
    ppermute x7, waiting for transfers between devices, body(): lax.ppermute(stripes[k % parts], 'adapter', [(i, i ^ k) for i in range(se...  4.57 us
    ppermute x1, waiting for transfers between devices, body(): other = lax.ppermute(partial, 'tensor', swap)  1.43 us
  transfers between devices with their start and end apart: 16, of which 5 were waited for; matrix products, arithmetic and copies ran while one was open for 3% of the time, Pallas kernels for 13%

profile of v8, /device:TPU:0, one launch (start us, length us, event | category | flops | bytes accessed | tf_op | source)
XLA Modules:
  0.0 71.0 jit_solution(17325482288024578493)
XLA Ops:
  0.0 1.2 %copy-done.2 = bf16[2,64,4096]{2,1,0:T(8,128)(2,1)S(1)} copy-done((bf16[2,64,4096]{2,1,0:T(8,128)(2,1)S(1)}, bf16[2,64,4096]{2,1,0:T(8,128)(2,1)}, u32[]{:S(2)}) %copy-start.2) | copy-done | bytes 1048600
  1.2 0.9 %copy-done.4 = bf16[2,64,512]{2,1,0:T(8,128)(2,1)S(1)} copy-done((bf16[2,64,512]{2,1,0:T(8,128)(2,1)S(1)}, bf16[2,64,512]{2,1,0:T(8,128)(2,1)}, u32[]{:S(2)}) %copy-start.4) | copy-done | bytes 131096
  2.2 5.1 %collective-permute-start = (bf16[2,8,4608]{2,1,0:T(8,128)(2,1)S(1)}, bf16[2,8,4608]{2,1,0:T(8,128)(2,1)S(1)}, u32[]{:S(2)}, u32[]{:S(2)}) collective-permute-start(bf16[2,8,4608]{2,1,0:T(8,128)(2,1)S(1)} %get-tuple-element.32), channel_id=1, source_target_pairs={{0,10},{2,8},{4,14},{6,12},{8,2},{10,0},{12,6},{14,4},{1,11},{3,9}... | collective-permute-start | bytes 442376 | tf_op jit(solution)/shard_map/ppermute | solution.py:216
  7.2 0.5 collective-permute-start.1
  7.7 1.3 %collective-permute-start.5 = (bf16[2,8,4608]{2,1,0:T(8,128)(2,1)S(1)}, bf16[2,8,4608]{2,1,0:T(8,128)(2,1)S(1)}, u32[]{:S(2)}, u32[]{:S(2)}) collective-permute-start(bf16[2,8,4608]{2,1,0:T(8,128)(2,1)S(1)} %get-tuple-element.35), channel_id=1, source_target_pairs={{0,12},{2,14},{4,8},{6,10},{8,4},{10,6},{12,0},{14,2},{1,13},{3,15... | collective-permute-start | bytes 442376 | tf_op jit(solution)/shard_map/ppermute | solution.py:216
  9.1 0.2 collective-permute-start.2
  9.3 3.9 %collective-permute-start.6 = (bf16[2,8,4608]{2,1,0:T(8,128)(2,1)S(1)}, bf16[2,8,4608]{2,1,0:T(8,128)(2,1)S(1)}, u32[]{:S(2)}, u32[]{:S(2)}) collective-permute-start(bf16[2,8,4608]{2,1,0:T(8,128)(2,1)S(1)} %get-tuple-element.36), channel_id=1, source_target_pairs={{0,14},{2,12},{4,10},{6,8},{8,6},{10,4},{12,2},{14,0},{1,15},{3,13... | collective-permute-start | bytes 442376 | tf_op jit(solution)/shard_map/ppermute | solution.py:216
  13.2 1.2 %dynamic-slice = u32[1]{0:T(128)} dynamic-slice(u32[32]{0:T(128)} %constant.14, u32[]{:T(128)S(6)} %add.4), dynamic_slice_sizes={1} | dynamic-slice | bytes 12
  15.1 4.6 %collective-permute-done.rest_5_ = bf16[2,8,4608]{2,1,0:T(8,128)(2,1)S(1)} collective-permute-done((bf16[2,8,4608]{2,1,0:T(8,128)(2,1)S(1)}, bf16[2,8,4608]{2,1,0:T(8,128)(2,1)S(1)}, u32[]{:S(2)}, u32[]{:S(2)}) %collective-permute-start) | collective-permute-done | bytes 147488 | tf_op jit(solution)/shard_map/ppermute | solution.py:216
  19.6 0.0 collective-permute-start.3
  19.6 0.0 collective-permute-done.1.rest_1_
  19.6 4.1 %collective-permute-start.4 = (bf16[2,8,4608]{2,1,0:T(8,128)(2,1)S(1)}, bf16[2,8,4608]{2,1,0:T(8,128)(2,1)S(1)}, u32[]{:S(2)}, u32[]{:S(2)}) collective-permute-start(bf16[2,8,4608]{2,1,0:T(8,128)(2,1)S(1)} %get-tuple-element.34.rest_0_), channel_id=1, source_target_pairs={{0,8},{2,10},{4,12},{6,14},{8,0},{10,2},{12,4},{14,6},{1,9},{3,11}... | collective-permute-start | bytes 442376 | tf_op jit(solution)/shard_map/ppermute | solution.py:216
  23.7 0.8 %fusion = s32[64]{0:T(128)S(1)} fusion(s32[64]{0:T(128)S(1)} %broadcast.4, u32[]{:T(128)} %bitcast.3, s32[4,1]{0,1:T(1,128)} %param.13, s32[4]{0:T(128)} %param.12), kind=kLoop, calls=%fused_computation.9 | loop fusion | flops 8 | bytes 292
  24.5 12.2 %all-reduce.asked_ref = s32[64]{0:T(128)S(1)} all-reduce(s32[64]{0:T(128)S(1)} %fusion), channel_id=2, replica_groups=mesh['groups'=2,'adapter'=8,'tensor'=2] {'groups','adapter'}, use_global_device_ids=true, to_apply=%add | all-reduce | flops 64 | bytes 512
  36.7 0.0 collective-permute-done.4.rest_4_
  36.7 0.0 collective-permute-done.5.rest_6_
  36.7 0.0 collective-permute-done.2.rest_2_
  36.7 0.0 collective-permute-done.6.rest_7_
  36.7 0.0 collective-permute-done.3.rest_3_
  36.7 0.9 %shard_map.74 = (bf16[4,8,4608]{2,1,0:T(8,128)(2,1)S(1)}, bf16[4,8,4608]{2,1,0:T(8,128)(2,1)S(1)}, bf16[4,8,4608]{2,1,0:T(8,128)(2,1)S(1)}, bf16[4,8,4608]{2,1,0...) custom-call(s32[64]{0:T(128)S(1)} %all-reduce.asked_ref, ...), custom_call_target="tpu_custom_call" | custom-call | tf_op jit(solution)/shard_map/pallas_call | solution.py:75
  37.6 0.4 collective-permute-start.7
  38.1 0.9 %collective-permute-start.8 = (bf16[4,8,4608]{2,1,0:T(8,128)(2,1)S(1)}, bf16[4,8,4608]{2,1,0:T(8,128)(2,1)S(1)}, u32[]{:S(2)}, u32[]{:S(2)}) collective-permute-start(bf16[4,8,4608]{2,1,0:T(8,128)(2,1)S(1)} %get-tuple-element.40), channel_id=1, source_target_pairs={{0,2},{2,0},{4,6},{6,4},{8,10},{10,8},{12,14},{14,12},{16,18},{18,... | collective-permute-start | bytes 884744 | tf_op jit(solution)/shard_map/ppermute | solution.py:233
  38.9 0.3 collective-permute-start.9
  39.2 2.5 %collective-permute-start.11 = (bf16[4,8,4608]{2,1,0:T(8,128)(2,1)S(1)}, bf16[4,8,4608]{2,1,0:T(8,128)(2,1)S(1)}, u32[]{:S(2)}, u32[]{:S(2)}) collective-permute-start(bf16[4,8,4608]{2,1,0:T(8,128)(2,1)S(1)} %get-tuple-element.45), channel_id=1, source_target_pairs={{0,6},{2,4},{4,2},{6,0},{8,14},{10,12},{12,10},{14,8},{16,22},{18,... | collective-permute-start | bytes 884744 | tf_op jit(solution)/shard_map/ppermute | solution.py:233
  41.7 2.1 %collective-permute-start.12 = (bf16[4,8,4608]{2,1,0:T(8,128)(2,1)S(1)}, bf16[4,8,4608]{2,1,0:T(8,128)(2,1)S(1)}, u32[]{:S(2)}, u32[]{:S(2)}) collective-permute-start(bf16[4,8,4608]{2,1,0:T(8,128)(2,1)S(1)} %get-tuple-element.46), channel_id=1, source_target_pairs={{0,18},{2,16},{4,22},{6,20},{8,26},{10,24},{12,30},{14,28},{16,2},... | collective-permute-start | bytes 884744 | tf_op jit(solution)/shard_map/ppermute | solution.py:233
  43.8 3.8 %collective-permute-done.7 = bf16[4,8,4608]{2,1,0:T(8,128)(2,1)S(1)} collective-permute-done((bf16[4,8,4608]{2,1,0:T(8,128)(2,1)S(1)}, bf16[4,8,4608]{2,1,0:T(8,128)(2,1)S(1)}, u32[]{:S(2)}, u32[]{:S(2)}) %collective-permute-start.7) | collective-permute-done | bytes 294944 | tf_op jit(solution)/shard_map/ppermute | solution.py:233
  47.6 0.1 collective-permute-start.13
  47.7 0.0 copy-done.3
  47.7 1.9 %copy-done = bf16[4,96,4096]{2,1,0:T(8,128)(2,1)S(1)} copy-done((bf16[4,96,4096]{2,1,0:T(8,128)(2,1)S(1)}, bf16[4,96,4096]{2,1,0:T(8,128)(2,1)}, u32[]{:S(2)}) %copy-start) | copy-done | bytes 3145752
  49.6 4.7 %shard_map.75.send_ref = f32[384,640]{1,0:T(8,128)S(1)} custom-call(s32[1]{0:T(128)} %bitcast.4.half_ref, bf16[384,4096]{1,0:T(8,128)(2,1)S(1)} %bitcast.12, bf16[4096,1024]{1,0:T(8,128)(2,1)} %weight_ref.3, bf16[128,4096]{1,0:T(8,128)(2,1)S(1)} %bitcast.15), custom_call_target="tpu_custom_call" | custom-call | tf_op jit(solution)/shard_map/pallas_call | solution.py:111
  54.4 4.5 %collective-permute-done.8 = bf16[4,8,4608]{2,1,0:T(8,128)(2,1)S(1)} collective-permute-done((bf16[4,8,4608]{2,1,0:T(8,128)(2,1)S(1)}, bf16[4,8,4608]{2,1,0:T(8,128)(2,1)S(1)}, u32[]{:S(2)}, u32[]{:S(2)}) %collective-permute-start.8) | collective-permute-done | bytes 294944 | tf_op jit(solution)/shard_map/ppermute | solution.py:233
  58.8 0.4 collective-permute-start.14
  59.3 0.0 collective-permute-done.9
  59.3 0.0 collective-permute-start.10
  59.3 0.0 copy-done.1
  59.3 0.0 copy-start.5
  59.3 0.0 copy-start.6
  59.3 3.7 %shard_map.76.keep_ref = f32[384,512]{1,0:T(8,128)S(1)} custom-call(s32[1]{0:T(128)} %bitcast.7.half_ref, bf16[384,4096]{1,0:T(8,128)(2,1)S(1)} %bitcast.13, bf16[4096,1024]{1,0:T(8,128)(2,1)} %weight_ref.3), custom_call_target="tpu_custom_call" | custom-call | tf_op jit(solution)/shard_map/pallas_call | solution.py:111
  63.0 0.0 collective-permute-done.10.arrived_ref
  63.1 0.8 %shard_map.77 = (f32[384,512]{1,0:T(8,128)S(1)}, f32[384,64]{1,0:T(8,128)S(1)}) custom-call(s32[4,6]{1,0:T(4,128)S(1)} %copy-done.6, f32[384,512]{1,0:T(8,128)S(1)} %shard_map.76.keep_ref, f32[384,640]{1,0:T(8,128)S(1)} %shard_map.75.send_ref, f32[384,640]{1,0:T(8,128)S(1)} %collective-permute-done.10.arrived_ref, bf16[128,512]{1,0:T(8,128)(2,1)S(1)} %bitcast.17), custom_call_target="tpu_custom_call" | custom-call | tf_op jit(solution)/shard_map/pallas_call | solution.py:150
  63.9 0.0 collective-permute-done.11
  63.9 0.0 collective-permute-done.12
  63.9 0.0 collective-permute-done.13
  63.9 3.4 %collective-permute-done.14 = bf16[4,8,4608]{2,1,0:T(8,128)(2,1)S(1)} collective-permute-done((bf16[4,8,4608]{2,1,0:T(8,128)(2,1)S(1)}, bf16[4,8,4608]{2,1,0:T(8,128)(2,1)S(1)}, u32[]{:S(2)}, u32[]{:S(2)}) %collective-permute-start.14) | collective-permute-done | bytes 294944 | tf_op jit(solution)/shard_map/ppermute | solution.py:233
  67.5 1.0 %shard_map.78.partial_ref = f32[384,64]{1,0:T(8,128)S(1)} custom-call(bf16[4,96,4096]{2,1,0:T(8,128)(2,1)S(1)} %copy-done.1, bf16[4,64,4608]{2,1,0:T(8,128)(2,1)S(1)} %constant_dynamic-update-slice_fusion.handed_ref.up_ref), custom_call_target="tpu_custom_call" | custom-call | tf_op jit(solution)/shard_map/pallas_call | solution.py:196
  68.5 0.1 collective-permute-start.15
  68.5 1.4 %collective-permute-done.15.other_ref = f32[384,64]{1,0:T(8,128)S(1)} collective-permute-done((f32[384,64]{1,0:T(8,128)S(1)}, f32[384,64]{1,0:T(8,128)S(1)}, u32[]{:S(2)}, u32[]{:S(2)}) %collective-permute-start.15) | collective-permute-done | bytes 98336 | tf_op jit(solution)/shard_map/ppermute | solution.py:252
  70.0 1.0 %shard_map.79 = bf16[4,96,512]{2,1,0:T(8,128)(2,1)} custom-call(f32[384,512]{1,0:T(8,128)S(1)} %get-tuple-element.49.base_ref, f32[384,64]{1,0:T(8,128)S(1)} %get-tuple-element.50.mask_ref, f32[384,64]{1,0:T(8,128)S(1)} %shard_map.78.partial_ref, f32[384,64]{1,0:T(8,128)S(1)} %collective-permute-done.15.other_ref, ...), custom_call_target="tpu_custom_call" | custom-call | tf_op jit(solution)/shard_map/pallas_call | solution.py:178
  (17 shorter events, 0.2 us)
Async XLA Ops:
  0.0 1.2 %copy-start.2 = (bf16[2,64,4096]{2,1,0:T(8,128)(2,1)S(1)}, bf16[2,64,4096]{2,1,0:T(8,128)(2,1)}, u32[]{:S(2)}) copy-start(bf16[2,64,4096]{2,1,0:T(8,128)(2,1)} %param.9) | copy-start | bytes 3145732
  1.2 0.9 %copy-start.4 = (bf16[2,64,512]{2,1,0:T(8,128)(2,1)S(1)}, bf16[2,64,512]{2,1,0:T(8,128)(2,1)}, u32[]{:S(2)}) copy-start(bf16[2,64,512]{2,1,0:T(8,128)(2,1)} %param.10) | copy-start | bytes 393220
  2.1 45.6 %copy-start.3 = (bf16[2,64,4096]{2,1,0:T(8,128)(2,1)S(1)}, bf16[2,64,4096]{2,1,0:T(8,128)(2,1)}, u32[]{:S(2)}) copy-start(bf16[2,64,4096]{2,1,0:T(8,128)(2,1)} %param.9) | copy-start | bytes 3145732
  2.2 17.5 %collective-permute-start = (bf16[2,8,4608]{2,1,0:T(8,128)(2,1)S(1)}, bf16[2,8,4608]{2,1,0:T(8,128)(2,1)S(1)}, u32[]{:S(2)}, u32[]{:S(2)}) collective-permute-start(bf16[2,8,4608]{2,1,0:T(8,128)(2,1)S(1)} %get-tuple-element.32), channel_id=1, source_target_pairs={{0,10},{2,8},{4,14},{6,12},{8,2},{10,0},{12,6},{14,4},{1,11},{3,9}... | collective-permute-start | bytes 442376 | tf_op jit(solution)/shard_map/ppermute | solution.py:216
  7.2 12.4 %collective-permute-start.1 = (bf16[2,8,4608]{2,1,0:T(8,128)(2,1)S(1)}, bf16[2,8,4608]{2,1,0:T(8,128)(2,1)S(1)}, u32[]{:S(2)}, u32[]{:S(2)}) collective-permute-start(bf16[2,8,4608]{2,1,0:T(8,128)(2,1)S(1)} %get-tuple-element.32), channel_id=1, source_target_pairs={{0,2},{2,0},{4,6},{6,4},{8,10},{10,8},{12,14},{14,12},{1,3},{3,1},... | collective-permute-start | bytes 442376 | tf_op jit(solution)/shard_map/ppermute | solution.py:216
  7.7 29.0 %collective-permute-start.5 = (bf16[2,8,4608]{2,1,0:T(8,128)(2,1)S(1)}, bf16[2,8,4608]{2,1,0:T(8,128)(2,1)S(1)}, u32[]{:S(2)}, u32[]{:S(2)}) collective-permute-start(bf16[2,8,4608]{2,1,0:T(8,128)(2,1)S(1)} %get-tuple-element.35), channel_id=1, source_target_pairs={{0,12},{2,14},{4,8},{6,10},{8,4},{10,6},{12,0},{14,2},{1,13},{3,15... | collective-permute-start | bytes 442376 | tf_op jit(solution)/shard_map/ppermute | solution.py:216
  9.1 27.6 %collective-permute-start.2 = (bf16[2,8,4608]{2,1,0:T(8,128)(2,1)S(1)}, bf16[2,8,4608]{2,1,0:T(8,128)(2,1)S(1)}, u32[]{:S(2)}, u32[]{:S(2)}) collective-permute-start(bf16[2,8,4608]{2,1,0:T(8,128)(2,1)S(1)} %get-tuple-element.35), channel_id=1, source_target_pairs={{0,4},{2,6},{4,0},{6,2},{8,12},{10,14},{12,8},{14,10},{1,5},{3,7},... | collective-permute-start | bytes 442376 | tf_op jit(solution)/shard_map/ppermute | solution.py:216
  9.3 27.4 %collective-permute-start.6 = (bf16[2,8,4608]{2,1,0:T(8,128)(2,1)S(1)}, bf16[2,8,4608]{2,1,0:T(8,128)(2,1)S(1)}, u32[]{:S(2)}, u32[]{:S(2)}) collective-permute-start(bf16[2,8,4608]{2,1,0:T(8,128)(2,1)S(1)} %get-tuple-element.36), channel_id=1, source_target_pairs={{0,14},{2,12},{4,10},{6,8},{8,6},{10,4},{12,2},{14,0},{1,15},{3,13... | collective-permute-start | bytes 442376 | tf_op jit(solution)/shard_map/ppermute | solution.py:216
  19.6 17.1 %collective-permute-start.3 = (bf16[2,8,4608]{2,1,0:T(8,128)(2,1)S(1)}, bf16[2,8,4608]{2,1,0:T(8,128)(2,1)S(1)}, u32[]{:S(2)}, u32[]{:S(2)}) collective-permute-start(bf16[2,8,4608]{2,1,0:T(8,128)(2,1)S(1)} %get-tuple-element.36), channel_id=1, source_target_pairs={{0,6},{2,4},{4,2},{6,0},{8,14},{10,12},{12,10},{14,8},{1,7},{3,5},... | collective-permute-start | bytes 442376 | tf_op jit(solution)/shard_map/ppermute | solution.py:216
  19.6 17.1 %collective-permute-start.4 = (bf16[2,8,4608]{2,1,0:T(8,128)(2,1)S(1)}, bf16[2,8,4608]{2,1,0:T(8,128)(2,1)S(1)}, u32[]{:S(2)}, u32[]{:S(2)}) collective-permute-start(bf16[2,8,4608]{2,1,0:T(8,128)(2,1)S(1)} %get-tuple-element.34.rest_0_), channel_id=1, source_target_pairs={{0,8},{2,10},{4,12},{6,14},{8,0},{10,2},{12,4},{14,6},{1,9},{3,11}... | collective-permute-start | bytes 442376 | tf_op jit(solution)/shard_map/ppermute | solution.py:216
  37.6 10.0 %collective-permute-start.7 = (bf16[4,8,4608]{2,1,0:T(8,128)(2,1)S(1)}, bf16[4,8,4608]{2,1,0:T(8,128)(2,1)S(1)}, u32[]{:S(2)}, u32[]{:S(2)}) collective-permute-start(bf16[4,8,4608]{2,1,0:T(8,128)(2,1)S(1)} %get-tuple-element.38), channel_id=1, source_target_pairs={{0,4},{2,6},{4,0},{6,2},{8,12},{10,14},{12,8},{14,10},{16,20},{18,... | collective-permute-start | bytes 884744 | tf_op jit(solution)/shard_map/ppermute | solution.py:233
  38.1 20.8 %collective-permute-start.8 = (bf16[4,8,4608]{2,1,0:T(8,128)(2,1)S(1)}, bf16[4,8,4608]{2,1,0:T(8,128)(2,1)S(1)}, u32[]{:S(2)}, u32[]{:S(2)}) collective-permute-start(bf16[4,8,4608]{2,1,0:T(8,128)(2,1)S(1)} %get-tuple-element.40), channel_id=1, source_target_pairs={{0,2},{2,0},{4,6},{6,4},{8,10},{10,8},{12,14},{14,12},{16,18},{18,... | collective-permute-start | bytes 884744 | tf_op jit(solution)/shard_map/ppermute | solution.py:233
  38.9 20.3 %collective-permute-start.9 = (bf16[4,8,4608]{2,1,0:T(8,128)(2,1)S(1)}, bf16[4,8,4608]{2,1,0:T(8,128)(2,1)S(1)}, u32[]{:S(2)}, u32[]{:S(2)}) collective-permute-start(bf16[4,8,4608]{2,1,0:T(8,128)(2,1)S(1)} %get-tuple-element.41), channel_id=1, source_target_pairs={{0,16},{2,18},{4,20},{6,22},{8,24},{10,26},{12,28},{14,30},{16,0},... | collective-permute-start | bytes 884744 | tf_op jit(solution)/shard_map/ppermute | solution.py:233
  39.2 24.7 %collective-permute-start.11 = (bf16[4,8,4608]{2,1,0:T(8,128)(2,1)S(1)}, bf16[4,8,4608]{2,1,0:T(8,128)(2,1)S(1)}, u32[]{:S(2)}, u32[]{:S(2)}) collective-permute-start(bf16[4,8,4608]{2,1,0:T(8,128)(2,1)S(1)} %get-tuple-element.45), channel_id=1, source_target_pairs={{0,6},{2,4},{4,2},{6,0},{8,14},{10,12},{12,10},{14,8},{16,22},{18,... | collective-permute-start | bytes 884744 | tf_op jit(solution)/shard_map/ppermute | solution.py:233
  41.7 22.2 %collective-permute-start.12 = (bf16[4,8,4608]{2,1,0:T(8,128)(2,1)S(1)}, bf16[4,8,4608]{2,1,0:T(8,128)(2,1)S(1)}, u32[]{:S(2)}, u32[]{:S(2)}) collective-permute-start(bf16[4,8,4608]{2,1,0:T(8,128)(2,1)S(1)} %get-tuple-element.46), channel_id=1, source_target_pairs={{0,18},{2,16},{4,22},{6,20},{8,26},{10,24},{12,30},{14,28},{16,2},... | collective-permute-start | bytes 884744 | tf_op jit(solution)/shard_map/ppermute | solution.py:233
  47.6 16.3 %collective-permute-start.13 = (bf16[4,8,4608]{2,1,0:T(8,128)(2,1)S(1)}, bf16[4,8,4608]{2,1,0:T(8,128)(2,1)S(1)}, u32[]{:S(2)}, u32[]{:S(2)}) collective-permute-start(bf16[4,8,4608]{2,1,0:T(8,128)(2,1)S(1)} %get-tuple-element.47), channel_id=1, source_target_pairs={{0,20},{2,22},{4,16},{6,18},{8,28},{10,30},{12,24},{14,26},{16,4},... | collective-permute-start | bytes 884744 | tf_op jit(solution)/shard_map/ppermute | solution.py:233
  47.7 1.9 %copy-start = (bf16[4,96,4096]{2,1,0:T(8,128)(2,1)S(1)}, bf16[4,96,4096]{2,1,0:T(8,128)(2,1)}, u32[]{:S(2)}) copy-start(bf16[4,96,4096]{2,1,0:T(8,128)(2,1)} %acts_ref.1) | copy-start | bytes 9437188
  49.6 9.7 %copy-start.1 = (bf16[4,96,4096]{2,1,0:T(8,128)(2,1)S(1)}, bf16[4,96,4096]{2,1,0:T(8,128)(2,1)}, u32[]{:S(2)}) copy-start(bf16[4,96,4096]{2,1,0:T(8,128)(2,1)} %acts_ref.1) | copy-start | bytes 9437188
  58.8 8.5 %collective-permute-start.14 = (bf16[4,8,4608]{2,1,0:T(8,128)(2,1)S(1)}, bf16[4,8,4608]{2,1,0:T(8,128)(2,1)S(1)}, u32[]{:S(2)}, u32[]{:S(2)}) collective-permute-start(bf16[4,8,4608]{2,1,0:T(8,128)(2,1)S(1)} %get-tuple-element.48), channel_id=1, source_target_pairs={{0,22},{2,20},{4,18},{6,16},{8,30},{10,28},{12,26},{14,24},{16,6},... | collective-permute-start | bytes 884744 | tf_op jit(solution)/shard_map/ppermute | solution.py:233
  59.3 3.8 %collective-permute-start.10 = (f32[384,640]{1,0:T(8,128)S(1)}, f32[384,640]{1,0:T(8,128)S(1)}, u32[]{:S(2)}, u32[]{:S(2)}) collective-permute-start(f32[384,640]{1,0:T(8,128)S(1)} %shard_map.75.send_ref), channel_id=1, source_target_pairs={{0,1},{1,0},{2,3},{3,2},{4,5},{5,4},{6,7},{7,6},{8,9},{9,8},{10,11... | collective-permute-start | bytes 2949128 | tf_op jit(solution)/shard_map/ppermute | solution.py:240
  59.3 3.8 %copy-start.5 = (bf16[2,64,512]{2,1,0:T(8,128)(2,1)S(1)}, bf16[2,64,512]{2,1,0:T(8,128)(2,1)}, u32[]{:S(2)}) copy-start(bf16[2,64,512]{2,1,0:T(8,128)(2,1)} %param.10) | copy-start | bytes 393220
  59.3 3.8 %copy-start.6 = (s32[4,6]{1,0:T(4,128)S(1)}, s32[4,6]{1,0:T(4,128)}, u32[]{:S(2)}) copy-start(s32[4,6]{1,0:T(4,128)} %slots_ref.1) | copy-start | bytes 292
  68.5 1.5 %collective-permute-start.15 = (f32[384,64]{1,0:T(8,128)S(1)}, f32[384,64]{1,0:T(8,128)S(1)}, u32[]{:S(2)}, u32[]{:S(2)}) collective-permute-start(f32[384,64]{1,0:T(8,128)S(1)} %shard_map.78.partial_ref), channel_id=1, source_target_pairs={{0,1},{1,0},{2,3},{3,2},{4,5},{5,4},{6,7},{7,6},{8,9},{9,8},{10,11... | collective-permute-start | bytes 294920 | tf_op jit(solution)/shard_map/ppermute | solution.py:252

commit v9 on v8

--- a/solution.py
+++ b/solution.py
@@ -214,7 +214,7 @@
     banked = {0: stripes[0]}
     for k in [1, 2, 3, 4, 5, 6, 7, *range(STRIPES, servers)]:
         banked[k] = lax.ppermute(stripes[k % parts], "adapter", [(i, i ^ k) for i in range(servers)])
-    early = [5]
+    early = [6]
     transfer_slot, *arrived = lax.optimization_barrier((transfer_slot, *[banked[k] for k in early]))
     banked.update(zip(early, arrived))
     banked = [banked[k] for k in range(servers)]

time: 71.2 us -> 69.1 us (0.971)
  waiting for transfers between devices: 17.7 us -> 10.9 us
  blocking collectives: 12.2 us -> 17.6 us
    unnamed x1, blocking collectives: 12.2 us -> 17.6 us
    ppermute x7, waiting for transfers between devices: 4.57 us -> 0.02 us  [body(): lax.ppermute(stripes[k % parts], 'adapter', [(i, i ^ k) for i in range(se...]
    ppermute x7, waiting for transfers between devices: 11.7 us -> 9.43 us  [body(): given[k] = lax.ppermute(picked[k], ('groups', 'adapter'), pairs)]
    ppermute x7, starting transfers between devices: 15.1 us -> 13.3 us  [body(): lax.ppermute(stripes[k % parts], 'adapter', [(i, i ^ k) for i in range(se...]
    ppermute x7, starting transfers between devices: 6.65 us -> 7.84 us  [body(): given[k] = lax.ppermute(picked[k], ('groups', 'adapter'), pairs)]
  transfers between devices with their start and end apart: 16 -> 16, of which waited for: 5 -> 4; matrix products, arithmetic and copies ran while one was open for 3% -> 3% of each run, Pallas kernels for 13% -> 13%
where the time goes in v9:
time: 69.1 us; the launch traced here: 68.9 us
  starting transfers between devices  21.2 us (31%)
  blocking collectives  17.6 us (25%)
  Pallas kernels  12.1 us (18%)
  waiting for transfers between devices  10.9 us (16%)
  local copies, waits for them, and re-layouts  5.45 us (8%)
  between operations  0.86 us (1%)
  other arithmetic  0.76 us (1%)
    unnamed x1, blocking collectives  17.6 us
    ppermute x7, starting transfers between devices, body(): lax.ppermute(stripes[k % parts], 'adapter', [(i, i ^ k) for i in range(se...  13.3 us
    ppermute x7, waiting for transfers between devices, body(): given[k] = lax.ppermute(picked[k], ('groups', 'adapter'), pairs)  9.43 us
    pallas_call x2, Pallas kernels, product(): pl.pallas_call(product_kernel, out_shape=out, grid_spec=pltpu.PrefetchSca...  8.43 us
    ppermute x7, starting transfers between devices, body(): given[k] = lax.ppermute(picked[k], ('groups', 'adapter'), pairs)  7.84 us
    unnamed x23, local copies, waits for them, and re-layouts  5.43 us
    ppermute x1, waiting for transfers between devices, body(): other = lax.ppermute(partial, 'tensor', swap)  1.43 us
  transfers between devices with their start and end apart: 16, of which 4 were waited for; matrix products, arithmetic and copies ran while one was open for 3% of the time, Pallas kernels for 13%

profile of v9, /device:TPU:0, one launch (start us, length us, event | category | flops | bytes accessed | tf_op | source)
XLA Modules:
  0.0 68.9 jit_solution(6272699452924555619)
XLA Ops:
  0.0 1.2 %copy-done.2 = bf16[2,64,4096]{2,1,0:T(8,128)(2,1)S(1)} copy-done((bf16[2,64,4096]{2,1,0:T(8,128)(2,1)S(1)}, bf16[2,64,4096]{2,1,0:T(8,128)(2,1)}, u32[]{:S(2)}) %copy-start.2) | copy-done | bytes 1048600
  1.2 0.9 %copy-done.4 = bf16[2,64,512]{2,1,0:T(8,128)(2,1)S(1)} copy-done((bf16[2,64,512]{2,1,0:T(8,128)(2,1)S(1)}, bf16[2,64,512]{2,1,0:T(8,128)(2,1)}, u32[]{:S(2)}) %copy-start.4) | copy-done | bytes 131096
  2.2 5.1 %collective-permute-start = (bf16[2,8,4608]{2,1,0:T(8,128)(2,1)S(1)}, bf16[2,8,4608]{2,1,0:T(8,128)(2,1)S(1)}, u32[]{:S(2)}, u32[]{:S(2)}) collective-permute-start(bf16[2,8,4608]{2,1,0:T(8,128)(2,1)S(1)} %get-tuple-element.32), channel_id=1, source_target_pairs={{0,12},{2,14},{4,8},{6,10},{8,4},{10,6},{12,0},{14,2},{1,13},{3,15... | collective-permute-start | bytes 442376 | tf_op jit(solution)/shard_map/ppermute | solution.py:216
  7.3 0.0 collective-permute-start.2
  7.3 1.7 %collective-permute-start.5 = (bf16[2,8,4608]{2,1,0:T(8,128)(2,1)S(1)}, bf16[2,8,4608]{2,1,0:T(8,128)(2,1)S(1)}, u32[]{:S(2)}, u32[]{:S(2)}) collective-permute-start(bf16[2,8,4608]{2,1,0:T(8,128)(2,1)S(1)} %get-tuple-element.35), channel_id=1, source_target_pairs={{0,10},{2,8},{4,14},{6,12},{8,2},{10,0},{12,6},{14,4},{1,11},{3,9}... | collective-permute-start | bytes 442376 | tf_op jit(solution)/shard_map/ppermute | solution.py:216
  9.0 0.4 collective-permute-start.1
  9.4 4.7 %collective-permute-start.6 = (bf16[2,8,4608]{2,1,0:T(8,128)(2,1)S(1)}, bf16[2,8,4608]{2,1,0:T(8,128)(2,1)S(1)}, u32[]{:S(2)}, u32[]{:S(2)}) collective-permute-start(bf16[2,8,4608]{2,1,0:T(8,128)(2,1)S(1)} %get-tuple-element.36), channel_id=1, source_target_pairs={{0,14},{2,12},{4,10},{6,8},{8,6},{10,4},{12,2},{14,0},{1,15},{3,13... | collective-permute-start | bytes 442376 | tf_op jit(solution)/shard_map/ppermute | solution.py:216
  14.1 1.2 %dynamic-slice = u32[1]{0:T(128)} dynamic-slice(u32[32]{0:T(128)} %constant.14, u32[]{:T(128)S(6)} %add.4), dynamic_slice_sizes={1} | dynamic-slice | bytes 12
  16.0 0.0 collective-permute-done.rest_6_
  16.0 1.0 %collective-permute-start.3 = (bf16[2,8,4608]{2,1,0:T(8,128)(2,1)S(1)}, bf16[2,8,4608]{2,1,0:T(8,128)(2,1)S(1)}, u32[]{:S(2)}, u32[]{:S(2)}) collective-permute-start(bf16[2,8,4608]{2,1,0:T(8,128)(2,1)S(1)} %get-tuple-element.36), channel_id=1, source_target_pairs={{0,6},{2,4},{4,2},{6,0},{8,14},{10,12},{12,10},{14,8},{1,7},{3,5},... | collective-permute-start | bytes 442376 | tf_op jit(solution)/shard_map/ppermute | solution.py:216
  17.0 0.0 collective-permute-done.2.rest_2_
  17.0 0.4 collective-permute-start.4
  17.4 0.8 %fusion = s32[64]{0:T(128)S(1)} fusion(s32[64]{0:T(128)S(1)} %broadcast.4, u32[]{:T(128)} %bitcast.3, s32[4,1]{0,1:T(1,128)} %param.13, s32[4]{0:T(128)} %param.12), kind=kLoop, calls=%fused_computation.9 | loop fusion | flops 8 | bytes 292
  18.1 17.6 %all-reduce.asked_ref = s32[64]{0:T(128)S(1)} all-reduce(s32[64]{0:T(128)S(1)} %fusion), channel_id=2, replica_groups=mesh['groups'=2,'adapter'=8,'tensor'=2] {'groups','adapter'}, use_global_device_ids=true, to_apply=%add | all-reduce | flops 64 | bytes 512
  35.7 0.0 collective-permute-done.4.rest_4_
  35.7 0.0 collective-permute-done.5.rest_5_
  35.7 0.0 collective-permute-done.1.rest_1_
  35.7 0.0 collective-permute-done.6.rest_7_
  35.7 0.0 collective-permute-done.3.rest_3_
  35.8 0.9 %shard_map.74 = (bf16[4,8,4608]{2,1,0:T(8,128)(2,1)S(1)}, bf16[4,8,4608]{2,1,0:T(8,128)(2,1)S(1)}, bf16[4,8,4608]{2,1,0:T(8,128)(2,1)S(1)}, bf16[4,8,4608]{2,1,0...) custom-call(s32[64]{0:T(128)S(1)} %all-reduce.asked_ref, ...), custom_call_target="tpu_custom_call" | custom-call | tf_op jit(solution)/shard_map/pallas_call | solution.py:75
  36.6 0.1 collective-permute-start.7
  36.7 1.6 %collective-permute-start.8 = (bf16[4,8,4608]{2,1,0:T(8,128)(2,1)S(1)}, bf16[4,8,4608]{2,1,0:T(8,128)(2,1)S(1)}, u32[]{:S(2)}, u32[]{:S(2)}) collective-permute-start(bf16[4,8,4608]{2,1,0:T(8,128)(2,1)S(1)} %get-tuple-element.40), channel_id=1, source_target_pairs={{0,2},{2,0},{4,6},{6,4},{8,10},{10,8},{12,14},{14,12},{16,18},{18,... | collective-permute-start | bytes 884744 | tf_op jit(solution)/shard_map/ppermute | solution.py:233
  38.3 0.5 collective-permute-start.9
  38.8 1.9 %collective-permute-start.11 = (bf16[4,8,4608]{2,1,0:T(8,128)(2,1)S(1)}, bf16[4,8,4608]{2,1,0:T(8,128)(2,1)S(1)}, u32[]{:S(2)}, u32[]{:S(2)}) collective-permute-start(bf16[4,8,4608]{2,1,0:T(8,128)(2,1)S(1)} %get-tuple-element.45), channel_id=1, source_target_pairs={{0,6},{2,4},{4,2},{6,0},{8,14},{10,12},{12,10},{14,8},{16,22},{18,... | collective-permute-start | bytes 884744 | tf_op jit(solution)/shard_map/ppermute | solution.py:233
  40.7 2.4 %collective-permute-start.12 = (bf16[4,8,4608]{2,1,0:T(8,128)(2,1)S(1)}, bf16[4,8,4608]{2,1,0:T(8,128)(2,1)S(1)}, u32[]{:S(2)}, u32[]{:S(2)}) collective-permute-start(bf16[4,8,4608]{2,1,0:T(8,128)(2,1)S(1)} %get-tuple-element.46), channel_id=1, source_target_pairs={{0,18},{2,16},{4,22},{6,20},{8,26},{10,24},{12,30},{14,28},{16,2},... | collective-permute-start | bytes 884744 | tf_op jit(solution)/shard_map/ppermute | solution.py:233
  43.2 3.4 %collective-permute-done.7 = bf16[4,8,4608]{2,1,0:T(8,128)(2,1)S(1)} collective-permute-done((bf16[4,8,4608]{2,1,0:T(8,128)(2,1)S(1)}, bf16[4,8,4608]{2,1,0:T(8,128)(2,1)S(1)}, u32[]{:S(2)}, u32[]{:S(2)}) %collective-permute-start.7) | collective-permute-done | bytes 294944 | tf_op jit(solution)/shard_map/ppermute | solution.py:233
  46.7 0.0 collective-permute-start.13
  46.7 0.0 copy-done.3
  46.7 1.9 %copy-done = bf16[4,96,4096]{2,1,0:T(8,128)(2,1)S(1)} copy-done((bf16[4,96,4096]{2,1,0:T(8,128)(2,1)S(1)}, bf16[4,96,4096]{2,1,0:T(8,128)(2,1)}, u32[]{:S(2)}) %copy-start) | copy-done | bytes 3145752
  48.6 4.7 %shard_map.75.send_ref = f32[384,640]{1,0:T(8,128)S(1)} custom-call(s32[1]{0:T(128)} %bitcast.4.half_ref, bf16[384,4096]{1,0:T(8,128)(2,1)S(1)} %bitcast.12, bf16[4096,1024]{1,0:T(8,128)(2,1)} %weight_ref.3, bf16[128,4096]{1,0:T(8,128)(2,1)S(1)} %bitcast.15), custom_call_target="tpu_custom_call" | custom-call | tf_op jit(solution)/shard_map/pallas_call | solution.py:111
  53.3 3.4 %collective-permute-done.8 = bf16[4,8,4608]{2,1,0:T(8,128)(2,1)S(1)} collective-permute-done((bf16[4,8,4608]{2,1,0:T(8,128)(2,1)S(1)}, bf16[4,8,4608]{2,1,0:T(8,128)(2,1)S(1)}, u32[]{:S(2)}, u32[]{:S(2)}) %collective-permute-start.8) | collective-permute-done | bytes 294944 | tf_op jit(solution)/shard_map/ppermute | solution.py:233
  56.7 1.3 %collective-permute-start.14 = (bf16[4,8,4608]{2,1,0:T(8,128)(2,1)S(1)}, bf16[4,8,4608]{2,1,0:T(8,128)(2,1)S(1)}, u32[]{:S(2)}, u32[]{:S(2)}) collective-permute-start(bf16[4,8,4608]{2,1,0:T(8,128)(2,1)S(1)} %get-tuple-element.48), channel_id=1, source_target_pairs={{0,22},{2,20},{4,18},{6,16},{8,30},{10,28},{12,26},{14,24},{16,6},... | collective-permute-start | bytes 884744 | tf_op jit(solution)/shard_map/ppermute | solution.py:233
  58.1 0.0 collective-permute-done.9
  58.1 0.0 collective-permute-start.10
  58.1 0.0 copy-done.1
  58.1 0.0 copy-start.5
  58.1 0.0 copy-start.6
  58.1 3.7 %shard_map.76.keep_ref = f32[384,512]{1,0:T(8,128)S(1)} custom-call(s32[1]{0:T(128)} %bitcast.7.half_ref, bf16[384,4096]{1,0:T(8,128)(2,1)S(1)} %bitcast.13, bf16[4096,1024]{1,0:T(8,128)(2,1)} %weight_ref.3), custom_call_target="tpu_custom_call" | custom-call | tf_op jit(solution)/shard_map/pallas_call | solution.py:111
  61.9 0.0 collective-permute-done.10.arrived_ref
  61.9 0.8 %shard_map.77 = (f32[384,512]{1,0:T(8,128)S(1)}, f32[384,64]{1,0:T(8,128)S(1)}) custom-call(s32[4,6]{1,0:T(4,128)S(1)} %copy-done.6, f32[384,512]{1,0:T(8,128)S(1)} %shard_map.76.keep_ref, f32[384,640]{1,0:T(8,128)S(1)} %shard_map.75.send_ref, f32[384,640]{1,0:T(8,128)S(1)} %collective-permute-done.10.arrived_ref, bf16[128,512]{1,0:T(8,128)(2,1)S(1)} %bitcast.17), custom_call_target="tpu_custom_call" | custom-call | tf_op jit(solution)/shard_map/pallas_call | solution.py:150
  62.7 0.0 collective-permute-done.11
  62.7 0.0 collective-permute-done.12
  62.7 0.0 collective-permute-done.13
  62.7 2.5 %collective-permute-done.14 = bf16[4,8,4608]{2,1,0:T(8,128)(2,1)S(1)} collective-permute-done((bf16[4,8,4608]{2,1,0:T(8,128)(2,1)S(1)}, bf16[4,8,4608]{2,1,0:T(8,128)(2,1)S(1)}, u32[]{:S(2)}, u32[]{:S(2)}) %collective-permute-start.14) | collective-permute-done | bytes 294944 | tf_op jit(solution)/shard_map/ppermute | solution.py:233
  65.4 1.0 %shard_map.78.partial_ref = f32[384,64]{1,0:T(8,128)S(1)} custom-call(bf16[4,96,4096]{2,1,0:T(8,128)(2,1)S(1)} %copy-done.1, bf16[4,64,4608]{2,1,0:T(8,128)(2,1)S(1)} %constant_dynamic-update-slice_fusion.handed_ref.up_ref), custom_call_target="tpu_custom_call" | custom-call | tf_op jit(solution)/shard_map/pallas_call | solution.py:196
  66.4 0.1 collective-permute-start.15
  66.5 1.4 %collective-permute-done.15.other_ref = f32[384,64]{1,0:T(8,128)S(1)} collective-permute-done((f32[384,64]{1,0:T(8,128)S(1)}, f32[384,64]{1,0:T(8,128)S(1)}, u32[]{:S(2)}, u32[]{:S(2)}) %collective-permute-start.15) | collective-permute-done | bytes 98336 | tf_op jit(solution)/shard_map/ppermute | solution.py:252
  67.9 1.0 %shard_map.79 = bf16[4,96,512]{2,1,0:T(8,128)(2,1)} custom-call(f32[384,512]{1,0:T(8,128)S(1)} %get-tuple-element.49.base_ref, f32[384,64]{1,0:T(8,128)S(1)} %get-tuple-element.50.mask_ref, f32[384,64]{1,0:T(8,128)S(1)} %shard_map.78.partial_ref, f32[384,64]{1,0:T(8,128)S(1)} %collective-permute-done.15.other_ref, ...), custom_call_target="tpu_custom_call" | custom-call | tf_op jit(solution)/shard_map/pallas_call | solution.py:178
  (17 shorter events, 0.2 us)
Async XLA Ops:
  0.0 1.2 %copy-start.2 = (bf16[2,64,4096]{2,1,0:T(8,128)(2,1)S(1)}, bf16[2,64,4096]{2,1,0:T(8,128)(2,1)}, u32[]{:S(2)}) copy-start(bf16[2,64,4096]{2,1,0:T(8,128)(2,1)} %param.9) | copy-start | bytes 3145732
  1.2 0.9 %copy-start.4 = (bf16[2,64,512]{2,1,0:T(8,128)(2,1)S(1)}, bf16[2,64,512]{2,1,0:T(8,128)(2,1)}, u32[]{:S(2)}) copy-start(bf16[2,64,512]{2,1,0:T(8,128)(2,1)} %param.10) | copy-start | bytes 393220
  2.1 44.5 %copy-start.3 = (bf16[2,64,4096]{2,1,0:T(8,128)(2,1)S(1)}, bf16[2,64,4096]{2,1,0:T(8,128)(2,1)}, u32[]{:S(2)}) copy-start(bf16[2,64,4096]{2,1,0:T(8,128)(2,1)} %param.9) | copy-start | bytes 3145732
  2.2 13.8 %collective-permute-start = (bf16[2,8,4608]{2,1,0:T(8,128)(2,1)S(1)}, bf16[2,8,4608]{2,1,0:T(8,128)(2,1)S(1)}, u32[]{:S(2)}, u32[]{:S(2)}) collective-permute-start(bf16[2,8,4608]{2,1,0:T(8,128)(2,1)S(1)} %get-tuple-element.32), channel_id=1, source_target_pairs={{0,12},{2,14},{4,8},{6,10},{8,4},{10,6},{12,0},{14,2},{1,13},{3,15... | collective-permute-start | bytes 442376 | tf_op jit(solution)/shard_map/ppermute | solution.py:216
  7.3 9.7 %collective-permute-start.2 = (bf16[2,8,4608]{2,1,0:T(8,128)(2,1)S(1)}, bf16[2,8,4608]{2,1,0:T(8,128)(2,1)S(1)}, u32[]{:S(2)}, u32[]{:S(2)}) collective-permute-start(bf16[2,8,4608]{2,1,0:T(8,128)(2,1)S(1)} %get-tuple-element.32), channel_id=1, source_target_pairs={{0,4},{2,6},{4,0},{6,2},{8,12},{10,14},{12,8},{14,10},{1,5},{3,7},... | collective-permute-start | bytes 442376 | tf_op jit(solution)/shard_map/ppermute | solution.py:216
  7.3 28.4 %collective-permute-start.5 = (bf16[2,8,4608]{2,1,0:T(8,128)(2,1)S(1)}, bf16[2,8,4608]{2,1,0:T(8,128)(2,1)S(1)}, u32[]{:S(2)}, u32[]{:S(2)}) collective-permute-start(bf16[2,8,4608]{2,1,0:T(8,128)(2,1)S(1)} %get-tuple-element.35), channel_id=1, source_target_pairs={{0,10},{2,8},{4,14},{6,12},{8,2},{10,0},{12,6},{14,4},{1,11},{3,9}... | collective-permute-start | bytes 442376 | tf_op jit(solution)/shard_map/ppermute | solution.py:216
  9.0 26.7 %collective-permute-start.1 = (bf16[2,8,4608]{2,1,0:T(8,128)(2,1)S(1)}, bf16[2,8,4608]{2,1,0:T(8,128)(2,1)S(1)}, u32[]{:S(2)}, u32[]{:S(2)}) collective-permute-start(bf16[2,8,4608]{2,1,0:T(8,128)(2,1)S(1)} %get-tuple-element.35), channel_id=1, source_target_pairs={{0,2},{2,0},{4,6},{6,4},{8,10},{10,8},{12,14},{14,12},{1,3},{3,1},... | collective-permute-start | bytes 442376 | tf_op jit(solution)/shard_map/ppermute | solution.py:216
  9.4 26.3 %collective-permute-start.6 = (bf16[2,8,4608]{2,1,0:T(8,128)(2,1)S(1)}, bf16[2,8,4608]{2,1,0:T(8,128)(2,1)S(1)}, u32[]{:S(2)}, u32[]{:S(2)}) collective-permute-start(bf16[2,8,4608]{2,1,0:T(8,128)(2,1)S(1)} %get-tuple-element.36), channel_id=1, source_target_pairs={{0,14},{2,12},{4,10},{6,8},{8,6},{10,4},{12,2},{14,0},{1,15},{3,13... | collective-permute-start | bytes 442376 | tf_op jit(solution)/shard_map/ppermute | solution.py:216
  16.0 19.8 %collective-permute-start.3 = (bf16[2,8,4608]{2,1,0:T(8,128)(2,1)S(1)}, bf16[2,8,4608]{2,1,0:T(8,128)(2,1)S(1)}, u32[]{:S(2)}, u32[]{:S(2)}) collective-permute-start(bf16[2,8,4608]{2,1,0:T(8,128)(2,1)S(1)} %get-tuple-element.36), channel_id=1, source_target_pairs={{0,6},{2,4},{4,2},{6,0},{8,14},{10,12},{12,10},{14,8},{1,7},{3,5},... | collective-permute-start | bytes 442376 | tf_op jit(solution)/shard_map/ppermute | solution.py:216
  17.0 18.7 %collective-permute-start.4 = (bf16[2,8,4608]{2,1,0:T(8,128)(2,1)S(1)}, bf16[2,8,4608]{2,1,0:T(8,128)(2,1)S(1)}, u32[]{:S(2)}, u32[]{:S(2)}) collective-permute-start(bf16[2,8,4608]{2,1,0:T(8,128)(2,1)S(1)} %get-tuple-element.34.rest_0_), channel_id=1, source_target_pairs={{0,8},{2,10},{4,12},{6,14},{8,0},{10,2},{12,4},{14,6},{1,9},{3,11}... | collective-permute-start | bytes 442376 | tf_op jit(solution)/shard_map/ppermute | solution.py:216
  36.6 10.0 %collective-permute-start.7 = (bf16[4,8,4608]{2,1,0:T(8,128)(2,1)S(1)}, bf16[4,8,4608]{2,1,0:T(8,128)(2,1)S(1)}, u32[]{:S(2)}, u32[]{:S(2)}) collective-permute-start(bf16[4,8,4608]{2,1,0:T(8,128)(2,1)S(1)} %get-tuple-element.38), channel_id=1, source_target_pairs={{0,4},{2,6},{4,0},{6,2},{8,12},{10,14},{12,8},{14,10},{16,20},{18,... | collective-permute-start | bytes 884744 | tf_op jit(solution)/shard_map/ppermute | solution.py:233
  36.7 20.0 %collective-permute-start.8 = (bf16[4,8,4608]{2,1,0:T(8,128)(2,1)S(1)}, bf16[4,8,4608]{2,1,0:T(8,128)(2,1)S(1)}, u32[]{:S(2)}, u32[]{:S(2)}) collective-permute-start(bf16[4,8,4608]{2,1,0:T(8,128)(2,1)S(1)} %get-tuple-element.40), channel_id=1, source_target_pairs={{0,2},{2,0},{4,6},{6,4},{8,10},{10,8},{12,14},{14,12},{16,18},{18,... | collective-permute-start | bytes 884744 | tf_op jit(solution)/shard_map/ppermute | solution.py:233
  38.3 19.8 %collective-permute-start.9 = (bf16[4,8,4608]{2,1,0:T(8,128)(2,1)S(1)}, bf16[4,8,4608]{2,1,0:T(8,128)(2,1)S(1)}, u32[]{:S(2)}, u32[]{:S(2)}) collective-permute-start(bf16[4,8,4608]{2,1,0:T(8,128)(2,1)S(1)} %get-tuple-element.41), channel_id=1, source_target_pairs={{0,16},{2,18},{4,20},{6,22},{8,24},{10,26},{12,28},{14,30},{16,0},... | collective-permute-start | bytes 884744 | tf_op jit(solution)/shard_map/ppermute | solution.py:233
  38.8 23.9 %collective-permute-start.11 = (bf16[4,8,4608]{2,1,0:T(8,128)(2,1)S(1)}, bf16[4,8,4608]{2,1,0:T(8,128)(2,1)S(1)}, u32[]{:S(2)}, u32[]{:S(2)}) collective-permute-start(bf16[4,8,4608]{2,1,0:T(8,128)(2,1)S(1)} %get-tuple-element.45), channel_id=1, source_target_pairs={{0,6},{2,4},{4,2},{6,0},{8,14},{10,12},{12,10},{14,8},{16,22},{18,... | collective-permute-start | bytes 884744 | tf_op jit(solution)/shard_map/ppermute | solution.py:233
  40.7 22.0 %collective-permute-start.12 = (bf16[4,8,4608]{2,1,0:T(8,128)(2,1)S(1)}, bf16[4,8,4608]{2,1,0:T(8,128)(2,1)S(1)}, u32[]{:S(2)}, u32[]{:S(2)}) collective-permute-start(bf16[4,8,4608]{2,1,0:T(8,128)(2,1)S(1)} %get-tuple-element.46), channel_id=1, source_target_pairs={{0,18},{2,16},{4,22},{6,20},{8,26},{10,24},{12,30},{14,28},{16,2},... | collective-permute-start | bytes 884744 | tf_op jit(solution)/shard_map/ppermute | solution.py:233
  46.7 16.1 %collective-permute-start.13 = (bf16[4,8,4608]{2,1,0:T(8,128)(2,1)S(1)}, bf16[4,8,4608]{2,1,0:T(8,128)(2,1)S(1)}, u32[]{:S(2)}, u32[]{:S(2)}) collective-permute-start(bf16[4,8,4608]{2,1,0:T(8,128)(2,1)S(1)} %get-tuple-element.47), channel_id=1, source_target_pairs={{0,20},{2,22},{4,16},{6,18},{8,28},{10,30},{12,24},{14,26},{16,4},... | collective-permute-start | bytes 884744 | tf_op jit(solution)/shard_map/ppermute | solution.py:233
  46.7 1.9 %copy-start = (bf16[4,96,4096]{2,1,0:T(8,128)(2,1)S(1)}, bf16[4,96,4096]{2,1,0:T(8,128)(2,1)}, u32[]{:S(2)}) copy-start(bf16[4,96,4096]{2,1,0:T(8,128)(2,1)} %acts_ref.1) | copy-start | bytes 9437188
  48.5 9.5 %copy-start.1 = (bf16[4,96,4096]{2,1,0:T(8,128)(2,1)S(1)}, bf16[4,96,4096]{2,1,0:T(8,128)(2,1)}, u32[]{:S(2)}) copy-start(bf16[4,96,4096]{2,1,0:T(8,128)(2,1)} %acts_ref.1) | copy-start | bytes 9437188
  56.7 8.5 %collective-permute-start.14 = (bf16[4,8,4608]{2,1,0:T(8,128)(2,1)S(1)}, bf16[4,8,4608]{2,1,0:T(8,128)(2,1)S(1)}, u32[]{:S(2)}, u32[]{:S(2)}) collective-permute-start(bf16[4,8,4608]{2,1,0:T(8,128)(2,1)S(1)} %get-tuple-element.48), channel_id=1, source_target_pairs={{0,22},{2,20},{4,18},{6,16},{8,30},{10,28},{12,26},{14,24},{16,6},... | collective-permute-start | bytes 884744 | tf_op jit(solution)/shard_map/ppermute | solution.py:233
  58.1 3.8 %collective-permute-start.10 = (f32[384,640]{1,0:T(8,128)S(1)}, f32[384,640]{1,0:T(8,128)S(1)}, u32[]{:S(2)}, u32[]{:S(2)}) collective-permute-start(f32[384,640]{1,0:T(8,128)S(1)} %shard_map.75.send_ref), channel_id=1, source_target_pairs={{0,1},{1,0},{2,3},{3,2},{4,5},{5,4},{6,7},{7,6},{8,9},{9,8},{10,11... | collective-permute-start | bytes 2949128 | tf_op jit(solution)/shard_map/ppermute | solution.py:240
  58.1 3.8 %copy-start.5 = (bf16[2,64,512]{2,1,0:T(8,128)(2,1)S(1)}, bf16[2,64,512]{2,1,0:T(8,128)(2,1)}, u32[]{:S(2)}) copy-start(bf16[2,64,512]{2,1,0:T(8,128)(2,1)} %param.10) | copy-start | bytes 393220
  58.1 3.8 %copy-start.6 = (s32[4,6]{1,0:T(4,128)S(1)}, s32[4,6]{1,0:T(4,128)}, u32[]{:S(2)}) copy-start(s32[4,6]{1,0:T(4,128)} %slots_ref.1) | copy-start | bytes 292
  66.4 1.5 %collective-permute-start.15 = (f32[384,64]{1,0:T(8,128)S(1)}, f32[384,64]{1,0:T(8,128)S(1)}, u32[]{:S(2)}, u32[]{:S(2)}) collective-permute-start(f32[384,64]{1,0:T(8,128)S(1)} %shard_map.78.partial_ref), channel_id=1, source_target_pairs={{0,1},{1,0},{2,3},{3,2},{4,5},{5,4},{6,7},{7,6},{8,9},{9,8},{10,11... | collective-permute-start | bytes 294920 | tf_op jit(solution)/shard_map/ppermute | solution.py:252

commit v10 on v9

--- a/solution.py
+++ b/solution.py
@@ -165,7 +165,11 @@
     steps, rows, narrow = out_ref.shape
     for step in range(steps):
         here = slice(step * rows, (step + 1) * rows)
-        reduced = ((partial_ref[here] + other_ref[here]) * mask_ref[here]).astype(jnp.bfloat16)
+        if step % 2 == 0:
+            pair = slice(step // 2 * rows, (step // 2 + 1) * rows)
+            both = partial_ref[pair] + other_ref[pair]
+        rank = mask_ref.shape[1]
+        reduced = (both[:, step % 2 * rank:(step % 2 + 1) * rank] * mask_ref[here]).astype(jnp.bfloat16)
         up = up_ref[step, :, up_ref.shape[2] - narrow:]
         low_rank = jnp.dot(reduced, up, preferred_element_type=jnp.float32)
         out_ref[step] = (base_ref[here] + low_rank).astype(out_ref.dtype)
@@ -187,7 +191,9 @@
 def rank_kernel(acts_ref, handed_ref, out_ref):
     steps, rows, wide = acts_ref.shape
     for step in range(steps):
-        out_ref[step * rows:(step + 1) * rows] = contract_last(acts_ref[step], handed_ref[step, :, :wide])
+        place, rank = step // 2 * rows, handed_ref.shape[1]
+        out_ref[place:place + rows, step % 2 * rank:(step % 2 + 1) * rank] = contract_last(
+            acts_ref[step], handed_ref[step, :, :wide])
 
 
 def rank_part(acts, handed):
@@ -195,7 +201,7 @@
     vmem = pl.BlockSpec(memory_space=pltpu.VMEM)
     return pl.pallas_call(
         rank_kernel,
-        out_shape=jax.ShapeDtypeStruct((steps * rows, handed.shape[1]), jnp.float32),
+        out_shape=jax.ShapeDtypeStruct((steps // 2 * rows, 2 * handed.shape[1]), jnp.float32),
         in_specs=[vmem, vmem],
         out_specs=vmem,
         compiler_params=pltpu.CompilerParams(vmem_limit_bytes=16 << 20),
@@ -224,7 +230,7 @@
 
     picked = pick_stripes(asked, banked, steps)
     given = {0: picked[0]}
-    for k in (4, 1, 2, 7, 3, 5, 6):
+    for k in (7, 3, 4, 1, 2, 6, 5):
         pairs = []
         for g in range(groups):
             for i in range(servers):

time: 69.1 us -> 69.2 us (level)
  no operation moved by 1% of the time
where the time goes in v10:
time: 69.2 us; the launch traced here: 68.9 us
  starting transfers between devices  21.2 us (31%)
  blocking collectives  17.6 us (25%)
  Pallas kernels  12.3 us (18%)
  waiting for transfers between devices  10.7 us (15%)
  local copies, waits for them, and re-layouts  5.45 us (8%)
  between operations  0.86 us (1%)
  other arithmetic  0.76 us (1%)
    unnamed x1, blocking collectives  17.6 us
    ppermute x7, starting transfers between devices, body(): lax.ppermute(stripes[k % parts], 'adapter', [(i, i ^ k) for i in range(se...  13.3 us
    ppermute x7, waiting for transfers between devices, body(): given[k] = lax.ppermute(picked[k], ('groups', 'adapter'), pairs)  9.43 us
    pallas_call x2, Pallas kernels, product(): pl.pallas_call(product_kernel, out_shape=out, grid_spec=pltpu.PrefetchSca...  8.43 us
    ppermute x7, starting transfers between devices, body(): given[k] = lax.ppermute(picked[k], ('groups', 'adapter'), pairs)  7.84 us
    unnamed x23, local copies, waits for them, and re-layouts  5.43 us
  transfers between devices with their start and end apart: 16, of which 4 were waited for; matrix products, arithmetic and copies ran while one was open for 3% of the time, Pallas kernels for 13%

profile of v10, /device:TPU:0, one launch (start us, length us, event | category | flops | bytes accessed | tf_op | source)
XLA Modules:
  0.0 68.9 jit_solution(15195378652293557701)
XLA Ops:
  0.0 1.2 %copy-done.2 = bf16[2,64,4096]{2,1,0:T(8,128)(2,1)S(1)} copy-done((bf16[2,64,4096]{2,1,0:T(8,128)(2,1)S(1)}, bf16[2,64,4096]{2,1,0:T(8,128)(2,1)}, u32[]{:S(2)}) %copy-start.2) | copy-done | bytes 1048600
  1.2 0.9 %copy-done.4 = bf16[2,64,512]{2,1,0:T(8,128)(2,1)S(1)} copy-done((bf16[2,64,512]{2,1,0:T(8,128)(2,1)S(1)}, bf16[2,64,512]{2,1,0:T(8,128)(2,1)}, u32[]{:S(2)}) %copy-start.4) | copy-done | bytes 131096
  2.2 5.1 %collective-permute-start = (bf16[2,8,4608]{2,1,0:T(8,128)(2,1)S(1)}, bf16[2,8,4608]{2,1,0:T(8,128)(2,1)S(1)}, u32[]{:S(2)}, u32[]{:S(2)}) collective-permute-start(bf16[2,8,4608]{2,1,0:T(8,128)(2,1)S(1)} %get-tuple-element.32), channel_id=1, source_target_pairs={{0,12},{2,14},{4,8},{6,10},{8,4},{10,6},{12,0},{14,2},{1,13},{3,15... | collective-permute-start | bytes 442376 | tf_op jit(solution)/shard_map/ppermute | solution.py:222
  7.3 0.0 collective-permute-start.2
  7.3 1.7 %collective-permute-start.5 = (bf16[2,8,4608]{2,1,0:T(8,128)(2,1)S(1)}, bf16[2,8,4608]{2,1,0:T(8,128)(2,1)S(1)}, u32[]{:S(2)}, u32[]{:S(2)}) collective-permute-start(bf16[2,8,4608]{2,1,0:T(8,128)(2,1)S(1)} %get-tuple-element.35), channel_id=1, source_target_pairs={{0,10},{2,8},{4,14},{6,12},{8,2},{10,0},{12,6},{14,4},{1,11},{3,9}... | collective-permute-start | bytes 442376 | tf_op jit(solution)/shard_map/ppermute | solution.py:222
  9.0 0.4 collective-permute-start.1
  9.4 4.7 %collective-permute-start.6 = (bf16[2,8,4608]{2,1,0:T(8,128)(2,1)S(1)}, bf16[2,8,4608]{2,1,0:T(8,128)(2,1)S(1)}, u32[]{:S(2)}, u32[]{:S(2)}) collective-permute-start(bf16[2,8,4608]{2,1,0:T(8,128)(2,1)S(1)} %get-tuple-element.36), channel_id=1, source_target_pairs={{0,14},{2,12},{4,10},{6,8},{8,6},{10,4},{12,2},{14,0},{1,15},{3,13... | collective-permute-start | bytes 442376 | tf_op jit(solution)/shard_map/ppermute | solution.py:222
  14.1 1.2 %dynamic-slice = u32[1]{0:T(128)} dynamic-slice(u32[32]{0:T(128)} %constant.14, u32[]{:T(128)S(6)} %add.4), dynamic_slice_sizes={1} | dynamic-slice | bytes 12
  16.0 0.0 collective-permute-done.rest_6_
  16.0 1.0 %collective-permute-start.3 = (bf16[2,8,4608]{2,1,0:T(8,128)(2,1)S(1)}, bf16[2,8,4608]{2,1,0:T(8,128)(2,1)S(1)}, u32[]{:S(2)}, u32[]{:S(2)}) collective-permute-start(bf16[2,8,4608]{2,1,0:T(8,128)(2,1)S(1)} %get-tuple-element.36), channel_id=1, source_target_pairs={{0,6},{2,4},{4,2},{6,0},{8,14},{10,12},{12,10},{14,8},{1,7},{3,5},... | collective-permute-start | bytes 442376 | tf_op jit(solution)/shard_map/ppermute | solution.py:222
  17.0 0.0 collective-permute-done.2.rest_2_
  17.0 0.4 collective-permute-start.4
  17.4 0.8 %fusion = s32[64]{0:T(128)S(1)} fusion(s32[64]{0:T(128)S(1)} %broadcast.4, u32[]{:T(128)} %bitcast.3, s32[4,1]{0,1:T(1,128)} %param.13, s32[4]{0:T(128)} %param.12), kind=kLoop, calls=%fused_computation.9 | loop fusion | flops 8 | bytes 292
  18.1 17.6 %all-reduce.asked_ref = s32[64]{0:T(128)S(1)} all-reduce(s32[64]{0:T(128)S(1)} %fusion), channel_id=2, replica_groups=mesh['groups'=2,'adapter'=8,'tensor'=2] {'groups','adapter'}, use_global_device_ids=true, to_apply=%add | all-reduce | flops 64 | bytes 512
  35.7 0.0 collective-permute-done.4.rest_4_
  35.7 0.0 collective-permute-done.5.rest_5_
  35.7 0.0 collective-permute-done.1.rest_1_
  35.7 0.0 collective-permute-done.6.rest_7_
  35.7 0.0 collective-permute-done.3.rest_3_
  35.8 0.9 %shard_map.74 = (bf16[4,8,4608]{2,1,0:T(8,128)(2,1)S(1)}, bf16[4,8,4608]{2,1,0:T(8,128)(2,1)S(1)}, bf16[4,8,4608]{2,1,0:T(8,128)(2,1)S(1)}, bf16[4,8,4608]{2,1,0...) custom-call(s32[64]{0:T(128)S(1)} %all-reduce.asked_ref, ...), custom_call_target="tpu_custom_call" | custom-call | tf_op jit(solution)/shard_map/pallas_call | solution.py:75
  36.6 0.1 collective-permute-start.7
  36.7 1.6 %collective-permute-start.8 = (bf16[4,8,4608]{2,1,0:T(8,128)(2,1)S(1)}, bf16[4,8,4608]{2,1,0:T(8,128)(2,1)S(1)}, u32[]{:S(2)}, u32[]{:S(2)}) collective-permute-start(bf16[4,8,4608]{2,1,0:T(8,128)(2,1)S(1)} %get-tuple-element.40), channel_id=1, source_target_pairs={{0,2},{2,0},{4,6},{6,4},{8,10},{10,8},{12,14},{14,12},{16,18},{18,... | collective-permute-start | bytes 884744 | tf_op jit(solution)/shard_map/ppermute | solution.py:239
  38.3 0.5 collective-permute-start.9
  38.8 1.9 %collective-permute-start.11 = (bf16[4,8,4608]{2,1,0:T(8,128)(2,1)S(1)}, bf16[4,8,4608]{2,1,0:T(8,128)(2,1)S(1)}, u32[]{:S(2)}, u32[]{:S(2)}) collective-permute-start(bf16[4,8,4608]{2,1,0:T(8,128)(2,1)S(1)} %get-tuple-element.45), channel_id=1, source_target_pairs={{0,6},{2,4},{4,2},{6,0},{8,14},{10,12},{12,10},{14,8},{16,22},{18,... | collective-permute-start | bytes 884744 | tf_op jit(solution)/shard_map/ppermute | solution.py:239
  40.7 2.4 %collective-permute-start.12 = (bf16[4,8,4608]{2,1,0:T(8,128)(2,1)S(1)}, bf16[4,8,4608]{2,1,0:T(8,128)(2,1)S(1)}, u32[]{:S(2)}, u32[]{:S(2)}) collective-permute-start(bf16[4,8,4608]{2,1,0:T(8,128)(2,1)S(1)} %get-tuple-element.46), channel_id=1, source_target_pairs={{0,18},{2,16},{4,22},{6,20},{8,26},{10,24},{12,30},{14,28},{16,2},... | collective-permute-start | bytes 884744 | tf_op jit(solution)/shard_map/ppermute | solution.py:239
  43.2 3.4 %collective-permute-done.7 = bf16[4,8,4608]{2,1,0:T(8,128)(2,1)S(1)} collective-permute-done((bf16[4,8,4608]{2,1,0:T(8,128)(2,1)S(1)}, bf16[4,8,4608]{2,1,0:T(8,128)(2,1)S(1)}, u32[]{:S(2)}, u32[]{:S(2)}) %collective-permute-start.7) | collective-permute-done | bytes 294944 | tf_op jit(solution)/shard_map/ppermute | solution.py:239
  46.7 0.0 collective-permute-start.13
  46.7 0.0 copy-done.3
  46.7 1.9 %copy-done = bf16[4,96,4096]{2,1,0:T(8,128)(2,1)S(1)} copy-done((bf16[4,96,4096]{2,1,0:T(8,128)(2,1)S(1)}, bf16[4,96,4096]{2,1,0:T(8,128)(2,1)}, u32[]{:S(2)}) %copy-start) | copy-done | bytes 3145752
  48.6 4.7 %shard_map.75.send_ref = f32[384,640]{1,0:T(8,128)S(1)} custom-call(s32[1]{0:T(128)} %bitcast.4.half_ref, bf16[384,4096]{1,0:T(8,128)(2,1)S(1)} %bitcast.12, bf16[4096,1024]{1,0:T(8,128)(2,1)} %weight_ref.3, bf16[128,4096]{1,0:T(8,128)(2,1)S(1)} %bitcast.15), custom_call_target="tpu_custom_call" | custom-call | tf_op jit(solution)/shard_map/pallas_call | solution.py:111
  53.3 3.4 %collective-permute-done.8 = bf16[4,8,4608]{2,1,0:T(8,128)(2,1)S(1)} collective-permute-done((bf16[4,8,4608]{2,1,0:T(8,128)(2,1)S(1)}, bf16[4,8,4608]{2,1,0:T(8,128)(2,1)S(1)}, u32[]{:S(2)}, u32[]{:S(2)}) %collective-permute-start.8) | collective-permute-done | bytes 294944 | tf_op jit(solution)/shard_map/ppermute | solution.py:239
  56.7 1.3 %collective-permute-start.14 = (bf16[4,8,4608]{2,1,0:T(8,128)(2,1)S(1)}, bf16[4,8,4608]{2,1,0:T(8,128)(2,1)S(1)}, u32[]{:S(2)}, u32[]{:S(2)}) collective-permute-start(bf16[4,8,4608]{2,1,0:T(8,128)(2,1)S(1)} %get-tuple-element.48), channel_id=1, source_target_pairs={{0,22},{2,20},{4,18},{6,16},{8,30},{10,28},{12,26},{14,24},{16,6},... | collective-permute-start | bytes 884744 | tf_op jit(solution)/shard_map/ppermute | solution.py:239
  58.1 0.0 collective-permute-done.9
  58.1 0.0 collective-permute-start.10
  58.1 0.0 copy-done.1
  58.1 0.0 copy-start.5
  58.1 0.0 copy-start.6
  58.1 3.7 %shard_map.76.keep_ref = f32[384,512]{1,0:T(8,128)S(1)} custom-call(s32[1]{0:T(128)} %bitcast.7.half_ref, bf16[384,4096]{1,0:T(8,128)(2,1)S(1)} %bitcast.13, bf16[4096,1024]{1,0:T(8,128)(2,1)} %weight_ref.3), custom_call_target="tpu_custom_call" | custom-call | tf_op jit(solution)/shard_map/pallas_call | solution.py:111
  61.9 0.0 collective-permute-done.10.arrived_ref
  61.9 0.8 %shard_map.77 = (f32[384,512]{1,0:T(8,128)S(1)}, f32[384,64]{1,0:T(8,128)S(1)}) custom-call(s32[4,6]{1,0:T(4,128)S(1)} %copy-done.6, f32[384,512]{1,0:T(8,128)S(1)} %shard_map.76.keep_ref, f32[384,640]{1,0:T(8,128)S(1)} %shard_map.75.send_ref, f32[384,640]{1,0:T(8,128)S(1)} %collective-permute-done.10.arrived_ref, bf16[128,512]{1,0:T(8,128)(2,1)S(1)} %bitcast.17), custom_call_target="tpu_custom_call" | custom-call | tf_op jit(solution)/shard_map/pallas_call | solution.py:150
  62.7 0.0 collective-permute-done.11
  62.7 0.0 collective-permute-done.12
  62.7 0.0 collective-permute-done.13
  62.7 2.5 %collective-permute-done.14 = bf16[4,8,4608]{2,1,0:T(8,128)(2,1)S(1)} collective-permute-done((bf16[4,8,4608]{2,1,0:T(8,128)(2,1)S(1)}, bf16[4,8,4608]{2,1,0:T(8,128)(2,1)S(1)}, u32[]{:S(2)}, u32[]{:S(2)}) %collective-permute-start.14) | collective-permute-done | bytes 294944 | tf_op jit(solution)/shard_map/ppermute | solution.py:239
  65.4 1.0 %shard_map.78.partial_ref = f32[192,128]{1,0:T(8,128)S(1)} custom-call(bf16[4,96,4096]{2,1,0:T(8,128)(2,1)S(1)} %copy-done.1, bf16[4,64,4608]{2,1,0:T(8,128)(2,1)S(1)} %constant_dynamic-update-slice_fusion.handed_ref.up_ref), custom_call_target="tpu_custom_call" | custom-call | tf_op jit(solution)/shard_map/pallas_call | solution.py:202
  66.4 0.1 collective-permute-start.15
  66.5 1.3 %collective-permute-done.15.other_ref = f32[192,128]{1,0:T(8,128)S(1)} collective-permute-done((f32[192,128]{1,0:T(8,128)S(1)}, f32[192,128]{1,0:T(8,128)S(1)}, u32[]{:S(2)}, u32[]{:S(2)}) %collective-permute-start.15) | collective-permute-done | bytes 98336 | tf_op jit(solution)/shard_map/ppermute | solution.py:258
  67.8 1.1 %shard_map.79 = bf16[4,96,512]{2,1,0:T(8,128)(2,1)} custom-call(f32[384,512]{1,0:T(8,128)S(1)} %get-tuple-element.49.base_ref, f32[384,64]{1,0:T(8,128)S(1)} %get-tuple-element.50.mask_ref, f32[192,128]{1,0:T(8,128)S(1)} %shard_map.78.partial_ref, f32[192,128]{1,0:T(8,128)S(1)} %collective-permute-done.15.other_ref, ...), custom_call_target="tpu_custom_call" | custom-call | tf_op jit(solution)/shard_map/pallas_call | solution.py:182
  (17 shorter events, 0.2 us)
Async XLA Ops:
  0.0 1.2 %copy-start.2 = (bf16[2,64,4096]{2,1,0:T(8,128)(2,1)S(1)}, bf16[2,64,4096]{2,1,0:T(8,128)(2,1)}, u32[]{:S(2)}) copy-start(bf16[2,64,4096]{2,1,0:T(8,128)(2,1)} %param.9) | copy-start | bytes 3145732
  1.2 0.9 %copy-start.4 = (bf16[2,64,512]{2,1,0:T(8,128)(2,1)S(1)}, bf16[2,64,512]{2,1,0:T(8,128)(2,1)}, u32[]{:S(2)}) copy-start(bf16[2,64,512]{2,1,0:T(8,128)(2,1)} %param.10) | copy-start | bytes 393220
  2.1 44.5 %copy-start.3 = (bf16[2,64,4096]{2,1,0:T(8,128)(2,1)S(1)}, bf16[2,64,4096]{2,1,0:T(8,128)(2,1)}, u32[]{:S(2)}) copy-start(bf16[2,64,4096]{2,1,0:T(8,128)(2,1)} %param.9) | copy-start | bytes 3145732
  2.2 13.8 %collective-permute-start = (bf16[2,8,4608]{2,1,0:T(8,128)(2,1)S(1)}, bf16[2,8,4608]{2,1,0:T(8,128)(2,1)S(1)}, u32[]{:S(2)}, u32[]{:S(2)}) collective-permute-start(bf16[2,8,4608]{2,1,0:T(8,128)(2,1)S(1)} %get-tuple-element.32), channel_id=1, source_target_pairs={{0,12},{2,14},{4,8},{6,10},{8,4},{10,6},{12,0},{14,2},{1,13},{3,15... | collective-permute-start | bytes 442376 | tf_op jit(solution)/shard_map/ppermute | solution.py:222
  7.3 9.7 %collective-permute-start.2 = (bf16[2,8,4608]{2,1,0:T(8,128)(2,1)S(1)}, bf16[2,8,4608]{2,1,0:T(8,128)(2,1)S(1)}, u32[]{:S(2)}, u32[]{:S(2)}) collective-permute-start(bf16[2,8,4608]{2,1,0:T(8,128)(2,1)S(1)} %get-tuple-element.32), channel_id=1, source_target_pairs={{0,4},{2,6},{4,0},{6,2},{8,12},{10,14},{12,8},{14,10},{1,5},{3,7},... | collective-permute-start | bytes 442376 | tf_op jit(solution)/shard_map/ppermute | solution.py:222
  7.3 28.4 %collective-permute-start.5 = (bf16[2,8,4608]{2,1,0:T(8,128)(2,1)S(1)}, bf16[2,8,4608]{2,1,0:T(8,128)(2,1)S(1)}, u32[]{:S(2)}, u32[]{:S(2)}) collective-permute-start(bf16[2,8,4608]{2,1,0:T(8,128)(2,1)S(1)} %get-tuple-element.35), channel_id=1, source_target_pairs={{0,10},{2,8},{4,14},{6,12},{8,2},{10,0},{12,6},{14,4},{1,11},{3,9}... | collective-permute-start | bytes 442376 | tf_op jit(solution)/shard_map/ppermute | solution.py:222
  9.0 26.7 %collective-permute-start.1 = (bf16[2,8,4608]{2,1,0:T(8,128)(2,1)S(1)}, bf16[2,8,4608]{2,1,0:T(8,128)(2,1)S(1)}, u32[]{:S(2)}, u32[]{:S(2)}) collective-permute-start(bf16[2,8,4608]{2,1,0:T(8,128)(2,1)S(1)} %get-tuple-element.35), channel_id=1, source_target_pairs={{0,2},{2,0},{4,6},{6,4},{8,10},{10,8},{12,14},{14,12},{1,3},{3,1},... | collective-permute-start | bytes 442376 | tf_op jit(solution)/shard_map/ppermute | solution.py:222
  9.4 26.3 %collective-permute-start.6 = (bf16[2,8,4608]{2,1,0:T(8,128)(2,1)S(1)}, bf16[2,8,4608]{2,1,0:T(8,128)(2,1)S(1)}, u32[]{:S(2)}, u32[]{:S(2)}) collective-permute-start(bf16[2,8,4608]{2,1,0:T(8,128)(2,1)S(1)} %get-tuple-element.36), channel_id=1, source_target_pairs={{0,14},{2,12},{4,10},{6,8},{8,6},{10,4},{12,2},{14,0},{1,15},{3,13... | collective-permute-start | bytes 442376 | tf_op jit(solution)/shard_map/ppermute | solution.py:222
  16.0 19.8 %collective-permute-start.3 = (bf16[2,8,4608]{2,1,0:T(8,128)(2,1)S(1)}, bf16[2,8,4608]{2,1,0:T(8,128)(2,1)S(1)}, u32[]{:S(2)}, u32[]{:S(2)}) collective-permute-start(bf16[2,8,4608]{2,1,0:T(8,128)(2,1)S(1)} %get-tuple-element.36), channel_id=1, source_target_pairs={{0,6},{2,4},{4,2},{6,0},{8,14},{10,12},{12,10},{14,8},{1,7},{3,5},... | collective-permute-start | bytes 442376 | tf_op jit(solution)/shard_map/ppermute | solution.py:222
  17.0 18.7 %collective-permute-start.4 = (bf16[2,8,4608]{2,1,0:T(8,128)(2,1)S(1)}, bf16[2,8,4608]{2,1,0:T(8,128)(2,1)S(1)}, u32[]{:S(2)}, u32[]{:S(2)}) collective-permute-start(bf16[2,8,4608]{2,1,0:T(8,128)(2,1)S(1)} %get-tuple-element.34.rest_0_), channel_id=1, source_target_pairs={{0,8},{2,10},{4,12},{6,14},{8,0},{10,2},{12,4},{14,6},{1,9},{3,11}... | collective-permute-start | bytes 442376 | tf_op jit(solution)/shard_map/ppermute | solution.py:222
  36.6 10.0 %collective-permute-start.7 = (bf16[4,8,4608]{2,1,0:T(8,128)(2,1)S(1)}, bf16[4,8,4608]{2,1,0:T(8,128)(2,1)S(1)}, u32[]{:S(2)}, u32[]{:S(2)}) collective-permute-start(bf16[4,8,4608]{2,1,0:T(8,128)(2,1)S(1)} %get-tuple-element.38), channel_id=1, source_target_pairs={{0,4},{2,6},{4,0},{6,2},{8,12},{10,14},{12,8},{14,10},{16,20},{18,... | collective-permute-start | bytes 884744 | tf_op jit(solution)/shard_map/ppermute | solution.py:239
  36.7 20.0 %collective-permute-start.8 = (bf16[4,8,4608]{2,1,0:T(8,128)(2,1)S(1)}, bf16[4,8,4608]{2,1,0:T(8,128)(2,1)S(1)}, u32[]{:S(2)}, u32[]{:S(2)}) collective-permute-start(bf16[4,8,4608]{2,1,0:T(8,128)(2,1)S(1)} %get-tuple-element.40), channel_id=1, source_target_pairs={{0,2},{2,0},{4,6},{6,4},{8,10},{10,8},{12,14},{14,12},{16,18},{18,... | collective-permute-start | bytes 884744 | tf_op jit(solution)/shard_map/ppermute | solution.py:239
  38.3 19.8 %collective-permute-start.9 = (bf16[4,8,4608]{2,1,0:T(8,128)(2,1)S(1)}, bf16[4,8,4608]{2,1,0:T(8,128)(2,1)S(1)}, u32[]{:S(2)}, u32[]{:S(2)}) collective-permute-start(bf16[4,8,4608]{2,1,0:T(8,128)(2,1)S(1)} %get-tuple-element.41), channel_id=1, source_target_pairs={{0,16},{2,18},{4,20},{6,22},{8,24},{10,26},{12,28},{14,30},{16,0},... | collective-permute-start | bytes 884744 | tf_op jit(solution)/shard_map/ppermute | solution.py:239
  38.8 23.9 %collective-permute-start.11 = (bf16[4,8,4608]{2,1,0:T(8,128)(2,1)S(1)}, bf16[4,8,4608]{2,1,0:T(8,128)(2,1)S(1)}, u32[]{:S(2)}, u32[]{:S(2)}) collective-permute-start(bf16[4,8,4608]{2,1,0:T(8,128)(2,1)S(1)} %get-tuple-element.45), channel_id=1, source_target_pairs={{0,6},{2,4},{4,2},{6,0},{8,14},{10,12},{12,10},{14,8},{16,22},{18,... | collective-permute-start | bytes 884744 | tf_op jit(solution)/shard_map/ppermute | solution.py:239
  40.7 22.0 %collective-permute-start.12 = (bf16[4,8,4608]{2,1,0:T(8,128)(2,1)S(1)}, bf16[4,8,4608]{2,1,0:T(8,128)(2,1)S(1)}, u32[]{:S(2)}, u32[]{:S(2)}) collective-permute-start(bf16[4,8,4608]{2,1,0:T(8,128)(2,1)S(1)} %get-tuple-element.46), channel_id=1, source_target_pairs={{0,18},{2,16},{4,22},{6,20},{8,26},{10,24},{12,30},{14,28},{16,2},... | collective-permute-start | bytes 884744 | tf_op jit(solution)/shard_map/ppermute | solution.py:239
  46.7 16.1 %collective-permute-start.13 = (bf16[4,8,4608]{2,1,0:T(8,128)(2,1)S(1)}, bf16[4,8,4608]{2,1,0:T(8,128)(2,1)S(1)}, u32[]{:S(2)}, u32[]{:S(2)}) collective-permute-start(bf16[4,8,4608]{2,1,0:T(8,128)(2,1)S(1)} %get-tuple-element.47), channel_id=1, source_target_pairs={{0,20},{2,22},{4,16},{6,18},{8,28},{10,30},{12,24},{14,26},{16,4},... | collective-permute-start | bytes 884744 | tf_op jit(solution)/shard_map/ppermute | solution.py:239
  46.7 1.9 %copy-start = (bf16[4,96,4096]{2,1,0:T(8,128)(2,1)S(1)}, bf16[4,96,4096]{2,1,0:T(8,128)(2,1)}, u32[]{:S(2)}) copy-start(bf16[4,96,4096]{2,1,0:T(8,128)(2,1)} %acts_ref.1) | copy-start | bytes 9437188
  48.5 9.5 %copy-start.1 = (bf16[4,96,4096]{2,1,0:T(8,128)(2,1)S(1)}, bf16[4,96,4096]{2,1,0:T(8,128)(2,1)}, u32[]{:S(2)}) copy-start(bf16[4,96,4096]{2,1,0:T(8,128)(2,1)} %acts_ref.1) | copy-start | bytes 9437188
  56.7 8.5 %collective-permute-start.14 = (bf16[4,8,4608]{2,1,0:T(8,128)(2,1)S(1)}, bf16[4,8,4608]{2,1,0:T(8,128)(2,1)S(1)}, u32[]{:S(2)}, u32[]{:S(2)}) collective-permute-start(bf16[4,8,4608]{2,1,0:T(8,128)(2,1)S(1)} %get-tuple-element.48), channel_id=1, source_target_pairs={{0,22},{2,20},{4,18},{6,16},{8,30},{10,28},{12,26},{14,24},{16,6},... | collective-permute-start | bytes 884744 | tf_op jit(solution)/shard_map/ppermute | solution.py:239
  58.1 3.8 %collective-permute-start.10 = (f32[384,640]{1,0:T(8,128)S(1)}, f32[384,640]{1,0:T(8,128)S(1)}, u32[]{:S(2)}, u32[]{:S(2)}) collective-permute-start(f32[384,640]{1,0:T(8,128)S(1)} %shard_map.75.send_ref), channel_id=1, source_target_pairs={{0,1},{1,0},{2,3},{3,2},{4,5},{5,4},{6,7},{7,6},{8,9},{9,8},{10,11... | collective-permute-start | bytes 2949128 | tf_op jit(solution)/shard_map/ppermute | solution.py:246
  58.1 3.8 %copy-start.5 = (bf16[2,64,512]{2,1,0:T(8,128)(2,1)S(1)}, bf16[2,64,512]{2,1,0:T(8,128)(2,1)}, u32[]{:S(2)}) copy-start(bf16[2,64,512]{2,1,0:T(8,128)(2,1)} %param.10) | copy-start | bytes 393220
  58.1 3.8 %copy-start.6 = (s32[4,6]{1,0:T(4,128)S(1)}, s32[4,6]{1,0:T(4,128)}, u32[]{:S(2)}) copy-start(s32[4,6]{1,0:T(4,128)} %slots_ref.1) | copy-start | bytes 292
  66.4 1.4 %collective-permute-start.15 = (f32[192,128]{1,0:T(8,128)S(1)}, f32[192,128]{1,0:T(8,128)S(1)}, u32[]{:S(2)}, u32[]{:S(2)}) collective-permute-start(f32[192,128]{1,0:T(8,128)S(1)} %shard_map.78.partial_ref), channel_id=1, source_target_pairs={{0,1},{1,0},{2,3},{3,2},{4,5},{5,4},{6,7},{7,6},{8,9},{9,8},{10,11... | collective-permute-start | bytes 294920 | tf_op jit(solution)/shard_map/ppermute | solution.py:258

commit v11 on v10

--- a/solution.py
+++ b/solution.py
@@ -220,7 +220,7 @@
     banked = {0: stripes[0]}
     for k in [1, 2, 3, 4, 5, 6, 7, *range(STRIPES, servers)]:
         banked[k] = lax.ppermute(stripes[k % parts], "adapter", [(i, i ^ k) for i in range(servers)])
-    early = [6]
+    early = [2, 6]
     transfer_slot, *arrived = lax.optimization_barrier((transfer_slot, *[banked[k] for k in early]))
     banked.update(zip(early, arrived))
     banked = [banked[k] for k in range(servers)]

time: 69.2 us -> 69.2 us (level)
  no operation moved by 1% of the time
where the time goes in v11:
time: 69.2 us; the launch traced here: 68.9 us
  starting transfers between devices  21.2 us (31%)
  blocking collectives  17.6 us (25%)
  Pallas kernels  12.3 us (18%)
  waiting for transfers between devices  10.7 us (15%)
  local copies, waits for them, and re-layouts  5.45 us (8%)
  between operations  0.86 us (1%)
  other arithmetic  0.76 us (1%)
    unnamed x1, blocking collectives  17.6 us
    ppermute x7, starting transfers between devices, body(): lax.ppermute(stripes[k % parts], 'adapter', [(i, i ^ k) for i in range(se...  13.3 us
    ppermute x7, waiting for transfers between devices, body(): given[k] = lax.ppermute(picked[k], ('groups', 'adapter'), pairs)  9.43 us
    pallas_call x2, Pallas kernels, product(): pl.pallas_call(product_kernel, out_shape=out, grid_spec=pltpu.PrefetchSca...  8.43 us
    ppermute x7, starting transfers between devices, body(): given[k] = lax.ppermute(picked[k], ('groups', 'adapter'), pairs)  7.84 us
    unnamed x23, local copies, waits for them, and re-layouts  5.43 us
  transfers between devices with their start and end apart: 16, of which 4 were waited for; matrix products, arithmetic and copies ran while one was open for 3% of the time, Pallas kernels for 13%

profile of v11, /device:TPU:0, one launch (start us, length us, event | category | flops | bytes accessed | tf_op | source)
XLA Modules:
  0.0 68.9 jit_solution(15195378652293557701)
XLA Ops:
  0.0 1.2 %copy-done.2 = bf16[2,64,4096]{2,1,0:T(8,128)(2,1)S(1)} copy-done((bf16[2,64,4096]{2,1,0:T(8,128)(2,1)S(1)}, bf16[2,64,4096]{2,1,0:T(8,128)(2,1)}, u32[]{:S(2)}) %copy-start.2) | copy-done | bytes 1048600
  1.2 0.9 %copy-done.4 = bf16[2,64,512]{2,1,0:T(8,128)(2,1)S(1)} copy-done((bf16[2,64,512]{2,1,0:T(8,128)(2,1)S(1)}, bf16[2,64,512]{2,1,0:T(8,128)(2,1)}, u32[]{:S(2)}) %copy-start.4) | copy-done | bytes 131096
  2.2 5.1 %collective-permute-start.1 = (bf16[2,8,4608]{2,1,0:T(8,128)(2,1)S(1)}, bf16[2,8,4608]{2,1,0:T(8,128)(2,1)S(1)}, u32[]{:S(2)}, u32[]{:S(2)}) collective-permute-start(bf16[2,8,4608]{2,1,0:T(8,128)(2,1)S(1)} %get-tuple-element.33), channel_id=1, source_target_pairs={{0,12},{2,14},{4,8},{6,10},{8,4},{10,6},{12,0},{14,2},{1,13},{3,15... | collective-permute-start | bytes 442376 | tf_op jit(solution)/shard_map/ppermute | solution.py:222
  7.3 0.0 collective-permute-start
  7.3 1.7 %collective-permute-start.5 = (bf16[2,8,4608]{2,1,0:T(8,128)(2,1)S(1)}, bf16[2,8,4608]{2,1,0:T(8,128)(2,1)S(1)}, u32[]{:S(2)}, u32[]{:S(2)}) collective-permute-start(bf16[2,8,4608]{2,1,0:T(8,128)(2,1)S(1)} %get-tuple-element.36), channel_id=1, source_target_pairs={{0,10},{2,8},{4,14},{6,12},{8,2},{10,0},{12,6},{14,4},{1,11},{3,9}... | collective-permute-start | bytes 442376 | tf_op jit(solution)/shard_map/ppermute | solution.py:222
  9.0 0.4 collective-permute-start.2
  9.4 4.7 %collective-permute-start.6 = (bf16[2,8,4608]{2,1,0:T(8,128)(2,1)S(1)}, bf16[2,8,4608]{2,1,0:T(8,128)(2,1)S(1)}, u32[]{:S(2)}, u32[]{:S(2)}) collective-permute-start(bf16[2,8,4608]{2,1,0:T(8,128)(2,1)S(1)} %get-tuple-element.38), channel_id=1, source_target_pairs={{0,14},{2,12},{4,10},{6,8},{8,6},{10,4},{12,2},{14,0},{1,15},{3,13... | collective-permute-start | bytes 442376 | tf_op jit(solution)/shard_map/ppermute | solution.py:222
  14.1 1.2 %dynamic-slice = u32[1]{0:T(128)} dynamic-slice(u32[32]{0:T(128)} %constant.14, u32[]{:T(128)S(6)} %add.4), dynamic_slice_sizes={1} | dynamic-slice | bytes 12
  16.0 0.0 collective-permute-done.1.rest_6_
  16.0 1.0 %collective-permute-start.3 = (bf16[2,8,4608]{2,1,0:T(8,128)(2,1)S(1)}, bf16[2,8,4608]{2,1,0:T(8,128)(2,1)S(1)}, u32[]{:S(2)}, u32[]{:S(2)}) collective-permute-start(bf16[2,8,4608]{2,1,0:T(8,128)(2,1)S(1)} %get-tuple-element.38), channel_id=1, source_target_pairs={{0,6},{2,4},{4,2},{6,0},{8,14},{10,12},{12,10},{14,8},{1,7},{3,5},... | collective-permute-start | bytes 442376 | tf_op jit(solution)/shard_map/ppermute | solution.py:222
  17.0 0.0 collective-permute-done.rest_2_
  17.0 0.4 collective-permute-start.4
  17.4 0.8 %fusion = s32[64]{0:T(128)S(1)} fusion(s32[64]{0:T(128)S(1)} %broadcast.4, u32[]{:T(128)} %bitcast.3, s32[4,1]{0,1:T(1,128)} %param.13, s32[4]{0:T(128)} %param.12), kind=kLoop, calls=%fused_computation.9 | loop fusion | flops 8 | bytes 292
  18.1 17.6 %all-reduce.asked_ref = s32[64]{0:T(128)S(1)} all-reduce(s32[64]{0:T(128)S(1)} %fusion), channel_id=2, replica_groups=mesh['groups'=2,'adapter'=8,'tensor'=2] {'groups','adapter'}, use_global_device_ids=true, to_apply=%add | all-reduce | flops 64 | bytes 512
  35.7 0.0 collective-permute-done.4.rest_4_
  35.7 0.0 collective-permute-done.5.rest_5_
  35.7 0.0 collective-permute-done.2.rest_1_
  35.7 0.0 collective-permute-done.6.rest_7_
  35.7 0.0 collective-permute-done.3.rest_3_
  35.8 0.9 %shard_map.74 = (bf16[4,8,4608]{2,1,0:T(8,128)(2,1)S(1)}, bf16[4,8,4608]{2,1,0:T(8,128)(2,1)S(1)}, bf16[4,8,4608]{2,1,0:T(8,128)(2,1)S(1)}, bf16[4,8,4608]{2,1,0...) custom-call(s32[64]{0:T(128)S(1)} %all-reduce.asked_ref, ...), custom_call_target="tpu_custom_call" | custom-call | tf_op jit(solution)/shard_map/pallas_call | solution.py:75
  36.6 0.1 collective-permute-start.7
  36.7 1.6 %collective-permute-start.8 = (bf16[4,8,4608]{2,1,0:T(8,128)(2,1)S(1)}, bf16[4,8,4608]{2,1,0:T(8,128)(2,1)S(1)}, u32[]{:S(2)}, u32[]{:S(2)}) collective-permute-start(bf16[4,8,4608]{2,1,0:T(8,128)(2,1)S(1)} %get-tuple-element.42), channel_id=1, source_target_pairs={{0,2},{2,0},{4,6},{6,4},{8,10},{10,8},{12,14},{14,12},{16,18},{18,... | collective-permute-start | bytes 884744 | tf_op jit(solution)/shard_map/ppermute | solution.py:239
  38.3 0.5 collective-permute-start.9
  38.8 1.9 %collective-permute-start.11 = (bf16[4,8,4608]{2,1,0:T(8,128)(2,1)S(1)}, bf16[4,8,4608]{2,1,0:T(8,128)(2,1)S(1)}, u32[]{:S(2)}, u32[]{:S(2)}) collective-permute-start(bf16[4,8,4608]{2,1,0:T(8,128)(2,1)S(1)} %get-tuple-element.47), channel_id=1, source_target_pairs={{0,6},{2,4},{4,2},{6,0},{8,14},{10,12},{12,10},{14,8},{16,22},{18,... | collective-permute-start | bytes 884744 | tf_op jit(solution)/shard_map/ppermute | solution.py:239
  40.7 2.4 %collective-permute-start.12 = (bf16[4,8,4608]{2,1,0:T(8,128)(2,1)S(1)}, bf16[4,8,4608]{2,1,0:T(8,128)(2,1)S(1)}, u32[]{:S(2)}, u32[]{:S(2)}) collective-permute-start(bf16[4,8,4608]{2,1,0:T(8,128)(2,1)S(1)} %get-tuple-element.48), channel_id=1, source_target_pairs={{0,18},{2,16},{4,22},{6,20},{8,26},{10,24},{12,30},{14,28},{16,2},... | collective-permute-start | bytes 884744 | tf_op jit(solution)/shard_map/ppermute | solution.py:239
  43.2 3.4 %collective-permute-done.7 = bf16[4,8,4608]{2,1,0:T(8,128)(2,1)S(1)} collective-permute-done((bf16[4,8,4608]{2,1,0:T(8,128)(2,1)S(1)}, bf16[4,8,4608]{2,1,0:T(8,128)(2,1)S(1)}, u32[]{:S(2)}, u32[]{:S(2)}) %collective-permute-start.7) | collective-permute-done | bytes 294944 | tf_op jit(solution)/shard_map/ppermute | solution.py:239
  46.7 0.0 collective-permute-start.13
  46.7 0.0 copy-done.3
  46.7 1.9 %copy-done = bf16[4,96,4096]{2,1,0:T(8,128)(2,1)S(1)} copy-done((bf16[4,96,4096]{2,1,0:T(8,128)(2,1)S(1)}, bf16[4,96,4096]{2,1,0:T(8,128)(2,1)}, u32[]{:S(2)}) %copy-start) | copy-done | bytes 3145752
  48.6 4.7 %shard_map.75.send_ref = f32[384,640]{1,0:T(8,128)S(1)} custom-call(s32[1]{0:T(128)} %bitcast.4.half_ref, bf16[384,4096]{1,0:T(8,128)(2,1)S(1)} %bitcast.12, bf16[4096,1024]{1,0:T(8,128)(2,1)} %weight_ref.3, bf16[128,4096]{1,0:T(8,128)(2,1)S(1)} %bitcast.15), custom_call_target="tpu_custom_call" | custom-call | tf_op jit(solution)/shard_map/pallas_call | solution.py:111
  53.3 3.4 %collective-permute-done.8 = bf16[4,8,4608]{2,1,0:T(8,128)(2,1)S(1)} collective-permute-done((bf16[4,8,4608]{2,1,0:T(8,128)(2,1)S(1)}, bf16[4,8,4608]{2,1,0:T(8,128)(2,1)S(1)}, u32[]{:S(2)}, u32[]{:S(2)}) %collective-permute-start.8) | collective-permute-done | bytes 294944 | tf_op jit(solution)/shard_map/ppermute | solution.py:239
  56.7 1.3 %collective-permute-start.14 = (bf16[4,8,4608]{2,1,0:T(8,128)(2,1)S(1)}, bf16[4,8,4608]{2,1,0:T(8,128)(2,1)S(1)}, u32[]{:S(2)}, u32[]{:S(2)}) collective-permute-start(bf16[4,8,4608]{2,1,0:T(8,128)(2,1)S(1)} %get-tuple-element.50), channel_id=1, source_target_pairs={{0,22},{2,20},{4,18},{6,16},{8,30},{10,28},{12,26},{14,24},{16,6},... | collective-permute-start | bytes 884744 | tf_op jit(solution)/shard_map/ppermute | solution.py:239
  58.1 0.0 collective-permute-done.9
  58.1 0.0 collective-permute-start.10
  58.1 0.0 copy-done.1
  58.1 0.0 copy-start.5
  58.1 0.0 copy-start.6
  58.1 3.7 %shard_map.76.keep_ref = f32[384,512]{1,0:T(8,128)S(1)} custom-call(s32[1]{0:T(128)} %bitcast.7.half_ref, bf16[384,4096]{1,0:T(8,128)(2,1)S(1)} %bitcast.13, bf16[4096,1024]{1,0:T(8,128)(2,1)} %weight_ref.3), custom_call_target="tpu_custom_call" | custom-call | tf_op jit(solution)/shard_map/pallas_call | solution.py:111
  61.9 0.0 collective-permute-done.10.arrived_ref
  61.9 0.8 %shard_map.77 = (f32[384,512]{1,0:T(8,128)S(1)}, f32[384,64]{1,0:T(8,128)S(1)}) custom-call(s32[4,6]{1,0:T(4,128)S(1)} %copy-done.6, f32[384,512]{1,0:T(8,128)S(1)} %shard_map.76.keep_ref, f32[384,640]{1,0:T(8,128)S(1)} %shard_map.75.send_ref, f32[384,640]{1,0:T(8,128)S(1)} %collective-permute-done.10.arrived_ref, bf16[128,512]{1,0:T(8,128)(2,1)S(1)} %bitcast.17), custom_call_target="tpu_custom_call" | custom-call | tf_op jit(solution)/shard_map/pallas_call | solution.py:150
  62.7 0.0 collective-permute-done.11
  62.7 0.0 collective-permute-done.12
  62.7 0.0 collective-permute-done.13
  62.7 2.5 %collective-permute-done.14 = bf16[4,8,4608]{2,1,0:T(8,128)(2,1)S(1)} collective-permute-done((bf16[4,8,4608]{2,1,0:T(8,128)(2,1)S(1)}, bf16[4,8,4608]{2,1,0:T(8,128)(2,1)S(1)}, u32[]{:S(2)}, u32[]{:S(2)}) %collective-permute-start.14) | collective-permute-done | bytes 294944 | tf_op jit(solution)/shard_map/ppermute | solution.py:239
  65.4 1.0 %shard_map.78.partial_ref = f32[192,128]{1,0:T(8,128)S(1)} custom-call(bf16[4,96,4096]{2,1,0:T(8,128)(2,1)S(1)} %copy-done.1, bf16[4,64,4608]{2,1,0:T(8,128)(2,1)S(1)} %constant_dynamic-update-slice_fusion.handed_ref.up_ref), custom_call_target="tpu_custom_call" | custom-call | tf_op jit(solution)/shard_map/pallas_call | solution.py:202
  66.4 0.1 collective-permute-start.15
  66.5 1.3 %collective-permute-done.15.other_ref = f32[192,128]{1,0:T(8,128)S(1)} collective-permute-done((f32[192,128]{1,0:T(8,128)S(1)}, f32[192,128]{1,0:T(8,128)S(1)}, u32[]{:S(2)}, u32[]{:S(2)}) %collective-permute-start.15) | collective-permute-done | bytes 98336 | tf_op jit(solution)/shard_map/ppermute | solution.py:258
  67.8 1.1 %shard_map.79 = bf16[4,96,512]{2,1,0:T(8,128)(2,1)} custom-call(f32[384,512]{1,0:T(8,128)S(1)} %get-tuple-element.51.base_ref, f32[384,64]{1,0:T(8,128)S(1)} %get-tuple-element.52.mask_ref, f32[192,128]{1,0:T(8,128)S(1)} %shard_map.78.partial_ref, f32[192,128]{1,0:T(8,128)S(1)} %collective-permute-done.15.other_ref, ...), custom_call_target="tpu_custom_call" | custom-call | tf_op jit(solution)/shard_map/pallas_call | solution.py:182
  (17 shorter events, 0.2 us)
Async XLA Ops:
  0.0 1.2 %copy-start.2 = (bf16[2,64,4096]{2,1,0:T(8,128)(2,1)S(1)}, bf16[2,64,4096]{2,1,0:T(8,128)(2,1)}, u32[]{:S(2)}) copy-start(bf16[2,64,4096]{2,1,0:T(8,128)(2,1)} %param.9) | copy-start | bytes 3145732
  1.2 0.9 %copy-start.4 = (bf16[2,64,512]{2,1,0:T(8,128)(2,1)S(1)}, bf16[2,64,512]{2,1,0:T(8,128)(2,1)}, u32[]{:S(2)}) copy-start(bf16[2,64,512]{2,1,0:T(8,128)(2,1)} %param.10) | copy-start | bytes 393220
  2.1 44.5 %copy-start.3 = (bf16[2,64,4096]{2,1,0:T(8,128)(2,1)S(1)}, bf16[2,64,4096]{2,1,0:T(8,128)(2,1)}, u32[]{:S(2)}) copy-start(bf16[2,64,4096]{2,1,0:T(8,128)(2,1)} %param.9) | copy-start | bytes 3145732
  2.2 13.8 %collective-permute-start.1 = (bf16[2,8,4608]{2,1,0:T(8,128)(2,1)S(1)}, bf16[2,8,4608]{2,1,0:T(8,128)(2,1)S(1)}, u32[]{:S(2)}, u32[]{:S(2)}) collective-permute-start(bf16[2,8,4608]{2,1,0:T(8,128)(2,1)S(1)} %get-tuple-element.33), channel_id=1, source_target_pairs={{0,12},{2,14},{4,8},{6,10},{8,4},{10,6},{12,0},{14,2},{1,13},{3,15... | collective-permute-start | bytes 442376 | tf_op jit(solution)/shard_map/ppermute | solution.py:222
  7.3 9.7 %collective-permute-start = (bf16[2,8,4608]{2,1,0:T(8,128)(2,1)S(1)}, bf16[2,8,4608]{2,1,0:T(8,128)(2,1)S(1)}, u32[]{:S(2)}, u32[]{:S(2)}) collective-permute-start(bf16[2,8,4608]{2,1,0:T(8,128)(2,1)S(1)} %get-tuple-element.33), channel_id=1, source_target_pairs={{0,4},{2,6},{4,0},{6,2},{8,12},{10,14},{12,8},{14,10},{1,5},{3,7},... | collective-permute-start | bytes 442376 | tf_op jit(solution)/shard_map/ppermute | solution.py:222
  7.3 28.4 %collective-permute-start.5 = (bf16[2,8,4608]{2,1,0:T(8,128)(2,1)S(1)}, bf16[2,8,4608]{2,1,0:T(8,128)(2,1)S(1)}, u32[]{:S(2)}, u32[]{:S(2)}) collective-permute-start(bf16[2,8,4608]{2,1,0:T(8,128)(2,1)S(1)} %get-tuple-element.36), channel_id=1, source_target_pairs={{0,10},{2,8},{4,14},{6,12},{8,2},{10,0},{12,6},{14,4},{1,11},{3,9}... | collective-permute-start | bytes 442376 | tf_op jit(solution)/shard_map/ppermute | solution.py:222
  9.0 26.7 %collective-permute-start.2 = (bf16[2,8,4608]{2,1,0:T(8,128)(2,1)S(1)}, bf16[2,8,4608]{2,1,0:T(8,128)(2,1)S(1)}, u32[]{:S(2)}, u32[]{:S(2)}) collective-permute-start(bf16[2,8,4608]{2,1,0:T(8,128)(2,1)S(1)} %get-tuple-element.36), channel_id=1, source_target_pairs={{0,2},{2,0},{4,6},{6,4},{8,10},{10,8},{12,14},{14,12},{1,3},{3,1},... | collective-permute-start | bytes 442376 | tf_op jit(solution)/shard_map/ppermute | solution.py:222
  9.4 26.3 %collective-permute-start.6 = (bf16[2,8,4608]{2,1,0:T(8,128)(2,1)S(1)}, bf16[2,8,4608]{2,1,0:T(8,128)(2,1)S(1)}, u32[]{:S(2)}, u32[]{:S(2)}) collective-permute-start(bf16[2,8,4608]{2,1,0:T(8,128)(2,1)S(1)} %get-tuple-element.38), channel_id=1, source_target_pairs={{0,14},{2,12},{4,10},{6,8},{8,6},{10,4},{12,2},{14,0},{1,15},{3,13... | collective-permute-start | bytes 442376 | tf_op jit(solution)/shard_map/ppermute | solution.py:222
  16.0 19.8 %collective-permute-start.3 = (bf16[2,8,4608]{2,1,0:T(8,128)(2,1)S(1)}, bf16[2,8,4608]{2,1,0:T(8,128)(2,1)S(1)}, u32[]{:S(2)}, u32[]{:S(2)}) collective-permute-start(bf16[2,8,4608]{2,1,0:T(8,128)(2,1)S(1)} %get-tuple-element.38), channel_id=1, source_target_pairs={{0,6},{2,4},{4,2},{6,0},{8,14},{10,12},{12,10},{14,8},{1,7},{3,5},... | collective-permute-start | bytes 442376 | tf_op jit(solution)/shard_map/ppermute | solution.py:222
  17.0 18.7 %collective-permute-start.4 = (bf16[2,8,4608]{2,1,0:T(8,128)(2,1)S(1)}, bf16[2,8,4608]{2,1,0:T(8,128)(2,1)S(1)}, u32[]{:S(2)}, u32[]{:S(2)}) collective-permute-start(bf16[2,8,4608]{2,1,0:T(8,128)(2,1)S(1)} %get-tuple-element.35.rest_0_), channel_id=1, source_target_pairs={{0,8},{2,10},{4,12},{6,14},{8,0},{10,2},{12,4},{14,6},{1,9},{3,11}... | collective-permute-start | bytes 442376 | tf_op jit(solution)/shard_map/ppermute | solution.py:222
  36.6 10.0 %collective-permute-start.7 = (bf16[4,8,4608]{2,1,0:T(8,128)(2,1)S(1)}, bf16[4,8,4608]{2,1,0:T(8,128)(2,1)S(1)}, u32[]{:S(2)}, u32[]{:S(2)}) collective-permute-start(bf16[4,8,4608]{2,1,0:T(8,128)(2,1)S(1)} %get-tuple-element.40), channel_id=1, source_target_pairs={{0,4},{2,6},{4,0},{6,2},{8,12},{10,14},{12,8},{14,10},{16,20},{18,... | collective-permute-start | bytes 884744 | tf_op jit(solution)/shard_map/ppermute | solution.py:239
  36.7 20.0 %collective-permute-start.8 = (bf16[4,8,4608]{2,1,0:T(8,128)(2,1)S(1)}, bf16[4,8,4608]{2,1,0:T(8,128)(2,1)S(1)}, u32[]{:S(2)}, u32[]{:S(2)}) collective-permute-start(bf16[4,8,4608]{2,1,0:T(8,128)(2,1)S(1)} %get-tuple-element.42), channel_id=1, source_target_pairs={{0,2},{2,0},{4,6},{6,4},{8,10},{10,8},{12,14},{14,12},{16,18},{18,... | collective-permute-start | bytes 884744 | tf_op jit(solution)/shard_map/ppermute | solution.py:239
  38.3 19.8 %collective-permute-start.9 = (bf16[4,8,4608]{2,1,0:T(8,128)(2,1)S(1)}, bf16[4,8,4608]{2,1,0:T(8,128)(2,1)S(1)}, u32[]{:S(2)}, u32[]{:S(2)}) collective-permute-start(bf16[4,8,4608]{2,1,0:T(8,128)(2,1)S(1)} %get-tuple-element.43), channel_id=1, source_target_pairs={{0,16},{2,18},{4,20},{6,22},{8,24},{10,26},{12,28},{14,30},{16,0},... | collective-permute-start | bytes 884744 | tf_op jit(solution)/shard_map/ppermute | solution.py:239
  38.8 23.9 %collective-permute-start.11 = (bf16[4,8,4608]{2,1,0:T(8,128)(2,1)S(1)}, bf16[4,8,4608]{2,1,0:T(8,128)(2,1)S(1)}, u32[]{:S(2)}, u32[]{:S(2)}) collective-permute-start(bf16[4,8,4608]{2,1,0:T(8,128)(2,1)S(1)} %get-tuple-element.47), channel_id=1, source_target_pairs={{0,6},{2,4},{4,2},{6,0},{8,14},{10,12},{12,10},{14,8},{16,22},{18,... | collective-permute-start | bytes 884744 | tf_op jit(solution)/shard_map/ppermute | solution.py:239
  40.7 22.0 %collective-permute-start.12 = (bf16[4,8,4608]{2,1,0:T(8,128)(2,1)S(1)}, bf16[4,8,4608]{2,1,0:T(8,128)(2,1)S(1)}, u32[]{:S(2)}, u32[]{:S(2)}) collective-permute-start(bf16[4,8,4608]{2,1,0:T(8,128)(2,1)S(1)} %get-tuple-element.48), channel_id=1, source_target_pairs={{0,18},{2,16},{4,22},{6,20},{8,26},{10,24},{12,30},{14,28},{16,2},... | collective-permute-start | bytes 884744 | tf_op jit(solution)/shard_map/ppermute | solution.py:239
  46.7 16.1 %collective-permute-start.13 = (bf16[4,8,4608]{2,1,0:T(8,128)(2,1)S(1)}, bf16[4,8,4608]{2,1,0:T(8,128)(2,1)S(1)}, u32[]{:S(2)}, u32[]{:S(2)}) collective-permute-start(bf16[4,8,4608]{2,1,0:T(8,128)(2,1)S(1)} %get-tuple-element.49), channel_id=1, source_target_pairs={{0,20},{2,22},{4,16},{6,18},{8,28},{10,30},{12,24},{14,26},{16,4},... | collective-permute-start | bytes 884744 | tf_op jit(solution)/shard_map/ppermute | solution.py:239
  46.7 1.9 %copy-start = (bf16[4,96,4096]{2,1,0:T(8,128)(2,1)S(1)}, bf16[4,96,4096]{2,1,0:T(8,128)(2,1)}, u32[]{:S(2)}) copy-start(bf16[4,96,4096]{2,1,0:T(8,128)(2,1)} %acts_ref.1) | copy-start | bytes 9437188
  48.5 9.5 %copy-start.1 = (bf16[4,96,4096]{2,1,0:T(8,128)(2,1)S(1)}, bf16[4,96,4096]{2,1,0:T(8,128)(2,1)}, u32[]{:S(2)}) copy-start(bf16[4,96,4096]{2,1,0:T(8,128)(2,1)} %acts_ref.1) | copy-start | bytes 9437188
  56.7 8.5 %collective-permute-start.14 = (bf16[4,8,4608]{2,1,0:T(8,128)(2,1)S(1)}, bf16[4,8,4608]{2,1,0:T(8,128)(2,1)S(1)}, u32[]{:S(2)}, u32[]{:S(2)}) collective-permute-start(bf16[4,8,4608]{2,1,0:T(8,128)(2,1)S(1)} %get-tuple-element.50), channel_id=1, source_target_pairs={{0,22},{2,20},{4,18},{6,16},{8,30},{10,28},{12,26},{14,24},{16,6},... | collective-permute-start | bytes 884744 | tf_op jit(solution)/shard_map/ppermute | solution.py:239
  58.1 3.8 %collective-permute-start.10 = (f32[384,640]{1,0:T(8,128)S(1)}, f32[384,640]{1,0:T(8,128)S(1)}, u32[]{:S(2)}, u32[]{:S(2)}) collective-permute-start(f32[384,640]{1,0:T(8,128)S(1)} %shard_map.75.send_ref), channel_id=1, source_target_pairs={{0,1},{1,0},{2,3},{3,2},{4,5},{5,4},{6,7},{7,6},{8,9},{9,8},{10,11... | collective-permute-start | bytes 2949128 | tf_op jit(solution)/shard_map/ppermute | solution.py:246
  58.1 3.8 %copy-start.5 = (bf16[2,64,512]{2,1,0:T(8,128)(2,1)S(1)}, bf16[2,64,512]{2,1,0:T(8,128)(2,1)}, u32[]{:S(2)}) copy-start(bf16[2,64,512]{2,1,0:T(8,128)(2,1)} %param.10) | copy-start | bytes 393220
  58.1 3.8 %copy-start.6 = (s32[4,6]{1,0:T(4,128)S(1)}, s32[4,6]{1,0:T(4,128)}, u32[]{:S(2)}) copy-start(s32[4,6]{1,0:T(4,128)} %slots_ref.1) | copy-start | bytes 292
  66.4 1.4 %collective-permute-start.15 = (f32[192,128]{1,0:T(8,128)S(1)}, f32[192,128]{1,0:T(8,128)S(1)}, u32[]{:S(2)}, u32[]{:S(2)}) collective-permute-start(f32[192,128]{1,0:T(8,128)S(1)} %shard_map.78.partial_ref), channel_id=1, source_target_pairs={{0,1},{1,0},{2,3},{3,2},{4,5},{5,4},{6,7},{7,6},{8,9},{9,8},{10,11... | collective-permute-start | bytes 294920 | tf_op jit(solution)/shard_map/ppermute | solution.py:258
